TPU v7x, 512 devices: a whole 4x8x8 slice. The times are simulated.
512 devices in a mesh: adapter: 64 (over z, y), tensor: 8 (over x, core).
Axes of the slice: x: 4, y: 8, z: 8, core: 2. Of those that a mesh axis runs over, the one named last changes fastest.
Arguments:
- tokens: bfloat16 [49152, 8192], P('adapter', 'tensor'), may hold values from -6 to 6
- value_weight: bfloat16 [8192, 1024], P('tensor'), may hold values from -0.0625 to 0.0625
- adapter_down: bfloat16 [512, 64, 8192], P('adapter', None, 'tensor'), may hold values from -0.0625 to 0.0625
- adapter_up_weight: bfloat16 [512, 64, 1024], P('adapter', None, 'tensor'), may hold values from -0.75 to 0.75
- adapter_ids: int32 [49152, 1], P('adapter'), may hold values from 0 to 511, as said below
Outputs:
- values: bfloat16 [49152, 1024], P('adapter', 'tensor')
Inputs may be any that keep to these rules, and one draw needn't show every extreme that they name: `adapter_ids`: adapter e is held by index e // 8 of adapter. Among the 768 tokens of one index of adapter (aligned blocks), no adapter id appears more than 3 times; in every block, all 8 adapters held by some one index of adapter each appear exactly 3 times; every adapter is used by some token.
All inputs are finite; a program needn't handle non-finite values.
Results may differ from a plain program's by a relative error of at most 0.017.
Values may be sent and summed in bfloat16 or wider, within the bound.
No kernel may reach another device: no remote copies, remote signals or barrier semaphores. Data moves between devices by JAX's collectives and lax.ppermute only.
A program may use at most 64 MiB of HBM per device.

v0:
```python
import jax
import jax.numpy as jnp
from jax import lax
from jax.sharding import Mesh
from jax.sharding import PartitionSpec as P

TENSOR = ("tensor_0", "tensor_1")


adapter_output_scale = 2.0


def cut_along(x, dim, size):
    before, after = (x.shape[:dim], x.shape[dim + 1 :])
    return jnp.moveaxis(x.reshape(*before, size, -1, *after), dim, 0)


def sent_and_summed(x, axis, dim):
    pieces = cut_along(x, dim, lax.axis_size(axis))
    arrived = lax.all_to_all(pieces, axis, split_axis=0, concat_axis=0, tiled=True)
    return arrived.astype(jnp.float32).sum(axis=0)


def whole_of(x, axes, dim):
    for axis in reversed(axes):
        x = lax.all_gather(x, axis, axis=dim, tiled=True)
    return x


def per_device(tokens, value_weight, adapter_down, adapter_up_weight, adapter_ids):
    owning_devices = lax.axis_size("adapter")
    resident_adapters = adapter_down.shape[0]
    tok_rows = tokens.shape[0]
    width_part = tokens.shape[1]
    output_portion = adapter_up_weight.shape[2]
    adapters = owning_devices * resident_adapters
    adapter_positions = max(2, 2 * tok_rows // adapters)
    ids = adapter_ids[:, 0]
    same = ids[:, None] == ids[None, :]
    lower = lax.broadcasted_iota(jnp.int32, (tok_rows, tok_rows), 0) > lax.broadcasted_iota(
        jnp.int32, (tok_rows, tok_rows), 1
    )
    slot_of = jnp.sum((same & lower).astype(jnp.int32), axis=1)
    position = (
        ids % resident_adapters * owning_devices + ids // resident_adapters
    ) * adapter_positions + slot_of
    partial_value = jnp.dot(tokens, value_weight, preferred_element_type=jnp.float32)
    base = sent_and_summed(partial_value.astype(jnp.bfloat16), TENSOR, 1)
    outgoing = (
        jnp.zeros(
            (resident_adapters * owning_devices * adapter_positions, width_part), tokens.dtype
        )
        .at[position]
        .set(tokens)
    )
    outgoing = outgoing.reshape(resident_adapters, owning_devices, adapter_positions, width_part)
    arrived = lax.all_to_all(outgoing, "adapter", split_axis=1, concat_axis=1, tiled=True)
    arrived = arrived.reshape(resident_adapters, owning_devices * adapter_positions, width_part)
    low_part = jnp.einsum("erd,esd->ers", adapter_down, arrived, preferred_element_type=jnp.float32)
    share = sent_and_summed(low_part.astype(jnp.bfloat16), TENSOR, 2).astype(jnp.bfloat16)
    rank_activations = whole_of(share, TENSOR, 2)
    adapter_contribution = jnp.einsum(
        "ers,erk->esk", rank_activations, adapter_up_weight, preferred_element_type=jnp.float32
    )
    adapter_contribution = (
        (adapter_output_scale * adapter_contribution)
        .astype(jnp.bfloat16)
        .reshape(resident_adapters, owning_devices, adapter_positions, output_portion)
    )
    back = lax.all_to_all(adapter_contribution, "adapter", split_axis=1, concat_axis=1, tiled=True)
    mine = back.reshape(resident_adapters * owning_devices * adapter_positions, output_portion)[
        position
    ]
    return (base + mine.astype(jnp.float32)).astype(jnp.bfloat16)


def solution(mesh):
    torus = Mesh(
        mesh.devices.reshape(mesh.shape["adapter"], 4, 2), ("adapter", "tensor_0", "tensor_1")
    )
    return jax.shard_map(
        per_device,
        mesh=torus,
        in_specs=(
            P("adapter", TENSOR),
            P(TENSOR, None),
            P("adapter", None, TENSOR),
            P("adapter", None, TENSOR),
            P("adapter", None),
        ),
        out_specs=P("adapter", TENSOR),
        check_vma=False,
    )
```

profile of v0, /device:TPU:8, one launch (start us, length us, event | category | flops | bytes accessed | tf_op | source)
XLA Modules:
  0.0 195.2 jit_solution(9645659341229189798)
XLA Ops:
  0.0 0.0 copy-start
  0.0 0.8 reduce.1
  0.9 0.4 convert_reduce_fusion.1
  1.2 0.7 fusion.13
  1.9 8.5 %scatter_custom_fusion = bf16[1536,1024]{1,0:T(8,128)(2,1)} fusion(s32[768]{0:T(1024)S(1)} %fusion.13, bf16[768,1024]{1,0:T(8,128)(2,1)} %param.5, bf16[]{:T(256)} %constant.32.clone.1), kind=kCustom, calls=%fused_computation.10 | custom fusion | bytes 3146240 | tf_op jit(solution)/shard_map/scatter | solution.py:54
  10.5 9.1 %reshape.21 = bf16[8,64,3,1024]{3,2,1,0:T(4,128)(2,1)} reshape(bf16[1536,1024]{1,0:T(8,128)(2,1)} %scatter_custom_fusion) | data formatting | bytes 6291456 | tf_op jit(solution)/shard_map/reshape | solution.py:56
  19.6 5.5 %copy.19 = bf16[8,64,3,1024]{3,0,2,1:T(8,128)(2,1)S(1)} copy(bf16[8,64,3,1024]{3,2,1,0:T(4,128)(2,1)} %reshape.21) | data formatting | bytes 6291456 | tf_op jit(solution)/shard_map/reshape | solution.py:56
  25.1 0.0 copy-start.2
  25.1 91.6 %all_to_all.20 = bf16[8,64,3,1024]{3,0,2,1:T(8,128)(2,1)S(1)} all-to-all(bf16[8,64,3,1024]{3,0,2,1:T(8,128)(2,1)S(1)} %copy.19), channel_id=1, replica_groups=mesh['adapter'=64,'tensor_0'=4,'tensor_1'=2] {'adapter'}, dimensions={1} | all-to-all | bytes 6291456 | tf_op jit(solution)/shard_map/all_to_all | solution.py:57
  116.7 0.0 copy-done.2
  116.7 1.9 fusion.10
  118.6 0.2 copy.21
  118.9 1.0 reshape.46
  119.9 4.3 %all-to-all-start.2 = ((bf16[8,2,6144]{2,1,0:T(2,128)(2,1)}), bf16[8,2,6144]{2,1,0:T(2,128)(2,1)S(1)}, u32[]{:S(2)}, u32[]{:S(2)}) async-start(bf16[8,2,6144]{2,1,0:T(2,128)(2,1)} %reshape.46), calls=%async_computation.2 | async-start | bytes 393216 | tf_op jit(solution)/shard_map/all_to_all | solution.py:20
  124.2 0.0 copy-done
  124.2 3.2 %fusion.5 = bf16[96,8,8,128]{3,2,1,0:T(8,128)(2,1)S(1)} fusion(bf16[768,1024]{1,0:T(8,128)(2,1)} %param.5, bf16[1024,1024]{1,0:T(8,128)(2,1)S(1)} %copy-done), kind=kOutput, calls=%fused_computation.12 | convolution fusion | flops 1611399168 | bytes 5242880 | tf_op jit(solution)/shard_map/dot_general | solution.py:47
  127.4 1.4 copy.34
  128.9 2.2 %all-to-all-done.2 = bf16[8,2,6144]{2,1,0:T(2,128)(2,1)S(1)} async-done(((bf16[8,2,6144]{2,1,0:T(2,128)(2,1)}), bf16[8,2,6144]{2,1,0:T(2,128)(2,1)S(1)}, u32[]{:S(2)}, u32[]{:S(2)}) %all-to-all-start.2) | async-done | bytes 196640 | tf_op jit(solution)/shard_map/all_to_all | solution.py:20
  131.0 0.0 copy-start.1
  131.0 4.4 %all-to-all-start = ((bf16[8,768,128]{2,1,0:T(8,128)(2,1)}), bf16[8,768,128]{2,1,0:T(8,128)(2,1)}, u32[]{:S(2)}, u32[]{:S(2)}) async-start(bf16[8,768,128]{2,1,0:T(8,128)(2,1)} %bitcast.25), calls=%async_computation | async-start | bytes 3145728 | tf_op jit(solution)/shard_map/all_to_all | solution.py:20
  135.4 0.3 reshape.47
  135.7 0.1 bitcast_reduce_fusion
  135.8 1.9 all_gather.6
  137.7 26.8 %all_gather.7 = bf16[8,64,192]{1,2,0:T(8,128)(2,1)S(1)} all-gather(bf16[8,64,48]{1,2,0:T(8,128)(2,1)S(1)} %all_gather.6), channel_id=1, replica_groups=mesh['adapter'=64,'tensor_0'=4,'tensor_1'=2] {'tensor_0'}, dimensions={2}, use_global_device_ids=true | all-gather | bytes 245760 | tf_op jit(solution)/shard_map/all_gather | solution.py:26
  164.5 0.0 copy-done.1
  164.5 0.2 fusion.6
  164.7 1.0 copy.23
  165.7 0.0 all-to-all-done
  165.7 11.6 %all-to-all-start.3 = ((bf16[8,64,3,128]{3,0,2,1:T(8,128)(2,1)}), bf16[8,64,3,128]{3,0,2,1:T(8,128)(2,1)S(1)}, u32[]{:S(2)}, u32[]{:S(2)}) async-start(bf16[8,64,3,128]{3,0,2,1:T(8,128)(2,1)} %bitcast.5), calls=%async_computation.3 | async-start | bytes 786432 | tf_op jit(solution)/shard_map/all_to_all | solution.py:70
  177.4 1.7 convert_reduce_fusion
  179.0 13.0 %all-to-all-done.3 = bf16[8,64,3,128]{3,0,2,1:T(8,128)(2,1)S(1)} async-done(((bf16[8,64,3,128]{3,0,2,1:T(8,128)(2,1)}), bf16[8,64,3,128]{3,0,2,1:T(8,128)(2,1)S(1)}, u32[]{:S(2)}, u32[]{:S(2)}) %all-to-all-start.3) | async-done | bytes 393248 | tf_op jit(solution)/shard_map/all_to_all | solution.py:70
  192.0 0.2 copy.24
  192.2 0.3 reshape.25
  192.6 1.9 gather_fusion
  194.4 0.7 add_convert_fusion
  (2 shorter events, 0.1 us)
Async XLA Ops:
  0.0 124.2 %copy-start = (bf16[1024,1024]{1,0:T(8,128)(2,1)S(1)}, bf16[1024,1024]{1,0:T(8,128)(2,1)}, u32[]{:S(2)}) copy-start(bf16[1024,1024]{1,0:T(8,128)(2,1)} %param.6) | copy-start | bytes 6291460
  25.1 91.6 %copy-start.2 = (bf16[8,64,1024]{2,1,0:T(8,128)(2,1)S(1)}, bf16[8,64,1024]{2,1,0:T(8,128)(2,1)}, u32[]{:S(2)}) copy-start(bf16[8,64,1024]{2,1,0:T(8,128)(2,1)} %param.7) | copy-start | bytes 3145732
  119.9 11.1 %all-to-all-start.2 = ((bf16[8,2,6144]{2,1,0:T(2,128)(2,1)}), bf16[8,2,6144]{2,1,0:T(2,128)(2,1)S(1)}, u32[]{:S(2)}, u32[]{:S(2)}) async-start(bf16[8,2,6144]{2,1,0:T(2,128)(2,1)} %reshape.46), calls=%async_computation.2 | async-start | bytes 393216 | tf_op jit(solution)/shard_map/all_to_all | solution.py:20
  131.0 33.5 %copy-start.1 = (bf16[8,64,128]{2,1,0:T(8,128)(2,1)S(1)}, bf16[8,64,128]{2,1,0:T(8,128)(2,1)}, u32[]{:S(2)}) copy-start(bf16[8,64,128]{2,1,0:T(8,128)(2,1)} %param.8) | copy-start | bytes 393220
  131.0 34.7 %all-to-all-start = ((bf16[8,768,128]{2,1,0:T(8,128)(2,1)}), bf16[8,768,128]{2,1,0:T(8,128)(2,1)}, u32[]{:S(2)}, u32[]{:S(2)}) async-start(bf16[8,768,128]{2,1,0:T(8,128)(2,1)} %bitcast.25), calls=%async_computation | async-start | bytes 3145728 | tf_op jit(solution)/shard_map/all_to_all | solution.py:20
  165.7 26.3 %all-to-all-start.3 = ((bf16[8,64,3,128]{3,0,2,1:T(8,128)(2,1)}), bf16[8,64,3,128]{3,0,2,1:T(8,128)(2,1)S(1)}, u32[]{:S(2)}, u32[]{:S(2)}) async-start(bf16[8,64,3,128]{3,0,2,1:T(8,128)(2,1)} %bitcast.5), calls=%async_computation.3 | async-start | bytes 786432 | tf_op jit(solution)/shard_map/all_to_all | solution.py:70
where the time goes:
time: 196 us; the launch traced here: 195 us
  blocking collectives  120 us (61%)
  local copies, waits for them, and re-layouts  29.5 us (15%)
  starting transfers between devices  20.3 us (10%)
  waiting for transfers between devices  15.2 us (8%)
  matrix products  5.35 us (3%)
  other arithmetic  4.4 us (2%)
    all_to_all x1, blocking collectives, per_device(): lax.all_to_all(outgoing, 'adapter', split_axis=1, concat_axis=1, tiled=True)  91.6 us
    all_gather x2, blocking collectives, whole_of(): x = lax.all_gather(x, axis, axis=dim, tiled=True)  28.7 us
    reshape x2, local copies, waits for them, and re-layouts, per_device(): outgoing.reshape(resident_adapters, owning_devices, adapter_positions, wi...  14.6 us
    all_to_all x1, waiting for transfers between devices, per_device(): lax.all_to_all(adapter_contribution, 'adapter', split_axis=1, concat_axis...  13 us
    all_to_all x1, starting transfers between devices, per_device(): lax.all_to_all(adapter_contribution, 'adapter', split_axis=1, concat_axis...  11.6 us
    all_to_all x2, starting transfers between devices, sent_and_summed(): lax.all_to_all(pieces, axis, split_axis=0, concat_axis=0, tiled=True)  8.72 us
    scatter x1, local copies, waits for them, and re-layouts, per_device(): outgoing = jnp.zeros((resident_adapters * owning_devices * adapter_positi...  8.53 us
  transfers between devices with their start and end apart: 3, of which 2 were waited for; matrix products, arithmetic and copies ran while one was open for 4% of the time, Pallas kernels for 0%

commit v1 on v0

v1 whole, which is shorter than its diff:
```python
import jax
import jax.numpy as jnp
from jax import lax
from jax.experimental import pallas as pl
from jax.experimental.pallas import tpu as pltpu
from jax.sharding import Mesh
from jax.sharding import PartitionSpec as P

TENSOR = ("tensor_0", "tensor_1")
MOST = 3

adapter_output_scale = 2.0


def swap(x, axes):
    return lax.all_to_all(x, axes, split_axis=0, concat_axis=0, tiled=True)


def place_rows(ids_row, ids_col, tokens, slots):
    rows, width = tokens.shape
    tile = 256

    def kernel(row_ref, col_ref, tok_ref, out_ref, at_col_ref, at_row_ref):
        @pl.when(pl.program_id(0) == 0)
        def _():
            row = row_ref[...]
            col = col_ref[...]
            same = row == col
            i = lax.broadcasted_iota(jnp.int32, (rows, rows), 0)
            j = lax.broadcasted_iota(jnp.int32, (rows, rows), 1)
            before_row = jnp.sum(jnp.where(same & (i < j), 1, 0), axis=0, keepdims=True)
            before_col = jnp.sum(jnp.where(same & (j < i), 1, 0), axis=1, keepdims=True)
            at_row_ref[...] = row * MOST + before_row
            at_col_ref[...] = col * MOST + before_col

        first = pl.program_id(0) * tile
        slot = lax.broadcasted_iota(jnp.int32, (tile, rows), 0) + first
        pick = jnp.where(slot == at_row_ref[...], 1.0, 0.0).astype(jnp.bfloat16)
        out_ref[...] = jnp.dot(pick, tok_ref[...], preferred_element_type=jnp.float32).astype(
            jnp.bfloat16
        )

    return pl.pallas_call(
        kernel,
        grid=(slots // tile,),
        in_specs=[
            pl.BlockSpec((1, rows), lambda i: (0, 0)),
            pl.BlockSpec((rows, 1), lambda i: (0, 0)),
            pl.BlockSpec((rows, width), lambda i: (0, 0)),
        ],
        out_specs=[
            pl.BlockSpec((tile, width), lambda i: (i, 0)),
            pl.BlockSpec((rows, 1), lambda i: (0, 0)),
        ],
        out_shape=[
            jax.ShapeDtypeStruct((slots, width), tokens.dtype),
            jax.ShapeDtypeStruct((rows, 1), jnp.int32),
        ],
        scratch_shapes=[pltpu.VMEM((1, rows), jnp.int32)],
        name="place_rows",
    )(ids_row, ids_col, tokens)


def value_pieces(tokens, weight, pieces):
    rows, width = tokens.shape
    cols = weight.shape[1] // pieces
    step = 2

    def kernel(tok_ref, w_ref, out_ref):
        part = jnp.dot(tok_ref[...], w_ref[...], preferred_element_type=jnp.float32)
        part = part.astype(jnp.bfloat16)
        for k in range(step):
            out_ref[k] = part[:, k * cols : (k + 1) * cols]

    return pl.pallas_call(
        kernel,
        grid=(pieces // step,),
        in_specs=[
            pl.BlockSpec((rows, width), lambda i: (0, 0)),
            pl.BlockSpec((width, step * cols), lambda i: (0, i)),
        ],
        out_specs=pl.BlockSpec((step, rows, cols), lambda i: (i, 0, 0)),
        out_shape=jax.ShapeDtypeStruct((pieces, rows, cols), jnp.bfloat16),
        name="value_pieces",
    )(tokens, weight)


def adapter_of(shape, first, group):
    slot = lax.broadcasted_iota(jnp.int32, shape, 0) + first
    return slot % group // MOST


def down_rows(arrived, down):
    slots, width = arrived.shape
    here, rank, _ = down.shape
    group = here * MOST
    half = slots // 2
    tile = 192
    pair = 2 * rank

    def kernel(lo_ref, hi_ref, down_ref, out_ref):
        weight = down_ref[...].reshape(here * rank, width)
        lane = lax.broadcasted_iota(jnp.int32, (tile, pair), 1)

        def rows_of(ref):
            full = lax.dot_general(
                ref[...], weight, (((1,), (1,)), ((), ())), preferred_element_type=jnp.float32
            )
            mine = adapter_of((tile, pair), 0, group)
            kept = jnp.zeros((tile, pair), jnp.float32)
            for k in range(here // 2):
                holder = jnp.where(lane < rank, 2 * k, 2 * k + 1)
                kept = kept + jnp.where(mine == holder, full[:, k * pair : (k + 1) * pair], 0.0)
            return kept + pltpu.roll(kept, rank, 1)

        out_ref[...] = jnp.where(lane < rank, rows_of(lo_ref), rows_of(hi_ref)).astype(
            jnp.bfloat16
        )

    steps = half // tile
    return pl.pallas_call(
        kernel,
        grid=(steps,),
        in_specs=[
            pl.BlockSpec((tile, width), lambda i: (i, 0)),
            pl.BlockSpec((tile, width), lambda i: (i + steps, 0)),
            pl.BlockSpec((here, rank, width), lambda i: (0, 0, 0)),
        ],
        out_specs=pl.BlockSpec((tile, pair), lambda i: (i, 0)),
        out_shape=jax.ShapeDtypeStruct((half, pair), jnp.bfloat16),
        name="down_rows",
    )(arrived, arrived, down)


def up_rows(low, up):
    half, pair = low.shape
    here, rank, cols = up.shape
    group = here * MOST

    def kernel(low_ref, up_ref, out_ref):
        weight = up_ref[...].reshape(here * rank, cols)
        low_wide = low_ref[...].astype(jnp.float32)
        turned = pltpu.roll(low_wide, rank, 1)
        lane = lax.broadcasted_iota(jnp.int32, (half, pair), 1)
        mine = adapter_of((half, pair), 0, group)
        for h in range(2):
            own = (lane < rank) == (h == 0)
            both = jnp.where(own, low_wide, turned)
            spread = []
            for k in range(here // 2):
                holder = jnp.where(lane < rank, 2 * k, 2 * k + 1)
                spread.append(jnp.where(mine == holder, both, 0.0).astype(jnp.bfloat16))
            acc = jnp.dot(
                jnp.concatenate(spread, axis=1), weight, preferred_element_type=jnp.float32
            )
            out_ref[h * half : (h + 1) * half, :] = (adapter_output_scale * acc).astype(
                jnp.bfloat16
            )

    return pl.pallas_call(
        kernel,
        out_shape=jax.ShapeDtypeStruct((2 * half, cols), jnp.bfloat16),
        name="up_rows",
    )(low, up)


def take_rows(at_col, back, base):
    rows, cols = base.shape
    slots = back.shape[0]

    def kernel(at_ref, back_ref, base_ref, out_ref):
        slot = lax.broadcasted_iota(jnp.int32, (rows, slots), 1)
        pick = jnp.where(slot == at_ref[...], 1.0, 0.0).astype(jnp.bfloat16)
        mine = jnp.dot(pick, back_ref[...], preferred_element_type=jnp.float32)
        out_ref[...] = (base_ref[...] + mine).astype(jnp.bfloat16)

    return pl.pallas_call(
        kernel,
        out_shape=jax.ShapeDtypeStruct((rows, cols), jnp.bfloat16),
        name="take_rows",
    )(at_col, back, base)


def per_device(tokens, value_weight, adapter_down, adapter_up_weight, adapter_ids):
    owners = lax.axis_size("adapter")
    groups = lax.axis_size(TENSOR)
    here, rank, _ = adapter_down.shape
    rows, width = tokens.shape
    cols = adapter_up_weight.shape[2]
    share = here * MOST
    slots = owners * share

    placed, at_col = place_rows(adapter_ids.reshape(1, rows), adapter_ids, tokens, slots)
    pieces = value_pieces(tokens, value_weight, groups)
    arrived_base = swap(pieces, TENSOR)
    arrived = swap(placed.reshape(owners, share, width), "adapter").reshape(slots, width)

    low_part = down_rows(arrived, adapter_down)
    low_sum = swap(low_part.reshape(groups, -1, 2 * rank), TENSOR)
    low_share = low_sum.astype(jnp.float32).sum(axis=0).astype(jnp.bfloat16)
    low = lax.all_gather(low_share, TENSOR[1], axis=0, tiled=True)
    low = lax.all_gather(low, TENSOR[0], axis=0, tiled=True)

    delta = up_rows(low, adapter_up_weight)
    back = swap(delta.reshape(owners, share, cols), "adapter").reshape(slots, cols)
    base = arrived_base.astype(jnp.float32).sum(axis=0)
    return take_rows(at_col, back, base)


def solution(mesh):
    torus = Mesh(
        mesh.devices.reshape(mesh.shape["adapter"], 4, 2), ("adapter", "tensor_0", "tensor_1")
    )
    return jax.shard_map(
        per_device,
        mesh=torus,
        in_specs=(
            P("adapter", TENSOR),
            P(TENSOR, None),
            P("adapter", None, TENSOR),
            P("adapter", None, TENSOR),
            P("adapter", None),
        ),
        out_specs=P("adapter", TENSOR),
        check_vma=False,
    )
```

time: 196 us -> 182 us (0.929)
  local copies, waits for them, and re-layouts: 29.5 us -> 2.36 us
  Pallas kernels: 0 us -> 23.6 us
  matrix products: 5.35 us -> 0 us
  other arithmetic: 4.4 us -> 1.01 us
    pallas_call x0 -> x5, Pallas kernels: none -> 23.6 us  [the longest x1 6.85 us: place_rows(): pl.pallas_call(kernel, grid=(slots // tile,), in_specs=[pl.BlockSpec((1,...]
    reshape x4 -> x0, local copies, waits for them, and re-layouts: 16.4 us -> none  [the longest x2 14.6 us: per_device(): outgoing.reshape(resident_adapters, owning_devices, adapter_positions, wi...]
    scatter x1 -> x0, local copies, waits for them, and re-layouts: 8.53 us -> none  [per_device(): outgoing = jnp.zeros((resident_adapters * owning_devices * adapter_positi...]
    dot_general x3 -> x0, matrix products: 5.35 us -> none  [the longest x1 3.2 us: per_device(): jnp.dot(tokens, value_weight, preferred_element_type=jnp.float32)]
  transfers between devices with their start and end apart: 3 -> 3, of which waited for: 2 -> 2; matrix products, arithmetic and copies ran while one was open for 4% -> 1% of each run, Pallas kernels for 0% -> 4%
where the time goes in v1:
time: 182 us; the launch traced here: 181 us
  blocking collectives  120 us (66%)
  Pallas kernels  23.6 us (13%)
  starting transfers between devices  19.4 us (11%)
  waiting for transfers between devices  14.7 us (8%)
  local copies, waits for them, and re-layouts  2.36 us (1%)
    all_to_all x1, blocking collectives, swap(): return lax.all_to_all(x, axes, split_axis=0, concat_axis=0, tiled=True)  91.8 us
    all_gather x1, blocking collectives, per_device(): low = lax.all_gather(low, TENSOR[0], axis=0, tiled=True)  26.6 us
    all_to_all x3, starting transfers between devices, swap(): return lax.all_to_all(x, axes, split_axis=0, concat_axis=0, tiled=True)  19.4 us
    all_to_all x3, waiting for transfers between devices, swap(): return lax.all_to_all(x, axes, split_axis=0, concat_axis=0, tiled=True)  14.7 us
    pallas_call x1, Pallas kernels, place_rows(): pl.pallas_call(kernel, grid=(slots // tile,), in_specs=[pl.BlockSpec((1,...  6.85 us
    pallas_call x1, Pallas kernels, down_rows(): pl.pallas_call(kernel, grid=(steps,), in_specs=[pl.BlockSpec((tile, width...  6.08 us
    pallas_call x1, Pallas kernels, value_pieces(): pl.pallas_call(kernel, grid=(pieces // step,), in_specs=[pl.BlockSpec((ro...  5.34 us
  transfers between devices with their start and end apart: 3, of which 2 were waited for; matrix products, arithmetic and copies ran while one was open for 1% of the time, Pallas kernels for 4%

profile of v1, /device:TPU:8, one launch (start us, length us, event | category | flops | bytes accessed | tf_op | source)
XLA Modules:
  0.0 181.4 jit_solution(1553285262163603023)
XLA Ops:
  0.0 1.6 copy.6.col_ref
  1.6 6.8 %place_rows.1 = (bf16[1536,1024]{1,0:T(8,128)(2,1)}, s32[768,1]{1,0:T(8,128)}) custom-call(s32[1,768]{1,0:T(1,128)} %bitcast.12, s32[768,1]{1,0:T(8,128)} %copy.6.col_ref, bf16[768,1024]{1,0:T(8,128)(2,1)} %tok_ref.3), custom_call_target="tpu_custom_call" | custom-call | tf_op jit(solution)/shard_map/place_rows/pallas_call | solution.py:43
  8.5 91.8 %all_to_all.20 = bf16[64,24,1024]{2,1,0:T(8,128)(2,1)} all-to-all(bf16[64,24,1024]{2,1,0:T(8,128)(2,1)} %bitcast.8), channel_id=1, replica_groups=mesh['adapter'=64,'tensor_0'=4,'tensor_1'=2] {'adapter'}, dimensions={0} | all-to-all | bytes 6291456 | tf_op jit(solution)/shard_map/all_to_all | solution.py:16
  100.2 6.1 %down_rows.1 = bf16[768,128]{1,0:T(8,128)(2,1)} custom-call(bf16[1536,1024]{1,0:T(8,128)(2,1)} %bitcast.6, bf16[1536,1024]{1,0:T(8,128)(2,1)} %bitcast.7, bf16[8,64,1024]{2,1,0:T(8,128)(2,1)} %down_ref.1), custom_call_target="tpu_custom_call" | custom-call | tf_op jit(solution)/shard_map/down_rows/pallas_call | solution.py:121
  106.3 4.3 %all-to-all-start.1 = ((bf16[8,96,128]{2,1,0:T(8,128)(2,1)}), bf16[8,96,128]{2,1,0:T(8,128)(2,1)S(1)}, u32[]{:S(2)}, u32[]{:S(2)}) async-start(bf16[8,96,128]{2,1,0:T(8,128)(2,1)} %bitcast.11), calls=%async_computation.1 | async-start | bytes 393216 | tf_op jit(solution)/shard_map/all_to_all | solution.py:16
  110.6 5.3 %value_pieces.1 = bf16[8,768,128]{2,1,0:T(8,128)(2,1)} custom-call(bf16[768,1024]{1,0:T(8,128)(2,1)} %tok_ref.3, bf16[1024,1024]{1,0:T(8,128)(2,1)} %w_ref.1), custom_call_target="tpu_custom_call" | custom-call | tf_op jit(solution)/shard_map/value_pieces/pallas_call | solution.py:75
  115.9 1.5 all-to-all-done.1
  117.4 3.6 %all-to-all-start.3 = ((bf16[8,768,128]{2,1,0:T(8,128)(2,1)}), bf16[8,768,128]{2,1,0:T(8,128)(2,1)S(1)}, u32[]{:S(2)}, u32[]{:S(2)}) async-start(bf16[8,768,128]{2,1,0:T(8,128)(2,1)} %value_pieces.1), calls=%async_computation.3 | async-start | bytes 3145728 | tf_op jit(solution)/shard_map/all_to_all | solution.py:16
  121.0 1.9 %all_gather.6 = bf16[192,128]{1,0:T(8,128)(2,1)S(1)} all-gather(bf16[96,128]{1,0:T(8,128)(2,1)S(1)} %reduce_sum.21), channel_id=1, replica_groups=mesh['adapter'=64,'tensor_0'=4,'tensor_1'=2] {'tensor_1'}, dimensions={0}, use_global_device_ids=true | all-gather | bytes 73728 | tf_op jit(solution)/shard_map/all_gather | solution.py:201
  122.9 26.6 %all_gather.7.low_ref = bf16[768,128]{1,0:T(8,128)(2,1)} all-gather(bf16[192,128]{1,0:T(8,128)(2,1)S(1)} %all_gather.6), channel_id=1, replica_groups=mesh['adapter'=64,'tensor_0'=4,'tensor_1'=2] {'tensor_0'}, dimensions={0}, use_global_device_ids=true | all-gather | bytes 245760 | tf_op jit(solution)/shard_map/all_gather | solution.py:202
  149.5 2.6 %up_rows.1 = bf16[1536,128]{1,0:T(8,128)(2,1)} custom-call(bf16[768,128]{1,0:T(8,128)(2,1)} %all_gather.7.low_ref, bf16[8,64,128]{2,1,0:T(8,128)(2,1)} %up_ref.1), custom_call_target="tpu_custom_call" | custom-call | tf_op jit(solution)/shard_map/up_rows/pallas_call | solution.py:160
  152.2 0.0 all-to-all-done.3
  152.2 11.5 %all-to-all-start.2 = ((bf16[64,24,128]{2,1,0:T(8,128)(2,1)}), bf16[64,24,128]{2,1,0:T(8,128)(2,1)S(1)}, u32[]{:S(2)}, u32[]{:S(2)}) async-start(bf16[64,24,128]{2,1,0:T(8,128)(2,1)} %bitcast.10), calls=%async_computation.2 | async-start | bytes 786432 | tf_op jit(solution)/shard_map/all_to_all | solution.py:16
  163.7 1.0 convert_reduce_fusion.base_ref
  164.6 13.2 %all-to-all-done.2 = bf16[64,24,128]{2,1,0:T(8,128)(2,1)S(1)} async-done(((bf16[64,24,128]{2,1,0:T(8,128)(2,1)}), bf16[64,24,128]{2,1,0:T(8,128)(2,1)S(1)}, u32[]{:S(2)}, u32[]{:S(2)}) %all-to-all-start.2) | async-done | bytes 393248 | tf_op jit(solution)/shard_map/all_to_all | solution.py:16
  177.9 0.0 copy-start
  177.9 0.7 copy-done
  178.6 2.7 %take_rows.1 = bf16[768,128]{1,0:T(8,128)(2,1)} custom-call(s32[768,1]{1,0:T(8,128)} %get-tuple-element.7.at_ref, bf16[1536,128]{1,0:T(8,128)(2,1)} %bitcast.9, f32[768,128]{1,0:T(8,128)} %convert_reduce_fusion.base_ref), custom_call_target="tpu_custom_call" | custom-call | tf_op jit(solution)/shard_map/take_rows/pallas_call | solution.py:177
  (1 shorter events, 0.0 us)
Async XLA Ops:
  106.3 11.1 %all-to-all-start.1 = ((bf16[8,96,128]{2,1,0:T(8,128)(2,1)}), bf16[8,96,128]{2,1,0:T(8,128)(2,1)S(1)}, u32[]{:S(2)}, u32[]{:S(2)}) async-start(bf16[8,96,128]{2,1,0:T(8,128)(2,1)} %bitcast.11), calls=%async_computation.1 | async-start | bytes 393216 | tf_op jit(solution)/shard_map/all_to_all | solution.py:16
  117.4 34.8 %all-to-all-start.3 = ((bf16[8,768,128]{2,1,0:T(8,128)(2,1)}), bf16[8,768,128]{2,1,0:T(8,128)(2,1)S(1)}, u32[]{:S(2)}, u32[]{:S(2)}) async-start(bf16[8,768,128]{2,1,0:T(8,128)(2,1)} %value_pieces.1), calls=%async_computation.3 | async-start | bytes 3145728 | tf_op jit(solution)/shard_map/all_to_all | solution.py:16
  152.2 25.7 %all-to-all-start.2 = ((bf16[64,24,128]{2,1,0:T(8,128)(2,1)}), bf16[64,24,128]{2,1,0:T(8,128)(2,1)S(1)}, u32[]{:S(2)}, u32[]{:S(2)}) async-start(bf16[64,24,128]{2,1,0:T(8,128)(2,1)} %bitcast.10), calls=%async_computation.2 | async-start | bytes 786432 | tf_op jit(solution)/shard_map/all_to_all | solution.py:16
  177.9 0.7 copy-start

commit v2 on v1

--- a/solution.py
+++ b/solution.py
@@ -6,8 +6,10 @@
 from jax.sharding import Mesh
 from jax.sharding import PartitionSpec as P
 
+
 TENSOR = ("tensor_0", "tensor_1")
 MOST = 3
+GRANT = pltpu.CompilerParams(vmem_limit_bytes=16 * 2**20)
 
 adapter_output_scale = 2.0
 
@@ -16,15 +18,15 @@
     return lax.all_to_all(x, axes, split_axis=0, concat_axis=0, tiled=True)
 
 
-def place_rows(ids_row, ids_col, tokens, slots):
+def place_rows(ids_row, tokens, slots):
     rows, width = tokens.shape
     tile = 256
 
-    def kernel(row_ref, col_ref, tok_ref, out_ref, at_col_ref, at_row_ref):
+    def kernel(row_ref, tok_ref, out_ref, at_col_ref, at_row_ref):
         @pl.when(pl.program_id(0) == 0)
         def _():
             row = row_ref[...]
-            col = col_ref[...]
+            col = jnp.broadcast_to(row, (128, rows)).T[:, :1]
             same = row == col
             i = lax.broadcasted_iota(jnp.int32, (rows, rows), 0)
             j = lax.broadcasted_iota(jnp.int32, (rows, rows), 1)
@@ -45,7 +47,6 @@
         grid=(slots // tile,),
         in_specs=[
             pl.BlockSpec((1, rows), lambda i: (0, 0)),
-            pl.BlockSpec((rows, 1), lambda i: (0, 0)),
             pl.BlockSpec((rows, width), lambda i: (0, 0)),
         ],
         out_specs=[
@@ -57,32 +58,56 @@
             jax.ShapeDtypeStruct((rows, 1), jnp.int32),
         ],
         scratch_shapes=[pltpu.VMEM((1, rows), jnp.int32)],
+        compiler_params=GRANT,
         name="place_rows",
-    )(ids_row, ids_col, tokens)
-
-
-def value_pieces(tokens, weight, pieces):
+    )(ids_row, tokens)
+
+
+def value_pieces(tokens, weight, at, pieces):
     rows, width = tokens.shape
     cols = weight.shape[1] // pieces
     step = 2
 
-    def kernel(tok_ref, w_ref, out_ref):
-        part = jnp.dot(tok_ref[...], w_ref[...], preferred_element_type=jnp.float32)
-        part = part.astype(jnp.bfloat16)
-        for k in range(step):
-            out_ref[k] = part[:, k * cols : (k + 1) * cols]
-
-    return pl.pallas_call(
-        kernel,
-        grid=(pieces // step,),
+    def kernel(at_ref, tok_ref, w_ref, *refs):
+        out_refs, part_ref = refs[:-1], refs[-1]
+        for first in range(0, pieces, step):
+            part = jnp.dot(
+                tok_ref[...],
+                w_ref[:, first * cols : (first + step) * cols],
+                preferred_element_type=jnp.float32,
+            ).astype(jnp.bfloat16)
+            for k in range(step):
+                part_ref[first + k] = part[:, k * cols : (k + 1) * cols]
+        for k in range(pieces):
+            out_refs[k][...] = part_ref[at_ref[0] ^ k]
+
+    return pl.pallas_call(
+        kernel,
         in_specs=[
-            pl.BlockSpec((rows, width), lambda i: (0, 0)),
-            pl.BlockSpec((width, step * cols), lambda i: (0, i)),
-        ],
-        out_specs=pl.BlockSpec((step, rows, cols), lambda i: (i, 0, 0)),
-        out_shape=jax.ShapeDtypeStruct((pieces, rows, cols), jnp.bfloat16),
+            pl.BlockSpec(memory_space=pltpu.SMEM),
+            pl.BlockSpec((rows, width), lambda: (0, 0)),
+            pl.BlockSpec(weight.shape, lambda: (0, 0)),
+        ],
+        out_shape=[jax.ShapeDtypeStruct((rows, cols), jnp.bfloat16)] * pieces,
+        scratch_shapes=[pltpu.VMEM((pieces, rows, cols), jnp.bfloat16)],
+        compiler_params=GRANT,
         name="value_pieces",
-    )(tokens, weight)
+    )(at, tokens, weight)
+
+
+def base_sum(parts):
+    def kernel(*refs):
+        total = refs[0][...].astype(jnp.float32)
+        for ref in refs[1:-1]:
+            total = total + ref[...].astype(jnp.float32)
+        refs[-1][...] = total
+
+    return pl.pallas_call(
+        kernel,
+        out_shape=jax.ShapeDtypeStruct(parts[0].shape, jnp.float32),
+        compiler_params=GRANT,
+        name="base_sum",
+    )(*parts)
 
 
 def adapter_of(shape, first, group):
@@ -128,6 +153,7 @@
         ],
         out_specs=pl.BlockSpec((tile, pair), lambda i: (i, 0)),
         out_shape=jax.ShapeDtypeStruct((half, pair), jnp.bfloat16),
+        compiler_params=GRANT,
         name="down_rows",
     )(arrived, arrived, down)
 
@@ -160,6 +186,7 @@
     return pl.pallas_call(
         kernel,
         out_shape=jax.ShapeDtypeStruct((2 * half, cols), jnp.bfloat16),
+        compiler_params=GRANT,
         name="up_rows",
     )(low, up)
 
@@ -177,11 +204,12 @@
     return pl.pallas_call(
         kernel,
         out_shape=jax.ShapeDtypeStruct((rows, cols), jnp.bfloat16),
+        compiler_params=GRANT,
         name="take_rows",
     )(at_col, back, base)
 
 
-def per_device(tokens, value_weight, adapter_down, adapter_up_weight, adapter_ids):
+def layer(tokens, value_weight, adapter_down, adapter_up_weight, adapter_ids):
     owners = lax.axis_size("adapter")
     groups = lax.axis_size(TENSOR)
     here, rank, _ = adapter_down.shape
@@ -190,20 +218,24 @@
     share = here * MOST
     slots = owners * share
 
-    placed, at_col = place_rows(adapter_ids.reshape(1, rows), adapter_ids, tokens, slots)
-    pieces = value_pieces(tokens, value_weight, groups)
-    arrived_base = swap(pieces, TENSOR)
-    arrived = swap(placed.reshape(owners, share, width), "adapter").reshape(slots, width)
+    placed, at_col = place_rows(adapter_ids.reshape(1, rows), tokens, slots)
+    arrived = swap(placed.reshape(owners, share, width), "adapter")
+    arrived = arrived.reshape(slots, width)
+    at = lax.axis_index(TENSOR).astype(jnp.int32).reshape(1)
+    pieces = value_pieces(tokens, value_weight, at, groups)
+    parts = [pieces[0]]
+    for k in range(1, groups):
+        parts.append(lax.ppermute(pieces[k], TENSOR, [(i, i ^ k) for i in range(groups)]))
+    base = base_sum(parts)
 
     low_part = down_rows(arrived, adapter_down)
     low_sum = swap(low_part.reshape(groups, -1, 2 * rank), TENSOR)
     low_share = low_sum.astype(jnp.float32).sum(axis=0).astype(jnp.bfloat16)
-    low = lax.all_gather(low_share, TENSOR[1], axis=0, tiled=True)
-    low = lax.all_gather(low, TENSOR[0], axis=0, tiled=True)
+    copies = jnp.broadcast_to(low_share[None], (groups, *low_share.shape))
+    low = swap(copies, TENSOR).reshape(slots // 2, 2 * rank)
 
     delta = up_rows(low, adapter_up_weight)
     back = swap(delta.reshape(owners, share, cols), "adapter").reshape(slots, cols)
-    base = arrived_base.astype(jnp.float32).sum(axis=0)
     return take_rows(at_col, back, base)
 
 
@@ -212,7 +244,7 @@
         mesh.devices.reshape(mesh.shape["adapter"], 4, 2), ("adapter", "tensor_0", "tensor_1")
     )
     return jax.shard_map(
-        per_device,
+        layer,
         mesh=torus,
         in_specs=(
             P("adapter", TENSOR),

time: 182 us -> 174 us (0.956)
  the two profiles are of different devices: /device:TPU:8 before, /device:TPU:1 now
where the time goes in v2:
time: 174 us
  blocking collectives  112 us (64%)
  starting transfers between devices  33.4 us (19%)
  Pallas kernels  13.2 us (8%)
  waiting for transfers between devices  11 us (6%)
  local copies, waits for them, and re-layouts  3.72 us (2%)
    all_to_all x3, blocking collectives, swap(): return lax.all_to_all(x, axes, split_axis=0, concat_axis=0, tiled=True)  112 us
    ppermute x7, starting transfers between devices, layer(): lax.ppermute(pieces[k], TENSOR, [(i, i ^ k) for i in range(groups)])  22.4 us
    ppermute x7, waiting for transfers between devices, layer(): lax.ppermute(pieces[k], TENSOR, [(i, i ^ k) for i in range(groups)])  11 us
    all_to_all x1, starting transfers between devices, swap(): return lax.all_to_all(x, axes, split_axis=0, concat_axis=0, tiled=True)  11 us
    pallas_call x1, Pallas kernels, place_rows(): pl.pallas_call(kernel, grid=(slots // tile,), in_specs=[pl.BlockSpec((1,...  4.22 us
    pallas_call x1, Pallas kernels, down_rows(): pl.pallas_call(kernel, grid=(steps,), in_specs=[pl.BlockSpec((tile, width...  3.73 us
    unnamed x12, local copies, waits for them, and re-layouts  3.69 us
  transfers between devices with their start and end apart: 8, of which 3 were waited for; matrix products, arithmetic and copies ran while one was open for 0% of the time, Pallas kernels for 1%

profile of v2, /device:TPU:1, one launch (start us, length us, event | category | flops | bytes accessed | tf_op | source)
XLA Modules:
  0.0 173.6 jit_solution(12026567953109378307)
XLA Ops:
  0.0 0.0 copy-start
  0.0 1.4 copy-done
  1.4 0.0 copy-start.5
  1.4 0.7 copy-done.5
  2.1 4.2 %place_rows.1 = (bf16[1536,1024]{1,0:T(8,128)(2,1)S(1)}, s32[768,1]{1,0:T(8,128)S(1)}) custom-call(s32[1,768]{1,0:T(1,128)S(1)} %bitcast.14, bf16[768,1024]{1,0:T(8,128)(2,1)S(1)} %copy-done), custom_call_target="tpu_custom_call" | custom-call | tf_op jit(solution)/shard_map/place_rows/pallas_call | solution.py:45
  6.3 0.0 copy-start.3
  6.3 89.6 %all_to_all.20 = bf16[64,24,1024]{2,1,0:T(8,128)(2,1)S(1)} all-to-all(bf16[64,24,1024]{2,1,0:T(8,128)(2,1)S(1)} %bitcast.10), channel_id=1, replica_groups=mesh['adapter'=64,'tensor_0'=4,'tensor_1'=2] {'adapter'}, dimensions={0} | all-to-all | bytes 6291456 | tf_op jit(solution)/shard_map/all_to_all | solution.py:18
  96.0 0.0 copy-done.3
  96.0 0.0 copy-start.4
  96.0 3.7 %down_rows.1 = bf16[768,128]{1,0:T(8,128)(2,1)S(1)} custom-call(bf16[1536,1024]{1,0:T(8,128)(2,1)S(1)} %bitcast.8, bf16[1536,1024]{1,0:T(8,128)(2,1)S(1)} %bitcast.9, bf16[8,64,1024]{2,1,0:T(8,128)(2,1)S(1)} %copy-done.3), custom_call_target="tpu_custom_call" | custom-call | tf_op jit(solution)/shard_map/down_rows/pallas_call | solution.py:146
  99.7 0.0 copy-start.1
  99.7 13.2 %all_to_all.21 = bf16[8,96,128]{2,1,0:T(8,128)(2,1)S(1)} all-to-all(bf16[8,96,128]{2,1,0:T(8,128)(2,1)S(1)} %bitcast.13), channel_id=1, replica_groups=mesh['adapter'=64,'tensor_0'=4,'tensor_1'=2] {'tensor_0','tensor_1'}, dimensions={0} | all-to-all | bytes 393216 | tf_op jit(solution)/shard_map/all_to_all | solution.py:18
  113.0 9.2 %all_to_all.22 = bf16[8,96,128]{2,1,0:T(8,128)(2,1)S(1)} all-to-all(bf16[8,96,128]{2,1,0:T(8,128)(2,1)S(1)} %broadcast_in_dim.2), channel_id=1, replica_groups=mesh['adapter'=64,'tensor_0'=4,'tensor_1'=2] {'tensor_0','tensor_1'}, dimensions={0} | all-to-all | bytes 393216 | tf_op jit(solution)/shard_map/all_to_all | solution.py:18
  122.2 0.0 copy-done.4
  122.2 1.6 up_rows.1
  123.8 11.0 %all-to-all-start.3 = ((bf16[64,24,128]{2,1,0:T(8,128)(2,1)}), bf16[64,24,128]{2,1,0:T(8,128)(2,1)S(1)}, u32[]{:S(2)}, u32[]{:S(2)}) async-start(bf16[64,24,128]{2,1,0:T(8,128)(2,1)} %bitcast.5), calls=%async_computation.3 | async-start | bytes 786432 | tf_op jit(solution)/shard_map/all_to_all | solution.py:18
  134.8 0.0 copy-done.1
  134.8 0.0 copy-start.2
  134.8 1.6 copy-done.2
  136.4 1.9 %value_pieces.1 = (bf16[768,128]{1,0:T(8,128)(2,1)S(1)}, bf16[768,128]{1,0:T(8,128)(2,1)S(1)}, bf16[768,128]{1,0:T(8,128)(2,1)S(1)}, bf16[768,128]{1,0:T(8,128)(...) custom-call(s32[1]{0:T(128)} %bitcast.7.at_ref, ...), custom_call_target="tpu_custom_call" | custom-call | tf_op jit(solution)/shard_map/value_pieces/pallas_call | solution.py:84
  138.3 3.1 %collective-permute-start = (bf16[768,128]{1,0:T(8,128)(2,1)S(1)}, bf16[768,128]{1,0:T(8,128)(2,1)S(1)}, u32[]{:S(2)}, u32[]{:S(2)}) collective-permute-start(bf16[768,128]{1,0:T(8,128)(2,1)S(1)} %get-tuple-element.18), channel_id=1, source_target_pairs={{0,1},{1,0},{2,3},{3,2},{4,5},{5,4},{6,7},{7,6},{8,9},{9,8},{10,11... | collective-permute-start | bytes 589832 | tf_op jit(solution)/shard_map/ppermute | solution.py:228
  141.5 2.2 %collective-permute-start.1 = (bf16[768,128]{1,0:T(8,128)(2,1)S(1)}, bf16[768,128]{1,0:T(8,128)(2,1)S(1)}, u32[]{:S(2)}, u32[]{:S(2)}) collective-permute-start(bf16[768,128]{1,0:T(8,128)(2,1)S(1)} %get-tuple-element.19), channel_id=1, source_target_pairs={{0,2},{1,3},{2,0},{3,1},{4,6},{5,7},{6,4},{7,5},{8,10},{9,11},{10,... | collective-permute-start | bytes 589832 | tf_op jit(solution)/shard_map/ppermute | solution.py:228
  143.7 3.3 %collective-permute-start.2 = (bf16[768,128]{1,0:T(8,128)(2,1)S(1)}, bf16[768,128]{1,0:T(8,128)(2,1)S(1)}, u32[]{:S(2)}, u32[]{:S(2)}) collective-permute-start(bf16[768,128]{1,0:T(8,128)(2,1)S(1)} %get-tuple-element.20), channel_id=1, source_target_pairs={{0,3},{1,2},{2,1},{3,0},{4,7},{5,6},{6,5},{7,4},{8,11},{9,10},{10,... | collective-permute-start | bytes 589832 | tf_op jit(solution)/shard_map/ppermute | solution.py:228
  146.9 2.3 %collective-permute-start.3 = (bf16[768,128]{1,0:T(8,128)(2,1)S(1)}, bf16[768,128]{1,0:T(8,128)(2,1)S(1)}, u32[]{:S(2)}, u32[]{:S(2)}) collective-permute-start(bf16[768,128]{1,0:T(8,128)(2,1)S(1)} %get-tuple-element.21), channel_id=1, source_target_pairs={{0,4},{1,5},{2,6},{3,7},{4,0},{5,1},{6,2},{7,3},{8,12},{9,13},{10,... | collective-permute-start | bytes 589832 | tf_op jit(solution)/shard_map/ppermute | solution.py:228
  149.3 4.8 %collective-permute-start.4 = (bf16[768,128]{1,0:T(8,128)(2,1)S(1)}, bf16[768,128]{1,0:T(8,128)(2,1)S(1)}, u32[]{:S(2)}, u32[]{:S(2)}) collective-permute-start(bf16[768,128]{1,0:T(8,128)(2,1)S(1)} %get-tuple-element.22), channel_id=1, source_target_pairs={{0,5},{1,4},{2,7},{3,6},{4,1},{5,0},{6,3},{7,2},{8,13},{9,12},{10,... | collective-permute-start | bytes 589832 | tf_op jit(solution)/shard_map/ppermute | solution.py:228
  154.1 0.0 collective-permute-done.refs_1_
  154.1 2.8 %collective-permute-start.5 = (bf16[768,128]{1,0:T(8,128)(2,1)S(1)}, bf16[768,128]{1,0:T(8,128)(2,1)S(1)}, u32[]{:S(2)}, u32[]{:S(2)}) collective-permute-start(bf16[768,128]{1,0:T(8,128)(2,1)S(1)} %get-tuple-element.23), channel_id=1, source_target_pairs={{0,6},{1,7},{2,4},{3,5},{4,2},{5,3},{6,0},{7,1},{8,14},{9,15},{10,... | collective-permute-start | bytes 589832 | tf_op jit(solution)/shard_map/ppermute | solution.py:228
  156.9 0.0 collective-permute-done.1.refs_2_
  156.9 3.9 %collective-permute-start.6 = (bf16[768,128]{1,0:T(8,128)(2,1)S(1)}, bf16[768,128]{1,0:T(8,128)(2,1)S(1)}, u32[]{:S(2)}, u32[]{:S(2)}) collective-permute-start(bf16[768,128]{1,0:T(8,128)(2,1)S(1)} %get-tuple-element.24), channel_id=1, source_target_pairs={{0,7},{1,6},{2,5},{3,4},{4,3},{5,2},{6,1},{7,0},{8,15},{9,14},{10,... | collective-permute-start | bytes 589832 | tf_op jit(solution)/shard_map/ppermute | solution.py:228
  160.8 0.0 collective-permute-done.2.refs_3_
  160.9 0.0 collective-permute-done.3.refs_4_
  160.9 2.4 %collective-permute-done.4.refs_5_ = bf16[768,128]{1,0:T(8,128)(2,1)S(1)} collective-permute-done((bf16[768,128]{1,0:T(8,128)(2,1)S(1)}, bf16[768,128]{1,0:T(8,128)(2,1)S(1)}, u32[]{:S(2)}, u32[]{:S(2)}) %collective-permute-start.4) | collective-permute-done | bytes 196640 | tf_op jit(solution)/shard_map/ppermute | solution.py:228
  163.3 4.4 %collective-permute-done.5.refs_6_ = bf16[768,128]{1,0:T(8,128)(2,1)S(1)} collective-permute-done((bf16[768,128]{1,0:T(8,128)(2,1)S(1)}, bf16[768,128]{1,0:T(8,128)(2,1)S(1)}, u32[]{:S(2)}, u32[]{:S(2)}) %collective-permute-start.5) | collective-permute-done | bytes 196640 | tf_op jit(solution)/shard_map/ppermute | solution.py:228
  167.7 4.2 %collective-permute-done.6.refs_7_ = bf16[768,128]{1,0:T(8,128)(2,1)S(1)} collective-permute-done((bf16[768,128]{1,0:T(8,128)(2,1)S(1)}, bf16[768,128]{1,0:T(8,128)(2,1)S(1)}, u32[]{:S(2)}, u32[]{:S(2)}) %collective-permute-start.6) | collective-permute-done | bytes 196640 | tf_op jit(solution)/shard_map/ppermute | solution.py:228
  171.9 0.2 base_sum.1.base_ref
  172.1 0.0 all-to-all-done.3
  172.1 1.5 take_rows.1
  (2 shorter events, 0.1 us)
Async XLA Ops:
  0.0 1.4 copy-start
  1.4 0.7 copy-start.5
  6.3 89.6 %copy-start.3 = (bf16[8,64,1024]{2,1,0:T(8,128)(2,1)S(1)}, bf16[8,64,1024]{2,1,0:T(8,128)(2,1)}, u32[]{:S(2)}) copy-start(bf16[8,64,1024]{2,1,0:T(8,128)(2,1)} %down_ref.1) | copy-start | bytes 3145732
  96.0 26.2 %copy-start.4 = (bf16[8,64,128]{2,1,0:T(8,128)(2,1)S(1)}, bf16[8,64,128]{2,1,0:T(8,128)(2,1)}, u32[]{:S(2)}) copy-start(bf16[8,64,128]{2,1,0:T(8,128)(2,1)} %up_ref.1) | copy-start | bytes 393220
  99.7 35.1 %copy-start.1 = (bf16[768,1024]{1,0:T(8,128)(2,1)S(1)}, bf16[768,1024]{1,0:T(8,128)(2,1)}, u32[]{:S(2)}) copy-start(bf16[768,1024]{1,0:T(8,128)(2,1)} %tok_ref.3) | copy-start | bytes 4718596
  123.8 48.3 %all-to-all-start.3 = ((bf16[64,24,128]{2,1,0:T(8,128)(2,1)}), bf16[64,24,128]{2,1,0:T(8,128)(2,1)S(1)}, u32[]{:S(2)}, u32[]{:S(2)}) async-start(bf16[64,24,128]{2,1,0:T(8,128)(2,1)} %bitcast.5), calls=%async_computation.3 | async-start | bytes 786432 | tf_op jit(solution)/shard_map/all_to_all | solution.py:18
  134.8 1.6 copy-start.2
  138.3 15.8 %collective-permute-start = (bf16[768,128]{1,0:T(8,128)(2,1)S(1)}, bf16[768,128]{1,0:T(8,128)(2,1)S(1)}, u32[]{:S(2)}, u32[]{:S(2)}) collective-permute-start(bf16[768,128]{1,0:T(8,128)(2,1)S(1)} %get-tuple-element.18), channel_id=1, source_target_pairs={{0,1},{1,0},{2,3},{3,2},{4,5},{5,4},{6,7},{7,6},{8,9},{9,8},{10,11... | collective-permute-start | bytes 589832 | tf_op jit(solution)/shard_map/ppermute | solution.py:228
  141.5 15.5 %collective-permute-start.1 = (bf16[768,128]{1,0:T(8,128)(2,1)S(1)}, bf16[768,128]{1,0:T(8,128)(2,1)S(1)}, u32[]{:S(2)}, u32[]{:S(2)}) collective-permute-start(bf16[768,128]{1,0:T(8,128)(2,1)S(1)} %get-tuple-element.19), channel_id=1, source_target_pairs={{0,2},{1,3},{2,0},{3,1},{4,6},{5,7},{6,4},{7,5},{8,10},{9,11},{10,... | collective-permute-start | bytes 589832 | tf_op jit(solution)/shard_map/ppermute | solution.py:228
  143.7 17.2 %collective-permute-start.2 = (bf16[768,128]{1,0:T(8,128)(2,1)S(1)}, bf16[768,128]{1,0:T(8,128)(2,1)S(1)}, u32[]{:S(2)}, u32[]{:S(2)}) collective-permute-start(bf16[768,128]{1,0:T(8,128)(2,1)S(1)} %get-tuple-element.20), channel_id=1, source_target_pairs={{0,3},{1,2},{2,1},{3,0},{4,7},{5,6},{6,5},{7,4},{8,11},{9,10},{10,... | collective-permute-start | bytes 589832 | tf_op jit(solution)/shard_map/ppermute | solution.py:228
  146.9 13.9 %collective-permute-start.3 = (bf16[768,128]{1,0:T(8,128)(2,1)S(1)}, bf16[768,128]{1,0:T(8,128)(2,1)S(1)}, u32[]{:S(2)}, u32[]{:S(2)}) collective-permute-start(bf16[768,128]{1,0:T(8,128)(2,1)S(1)} %get-tuple-element.21), channel_id=1, source_target_pairs={{0,4},{1,5},{2,6},{3,7},{4,0},{5,1},{6,2},{7,3},{8,12},{9,13},{10,... | collective-permute-start | bytes 589832 | tf_op jit(solution)/shard_map/ppermute | solution.py:228
  149.3 14.0 %collective-permute-start.4 = (bf16[768,128]{1,0:T(8,128)(2,1)S(1)}, bf16[768,128]{1,0:T(8,128)(2,1)S(1)}, u32[]{:S(2)}, u32[]{:S(2)}) collective-permute-start(bf16[768,128]{1,0:T(8,128)(2,1)S(1)} %get-tuple-element.22), channel_id=1, source_target_pairs={{0,5},{1,4},{2,7},{3,6},{4,1},{5,0},{6,3},{7,2},{8,13},{9,12},{10,... | collective-permute-start | bytes 589832 | tf_op jit(solution)/shard_map/ppermute | solution.py:228
  154.1 13.5 %collective-permute-start.5 = (bf16[768,128]{1,0:T(8,128)(2,1)S(1)}, bf16[768,128]{1,0:T(8,128)(2,1)S(1)}, u32[]{:S(2)}, u32[]{:S(2)}) collective-permute-start(bf16[768,128]{1,0:T(8,128)(2,1)S(1)} %get-tuple-element.23), channel_id=1, source_target_pairs={{0,6},{1,7},{2,4},{3,5},{4,2},{5,3},{6,0},{7,1},{8,14},{9,15},{10,... | collective-permute-start | bytes 589832 | tf_op jit(solution)/shard_map/ppermute | solution.py:228
  156.9 15.0 %collective-permute-start.6 = (bf16[768,128]{1,0:T(8,128)(2,1)S(1)}, bf16[768,128]{1,0:T(8,128)(2,1)S(1)}, u32[]{:S(2)}, u32[]{:S(2)}) collective-permute-start(bf16[768,128]{1,0:T(8,128)(2,1)S(1)} %get-tuple-element.24), channel_id=1, source_target_pairs={{0,7},{1,6},{2,5},{3,4},{4,3},{5,2},{6,1},{7,0},{8,15},{9,14},{10,... | collective-permute-start | bytes 589832 | tf_op jit(solution)/shard_map/ppermute | solution.py:228

commit v3 on v2

--- a/solution.py
+++ b/solution.py
@@ -8,7 +8,12 @@
 
 
 TENSOR = ("tensor_0", "tensor_1")
+ADAPTER = ("z", "y")
+HERE = 8
 MOST = 3
+MAIN = 2
+SIDE = 16
+LOST = 3e38
 GRANT = pltpu.CompilerParams(vmem_limit_bytes=16 * 2**20)
 
 adapter_output_scale = 2.0
@@ -18,7 +23,7 @@
     return lax.all_to_all(x, axes, split_axis=0, concat_axis=0, tiled=True)
 
 
-def place_rows(ids_row, tokens, slots):
+def full_place(ids_row, tokens, slots):
     rows, width = tokens.shape
     tile = 256
 
@@ -59,7 +64,7 @@
         ],
         scratch_shapes=[pltpu.VMEM((1, rows), jnp.int32)],
         compiler_params=GRANT,
-        name="place_rows",
+        name="full_place",
     )(ids_row, tokens)
 
 
@@ -115,7 +120,7 @@
     return slot % group // MOST
 
 
-def down_rows(arrived, down):
+def full_down(arrived, down):
     slots, width = arrived.shape
     here, rank, _ = down.shape
     group = here * MOST
@@ -154,11 +159,11 @@
         out_specs=pl.BlockSpec((tile, pair), lambda i: (i, 0)),
         out_shape=jax.ShapeDtypeStruct((half, pair), jnp.bfloat16),
         compiler_params=GRANT,
-        name="down_rows",
+        name="full_down",
     )(arrived, arrived, down)
 
 
-def up_rows(low, up):
+def full_up(low, up):
     half, pair = low.shape
     here, rank, cols = up.shape
     group = here * MOST
@@ -187,11 +192,11 @@
         kernel,
         out_shape=jax.ShapeDtypeStruct((2 * half, cols), jnp.bfloat16),
         compiler_params=GRANT,
-        name="up_rows",
+        name="full_up",
     )(low, up)
 
 
-def take_rows(at_col, back, base):
+def full_take(at_col, back, base):
     rows, cols = base.shape
     slots = back.shape[0]
 
@@ -205,54 +210,389 @@
         kernel,
         out_shape=jax.ShapeDtypeStruct((rows, cols), jnp.bfloat16),
         compiler_params=GRANT,
-        name="take_rows",
+        name="full_take",
     )(at_col, back, base)
 
 
-def layer(tokens, value_weight, adapter_down, adapter_up_weight, adapter_ids):
-    owners = lax.axis_size("adapter")
-    groups = lax.axis_size(TENSOR)
-    here, rank, _ = adapter_down.shape
+def scalar_spec():
+    return pl.BlockSpec(memory_space=pltpu.SMEM)
+
+
+def count_before(row, col, also_col=None):
+    n = row.shape[1]
+    j = lax.broadcasted_iota(jnp.int32, (n, n), 0)
+    i = lax.broadcasted_iota(jnp.int32, (n, n), 1)
+    hit = (row == col) & (j < i)
+    if also_col is not None:
+        hit = hit & also_col
+    return jnp.sum(jnp.where(hit, 1, 0), axis=0, keepdims=True)
+
+
+def to_col(row):
+    return jnp.broadcast_to(row, (128, row.shape[1])).T[:, :1]
+
+
+def pick_rows(at_row, slots, first=0):
+    n = at_row.shape[1]
+    slot = lax.broadcasted_iota(jnp.int32, (slots, n), 0) + first
+    return jnp.where(slot == at_row, 1.0, 0.0).astype(jnp.bfloat16)
+
+
+def place_main(ids_row, tokens, slots):
+    rows, width = tokens.shape
+    tile = 256
+
+    def kernel(row_ref, tok_ref, out_ref, seen_ref, at_col_ref):
+        @pl.when(pl.program_id(0) == 0)
+        def _():
+            row = row_ref[...]
+            seen = count_before(row, to_col(row))
+            seen_ref[...] = seen
+            spot = row % HERE
+            back = row // HERE * (HERE * MOST) + jnp.where(
+                seen < MAIN, spot * MAIN + seen, HERE * MAIN + spot
+            )
+            at_col_ref[...] = to_col(back)
+
+        at_row = jnp.where(seen_ref[...] < MAIN, row_ref[...] * MAIN + seen_ref[...], -1)
+        pick = pick_rows(at_row, tile, pl.program_id(0) * tile)
+        out_ref[...] = jnp.dot(pick, tok_ref[...], preferred_element_type=jnp.float32).astype(
+            jnp.bfloat16
+        )
+
+    return pl.pallas_call(
+        kernel,
+        grid=(slots // tile,),
+        in_specs=[
+            pl.BlockSpec((1, rows), lambda i: (0, 0)),
+            pl.BlockSpec((rows, width), lambda i: (0, 0)),
+        ],
+        out_specs=[
+            pl.BlockSpec((tile, width), lambda i: (i, 0)),
+            pl.BlockSpec((1, rows), lambda i: (0, 0)),
+            pl.BlockSpec((rows, 1), lambda i: (0, 0)),
+        ],
+        out_shape=[
+            jax.ShapeDtypeStruct((slots, width), tokens.dtype),
+            jax.ShapeDtypeStruct((1, rows), jnp.int32),
+            jax.ShapeDtypeStruct((rows, 1), jnp.int32),
+        ],
+        compiler_params=GRANT,
+        name="place_main",
+    )(ids_row, tokens)
+
+
+def bucket(rows_of, key, key_col, code, valid, valid_col, flag, out_refs, block_ref, at):
+    n = key.shape[1]
+    width = rows_of.shape[1]
+    q = count_before(key, key_col, valid_col)
+    fits = valid & (q < SIDE - 1)
+    lost = jnp.max(jnp.where(valid & (q >= SIDE - 1), 1.0, 0.0), axis=1, keepdims=True)
+    flag = jnp.maximum(flag, lost)
+    pick = pick_rows(jnp.where(fits, key * SIDE + q, -1), 8 * SIDE)
+    data = jnp.dot(pick, rows_of, preferred_element_type=jnp.float32)
+    which = lax.broadcasted_iota(jnp.int32, (8, n), 0)
+    owned = jnp.where(fits & (which == key), (code + 1).astype(jnp.float32), 0.0)
+    place = lax.broadcasted_iota(jnp.int32, (128, n), 0)
+    there = jnp.where(place == q, 1.0, 0.0)
+    codes = lax.dot_general(
+        owned.astype(jnp.bfloat16),
+        there.astype(jnp.bfloat16),
+        (((1,), (1,)), ((), ())),
+        preferred_element_type=jnp.float32,
+    )
+    lane = lax.broadcasted_iota(jnp.int32, (8, 128), 1)
+    codes = jnp.where(lane == 127, flag, codes)
+    wide = jnp.concatenate([codes, jnp.zeros((8, width - 128), jnp.float32)], axis=1)
+    row = lax.broadcasted_iota(jnp.int32, (SIDE, width), 0)
+    for k in range(8):
+        note = jnp.broadcast_to(wide[k : k + 1], (SIDE, width))
+        block_ref[k] = jnp.where(
+            row == SIDE - 1, note, data[k * SIDE : (k + 1) * SIDE]
+        ).astype(jnp.bfloat16)
+    for k in range(8):
+        out_refs[k][...] = block_ref[at ^ k]
+
+
+def read_codes(in_refs):
+    n = 8 * SIDE
+    lane = lax.broadcasted_iota(jnp.int32, (8, n), 1)
+    codes = jnp.zeros((8, n), jnp.float32)
+    flag = jnp.zeros((1, 1), jnp.float32)
+    for k in range(8):
+        block = in_refs[k][...].astype(jnp.float32)
+        note = block[SIDE - 1 : SIDE, :n]
+        flag = jnp.maximum(flag, note[:, 127:128])
+        own = jnp.where(lane < SIDE - 1, jnp.broadcast_to(note, (8, n)), 0.0)
+        codes = codes + (pltpu.roll(own, k * SIDE, 1) if k else own)
+    return codes[:1].astype(jnp.int32) - 1, flag
+
+
+def side_first(at, seen, ids_row, tokens):
+    _, width = tokens.shape
+
+    def kernel(at_ref, seen_ref, row_ref, tok_ref, *refs):
+        row = row_ref[...]
+        third = seen_ref[...] >= MAIN
+        home = row // HERE
+        key = home % 8
+        marked = jnp.where(third, key, -1)
+        bucket(
+            tok_ref[...], key, to_col(marked), home // 8 * 8 + row % HERE, third, None,
+            jnp.zeros((1, 1), jnp.float32), refs[:8], refs[8], at_ref[0],
+        )
+
+    return pl.pallas_call(
+        kernel,
+        in_specs=[scalar_spec()] + [pl.BlockSpec(memory_space=pltpu.VMEM)] * 3,
+        out_shape=[jax.ShapeDtypeStruct((SIDE, width), jnp.bfloat16)] * 8,
+        scratch_shapes=[pltpu.VMEM((8, SIDE, width), jnp.bfloat16)],
+        compiler_params=GRANT,
+        name="side_first",
+    )(at, seen, ids_row, tokens)
+
+
+def side_second(at, blocks):
+    width = blocks[0].shape[1]
+    n = 8 * SIDE
+
+    def kernel(at_ref, *refs):
+        code, flag = read_codes(refs[:8])
+        valid = code >= 0
+        key = jnp.where(valid, code // 8, -1)
+        from_y = (lax.broadcasted_iota(jnp.int32, (1, n), 1) // SIDE) ^ at_ref[1]
+        rows_of = jnp.concatenate([ref[...] for ref in refs[:8]], axis=0)
+        bucket(
+            rows_of, key, to_col(key), from_y * 8 + code % 8, valid, None,
+            flag, refs[8:16], refs[16], at_ref[0],
+        )
+
+    return pl.pallas_call(
+        kernel,
+        in_specs=[scalar_spec()] + [pl.BlockSpec(memory_space=pltpu.VMEM)] * 8,
+        out_shape=[jax.ShapeDtypeStruct((SIDE, width), jnp.bfloat16)] * 8,
+        scratch_shapes=[pltpu.VMEM((8, SIDE, width), jnp.bfloat16)],
+        compiler_params=GRANT,
+        name="side_second",
+    )(at, *blocks)
+
+
+def fold(full, mine, rank):
+    pair = 2 * rank
+    lane = lax.broadcasted_iota(jnp.int32, (full.shape[0], pair), 1)
+    kept = jnp.zeros((full.shape[0], pair), jnp.float32)
+    for k in range(HERE // 2):
+        holder = jnp.where(lane < rank, 2 * k, 2 * k + 1)
+        kept = kept + jnp.where(mine == holder, full[:, k * pair : (k + 1) * pair], 0.0)
+    return kept + pltpu.roll(kept, rank, 1)
+
+
+def contract_last(x, y):
+    return lax.dot_general(x, y, (((1,), (1,)), ((), ())), preferred_element_type=jnp.float32)
+
+
+def side_low(at, blocks, down):
+    here, rank, width = down.shape
+    n = 8 * SIDE
+    thirds = 64 * here
+    pair = 2 * rank
+
+    def kernel(at_ref, *refs):
+        down_ref, out_ref, flag_ref = refs[8:]
+        code, flag = read_codes(refs[:8])
+        from_z = (lax.broadcasted_iota(jnp.int32, (1, n), 1) // SIDE) ^ at_ref[0]
+        slot = jnp.where(code >= 0, from_z * 64 + code, -1)
+        rows_of = jnp.concatenate([ref[...] for ref in refs[:8]], axis=0)
+        full = contract_last(rows_of, down_ref[...].reshape(here * rank, width))
+        mine = to_col(jnp.where(code >= 0, code % 8, -1))
+        low = fold(full, mine, rank).astype(jnp.bfloat16)
+        spread = jnp.dot(pick_rows(slot, thirds), low, preferred_element_type=jnp.float32)
+        lane = lax.broadcasted_iota(jnp.int32, (thirds // 2, pair), 1)
+        out_ref[...] = jnp.where(
+            lane < rank, spread[: thirds // 2], spread[thirds // 2 :]
+        ).astype(jnp.bfloat16)
+        flag_ref[...] = jnp.broadcast_to(flag, (8, 128))
+
+    return pl.pallas_call(
+        kernel,
+        in_specs=[scalar_spec()] + [pl.BlockSpec(memory_space=pltpu.VMEM)] * 9,
+        out_shape=[
+            jax.ShapeDtypeStruct((thirds // 2, pair), jnp.bfloat16),
+            jax.ShapeDtypeStruct((8, 128), jnp.float32),
+        ],
+        compiler_params=GRANT,
+        name="side_low",
+    )(at, *blocks, down)
+
+
+def down_main(arrived, thirds, down):
+    slots, width = arrived.shape
+    here, rank, _ = down.shape
+    half = slots // 2
+    tile = 256
+    pair = 2 * rank
+
+    def kernel(in_ref, thirds_ref, down_ref, out_ref):
+        weight = down_ref[...].reshape(here * rank, width)
+        lane = lax.broadcasted_iota(jnp.int32, (tile, pair), 1)
+        slot = lax.broadcasted_iota(jnp.int32, (tile, pair), 0)
+        mine = slot % (HERE * MAIN) // MAIN
+        for first in range(0, half, tile):
+            lo = fold(contract_last(in_ref[first : first + tile, :], weight), mine, rank)
+            hi = fold(
+                contract_last(in_ref[half + first : half + first + tile, :], weight), mine, rank
+            )
+            out_ref[first : first + tile, :] = jnp.where(lane < rank, lo, hi).astype(jnp.bfloat16)
+        out_ref[half:, :] = thirds_ref[...]
+
+    return pl.pallas_call(
+        kernel,
+        out_shape=jax.ShapeDtypeStruct((half + thirds.shape[0], pair), jnp.bfloat16),
+        compiler_params=GRANT,
+        name="down_main",
+    )(arrived, thirds, down)
+
+
+def up_main(low, flag, up):
+    here, rank, cols = up.shape
+    owners = 2 * low.shape[0] // (here * MOST)
+    half = owners * here * MAIN // 2
+
+    def kernel(low_ref, flag_ref, up_ref, out_ref):
+        weight = up_ref[...].reshape(here * rank, cols)
+
+        def mapped(part, per):
+            wide = part.astype(jnp.float32)
+            turned = pltpu.roll(wide, rank, 1)
+            lane = lax.broadcasted_iota(jnp.int32, wide.shape, 1)
+            slot = lax.broadcasted_iota(jnp.int32, wide.shape, 0)
+            mine = slot % (here * per) // per
+            halves = []
+            for h in range(2):
+                both = jnp.where((lane < rank) == (h == 0), wide, turned)
+                spread = []
+                for k in range(here // 2):
+                    holder = jnp.where(lane < rank, 2 * k, 2 * k + 1)
+                    spread.append(jnp.where(mine == holder, both, 0.0).astype(jnp.bfloat16))
+                halves.append(
+                    jnp.dot(
+                        jnp.concatenate(spread, axis=1), weight, preferred_element_type=jnp.float32
+                    )
+                )
+            acc = jnp.concatenate(halves, axis=0) * adapter_output_scale
+            return acc.reshape(owners, here * per, cols)
+
+        main = mapped(low_ref[:half, :], MAIN)
+        thirds = mapped(low_ref[half:, :], MOST - MAIN)
+        both = jnp.concatenate([main, thirds], axis=1).reshape(owners * here * MOST, cols)
+        out_ref[...] = jnp.where(flag_ref[:1, :1] > 0.0, LOST, both).astype(jnp.bfloat16)
+
+    return pl.pallas_call(
+        kernel,
+        out_shape=jax.ShapeDtypeStruct((owners * here * MOST, cols), jnp.bfloat16),
+        compiler_params=GRANT,
+        name="up_main",
+    )(low, flag, up)
+
+
+def take_main(at_col, back, base):
+    rows, cols = base.shape
+    slots = back.shape[0]
+
+    def kernel(at_ref, back_ref, base_ref, out_ref, lost_ref):
+        slot = lax.broadcasted_iota(jnp.int32, (rows, slots), 1)
+        pick = jnp.where(slot == at_ref[...], 1.0, 0.0).astype(jnp.bfloat16)
+        mine = jnp.dot(pick, back_ref[...], preferred_element_type=jnp.float32)
+        out_ref[...] = (base_ref[...] + mine).astype(jnp.bfloat16)
+        lost_ref[0] = (jnp.max(back_ref[...].astype(jnp.float32)) > LOST / 2).astype(jnp.int32)
+
+    return pl.pallas_call(
+        kernel,
+        out_specs=[pl.BlockSpec(memory_space=pltpu.VMEM), pl.BlockSpec(memory_space=pltpu.SMEM)],
+        out_shape=[
+            jax.ShapeDtypeStruct((rows, cols), jnp.bfloat16),
+            jax.ShapeDtypeStruct((1,), jnp.int32),
+        ],
+        compiler_params=GRANT,
+        name="take_main",
+    )(at_col, back, base)
+
+
+def low_of_all(low_part, groups):
+    rows, pair = low_part.shape
+    parts = swap(low_part.reshape(groups, rows // groups, pair), TENSOR)
+    share = parts.astype(jnp.float32).sum(axis=0).astype(jnp.bfloat16)
+    copies = jnp.broadcast_to(share[None], (groups, *share.shape))
+    return swap(copies, TENSOR).reshape(rows, pair)
+
+
+def whole_exchange(tokens, adapter_down, adapter_up_weight, adapter_ids, base):
     rows, width = tokens.shape
     cols = adapter_up_weight.shape[2]
-    share = here * MOST
-    slots = owners * share
-
-    placed, at_col = place_rows(adapter_ids.reshape(1, rows), tokens, slots)
-    arrived = swap(placed.reshape(owners, share, width), "adapter")
-    arrived = arrived.reshape(slots, width)
+    share = HERE * MOST
+    slots = 64 * share
+    placed, at_col = full_place(adapter_ids.reshape(1, rows), tokens, slots)
+    arrived = swap(placed.reshape(64, share, width), ADAPTER).reshape(slots, width)
+    low = low_of_all(full_down(arrived, adapter_down), lax.axis_size(TENSOR))
+    delta = full_up(low, adapter_up_weight)
+    back = swap(delta.reshape(64, share, cols), ADAPTER).reshape(slots, cols)
+    return full_take(at_col, back, base)
+
+
+def layer(tokens, value_weight, adapter_down, adapter_up_weight, adapter_ids):
+    groups = lax.axis_size(TENSOR)
+    rows, width = tokens.shape
+    cols = adapter_up_weight.shape[2]
+    ids_row = adapter_ids.reshape(1, rows)
+    at_z = lax.axis_index("z").astype(jnp.int32)
+    at_y = lax.axis_index("y").astype(jnp.int32)
+
+    placed, seen, at_col = place_main(ids_row, tokens, 64 * HERE * MAIN)
+    arrived = swap(placed.reshape(64, HERE * MAIN, width), ADAPTER)
+    arrived = arrived.reshape(64 * HERE * MAIN, width)
+
+    blocks = side_first(at_y.reshape(1), seen, ids_row, tokens)
+    blocks = xor_sends(blocks, "y")
+    blocks = side_second(jnp.stack([at_z, at_y]), blocks)
+    blocks = xor_sends(blocks, "z")
+    thirds, flag = side_low(at_z.reshape(1), blocks, adapter_down)
+
     at = lax.axis_index(TENSOR).astype(jnp.int32).reshape(1)
     pieces = value_pieces(tokens, value_weight, at, groups)
+    pieces = xor_sends(pieces, TENSOR)
+    base = base_sum(pieces)
+
+    low = low_of_all(down_main(arrived, thirds, adapter_down), groups)
+    delta = up_main(low, flag, adapter_up_weight)
+    back = swap(delta.reshape(64, HERE * MOST, cols), ADAPTER).reshape(64 * HERE * MOST, cols)
+    values, lost = take_main(at_col, back, base)
+    return lax.cond(
+        lost[0] > 0,
+        lambda: whole_exchange(tokens, adapter_down, adapter_up_weight, adapter_ids, base),
+        lambda: values,
+    )
+
+
+def xor_sends(pieces, axis):
+    size = lax.axis_size(axis)
     parts = [pieces[0]]
-    for k in range(1, groups):
-        parts.append(lax.ppermute(pieces[k], TENSOR, [(i, i ^ k) for i in range(groups)]))
-    base = base_sum(parts)
-
-    low_part = down_rows(arrived, adapter_down)
-    low_sum = swap(low_part.reshape(groups, -1, 2 * rank), TENSOR)
-    low_share = low_sum.astype(jnp.float32).sum(axis=0).astype(jnp.bfloat16)
-    copies = jnp.broadcast_to(low_share[None], (groups, *low_share.shape))
-    low = swap(copies, TENSOR).reshape(slots // 2, 2 * rank)
-
-    delta = up_rows(low, adapter_up_weight)
-    back = swap(delta.reshape(owners, share, cols), "adapter").reshape(slots, cols)
-    return take_rows(at_col, back, base)
+    for k in range(1, size):
+        parts.append(lax.ppermute(pieces[k], axis, [(i, i ^ k) for i in range(size)]))
+    return parts
 
 
 def solution(mesh):
-    torus = Mesh(
-        mesh.devices.reshape(mesh.shape["adapter"], 4, 2), ("adapter", "tensor_0", "tensor_1")
-    )
+    torus = Mesh(mesh.devices.reshape(8, 8, 4, 2), (*ADAPTER, *TENSOR))
     return jax.shard_map(
         layer,
         mesh=torus,
         in_specs=(
-            P("adapter", TENSOR),
+            P(ADAPTER, TENSOR),
             P(TENSOR, None),
-            P("adapter", None, TENSOR),
-            P("adapter", None, TENSOR),
-            P("adapter", None),
+            P(ADAPTER, None, TENSOR),
+            P(ADAPTER, None, TENSOR),
+            P(ADAPTER, None),
         ),
-        out_specs=P("adapter", TENSOR),
+        out_specs=P(ADAPTER, TENSOR),
         check_vma=False,
     )

time: 174 us -> 196 us (1.13)
  blocking collectives: 112 us -> 24.7 us
  starting transfers between devices: 33.4 us -> 102 us
  waiting for transfers between devices: 11 us -> 44.8 us
  Pallas kernels: 13.2 us -> 20.3 us
  local copies, waits for them, and re-layouts: 3.72 us -> 1.4 us
    all_to_all x3 -> x2, blocking collectives: 112 us -> 24.7 us  [swap(): return lax.all_to_all(x, axes, split_axis=0, concat_axis=0, tiled=True)]
    ppermute x7 -> x21, starting transfers between devices: 22.4 us -> 74.8 us  [xor_sends(): lax.ppermute(pieces[k], axis, [(i, i ^ k) for i in range(size)])]
    ppermute x7 -> x21, waiting for transfers between devices: 11 us -> 44.7 us  [xor_sends(): lax.ppermute(pieces[k], axis, [(i, i ^ k) for i in range(size)])]
    all_to_all x1 -> x2, starting transfers between devices: 11 us -> 27.1 us  [swap(): return lax.all_to_all(x, axes, split_axis=0, concat_axis=0, tiled=True)]
    pallas_call x4 -> x7, Pallas kernels: 11.1 us -> 16 us  [the longest x1 4.31 us: place_main(): pl.pallas_call(kernel, grid=(slots // tile,), in_specs=[pl.BlockSpec((1,...]
    unnamed x12, local copies, waits for them, and re-layouts: 3.69 us -> 1.37 us
  transfers between devices with their start and end apart: 8 -> 23, of which waited for: 3 -> 7; matrix products, arithmetic and copies ran while one was open for 0% -> 0% of each run, Pallas kernels for 1% -> 5%
where the time goes in v3:
time: 196 us; the launch traced here: 195 us
  starting transfers between devices  102 us (52%)
  waiting for transfers between devices  44.8 us (23%)
  blocking collectives  24.7 us (13%)
  Pallas kernels  20.3 us (10%)
    ppermute x21, starting transfers between devices, xor_sends(): lax.ppermute(pieces[k], axis, [(i, i ^ k) for i in range(size)])  74.8 us
    ppermute x21, waiting for transfers between devices, xor_sends(): lax.ppermute(pieces[k], axis, [(i, i ^ k) for i in range(size)])  44.7 us
    all_to_all x2, starting transfers between devices, swap(): return lax.all_to_all(x, axes, split_axis=0, concat_axis=0, tiled=True)  27.1 us
    all_to_all x2, blocking collectives, swap(): return lax.all_to_all(x, axes, split_axis=0, concat_axis=0, tiled=True)  24.7 us
    pallas_call x1, Pallas kernels, place_main(): pl.pallas_call(kernel, grid=(slots // tile,), in_specs=[pl.BlockSpec((1,...  4.31 us
  transfers between devices with their start and end apart: 23, of which 7 were waited for; matrix products, arithmetic and copies ran while one was open for 0% of the time, Pallas kernels for 5%

profile of v3, /device:TPU:1, one launch (start us, length us, event | category | flops | bytes accessed | tf_op | source)
XLA Modules:
  0.0 194.7 jit_solution(1626452662929198642)
XLA Ops:
  0.0 4.3 %place_main.1 = (bf16[1024,1024]{1,0:T(8,128)(2,1)S(1)}, s32[1,768]{1,0:T(1,128)S(1)}, s32[768,1]{1,0:T(8,128)S(1)}) custom-call(s32[1,768]{1,0:T(1,128)} %bitcast.30, bf16[768,1024]{1,0:T(8,128)(2,1)} %tok_ref.5), custom_call_target="tpu_custom_call" | custom-call | tf_op jit(solution)/shard_map/place_main/pallas_call | solution.py:263
  4.3 1.3 copy-done.1
  5.7 17.3 %all-to-all-start.4 = ((bf16[64,16,1024]{2,1,0:T(8,128)(2,1)}), bf16[64,16,1024]{2,1,0:T(8,128)(2,1)S(1)}, u32[]{:S(2)}, u32[]{:S(2)}) async-start(bf16[64,16,1024]{2,1,0:T(8,128)(2,1)} %bitcast.22), calls=%async_computation.4 | async-start | bytes 4194304 | tf_op jit(solution)/shard_map/all_to_all | solution.py:23
  23.0 2.2 %side_first.1 = (bf16[16,1024]{1,0:T(8,128)(2,1)S(1)}, bf16[16,1024]{1,0:T(8,128)(2,1)S(1)}, bf16[16,1024]{1,0:T(8,128)(2,1)S(1)}, bf16[16,1024]{1,0:T(8,128)(2,...) custom-call(s32[1]{0:T(128)} %bitcast.11.at_ref, ...), custom_call_target="tpu_custom_call" | custom-call | tf_op jit(solution)/shard_map/side_first/pallas_call | solution.py:345
  25.2 2.9 %collective-permute-start = (bf16[16,1024]{1,0:T(8,128)(2,1)S(1)}, bf16[16,1024]{1,0:T(8,128)(2,1)S(1)}, u32[]{:S(2)}, u32[]{:S(2)}) collective-permute-start(bf16[16,1024]{1,0:T(8,128)(2,1)S(1)} %get-tuple-element.61), channel_id=1, source_target_pairs={{0,8},{8,0},{16,24},{24,16},{32,40},{40,32},{48,56},{56,48},{1,9},... | collective-permute-start | bytes 98312 | tf_op jit(solution)/shard_map/ppermute | solution.py:580
  28.1 4.0 %collective-permute-start.1 = (bf16[16,1024]{1,0:T(8,128)(2,1)S(1)}, bf16[16,1024]{1,0:T(8,128)(2,1)S(1)}, u32[]{:S(2)}, u32[]{:S(2)}) collective-permute-start(bf16[16,1024]{1,0:T(8,128)(2,1)S(1)} %get-tuple-element.62), channel_id=1, source_target_pairs={{0,16},{8,24},{16,0},{24,8},{32,48},{40,56},{48,32},{56,40},{1,17}... | collective-permute-start | bytes 98312 | tf_op jit(solution)/shard_map/ppermute | solution.py:580
  32.1 2.4 %collective-permute-start.2 = (bf16[16,1024]{1,0:T(8,128)(2,1)S(1)}, bf16[16,1024]{1,0:T(8,128)(2,1)S(1)}, u32[]{:S(2)}, u32[]{:S(2)}) collective-permute-start(bf16[16,1024]{1,0:T(8,128)(2,1)S(1)} %get-tuple-element.63), channel_id=1, source_target_pairs={{0,24},{8,16},{16,8},{24,0},{32,56},{40,48},{48,40},{56,32},{1,25}... | collective-permute-start | bytes 98312 | tf_op jit(solution)/shard_map/ppermute | solution.py:580
  34.5 6.8 %collective-permute-start.3 = (bf16[16,1024]{1,0:T(8,128)(2,1)S(1)}, bf16[16,1024]{1,0:T(8,128)(2,1)S(1)}, u32[]{:S(2)}, u32[]{:S(2)}) collective-permute-start(bf16[16,1024]{1,0:T(8,128)(2,1)S(1)} %get-tuple-element.64), channel_id=1, source_target_pairs={{0,32},{8,40},{16,48},{24,56},{32,0},{40,8},{48,16},{56,24},{1,33}... | collective-permute-start | bytes 98312 | tf_op jit(solution)/shard_map/ppermute | solution.py:580
  41.3 1.9 collective-permute-start.4
  43.2 25.7 %collective-permute-done.refs_1_ = bf16[16,1024]{1,0:T(8,128)(2,1)S(1)} collective-permute-done((bf16[16,1024]{1,0:T(8,128)(2,1)S(1)}, bf16[16,1024]{1,0:T(8,128)(2,1)S(1)}, u32[]{:S(2)}, u32[]{:S(2)}) %collective-permute-start) | collective-permute-done | bytes 32800 | tf_op jit(solution)/shard_map/ppermute | solution.py:580
  69.0 7.3 %collective-permute-start.5 = (bf16[16,1024]{1,0:T(8,128)(2,1)S(1)}, bf16[16,1024]{1,0:T(8,128)(2,1)S(1)}, u32[]{:S(2)}, u32[]{:S(2)}) collective-permute-start(bf16[16,1024]{1,0:T(8,128)(2,1)S(1)} %get-tuple-element.66), channel_id=1, source_target_pairs={{0,48},{8,56},{16,32},{24,40},{32,16},{40,24},{48,0},{56,8},{1,49}... | collective-permute-start | bytes 98312 | tf_op jit(solution)/shard_map/ppermute | solution.py:580
  76.3 0.0 collective-permute-done.1.refs_2_
  76.3 1.9 collective-permute-start.6
  78.2 0.1 pad_add_fusion.at_ref
  78.3 0.0 collective-permute-done.2.refs_3_
  78.3 0.0 collective-permute-done.3.refs_4_
  78.3 0.0 collective-permute-done.4.refs_5_
  78.3 0.3 collective-permute-done.5.refs_6_
  78.6 3.7 %collective-permute-done.6.refs_7_ = bf16[16,1024]{1,0:T(8,128)(2,1)S(1)} collective-permute-done((bf16[16,1024]{1,0:T(8,128)(2,1)S(1)}, bf16[16,1024]{1,0:T(8,128)(2,1)S(1)}, u32[]{:S(2)}, u32[]{:S(2)}) %collective-permute-start.6) | collective-permute-done | bytes 32800 | tf_op jit(solution)/shard_map/ppermute | solution.py:580
  82.3 1.0 side_second.1
  83.3 1.9 collective-permute-start.7
  85.3 4.1 %collective-permute-start.8 = (bf16[16,1024]{1,0:T(8,128)(2,1)S(1)}, bf16[16,1024]{1,0:T(8,128)(2,1)S(1)}, u32[]{:S(2)}, u32[]{:S(2)}) collective-permute-start(bf16[16,1024]{1,0:T(8,128)(2,1)S(1)} %get-tuple-element.70), channel_id=1, source_target_pairs={{0,128},{64,192},{128,0},{192,64},{256,384},{320,448},{384,256},{4... | collective-permute-start | bytes 98312 | tf_op jit(solution)/shard_map/ppermute | solution.py:580
  89.4 3.2 %collective-permute-start.9 = (bf16[16,1024]{1,0:T(8,128)(2,1)S(1)}, bf16[16,1024]{1,0:T(8,128)(2,1)S(1)}, u32[]{:S(2)}, u32[]{:S(2)}) collective-permute-start(bf16[16,1024]{1,0:T(8,128)(2,1)S(1)} %get-tuple-element.71), channel_id=1, source_target_pairs={{0,192},{64,128},{128,64},{192,0},{256,448},{320,384},{384,320},{4... | collective-permute-start | bytes 98312 | tf_op jit(solution)/shard_map/ppermute | solution.py:580
  92.6 6.1 %collective-permute-start.10 = (bf16[16,1024]{1,0:T(8,128)(2,1)S(1)}, bf16[16,1024]{1,0:T(8,128)(2,1)S(1)}, u32[]{:S(2)}, u32[]{:S(2)}) collective-permute-start(bf16[16,1024]{1,0:T(8,128)(2,1)S(1)} %get-tuple-element.72), channel_id=1, source_target_pairs={{0,256},{64,320},{128,384},{192,448},{256,0},{320,64},{384,128},{4... | collective-permute-start | bytes 98312 | tf_op jit(solution)/shard_map/ppermute | solution.py:580
  98.7 1.9 collective-permute-start.11
  100.7 0.0 collective-permute-done.7.refs_1_
  100.7 5.6 %collective-permute-start.12 = (bf16[16,1024]{1,0:T(8,128)(2,1)S(1)}, bf16[16,1024]{1,0:T(8,128)(2,1)S(1)}, u32[]{:S(2)}, u32[]{:S(2)}) collective-permute-start(bf16[16,1024]{1,0:T(8,128)(2,1)S(1)} %get-tuple-element.74), channel_id=1, source_target_pairs={{0,384},{64,448},{128,256},{192,320},{256,128},{320,192},{384,0},{... | collective-permute-start | bytes 98312 | tf_op jit(solution)/shard_map/ppermute | solution.py:580
  106.3 0.0 collective-permute-done.8.refs_2_
  106.3 2.1 %collective-permute-start.13 = (bf16[16,1024]{1,0:T(8,128)(2,1)S(1)}, bf16[16,1024]{1,0:T(8,128)(2,1)S(1)}, u32[]{:S(2)}, u32[]{:S(2)}) collective-permute-start(bf16[16,1024]{1,0:T(8,128)(2,1)S(1)} %get-tuple-element.75), channel_id=1, source_target_pairs={{0,448},{64,384},{128,320},{192,256},{256,192},{320,128},{384,64},... | collective-permute-start | bytes 98312 | tf_op jit(solution)/shard_map/ppermute | solution.py:580
  108.4 0.0 collective-permute-done.9.refs_3_
  108.4 0.0 collective-permute-done.10.refs_4_
  108.4 0.0 collective-permute-done.11.refs_5_
  108.4 0.0 collective-permute-done.12.refs_6_
  108.4 4.0 %collective-permute-done.13.refs_7_ = bf16[16,1024]{1,0:T(8,128)(2,1)S(1)} collective-permute-done((bf16[16,1024]{1,0:T(8,128)(2,1)S(1)}, bf16[16,1024]{1,0:T(8,128)(2,1)S(1)}, u32[]{:S(2)}, u32[]{:S(2)}) %collective-permute-start.13) | collective-permute-done | bytes 32800 | tf_op jit(solution)/shard_map/ppermute | solution.py:580
  112.4 1.9 side_low.1
  114.4 0.0 all-to-all-done.4
  114.4 0.0 copy-start.5
  114.4 2.6 %down_main.1 = bf16[768,128]{1,0:T(8,128)(2,1)S(1)} custom-call(bf16[1024,1024]{1,0:T(8,128)(2,1)S(1)} %bitcast.20, bf16[256,128]{1,0:T(8,128)(2,1)S(1)} %get-tuple-element.76.thirds_ref, bf16[8,64,1024]{2,1,0:T(8,128)(2,1)} %down_ref.1), custom_call_target="tpu_custom_call" | custom-call | tf_op jit(solution)/shard_map/down_main/pallas_call | solution.py:448
  117.0 0.0 copy-start
  117.0 15.5 %all_to_all.40 = bf16[8,96,128]{2,1,0:T(8,128)(2,1)S(1)} all-to-all(bf16[8,96,128]{2,1,0:T(8,128)(2,1)S(1)} %bitcast.28), channel_id=1, replica_groups=mesh['z'=8,'y'=8,'tensor_0'=4,'tensor_1'=2] {'tensor_0','tensor_1'}, dimensions={0} | all-to-all | bytes 393216 | tf_op jit(solution)/shard_map/all_to_all | solution.py:23
  132.6 9.2 %all_to_all.41 = bf16[8,96,128]{2,1,0:T(8,128)(2,1)S(1)} all-to-all(bf16[8,96,128]{2,1,0:T(8,128)(2,1)S(1)} %broadcast_in_dim.4), channel_id=1, replica_groups=mesh['z'=8,'y'=8,'tensor_0'=4,'tensor_1'=2] {'tensor_0','tensor_1'}, dimensions={0} | all-to-all | bytes 393216 | tf_op jit(solution)/shard_map/all_to_all | solution.py:23
  141.8 1.4 up_main.1
  143.2 9.9 %all-to-all-start.7 = ((bf16[64,24,128]{2,1,0:T(8,128)(2,1)}), bf16[64,24,128]{2,1,0:T(8,128)(2,1)S(1)}, u32[]{:S(2)}, u32[]{:S(2)}) async-start(bf16[64,24,128]{2,1,0:T(8,128)(2,1)} %bitcast.14), calls=%async_computation.7 | async-start | bytes 786432 | tf_op jit(solution)/shard_map/all_to_all | solution.py:23
  153.1 3.3 %value_pieces.1 = (bf16[768,128]{1,0:T(8,128)(2,1)S(1)}, bf16[768,128]{1,0:T(8,128)(2,1)S(1)}, bf16[768,128]{1,0:T(8,128)(2,1)S(1)}, bf16[768,128]{1,0:T(8,128)(...) custom-call(s32[1]{0:T(128)} %bitcast.16.at_ref, ...), custom_call_target="tpu_custom_call" | custom-call | tf_op jit(solution)/shard_map/value_pieces/pallas_call | solution.py:89
  156.4 0.0 copy-start.2
  156.4 0.0 copy-start.3
  156.4 3.3 %collective-permute-start.14 = (bf16[768,128]{1,0:T(8,128)(2,1)S(1)}, bf16[768,128]{1,0:T(8,128)(2,1)S(1)}, u32[]{:S(2)}, u32[]{:S(2)}) collective-permute-start(bf16[768,128]{1,0:T(8,128)(2,1)S(1)} %get-tuple-element.79), channel_id=1, source_target_pairs={{0,1},{1,0},{2,3},{3,2},{4,5},{5,4},{6,7},{7,6},{8,9},{9,8},{10,11... | collective-permute-start | bytes 589832 | tf_op jit(solution)/shard_map/ppermute | solution.py:580
  159.7 2.2 %collective-permute-start.15 = (bf16[768,128]{1,0:T(8,128)(2,1)S(1)}, bf16[768,128]{1,0:T(8,128)(2,1)S(1)}, u32[]{:S(2)}, u32[]{:S(2)}) collective-permute-start(bf16[768,128]{1,0:T(8,128)(2,1)S(1)} %get-tuple-element.80), channel_id=1, source_target_pairs={{0,2},{1,3},{2,0},{3,1},{4,6},{5,7},{6,4},{7,5},{8,10},{9,11},{10,... | collective-permute-start | bytes 589832 | tf_op jit(solution)/shard_map/ppermute | solution.py:580
  161.9 3.3 %collective-permute-start.16 = (bf16[768,128]{1,0:T(8,128)(2,1)S(1)}, bf16[768,128]{1,0:T(8,128)(2,1)S(1)}, u32[]{:S(2)}, u32[]{:S(2)}) collective-permute-start(bf16[768,128]{1,0:T(8,128)(2,1)S(1)} %get-tuple-element.81), channel_id=1, source_target_pairs={{0,3},{1,2},{2,1},{3,0},{4,7},{5,6},{6,5},{7,4},{8,11},{9,10},{10,... | collective-permute-start | bytes 589832 | tf_op jit(solution)/shard_map/ppermute | solution.py:580
  165.2 2.3 %collective-permute-start.17 = (bf16[768,128]{1,0:T(8,128)(2,1)S(1)}, bf16[768,128]{1,0:T(8,128)(2,1)S(1)}, u32[]{:S(2)}, u32[]{:S(2)}) collective-permute-start(bf16[768,128]{1,0:T(8,128)(2,1)S(1)} %get-tuple-element.82), channel_id=1, source_target_pairs={{0,4},{1,5},{2,6},{3,7},{4,0},{5,1},{6,2},{7,3},{8,12},{9,13},{10,... | collective-permute-start | bytes 589832 | tf_op jit(solution)/shard_map/ppermute | solution.py:580
  167.5 4.8 %collective-permute-start.18 = (bf16[768,128]{1,0:T(8,128)(2,1)S(1)}, bf16[768,128]{1,0:T(8,128)(2,1)S(1)}, u32[]{:S(2)}, u32[]{:S(2)}) collective-permute-start(bf16[768,128]{1,0:T(8,128)(2,1)S(1)} %get-tuple-element.83), channel_id=1, source_target_pairs={{0,5},{1,4},{2,7},{3,6},{4,1},{5,0},{6,3},{7,2},{8,13},{9,12},{10,... | collective-permute-start | bytes 589832 | tf_op jit(solution)/shard_map/ppermute | solution.py:580
  172.3 0.0 collective-permute-done.14.refs_1_
  172.4 2.8 %collective-permute-start.19 = (bf16[768,128]{1,0:T(8,128)(2,1)S(1)}, bf16[768,128]{1,0:T(8,128)(2,1)S(1)}, u32[]{:S(2)}, u32[]{:S(2)}) collective-permute-start(bf16[768,128]{1,0:T(8,128)(2,1)S(1)} %get-tuple-element.84), channel_id=1, source_target_pairs={{0,6},{1,7},{2,4},{3,5},{4,2},{5,3},{6,0},{7,1},{8,14},{9,15},{10,... | collective-permute-start | bytes 589832 | tf_op jit(solution)/shard_map/ppermute | solution.py:580
  175.1 0.0 collective-permute-done.15.refs_2_
  175.2 3.9 %collective-permute-start.20 = (bf16[768,128]{1,0:T(8,128)(2,1)S(1)}, bf16[768,128]{1,0:T(8,128)(2,1)S(1)}, u32[]{:S(2)}, u32[]{:S(2)}) collective-permute-start(bf16[768,128]{1,0:T(8,128)(2,1)S(1)} %get-tuple-element.85), channel_id=1, source_target_pairs={{0,7},{1,6},{2,5},{3,4},{4,3},{5,2},{6,1},{7,0},{8,15},{9,14},{10,... | collective-permute-start | bytes 589832 | tf_op jit(solution)/shard_map/ppermute | solution.py:580
  179.1 0.0 collective-permute-done.16.refs_3_
  179.1 0.0 collective-permute-done.17.refs_4_
  179.1 2.5 %collective-permute-done.18.refs_5_ = bf16[768,128]{1,0:T(8,128)(2,1)S(1)} collective-permute-done((bf16[768,128]{1,0:T(8,128)(2,1)S(1)}, bf16[768,128]{1,0:T(8,128)(2,1)S(1)}, u32[]{:S(2)}, u32[]{:S(2)}) %collective-permute-start.18) | collective-permute-done | bytes 196640 | tf_op jit(solution)/shard_map/ppermute | solution.py:580
  181.5 4.4 %collective-permute-done.19.refs_6_ = bf16[768,128]{1,0:T(8,128)(2,1)S(1)} collective-permute-done((bf16[768,128]{1,0:T(8,128)(2,1)S(1)}, bf16[768,128]{1,0:T(8,128)(2,1)S(1)}, u32[]{:S(2)}, u32[]{:S(2)}) %collective-permute-start.19) | collective-permute-done | bytes 196640 | tf_op jit(solution)/shard_map/ppermute | solution.py:580
  185.9 4.2 %collective-permute-done.20.refs_7_ = bf16[768,128]{1,0:T(8,128)(2,1)S(1)} collective-permute-done((bf16[768,128]{1,0:T(8,128)(2,1)S(1)}, bf16[768,128]{1,0:T(8,128)(2,1)S(1)}, u32[]{:S(2)}, u32[]{:S(2)}) %collective-permute-start.20) | collective-permute-done | bytes 196640 | tf_op jit(solution)/shard_map/ppermute | solution.py:580
  190.1 0.9 base_sum.1.base_ref
  191.1 0.0 all-to-all-done.7
  191.1 2.5 %take_main.1 = (bf16[768,128]{1,0:T(8,128)(2,1)}, s32[1]{0:T(128)}) custom-call(s32[768,1]{1,0:T(8,128)S(1)} %get-tuple-element.57.at_ref, bf16[1536,128]{1,0:T(8,128)(2,1)S(1)} %bitcast.23, f32[768,128]{1,0:T(8,128)} %base_sum.1.base_ref), custom_call_target="tpu_custom_call" | custom-call | tf_op jit(solution)/shard_map/take_main/pallas_call | solution.py:509
  194.3 0.2 conditional.1
  (9 shorter events, 0.1 us)
Async XLA Ops:
  4.3 1.3 copy-start.1
  5.7 17.3 %copy-start.6 = (s32[768,1]{0,1:T(1,128)S(1)}, s32[768,1]{0,1:T(1,128)}, u32[]{:S(2)}) copy-start(s32[768,1]{0,1:T(1,128)} %param.11) | copy-start | bytes 9220
  5.7 108.7 %all-to-all-start.4 = ((bf16[64,16,1024]{2,1,0:T(8,128)(2,1)}), bf16[64,16,1024]{2,1,0:T(8,128)(2,1)S(1)}, u32[]{:S(2)}, u32[]{:S(2)}) async-start(bf16[64,16,1024]{2,1,0:T(8,128)(2,1)} %bitcast.22), calls=%async_computation.4 | async-start | bytes 4194304 | tf_op jit(solution)/shard_map/all_to_all | solution.py:23
  25.2 43.8 %collective-permute-start = (bf16[16,1024]{1,0:T(8,128)(2,1)S(1)}, bf16[16,1024]{1,0:T(8,128)(2,1)S(1)}, u32[]{:S(2)}, u32[]{:S(2)}) collective-permute-start(bf16[16,1024]{1,0:T(8,128)(2,1)S(1)} %get-tuple-element.61), channel_id=1, source_target_pairs={{0,8},{8,0},{16,24},{24,16},{32,40},{40,32},{48,56},{56,48},{1,9},... | collective-permute-start | bytes 98312 | tf_op jit(solution)/shard_map/ppermute | solution.py:580
  28.1 48.2 %collective-permute-start.1 = (bf16[16,1024]{1,0:T(8,128)(2,1)S(1)}, bf16[16,1024]{1,0:T(8,128)(2,1)S(1)}, u32[]{:S(2)}, u32[]{:S(2)}) collective-permute-start(bf16[16,1024]{1,0:T(8,128)(2,1)S(1)} %get-tuple-element.62), channel_id=1, source_target_pairs={{0,16},{8,24},{16,0},{24,8},{32,48},{40,56},{48,32},{56,40},{1,17}... | collective-permute-start | bytes 98312 | tf_op jit(solution)/shard_map/ppermute | solution.py:580
  32.1 46.2 %collective-permute-start.2 = (bf16[16,1024]{1,0:T(8,128)(2,1)S(1)}, bf16[16,1024]{1,0:T(8,128)(2,1)S(1)}, u32[]{:S(2)}, u32[]{:S(2)}) collective-permute-start(bf16[16,1024]{1,0:T(8,128)(2,1)S(1)} %get-tuple-element.63), channel_id=1, source_target_pairs={{0,24},{8,16},{16,8},{24,0},{32,56},{40,48},{48,40},{56,32},{1,25}... | collective-permute-start | bytes 98312 | tf_op jit(solution)/shard_map/ppermute | solution.py:580
  34.5 43.9 %collective-permute-start.3 = (bf16[16,1024]{1,0:T(8,128)(2,1)S(1)}, bf16[16,1024]{1,0:T(8,128)(2,1)S(1)}, u32[]{:S(2)}, u32[]{:S(2)}) collective-permute-start(bf16[16,1024]{1,0:T(8,128)(2,1)S(1)} %get-tuple-element.64), channel_id=1, source_target_pairs={{0,32},{8,40},{16,48},{24,56},{32,0},{40,8},{48,16},{56,24},{1,33}... | collective-permute-start | bytes 98312 | tf_op jit(solution)/shard_map/ppermute | solution.py:580
  41.3 37.0 %collective-permute-start.4 = (bf16[16,1024]{1,0:T(8,128)(2,1)S(1)}, bf16[16,1024]{1,0:T(8,128)(2,1)S(1)}, u32[]{:S(2)}, u32[]{:S(2)}) collective-permute-start(bf16[16,1024]{1,0:T(8,128)(2,1)S(1)} %get-tuple-element.65), channel_id=1, source_target_pairs={{0,40},{8,32},{16,56},{24,48},{32,8},{40,0},{48,24},{56,16},{1,41}... | collective-permute-start | bytes 98312 | tf_op jit(solution)/shard_map/ppermute | solution.py:580
  69.0 9.6 %collective-permute-start.5 = (bf16[16,1024]{1,0:T(8,128)(2,1)S(1)}, bf16[16,1024]{1,0:T(8,128)(2,1)S(1)}, u32[]{:S(2)}, u32[]{:S(2)}) collective-permute-start(bf16[16,1024]{1,0:T(8,128)(2,1)S(1)} %get-tuple-element.66), channel_id=1, source_target_pairs={{0,48},{8,56},{16,32},{24,40},{32,16},{40,24},{48,0},{56,8},{1,49}... | collective-permute-start | bytes 98312 | tf_op jit(solution)/shard_map/ppermute | solution.py:580
  76.3 6.0 %collective-permute-start.6 = (bf16[16,1024]{1,0:T(8,128)(2,1)S(1)}, bf16[16,1024]{1,0:T(8,128)(2,1)S(1)}, u32[]{:S(2)}, u32[]{:S(2)}) collective-permute-start(bf16[16,1024]{1,0:T(8,128)(2,1)S(1)} %get-tuple-element.67), channel_id=1, source_target_pairs={{0,56},{8,48},{16,40},{24,32},{32,24},{40,16},{48,8},{56,0},{1,57}... | collective-permute-start | bytes 98312 | tf_op jit(solution)/shard_map/ppermute | solution.py:580
  83.3 17.3 %collective-permute-start.7 = (bf16[16,1024]{1,0:T(8,128)(2,1)S(1)}, bf16[16,1024]{1,0:T(8,128)(2,1)S(1)}, u32[]{:S(2)}, u32[]{:S(2)}) collective-permute-start(bf16[16,1024]{1,0:T(8,128)(2,1)S(1)} %get-tuple-element.69), channel_id=1, source_target_pairs={{0,64},{64,0},{128,192},{192,128},{256,320},{320,256},{384,448},{4... | collective-permute-start | bytes 98312 | tf_op jit(solution)/shard_map/ppermute | solution.py:580
  85.3 21.0 %collective-permute-start.8 = (bf16[16,1024]{1,0:T(8,128)(2,1)S(1)}, bf16[16,1024]{1,0:T(8,128)(2,1)S(1)}, u32[]{:S(2)}, u32[]{:S(2)}) collective-permute-start(bf16[16,1024]{1,0:T(8,128)(2,1)S(1)} %get-tuple-element.70), channel_id=1, source_target_pairs={{0,128},{64,192},{128,0},{192,64},{256,384},{320,448},{384,256},{4... | collective-permute-start | bytes 98312 | tf_op jit(solution)/shard_map/ppermute | solution.py:580
  89.4 19.0 %collective-permute-start.9 = (bf16[16,1024]{1,0:T(8,128)(2,1)S(1)}, bf16[16,1024]{1,0:T(8,128)(2,1)S(1)}, u32[]{:S(2)}, u32[]{:S(2)}) collective-permute-start(bf16[16,1024]{1,0:T(8,128)(2,1)S(1)} %get-tuple-element.71), channel_id=1, source_target_pairs={{0,192},{64,128},{128,64},{192,0},{256,448},{320,384},{384,320},{4... | collective-permute-start | bytes 98312 | tf_op jit(solution)/shard_map/ppermute | solution.py:580
  92.6 15.7 %collective-permute-start.10 = (bf16[16,1024]{1,0:T(8,128)(2,1)S(1)}, bf16[16,1024]{1,0:T(8,128)(2,1)S(1)}, u32[]{:S(2)}, u32[]{:S(2)}) collective-permute-start(bf16[16,1024]{1,0:T(8,128)(2,1)S(1)} %get-tuple-element.72), channel_id=1, source_target_pairs={{0,256},{64,320},{128,384},{192,448},{256,0},{320,64},{384,128},{4... | collective-permute-start | bytes 98312 | tf_op jit(solution)/shard_map/ppermute | solution.py:580
  98.7 9.6 %collective-permute-start.11 = (bf16[16,1024]{1,0:T(8,128)(2,1)S(1)}, bf16[16,1024]{1,0:T(8,128)(2,1)S(1)}, u32[]{:S(2)}, u32[]{:S(2)}) collective-permute-start(bf16[16,1024]{1,0:T(8,128)(2,1)S(1)} %get-tuple-element.73), channel_id=1, source_target_pairs={{0,320},{64,256},{128,448},{192,384},{256,64},{320,0},{384,192},{4... | collective-permute-start | bytes 98312 | tf_op jit(solution)/shard_map/ppermute | solution.py:580
  100.7 7.7 %collective-permute-start.12 = (bf16[16,1024]{1,0:T(8,128)(2,1)S(1)}, bf16[16,1024]{1,0:T(8,128)(2,1)S(1)}, u32[]{:S(2)}, u32[]{:S(2)}) collective-permute-start(bf16[16,1024]{1,0:T(8,128)(2,1)S(1)} %get-tuple-element.74), channel_id=1, source_target_pairs={{0,384},{64,448},{128,256},{192,320},{256,128},{320,192},{384,0},{... | collective-permute-start | bytes 98312 | tf_op jit(solution)/shard_map/ppermute | solution.py:580
  106.3 6.1 %collective-permute-start.13 = (bf16[16,1024]{1,0:T(8,128)(2,1)S(1)}, bf16[16,1024]{1,0:T(8,128)(2,1)S(1)}, u32[]{:S(2)}, u32[]{:S(2)}) collective-permute-start(bf16[16,1024]{1,0:T(8,128)(2,1)S(1)} %get-tuple-element.75), channel_id=1, source_target_pairs={{0,448},{64,384},{128,320},{192,256},{256,192},{320,128},{384,64},... | collective-permute-start | bytes 98312 | tf_op jit(solution)/shard_map/ppermute | solution.py:580
  114.4 27.4 %copy-start.5 = (bf16[8,64,128]{2,1,0:T(8,128)(2,1)S(1)}, bf16[8,64,128]{2,1,0:T(8,128)(2,1)}, u32[]{:S(2)}) copy-start(bf16[8,64,128]{2,1,0:T(8,128)(2,1)} %up_ref.1) | copy-start | bytes 393220
  117.0 36.0 %copy-start = (bf16[1024,1024]{1,0:T(8,128)(2,1)S(1)}, bf16[1024,1024]{1,0:T(8,128)(2,1)}, u32[]{:S(2)}) copy-start(bf16[1024,1024]{1,0:T(8,128)(2,1)} %w_ref.1) | copy-start | bytes 6291460
  143.2 47.9 %all-to-all-start.7 = ((bf16[64,24,128]{2,1,0:T(8,128)(2,1)}), bf16[64,24,128]{2,1,0:T(8,128)(2,1)S(1)}, u32[]{:S(2)}, u32[]{:S(2)}) async-start(bf16[64,24,128]{2,1,0:T(8,128)(2,1)} %bitcast.14), calls=%async_computation.7 | async-start | bytes 786432 | tf_op jit(solution)/shard_map/all_to_all | solution.py:23
  156.4 37.9 %copy-start.2 = (bf16[768,1024]{1,0:T(8,128)(2,1)S(1)}, bf16[768,1024]{1,0:T(8,128)(2,1)}, u32[]{:S(2)}) copy-start(bf16[768,1024]{1,0:T(8,128)(2,1)} %tok_ref.5) | copy-start | bytes 4718596
  156.4 37.9 %copy-start.3 = (bf16[8,64,1024]{2,1,0:T(8,128)(2,1)S(1)}, bf16[8,64,1024]{2,1,0:T(8,128)(2,1)}, u32[]{:S(2)}) copy-start(bf16[8,64,1024]{2,1,0:T(8,128)(2,1)} %down_ref.1) | copy-start | bytes 3145732
  156.4 16.0 %collective-permute-start.14 = (bf16[768,128]{1,0:T(8,128)(2,1)S(1)}, bf16[768,128]{1,0:T(8,128)(2,1)S(1)}, u32[]{:S(2)}, u32[]{:S(2)}) collective-permute-start(bf16[768,128]{1,0:T(8,128)(2,1)S(1)} %get-tuple-element.79), channel_id=1, source_target_pairs={{0,1},{1,0},{2,3},{3,2},{4,5},{5,4},{6,7},{7,6},{8,9},{9,8},{10,11... | collective-permute-start | bytes 589832 | tf_op jit(solution)/shard_map/ppermute | solution.py:580
  159.7 15.5 %collective-permute-start.15 = (bf16[768,128]{1,0:T(8,128)(2,1)S(1)}, bf16[768,128]{1,0:T(8,128)(2,1)S(1)}, u32[]{:S(2)}, u32[]{:S(2)}) collective-permute-start(bf16[768,128]{1,0:T(8,128)(2,1)S(1)} %get-tuple-element.80), channel_id=1, source_target_pairs={{0,2},{1,3},{2,0},{3,1},{4,6},{5,7},{6,4},{7,5},{8,10},{9,11},{10,... | collective-permute-start | bytes 589832 | tf_op jit(solution)/shard_map/ppermute | solution.py:580
  161.9 17.2 %collective-permute-start.16 = (bf16[768,128]{1,0:T(8,128)(2,1)S(1)}, bf16[768,128]{1,0:T(8,128)(2,1)S(1)}, u32[]{:S(2)}, u32[]{:S(2)}) collective-permute-start(bf16[768,128]{1,0:T(8,128)(2,1)S(1)} %get-tuple-element.81), channel_id=1, source_target_pairs={{0,3},{1,2},{2,1},{3,0},{4,7},{5,6},{6,5},{7,4},{8,11},{9,10},{10,... | collective-permute-start | bytes 589832 | tf_op jit(solution)/shard_map/ppermute | solution.py:580
  165.2 13.9 %collective-permute-start.17 = (bf16[768,128]{1,0:T(8,128)(2,1)S(1)}, bf16[768,128]{1,0:T(8,128)(2,1)S(1)}, u32[]{:S(2)}, u32[]{:S(2)}) collective-permute-start(bf16[768,128]{1,0:T(8,128)(2,1)S(1)} %get-tuple-element.82), channel_id=1, source_target_pairs={{0,4},{1,5},{2,6},{3,7},{4,0},{5,1},{6,2},{7,3},{8,12},{9,13},{10,... | collective-permute-start | bytes 589832 | tf_op jit(solution)/shard_map/ppermute | solution.py:580
  167.5 14.0 %collective-permute-start.18 = (bf16[768,128]{1,0:T(8,128)(2,1)S(1)}, bf16[768,128]{1,0:T(8,128)(2,1)S(1)}, u32[]{:S(2)}, u32[]{:S(2)}) collective-permute-start(bf16[768,128]{1,0:T(8,128)(2,1)S(1)} %get-tuple-element.83), channel_id=1, source_target_pairs={{0,5},{1,4},{2,7},{3,6},{4,1},{5,0},{6,3},{7,2},{8,13},{9,12},{10,... | collective-permute-start | bytes 589832 | tf_op jit(solution)/shard_map/ppermute | solution.py:580
  172.4 13.5 %collective-permute-start.19 = (bf16[768,128]{1,0:T(8,128)(2,1)S(1)}, bf16[768,128]{1,0:T(8,128)(2,1)S(1)}, u32[]{:S(2)}, u32[]{:S(2)}) collective-permute-start(bf16[768,128]{1,0:T(8,128)(2,1)S(1)} %get-tuple-element.84), channel_id=1, source_target_pairs={{0,6},{1,7},{2,4},{3,5},{4,2},{5,3},{6,0},{7,1},{8,14},{9,15},{10,... | collective-permute-start | bytes 589832 | tf_op jit(solution)/shard_map/ppermute | solution.py:580
  175.2 15.0 %collective-permute-start.20 = (bf16[768,128]{1,0:T(8,128)(2,1)S(1)}, bf16[768,128]{1,0:T(8,128)(2,1)S(1)}, u32[]{:S(2)}, u32[]{:S(2)}) collective-permute-start(bf16[768,128]{1,0:T(8,128)(2,1)S(1)} %get-tuple-element.85), channel_id=1, source_target_pairs={{0,7},{1,6},{2,5},{3,4},{4,3},{5,2},{6,1},{7,0},{8,15},{9,14},{10,... | collective-permute-start | bytes 589832 | tf_op jit(solution)/shard_map/ppermute | solution.py:580

commit v4 on v3

--- a/solution.py
+++ b/solution.py
@@ -13,6 +13,8 @@
 MOST = 3
 MAIN = 2
 SIDE = 16
+STAY = (0, 4, 2, 6)
+LEAVE = (1, 5, 3, 7)
 LOST = 3e38
 GRANT = pltpu.CompilerParams(vmem_limit_bytes=16 * 2**20)
 
@@ -73,8 +75,7 @@
     cols = weight.shape[1] // pieces
     step = 2
 
-    def kernel(at_ref, tok_ref, w_ref, *refs):
-        out_refs, part_ref = refs[:-1], refs[-1]
+    def kernel(at_ref, tok_ref, w_ref, own_ref, other_ref, part_ref):
         for first in range(0, pieces, step):
             part = jnp.dot(
                 tok_ref[...],
@@ -83,8 +84,9 @@
             ).astype(jnp.bfloat16)
             for k in range(step):
                 part_ref[first + k] = part[:, k * cols : (k + 1) * cols]
-        for k in range(pieces):
-            out_refs[k][...] = part_ref[at_ref[0] ^ k]
+        for k in range(pieces // 2):
+            own_ref[k] = part_ref[at_ref[0] ^ (2 * k)]
+            other_ref[k] = part_ref[at_ref[0] ^ (2 * k + 1)]
 
     return pl.pallas_call(
         kernel,
@@ -93,17 +95,33 @@
             pl.BlockSpec((rows, width), lambda: (0, 0)),
             pl.BlockSpec(weight.shape, lambda: (0, 0)),
         ],
-        out_shape=[jax.ShapeDtypeStruct((rows, cols), jnp.bfloat16)] * pieces,
+        out_shape=[jax.ShapeDtypeStruct((pieces // 2, rows, cols), jnp.bfloat16)] * 2,
         scratch_shapes=[pltpu.VMEM((pieces, rows, cols), jnp.bfloat16)],
         compiler_params=GRANT,
         name="value_pieces",
     )(at, tokens, weight)
 
 
-def base_sum(parts):
-    def kernel(*refs):
-        total = refs[0][...].astype(jnp.float32)
-        for ref in refs[1:-1]:
+def pair_sum(own, other):
+    count, rows, cols = own.shape
+
+    def kernel(own_ref, other_ref, *out_refs):
+        for k in range(1, count):
+            total = own_ref[k].astype(jnp.float32) + other_ref[k].astype(jnp.float32)
+            out_refs[k - 1][...] = total.astype(jnp.bfloat16)
+
+    return pl.pallas_call(
+        kernel,
+        out_shape=[jax.ShapeDtypeStruct((rows, cols), jnp.bfloat16)] * (count - 1),
+        compiler_params=GRANT,
+        name="pair_sum",
+    )(own, other)
+
+
+def base_sum(own, other, parts):
+    def kernel(own_ref, other_ref, *refs):
+        total = own_ref[0].astype(jnp.float32) + other_ref[0].astype(jnp.float32)
+        for ref in refs[:-1]:
             total = total + ref[...].astype(jnp.float32)
         refs[-1][...] = total
 
@@ -112,7 +130,7 @@
         out_shape=jax.ShapeDtypeStruct(parts[0].shape, jnp.float32),
         compiler_params=GRANT,
         name="base_sum",
-    )(*parts)
+    )(own, other, *parts)
 
 
 def adapter_of(shape, first, group):
@@ -310,18 +328,38 @@
         block_ref[k] = jnp.where(
             row == SIDE - 1, note, data[k * SIDE : (k + 1) * SIDE]
         ).astype(jnp.bfloat16)
-    for k in range(8):
-        out_refs[k][...] = block_ref[at ^ k]
-
-
-def read_codes(in_refs):
+    for ref, order in zip(out_refs, (STAY, LEAVE)):
+        for i, k in enumerate(order):
+            ref[i * SIDE : (i + 1) * SIDE, :] = block_ref[at ^ k]
+
+
+def arrived_blocks(refs):
+    stay, first, second, third = refs
+    spots = [(stay, 0), (first, 0), (second, 0), (second, 2)] + [(third, i) for i in range(4)]
+    return [ref[i * SIDE : (i + 1) * SIDE, :] for ref, i in spots]
+
+
+def halving_sends(stay, leave, axis):
+    size = lax.axis_size(axis)
+
+    def send(x, step):
+        return lax.ppermute(x, axis, [(i, i ^ step) for i in range(size)])
+
+    half = 2 * SIDE
+    first = send(leave, 1)
+    second = send(jnp.concatenate([stay[half:], first[half:]]), 2)
+    last = [x[i * SIDE : (i + 1) * SIDE] for x, i in ((stay, 1), (first, 1), (second, 1), (second, 3))]
+    third = send(jnp.concatenate(last), 4)
+    return stay, first, second, third
+
+
+def read_codes(blocks):
     n = 8 * SIDE
     lane = lax.broadcasted_iota(jnp.int32, (8, n), 1)
     codes = jnp.zeros((8, n), jnp.float32)
     flag = jnp.zeros((1, 1), jnp.float32)
     for k in range(8):
-        block = in_refs[k][...].astype(jnp.float32)
-        note = block[SIDE - 1 : SIDE, :n]
+        note = blocks[k].astype(jnp.float32)[SIDE - 1 : SIDE, :n]
         flag = jnp.maximum(flag, note[:, 127:128])
         own = jnp.where(lane < SIDE - 1, jnp.broadcast_to(note, (8, n)), 0.0)
         codes = codes + (pltpu.roll(own, k * SIDE, 1) if k else own)
@@ -339,13 +377,13 @@
         marked = jnp.where(third, key, -1)
         bucket(
             tok_ref[...], key, to_col(marked), home // 8 * 8 + row % HERE, third, None,
-            jnp.zeros((1, 1), jnp.float32), refs[:8], refs[8], at_ref[0],
+            jnp.zeros((1, 1), jnp.float32), refs[:2], refs[2], at_ref[0],
         )
 
     return pl.pallas_call(
         kernel,
         in_specs=[scalar_spec()] + [pl.BlockSpec(memory_space=pltpu.VMEM)] * 3,
-        out_shape=[jax.ShapeDtypeStruct((SIDE, width), jnp.bfloat16)] * 8,
+        out_shape=[jax.ShapeDtypeStruct((4 * SIDE, width), jnp.bfloat16)] * 2,
         scratch_shapes=[pltpu.VMEM((8, SIDE, width), jnp.bfloat16)],
         compiler_params=GRANT,
         name="side_first",
@@ -357,20 +395,21 @@
     n = 8 * SIDE
 
     def kernel(at_ref, *refs):
-        code, flag = read_codes(refs[:8])
+        blocks = arrived_blocks(refs[:4])
+        code, flag = read_codes(blocks)
         valid = code >= 0
         key = jnp.where(valid, code // 8, -1)
         from_y = (lax.broadcasted_iota(jnp.int32, (1, n), 1) // SIDE) ^ at_ref[1]
-        rows_of = jnp.concatenate([ref[...] for ref in refs[:8]], axis=0)
+        rows_of = jnp.concatenate(blocks, axis=0)
         bucket(
             rows_of, key, to_col(key), from_y * 8 + code % 8, valid, None,
-            flag, refs[8:16], refs[16], at_ref[0],
+            flag, refs[4:6], refs[6], at_ref[0],
         )
 
     return pl.pallas_call(
         kernel,
-        in_specs=[scalar_spec()] + [pl.BlockSpec(memory_space=pltpu.VMEM)] * 8,
-        out_shape=[jax.ShapeDtypeStruct((SIDE, width), jnp.bfloat16)] * 8,
+        in_specs=[scalar_spec()] + [pl.BlockSpec(memory_space=pltpu.VMEM)] * 4,
+        out_shape=[jax.ShapeDtypeStruct((4 * SIDE, width), jnp.bfloat16)] * 2,
         scratch_shapes=[pltpu.VMEM((8, SIDE, width), jnp.bfloat16)],
         compiler_params=GRANT,
         name="side_second",
@@ -398,11 +437,12 @@
     pair = 2 * rank
 
     def kernel(at_ref, *refs):
-        down_ref, out_ref, flag_ref = refs[8:]
-        code, flag = read_codes(refs[:8])
+        down_ref, out_ref, flag_ref = refs[4:]
+        blocks = arrived_blocks(refs[:4])
+        code, flag = read_codes(blocks)
         from_z = (lax.broadcasted_iota(jnp.int32, (1, n), 1) // SIDE) ^ at_ref[0]
         slot = jnp.where(code >= 0, from_z * 64 + code, -1)
-        rows_of = jnp.concatenate([ref[...] for ref in refs[:8]], axis=0)
+        rows_of = jnp.concatenate(blocks, axis=0)
         full = contract_last(rows_of, down_ref[...].reshape(here * rank, width))
         mine = to_col(jnp.where(code >= 0, code % 8, -1))
         low = fold(full, mine, rank).astype(jnp.bfloat16)
@@ -415,7 +455,7 @@
 
     return pl.pallas_call(
         kernel,
-        in_specs=[scalar_spec()] + [pl.BlockSpec(memory_space=pltpu.VMEM)] * 9,
+        in_specs=[scalar_spec()] + [pl.BlockSpec(memory_space=pltpu.VMEM)] * 5,
         out_shape=[
             jax.ShapeDtypeStruct((thirds // 2, pair), jnp.bfloat16),
             jax.ShapeDtypeStruct((8, 128), jnp.float32),
@@ -552,15 +592,16 @@
     arrived = arrived.reshape(64 * HERE * MAIN, width)
 
     blocks = side_first(at_y.reshape(1), seen, ids_row, tokens)
-    blocks = xor_sends(blocks, "y")
+    blocks = halving_sends(*blocks, "y")
     blocks = side_second(jnp.stack([at_z, at_y]), blocks)
-    blocks = xor_sends(blocks, "z")
+    blocks = halving_sends(*blocks, "z")
     thirds, flag = side_low(at_z.reshape(1), blocks, adapter_down)
 
     at = lax.axis_index(TENSOR).astype(jnp.int32).reshape(1)
-    pieces = value_pieces(tokens, value_weight, at, groups)
-    pieces = xor_sends(pieces, TENSOR)
-    base = base_sum(pieces)
+    own, other = value_pieces(tokens, value_weight, at, groups)
+    other = lax.ppermute(other, TENSOR[1], [(0, 1), (1, 0)])
+    pairs = pair_sum(own, other)
+    base = base_sum(own, other, xor_sends(pairs, TENSOR[0]))
 
     low = low_of_all(down_main(arrived, thirds, adapter_down), groups)
     delta = up_main(low, flag, adapter_up_weight)
@@ -575,9 +616,9 @@
 
 def xor_sends(pieces, axis):
     size = lax.axis_size(axis)
-    parts = [pieces[0]]
+    parts = []
     for k in range(1, size):
-        parts.append(lax.ppermute(pieces[k], axis, [(i, i ^ k) for i in range(size)]))
+        parts.append(lax.ppermute(pieces[k - 1], axis, [(i, i ^ k) for i in range(size)]))
     return parts
 
 

time: 196 us -> 187 us (0.954)
  waiting for transfers between devices: 44.8 us -> 67.6 us
  starting transfers between devices: 102 us -> 83.4 us
  blocking collectives: 24.7 us -> 10.6 us
  local copies, waits for them, and re-layouts: 1.4 us -> 3.71 us
    ppermute x21 -> x10, starting transfers between devices: 74.8 us -> 43.1 us  [the longest x6 31.4 us: send(): return lax.ppermute(x, axis, [(i, i ^ step) for i in range(size)])]
    ppermute x21 -> x10, waiting for transfers between devices: 44.7 us -> 67.6 us  [the longest x6 59.7 us: send(): return lax.ppermute(x, axis, [(i, i ^ step) for i in range(size)])]
    all_to_all x2 -> x1, blocking collectives: 24.7 us -> 10.6 us  [swap(): return lax.all_to_all(x, axes, split_axis=0, concat_axis=0, tiled=True)]
    all_to_all x2 -> x3, starting transfers between devices: 27.1 us -> 40.3 us  [swap(): return lax.all_to_all(x, axes, split_axis=0, concat_axis=0, tiled=True)]
    unnamed x12 -> x14, local copies, waits for them, and re-layouts: 1.37 us -> 3.63 us
  transfers between devices with their start and end apart: 23 -> 13, of which waited for: 7 -> 8; matrix products, arithmetic and copies ran while one was open for 0% -> 0% of each run, Pallas kernels for 5% -> 5%
where the time goes in v4:
time: 187 us; the launch traced here: 186 us
  starting transfers between devices  83.4 us (45%)
  waiting for transfers between devices  67.6 us (36%)
  Pallas kernels  19.7 us (11%)
  blocking collectives  10.6 us (6%)
  local copies, waits for them, and re-layouts  3.71 us (2%)
    ppermute x6, waiting for transfers between devices, send(): return lax.ppermute(x, axis, [(i, i ^ step) for i in range(size)])  59.7 us
    all_to_all x3, starting transfers between devices, swap(): return lax.all_to_all(x, axes, split_axis=0, concat_axis=0, tiled=True)  40.3 us
    ppermute x6, starting transfers between devices, send(): return lax.ppermute(x, axis, [(i, i ^ step) for i in range(size)])  31.4 us
    all_to_all x1, blocking collectives, swap(): return lax.all_to_all(x, axes, split_axis=0, concat_axis=0, tiled=True)  10.6 us
    ppermute x3, starting transfers between devices, xor_sends(): lax.ppermute(pieces[k - 1], axis, [(i, i ^ k) for i in range(size)])  9.72 us
    ppermute x3, waiting for transfers between devices, xor_sends(): lax.ppermute(pieces[k - 1], axis, [(i, i ^ k) for i in range(size)])  7.9 us
    pallas_call x1, Pallas kernels, place_main(): pl.pallas_call(kernel, grid=(slots // tile,), in_specs=[pl.BlockSpec((1,...  4.31 us
  transfers between devices with their start and end apart: 13, of which 8 were waited for; matrix products, arithmetic and copies ran while one was open for 0% of the time, Pallas kernels for 5%

profile of v4, /device:TPU:1, one launch (start us, length us, event | category | flops | bytes accessed | tf_op | source)
XLA Modules:
  0.0 186.3 jit_solution(9674151787444455413)
XLA Ops:
  0.0 4.3 %place_main.1 = (bf16[1024,1024]{1,0:T(8,128)(2,1)S(1)}, s32[1,768]{1,0:T(1,128)S(1)}, s32[768,1]{1,0:T(8,128)S(1)}) custom-call(s32[1,768]{1,0:T(1,128)} %bitcast.29, bf16[768,1024]{1,0:T(8,128)(2,1)} %tok_ref.5), custom_call_target="tpu_custom_call" | custom-call | tf_op jit(solution)/shard_map/place_main/pallas_call | solution.py:281
  4.3 0.0 copy-start.1
  4.3 1.3 copy-done.1
  5.7 0.0 copy-start.6
  5.7 17.3 %all-to-all-start.4 = ((bf16[64,16,1024]{2,1,0:T(8,128)(2,1)}), bf16[64,16,1024]{2,1,0:T(8,128)(2,1)S(1)}, u32[]{:S(2)}, u32[]{:S(2)}) async-start(bf16[64,16,1024]{2,1,0:T(8,128)(2,1)} %bitcast.22), calls=%async_computation.4 | async-start | bytes 4194304 | tf_op jit(solution)/shard_map/all_to_all | solution.py:25
  23.0 0.0 copy-done.6
  23.0 2.2 %side_first.1 = (bf16[64,1024]{1,0:T(8,128)(2,1)S(1)}, bf16[64,1024]{1,0:T(8,128)(2,1)S(1)}) custom-call(s32[1]{0:T(128)} %bitcast.11.at_ref, s32[1,768]{1,0:T(1,128)S(1)} %get-tuple-element.44.seen_ref, s32[1,768]{1,0:T(1,128)S(1)} %bitcast.30, bf16[768,1024]{1,0:T(8,128)(2,1)} %tok_ref.5), custom_call_target="tpu_custom_call" | custom-call | tf_op jit(solution)/shard_map/side_first/pallas_call | solution.py:383
  25.2 2.9 %collective-permute-start = (bf16[64,1024]{1,0:T(8,128)(2,1)S(1)}, bf16[64,1024]{1,0:T(8,128)(2,1)S(1)}, u32[]{:S(2)}, u32[]{:S(2)}) collective-permute-start(bf16[64,1024]{1,0:T(8,128)(2,1)S(1)} %get-tuple-element.46), channel_id=1, source_target_pairs={{0,8},{8,0},{16,24},{24,16},{32,40},{40,32},{48,56},{56,48},{1,9},... | collective-permute-start | bytes 393224 | tf_op jit(solution)/shard_map/ppermute | solution.py:346
  28.1 43.0 %collective-permute-done.refs_1_ = bf16[64,1024]{1,0:T(8,128)(2,1)S(1)} collective-permute-done((bf16[64,1024]{1,0:T(8,128)(2,1)S(1)}, bf16[64,1024]{1,0:T(8,128)(2,1)S(1)}, u32[]{:S(2)}, u32[]{:S(2)}) %collective-permute-start) | collective-permute-done | bytes 131104 | tf_op jit(solution)/shard_map/ppermute | solution.py:346
  71.2 4.1 %collective-permute-start.1 = (bf16[64,1024]{1,0:T(8,128)(2,1)S(1)}, bf16[64,1024]{1,0:T(8,128)(2,1)S(1)}, u32[]{:S(2)}, u32[]{:S(2)}) collective-permute-start(bf16[64,1024]{1,0:T(8,128)(2,1)S(1)} %pad_maximum_fusion), channel_id=1, source_target_pairs={{0,16},{8,24},{16,0},{24,8},{32,48},{40,56},{48,32},{56,40},{1,17}... | collective-permute-start | bytes 393224 | tf_op jit(solution)/shard_map/ppermute | solution.py:346
  75.3 5.6 %collective-permute-done.1.refs_2_ = bf16[64,1024]{1,0:T(8,128)(2,1)S(1)} collective-permute-done((bf16[64,1024]{1,0:T(8,128)(2,1)S(1)}, bf16[64,1024]{1,0:T(8,128)(2,1)S(1)}, u32[]{:S(2)}, u32[]{:S(2)}) %collective-permute-start.1) | collective-permute-done | bytes 131104 | tf_op jit(solution)/shard_map/ppermute | solution.py:346
  80.9 7.1 %collective-permute-start.2 = (bf16[64,1024]{1,0:T(8,128)(2,1)S(1)}, bf16[64,1024]{1,0:T(8,128)(2,1)S(1)}, u32[]{:S(2)}, u32[]{:S(2)}) collective-permute-start(bf16[64,1024]{1,0:T(8,128)(2,1)S(1)} %pad_maximum_fusion.1), channel_id=1, source_target_pairs={{0,32},{8,40},{16,48},{24,56},{32,0},{40,8},{48,16},{56,24},{1,33}... | collective-permute-start | bytes 393224 | tf_op jit(solution)/shard_map/ppermute | solution.py:346
  88.0 0.0 copy-start.2
  88.0 0.1 pad_add_fusion.at_ref
  88.1 2.5 %collective-permute-done.2.refs_3_ = bf16[64,1024]{1,0:T(8,128)(2,1)S(1)} collective-permute-done((bf16[64,1024]{1,0:T(8,128)(2,1)S(1)}, bf16[64,1024]{1,0:T(8,128)(2,1)S(1)}, u32[]{:S(2)}, u32[]{:S(2)}) %collective-permute-start.2) | collective-permute-done | bytes 131104 | tf_op jit(solution)/shard_map/ppermute | solution.py:346
  90.6 1.0 side_second.1
  91.7 5.8 %collective-permute-start.3 = (bf16[64,1024]{1,0:T(8,128)(2,1)S(1)}, bf16[64,1024]{1,0:T(8,128)(2,1)S(1)}, u32[]{:S(2)}, u32[]{:S(2)}) collective-permute-start(bf16[64,1024]{1,0:T(8,128)(2,1)S(1)} %get-tuple-element.48), channel_id=1, source_target_pairs={{0,64},{64,0},{128,192},{192,128},{256,320},{320,256},{384,448},{4... | collective-permute-start | bytes 393224 | tf_op jit(solution)/shard_map/ppermute | solution.py:346
  97.5 2.3 %collective-permute-done.3.refs_1_ = bf16[64,1024]{1,0:T(8,128)(2,1)S(1)} collective-permute-done((bf16[64,1024]{1,0:T(8,128)(2,1)S(1)}, bf16[64,1024]{1,0:T(8,128)(2,1)S(1)}, u32[]{:S(2)}, u32[]{:S(2)}) %collective-permute-start.3) | collective-permute-done | bytes 131104 | tf_op jit(solution)/shard_map/ppermute | solution.py:346
  99.8 4.2 %collective-permute-start.4 = (bf16[64,1024]{1,0:T(8,128)(2,1)S(1)}, bf16[64,1024]{1,0:T(8,128)(2,1)S(1)}, u32[]{:S(2)}, u32[]{:S(2)}) collective-permute-start(bf16[64,1024]{1,0:T(8,128)(2,1)S(1)} %pad_maximum_fusion.2), channel_id=1, source_target_pairs={{0,128},{64,192},{128,0},{192,64},{256,384},{320,448},{384,256},{4... | collective-permute-start | bytes 393224 | tf_op jit(solution)/shard_map/ppermute | solution.py:346
  104.0 3.8 %collective-permute-done.4.refs_2_ = bf16[64,1024]{1,0:T(8,128)(2,1)S(1)} collective-permute-done((bf16[64,1024]{1,0:T(8,128)(2,1)S(1)}, bf16[64,1024]{1,0:T(8,128)(2,1)S(1)}, u32[]{:S(2)}, u32[]{:S(2)}) %collective-permute-start.4) | collective-permute-done | bytes 131104 | tf_op jit(solution)/shard_map/ppermute | solution.py:346
  107.8 7.3 %collective-permute-start.5 = (bf16[64,1024]{1,0:T(8,128)(2,1)S(1)}, bf16[64,1024]{1,0:T(8,128)(2,1)S(1)}, u32[]{:S(2)}, u32[]{:S(2)}) collective-permute-start(bf16[64,1024]{1,0:T(8,128)(2,1)S(1)} %pad_maximum_fusion.3), channel_id=1, source_target_pairs={{0,256},{64,320},{128,384},{192,448},{256,0},{320,64},{384,128},{4... | collective-permute-start | bytes 393224 | tf_op jit(solution)/shard_map/ppermute | solution.py:346
  115.2 2.4 %collective-permute-done.5.refs_3_ = bf16[64,1024]{1,0:T(8,128)(2,1)S(1)} collective-permute-done((bf16[64,1024]{1,0:T(8,128)(2,1)S(1)}, bf16[64,1024]{1,0:T(8,128)(2,1)S(1)}, u32[]{:S(2)}, u32[]{:S(2)}) %collective-permute-start.5) | collective-permute-done | bytes 131104 | tf_op jit(solution)/shard_map/ppermute | solution.py:346
  117.6 0.0 copy-done.2
  117.6 0.7 side_low.1
  118.4 0.0 all-to-all-done.4
  118.4 3.3 %down_main.1 = bf16[768,128]{1,0:T(8,128)(2,1)} custom-call(bf16[1024,1024]{1,0:T(8,128)(2,1)S(1)} %bitcast.20, bf16[256,128]{1,0:T(8,128)(2,1)S(1)} %get-tuple-element.49.thirds_ref, bf16[8,64,1024]{2,1,0:T(8,128)(2,1)} %down_ref.1), custom_call_target="tpu_custom_call" | custom-call | tf_op jit(solution)/shard_map/down_main/pallas_call | solution.py:488
  121.6 10.0 %all-to-all-start.5 = ((bf16[8,96,128]{2,1,0:T(8,128)(2,1)}), bf16[8,96,128]{2,1,0:T(8,128)(2,1)S(1)}, u32[]{:S(2)}, u32[]{:S(2)}) async-start(bf16[8,96,128]{2,1,0:T(8,128)(2,1)} %bitcast.12), calls=%async_computation.5 | async-start | bytes 393216 | tf_op jit(solution)/shard_map/all_to_all | solution.py:25
  131.6 0.0 copy-start
  131.6 1.6 copy-done
  133.2 0.0 copy-start.5
  133.2 3.3 %value_pieces.1 = (bf16[4,768,128]{2,1,0:T(8,128)(2,1)S(1)}, bf16[4,768,128]{2,1,0:T(8,128)(2,1)S(1)}) custom-call(s32[1]{0:T(128)} %bitcast.16.at_ref, bf16[768,1024]{1,0:T(8,128)(2,1)} %tok_ref.5, bf16[1024,1024]{1,0:T(8,128)(2,1)S(1)} %copy-done), custom_call_target="tpu_custom_call" | custom-call | tf_op jit(solution)/shard_map/value_pieces/pallas_call | solution.py:91
  136.6 1.9 %collective-permute-start.6 = (bf16[4,768,128]{2,1,0:T(8,128)(2,1)S(1)}, bf16[4,768,128]{2,1,0:T(8,128)(2,1)S(1)}, u32[]{:S(2)}, u32[]{:S(2)}) collective-permute-start(bf16[4,768,128]{2,1,0:T(8,128)(2,1)S(1)} %get-tuple-element.52), channel_id=1, source_target_pairs={{0,1},{1,0},{2,3},{3,2},{4,5},{5,4},{6,7},{7,6},{8,9},{9,8},{10,11... | collective-permute-start | bytes 2359304 | tf_op jit(solution)/shard_map/ppermute | solution.py:602
  138.5 0.0 all-to-all-done.5
  138.6 10.6 %all_to_all.40 = bf16[8,96,128]{2,1,0:T(8,128)(2,1)S(1)} all-to-all(bf16[8,96,128]{2,1,0:T(8,128)(2,1)S(1)} %broadcast_in_dim.4), channel_id=1, replica_groups=mesh['z'=8,'y'=8,'tensor_0'=4,'tensor_1'=2] {'tensor_0','tensor_1'}, dimensions={0} | all-to-all | bytes 393216 | tf_op jit(solution)/shard_map/all_to_all | solution.py:25
  149.2 0.0 copy-done.5
  149.2 1.4 up_main.1
  150.5 13.0 %all-to-all-start.7 = ((bf16[64,24,128]{2,1,0:T(8,128)(2,1)}), bf16[64,24,128]{2,1,0:T(8,128)(2,1)S(1)}, u32[]{:S(2)}, u32[]{:S(2)}) async-start(bf16[64,24,128]{2,1,0:T(8,128)(2,1)} %bitcast.14), calls=%async_computation.7 | async-start | bytes 786432 | tf_op jit(solution)/shard_map/all_to_all | solution.py:25
  163.6 0.0 collective-permute-done.6.other_ref
  163.6 0.1 pair_sum.1
  163.7 0.0 copy-start.3
  163.7 2.3 %collective-permute-start.7 = (bf16[768,128]{1,0:T(8,128)(2,1)S(1)}, bf16[768,128]{1,0:T(8,128)(2,1)S(1)}, u32[]{:S(2)}, u32[]{:S(2)}) collective-permute-start(bf16[768,128]{1,0:T(8,128)(2,1)S(1)} %get-tuple-element.53), channel_id=1, source_target_pairs={{0,2},{2,0},{4,6},{6,4},{1,3},{3,1},{5,7},{7,5},{8,10},{10,8},{12,... | collective-permute-start | bytes 589832 | tf_op jit(solution)/shard_map/ppermute | solution.py:621
  166.1 3.7 %collective-permute-start.8 = (bf16[768,128]{1,0:T(8,128)(2,1)S(1)}, bf16[768,128]{1,0:T(8,128)(2,1)S(1)}, u32[]{:S(2)}, u32[]{:S(2)}) collective-permute-start(bf16[768,128]{1,0:T(8,128)(2,1)S(1)} %get-tuple-element.54), channel_id=1, source_target_pairs={{0,4},{2,6},{4,0},{6,2},{1,5},{3,7},{5,1},{7,3},{8,12},{10,14},{12... | collective-permute-start | bytes 589832 | tf_op jit(solution)/shard_map/ppermute | solution.py:621
  169.8 3.7 %collective-permute-start.9 = (bf16[768,128]{1,0:T(8,128)(2,1)S(1)}, bf16[768,128]{1,0:T(8,128)(2,1)S(1)}, u32[]{:S(2)}, u32[]{:S(2)}) collective-permute-start(bf16[768,128]{1,0:T(8,128)(2,1)S(1)} %get-tuple-element.55), channel_id=1, source_target_pairs={{0,6},{2,4},{4,2},{6,0},{1,7},{3,5},{5,3},{7,1},{8,14},{10,12},{12... | collective-permute-start | bytes 589832 | tf_op jit(solution)/shard_map/ppermute | solution.py:621
  173.5 0.0 collective-permute-done.7.refs_0_
  173.5 2.9 %collective-permute-done.8.refs_1_ = bf16[768,128]{1,0:T(8,128)(2,1)S(1)} collective-permute-done((bf16[768,128]{1,0:T(8,128)(2,1)S(1)}, bf16[768,128]{1,0:T(8,128)(2,1)S(1)}, u32[]{:S(2)}, u32[]{:S(2)}) %collective-permute-start.8) | collective-permute-done | bytes 196640 | tf_op jit(solution)/shard_map/ppermute | solution.py:621
  176.4 5.0 %collective-permute-done.9.refs_2_ = bf16[768,128]{1,0:T(8,128)(2,1)S(1)} collective-permute-done((bf16[768,128]{1,0:T(8,128)(2,1)S(1)}, bf16[768,128]{1,0:T(8,128)(2,1)S(1)}, u32[]{:S(2)}, u32[]{:S(2)}) %collective-permute-start.9) | collective-permute-done | bytes 196640 | tf_op jit(solution)/shard_map/ppermute | solution.py:621
  181.4 0.9 base_sum.1.base_ref
  182.3 0.0 all-to-all-done.7
  182.3 2.5 %take_main.1 = (bf16[768,128]{1,0:T(8,128)(2,1)S(1)}, s32[1]{0:T(128)}) custom-call(s32[768,1]{1,0:T(8,128)S(1)} %get-tuple-element.42.at_ref, bf16[1536,128]{1,0:T(8,128)(2,1)S(1)} %bitcast.23, f32[768,128]{1,0:T(8,128)} %base_sum.1.base_ref), custom_call_target="tpu_custom_call" | custom-call | tf_op jit(solution)/shard_map/take_main/pallas_call | solution.py:549
  185.4 0.0 copy-done.3
  185.4 0.2 conditional.1
  185.6 0.0 copy-start.7
  185.7 0.7 copy-done.7
  (16 shorter events, 0.1 us)
Async XLA Ops:
  4.3 1.4 copy-start.1
  5.7 17.3 %copy-start.6 = (s32[768,1]{0,1:T(1,128)S(1)}, s32[768,1]{0,1:T(1,128)}, u32[]{:S(2)}) copy-start(s32[768,1]{0,1:T(1,128)} %param.11) | copy-start | bytes 9220
  5.7 112.7 %all-to-all-start.4 = ((bf16[64,16,1024]{2,1,0:T(8,128)(2,1)}), bf16[64,16,1024]{2,1,0:T(8,128)(2,1)S(1)}, u32[]{:S(2)}, u32[]{:S(2)}) async-start(bf16[64,16,1024]{2,1,0:T(8,128)(2,1)} %bitcast.22), calls=%async_computation.4 | async-start | bytes 4194304 | tf_op jit(solution)/shard_map/all_to_all | solution.py:25
  25.2 46.0 %collective-permute-start = (bf16[64,1024]{1,0:T(8,128)(2,1)S(1)}, bf16[64,1024]{1,0:T(8,128)(2,1)S(1)}, u32[]{:S(2)}, u32[]{:S(2)}) collective-permute-start(bf16[64,1024]{1,0:T(8,128)(2,1)S(1)} %get-tuple-element.46), channel_id=1, source_target_pairs={{0,8},{8,0},{16,24},{24,16},{32,40},{40,32},{48,56},{56,48},{1,9},... | collective-permute-start | bytes 393224 | tf_op jit(solution)/shard_map/ppermute | solution.py:346
  71.2 9.7 %collective-permute-start.1 = (bf16[64,1024]{1,0:T(8,128)(2,1)S(1)}, bf16[64,1024]{1,0:T(8,128)(2,1)S(1)}, u32[]{:S(2)}, u32[]{:S(2)}) collective-permute-start(bf16[64,1024]{1,0:T(8,128)(2,1)S(1)} %pad_maximum_fusion), channel_id=1, source_target_pairs={{0,16},{8,24},{16,0},{24,8},{32,48},{40,56},{48,32},{56,40},{1,17}... | collective-permute-start | bytes 393224 | tf_op jit(solution)/shard_map/ppermute | solution.py:346
  80.9 9.7 %collective-permute-start.2 = (bf16[64,1024]{1,0:T(8,128)(2,1)S(1)}, bf16[64,1024]{1,0:T(8,128)(2,1)S(1)}, u32[]{:S(2)}, u32[]{:S(2)}) collective-permute-start(bf16[64,1024]{1,0:T(8,128)(2,1)S(1)} %pad_maximum_fusion.1), channel_id=1, source_target_pairs={{0,32},{8,40},{16,48},{24,56},{32,0},{40,8},{48,16},{56,24},{1,33}... | collective-permute-start | bytes 393224 | tf_op jit(solution)/shard_map/ppermute | solution.py:346
  88.0 29.6 %copy-start.2 = (bf16[8,64,1024]{2,1,0:T(8,128)(2,1)S(1)}, bf16[8,64,1024]{2,1,0:T(8,128)(2,1)}, u32[]{:S(2)}) copy-start(bf16[8,64,1024]{2,1,0:T(8,128)(2,1)} %down_ref.1) | copy-start | bytes 3145732
  91.7 8.1 %collective-permute-start.3 = (bf16[64,1024]{1,0:T(8,128)(2,1)S(1)}, bf16[64,1024]{1,0:T(8,128)(2,1)S(1)}, u32[]{:S(2)}, u32[]{:S(2)}) collective-permute-start(bf16[64,1024]{1,0:T(8,128)(2,1)S(1)} %get-tuple-element.48), channel_id=1, source_target_pairs={{0,64},{64,0},{128,192},{192,128},{256,320},{320,256},{384,448},{4... | collective-permute-start | bytes 393224 | tf_op jit(solution)/shard_map/ppermute | solution.py:346
  99.8 8.0 %collective-permute-start.4 = (bf16[64,1024]{1,0:T(8,128)(2,1)S(1)}, bf16[64,1024]{1,0:T(8,128)(2,1)S(1)}, u32[]{:S(2)}, u32[]{:S(2)}) collective-permute-start(bf16[64,1024]{1,0:T(8,128)(2,1)S(1)} %pad_maximum_fusion.2), channel_id=1, source_target_pairs={{0,128},{64,192},{128,0},{192,64},{256,384},{320,448},{384,256},{4... | collective-permute-start | bytes 393224 | tf_op jit(solution)/shard_map/ppermute | solution.py:346
  107.8 9.8 %collective-permute-start.5 = (bf16[64,1024]{1,0:T(8,128)(2,1)S(1)}, bf16[64,1024]{1,0:T(8,128)(2,1)S(1)}, u32[]{:S(2)}, u32[]{:S(2)}) collective-permute-start(bf16[64,1024]{1,0:T(8,128)(2,1)S(1)} %pad_maximum_fusion.3), channel_id=1, source_target_pairs={{0,256},{64,320},{128,384},{192,448},{256,0},{320,64},{384,128},{4... | collective-permute-start | bytes 393224 | tf_op jit(solution)/shard_map/ppermute | solution.py:346
  121.6 16.9 %all-to-all-start.5 = ((bf16[8,96,128]{2,1,0:T(8,128)(2,1)}), bf16[8,96,128]{2,1,0:T(8,128)(2,1)S(1)}, u32[]{:S(2)}, u32[]{:S(2)}) async-start(bf16[8,96,128]{2,1,0:T(8,128)(2,1)} %bitcast.12), calls=%async_computation.5 | async-start | bytes 393216 | tf_op jit(solution)/shard_map/all_to_all | solution.py:25
  131.6 1.6 copy-start
  133.2 15.9 %copy-start.5 = (bf16[8,64,128]{2,1,0:T(8,128)(2,1)S(1)}, bf16[8,64,128]{2,1,0:T(8,128)(2,1)}, u32[]{:S(2)}) copy-start(bf16[8,64,128]{2,1,0:T(8,128)(2,1)} %up_ref.1) | copy-start | bytes 393220
  136.6 27.0 %collective-permute-start.6 = (bf16[4,768,128]{2,1,0:T(8,128)(2,1)S(1)}, bf16[4,768,128]{2,1,0:T(8,128)(2,1)S(1)}, u32[]{:S(2)}, u32[]{:S(2)}) collective-permute-start(bf16[4,768,128]{2,1,0:T(8,128)(2,1)S(1)} %get-tuple-element.52), channel_id=1, source_target_pairs={{0,1},{1,0},{2,3},{3,2},{4,5},{5,4},{6,7},{7,6},{8,9},{9,8},{10,11... | collective-permute-start | bytes 2359304 | tf_op jit(solution)/shard_map/ppermute | solution.py:602
  150.5 31.7 %all-to-all-start.7 = ((bf16[64,24,128]{2,1,0:T(8,128)(2,1)}), bf16[64,24,128]{2,1,0:T(8,128)(2,1)S(1)}, u32[]{:S(2)}, u32[]{:S(2)}) async-start(bf16[64,24,128]{2,1,0:T(8,128)(2,1)} %bitcast.14), calls=%async_computation.7 | async-start | bytes 786432 | tf_op jit(solution)/shard_map/all_to_all | solution.py:25
  163.7 21.7 %copy-start.3 = (bf16[8,64,1024]{2,1,0:T(8,128)(2,1)S(1)}, bf16[8,64,1024]{2,1,0:T(8,128)(2,1)}, u32[]{:S(2)}) copy-start(bf16[8,64,1024]{2,1,0:T(8,128)(2,1)} %down_ref.1) | copy-start | bytes 3145732
  163.7 9.7 %collective-permute-start.7 = (bf16[768,128]{1,0:T(8,128)(2,1)S(1)}, bf16[768,128]{1,0:T(8,128)(2,1)S(1)}, u32[]{:S(2)}, u32[]{:S(2)}) collective-permute-start(bf16[768,128]{1,0:T(8,128)(2,1)S(1)} %get-tuple-element.53), channel_id=1, source_target_pairs={{0,2},{2,0},{4,6},{6,4},{1,3},{3,1},{5,7},{7,5},{8,10},{10,8},{12,... | collective-permute-start | bytes 589832 | tf_op jit(solution)/shard_map/ppermute | solution.py:621
  166.1 10.3 %collective-permute-start.8 = (bf16[768,128]{1,0:T(8,128)(2,1)S(1)}, bf16[768,128]{1,0:T(8,128)(2,1)S(1)}, u32[]{:S(2)}, u32[]{:S(2)}) collective-permute-start(bf16[768,128]{1,0:T(8,128)(2,1)S(1)} %get-tuple-element.54), channel_id=1, source_target_pairs={{0,4},{2,6},{4,0},{6,2},{1,5},{3,7},{5,1},{7,3},{8,12},{10,14},{12... | collective-permute-start | bytes 589832 | tf_op jit(solution)/shard_map/ppermute | solution.py:621
  169.8 11.6 %collective-permute-start.9 = (bf16[768,128]{1,0:T(8,128)(2,1)S(1)}, bf16[768,128]{1,0:T(8,128)(2,1)S(1)}, u32[]{:S(2)}, u32[]{:S(2)}) collective-permute-start(bf16[768,128]{1,0:T(8,128)(2,1)S(1)} %get-tuple-element.55), channel_id=1, source_target_pairs={{0,6},{2,4},{4,2},{6,0},{1,7},{3,5},{5,3},{7,1},{8,14},{10,12},{12... | collective-permute-start | bytes 589832 | tf_op jit(solution)/shard_map/ppermute | solution.py:621
  185.6 0.7 copy-start.7

commit v5 on v4

--- a/solution.py
+++ b/solution.py
@@ -236,14 +236,11 @@
     return pl.BlockSpec(memory_space=pltpu.SMEM)
 
 
-def count_before(row, col, also_col=None):
+def count_before(row, col):
     n = row.shape[1]
     j = lax.broadcasted_iota(jnp.int32, (n, n), 0)
     i = lax.broadcasted_iota(jnp.int32, (n, n), 1)
-    hit = (row == col) & (j < i)
-    if also_col is not None:
-        hit = hit & also_col
-    return jnp.sum(jnp.where(hit, 1, 0), axis=0, keepdims=True)
+    return jnp.sum(jnp.where((row == col) & (j < i), 1, 0), axis=0, keepdims=True)
 
 
 def to_col(row):
@@ -256,22 +253,11 @@
     return jnp.where(slot == at_row, 1.0, 0.0).astype(jnp.bfloat16)
 
 
-def place_main(ids_row, tokens, slots):
+def place_main(ids_row, seen, tokens, slots):
     rows, width = tokens.shape
     tile = 256
 
-    def kernel(row_ref, tok_ref, out_ref, seen_ref, at_col_ref):
-        @pl.when(pl.program_id(0) == 0)
-        def _():
-            row = row_ref[...]
-            seen = count_before(row, to_col(row))
-            seen_ref[...] = seen
-            spot = row % HERE
-            back = row // HERE * (HERE * MOST) + jnp.where(
-                seen < MAIN, spot * MAIN + seen, HERE * MAIN + spot
-            )
-            at_col_ref[...] = to_col(back)
-
+    def kernel(row_ref, seen_ref, tok_ref, out_ref):
         at_row = jnp.where(seen_ref[...] < MAIN, row_ref[...] * MAIN + seen_ref[...], -1)
         pick = pick_rows(at_row, tile, pl.program_id(0) * tile)
         out_ref[...] = jnp.dot(pick, tok_ref[...], preferred_element_type=jnp.float32).astype(
@@ -283,27 +269,20 @@
         grid=(slots // tile,),
         in_specs=[
             pl.BlockSpec((1, rows), lambda i: (0, 0)),
+            pl.BlockSpec((1, rows), lambda i: (0, 0)),
             pl.BlockSpec((rows, width), lambda i: (0, 0)),
         ],
-        out_specs=[
-            pl.BlockSpec((tile, width), lambda i: (i, 0)),
-            pl.BlockSpec((1, rows), lambda i: (0, 0)),
-            pl.BlockSpec((rows, 1), lambda i: (0, 0)),
-        ],
-        out_shape=[
-            jax.ShapeDtypeStruct((slots, width), tokens.dtype),
-            jax.ShapeDtypeStruct((1, rows), jnp.int32),
-            jax.ShapeDtypeStruct((rows, 1), jnp.int32),
-        ],
+        out_specs=pl.BlockSpec((tile, width), lambda i: (i, 0)),
+        out_shape=jax.ShapeDtypeStruct((slots, width), tokens.dtype),
         compiler_params=GRANT,
         name="place_main",
-    )(ids_row, tokens)
-
-
-def bucket(rows_of, key, key_col, code, valid, valid_col, flag, out_refs, block_ref, at):
+    )(ids_row, seen, tokens)
+
+
+def bucket(rows_of, key, key_col, code, valid, flag, store):
     n = key.shape[1]
     width = rows_of.shape[1]
-    q = count_before(key, key_col, valid_col)
+    q = count_before(key, key_col)
     fits = valid & (q < SIDE - 1)
     lost = jnp.max(jnp.where(valid & (q >= SIDE - 1), 1.0, 0.0), axis=1, keepdims=True)
     flag = jnp.maximum(flag, lost)
@@ -325,12 +304,8 @@
     row = lax.broadcasted_iota(jnp.int32, (SIDE, width), 0)
     for k in range(8):
         note = jnp.broadcast_to(wide[k : k + 1], (SIDE, width))
-        block_ref[k] = jnp.where(
-            row == SIDE - 1, note, data[k * SIDE : (k + 1) * SIDE]
-        ).astype(jnp.bfloat16)
-    for ref, order in zip(out_refs, (STAY, LEAVE)):
-        for i, k in enumerate(order):
-            ref[i * SIDE : (i + 1) * SIDE, :] = block_ref[at ^ k]
+        block = jnp.where(row == SIDE - 1, note, data[k * SIDE : (k + 1) * SIDE])
+        store(k, block.astype(jnp.bfloat16))
 
 
 def arrived_blocks(refs):
@@ -366,54 +341,68 @@
     return codes[:1].astype(jnp.int32) - 1, flag
 
 
-def side_first(at, seen, ids_row, tokens):
-    _, width = tokens.shape
-
-    def kernel(at_ref, seen_ref, row_ref, tok_ref, *refs):
+def side_first(ids_row, tokens):
+    rows, width = tokens.shape
+
+    def kernel(row_ref, tok_ref, out_ref, seen_ref, at_col_ref):
         row = row_ref[...]
-        third = seen_ref[...] >= MAIN
+        seen = count_before(row, to_col(row))
+        seen_ref[...] = seen
         home = row // HERE
+        spot = row % HERE
+        back = home * (HERE * MOST) + jnp.where(
+            seen < MAIN, spot * MAIN + seen, HERE * MAIN + spot
+        )
+        at_col_ref[...] = to_col(back)
+        third = seen >= MAIN
         key = home % 8
-        marked = jnp.where(third, key, -1)
+
+        def store(k, block):
+            out_ref[k * SIDE : (k + 1) * SIDE, :] = block
+
         bucket(
-            tok_ref[...], key, to_col(marked), home // 8 * 8 + row % HERE, third, None,
-            jnp.zeros((1, 1), jnp.float32), refs[:2], refs[2], at_ref[0],
+            tok_ref[...], key, to_col(jnp.where(third, key, -1)), home // 8 * 8 + spot, third,
+            jnp.zeros((1, 1), jnp.float32), store,
         )
 
     return pl.pallas_call(
         kernel,
-        in_specs=[scalar_spec()] + [pl.BlockSpec(memory_space=pltpu.VMEM)] * 3,
-        out_shape=[jax.ShapeDtypeStruct((4 * SIDE, width), jnp.bfloat16)] * 2,
-        scratch_shapes=[pltpu.VMEM((8, SIDE, width), jnp.bfloat16)],
+        out_shape=[
+            jax.ShapeDtypeStruct((8 * SIDE, width), jnp.bfloat16),
+            jax.ShapeDtypeStruct((1, rows), jnp.int32),
+            jax.ShapeDtypeStruct((rows, 1), jnp.int32),
+        ],
         compiler_params=GRANT,
         name="side_first",
-    )(at, seen, ids_row, tokens)
-
-
-def side_second(at, blocks):
-    width = blocks[0].shape[1]
-    n = 8 * SIDE
-
-    def kernel(at_ref, *refs):
-        blocks = arrived_blocks(refs[:4])
+    )(ids_row, tokens)
+
+
+def side_second(at, arrived):
+    n, width = arrived.shape
+
+    def kernel(at_ref, in_ref, stay_ref, leave_ref, block_ref):
+        blocks = [in_ref[k * SIDE : (k + 1) * SIDE, :] for k in range(8)]
         code, flag = read_codes(blocks)
         valid = code >= 0
         key = jnp.where(valid, code // 8, -1)
-        from_y = (lax.broadcasted_iota(jnp.int32, (1, n), 1) // SIDE) ^ at_ref[1]
-        rows_of = jnp.concatenate(blocks, axis=0)
-        bucket(
-            rows_of, key, to_col(key), from_y * 8 + code % 8, valid, None,
-            flag, refs[4:6], refs[6], at_ref[0],
-        )
-
-    return pl.pallas_call(
-        kernel,
-        in_specs=[scalar_spec()] + [pl.BlockSpec(memory_space=pltpu.VMEM)] * 4,
+        from_y = lax.broadcasted_iota(jnp.int32, (1, n), 1) // SIDE
+
+        def store(k, block):
+            block_ref[k] = block
+
+        bucket(in_ref[...], key, to_col(key), from_y * 8 + code % 8, valid, flag, store)
+        for ref, order in ((stay_ref, STAY), (leave_ref, LEAVE)):
+            for i, k in enumerate(order):
+                ref[i * SIDE : (i + 1) * SIDE, :] = block_ref[at_ref[0] ^ k]
+
+    return pl.pallas_call(
+        kernel,
+        in_specs=[scalar_spec(), pl.BlockSpec(memory_space=pltpu.VMEM)],
         out_shape=[jax.ShapeDtypeStruct((4 * SIDE, width), jnp.bfloat16)] * 2,
         scratch_shapes=[pltpu.VMEM((8, SIDE, width), jnp.bfloat16)],
         compiler_params=GRANT,
         name="side_second",
-    )(at, *blocks)
+    )(at, arrived)
 
 
 def fold(full, mine, rank):
@@ -585,15 +574,14 @@
     cols = adapter_up_weight.shape[2]
     ids_row = adapter_ids.reshape(1, rows)
     at_z = lax.axis_index("z").astype(jnp.int32)
-    at_y = lax.axis_index("y").astype(jnp.int32)
-
-    placed, seen, at_col = place_main(ids_row, tokens, 64 * HERE * MAIN)
+
+    blocks, seen, at_col = side_first(ids_row, tokens)
+    blocks = swap(blocks.reshape(8, SIDE, width), "y").reshape(8 * SIDE, width)
+    placed = place_main(ids_row, seen, tokens, 64 * HERE * MAIN)
     arrived = swap(placed.reshape(64, HERE * MAIN, width), ADAPTER)
     arrived = arrived.reshape(64 * HERE * MAIN, width)
 
-    blocks = side_first(at_y.reshape(1), seen, ids_row, tokens)
-    blocks = halving_sends(*blocks, "y")
-    blocks = side_second(jnp.stack([at_z, at_y]), blocks)
+    blocks = side_second(at_z.reshape(1), blocks)
     blocks = halving_sends(*blocks, "z")
     thirds, flag = side_low(at_z.reshape(1), blocks, adapter_down)
 

time: 187 us -> 170 us (0.909)
  starting transfers between devices: 83.4 us -> 71.8 us
  waiting for transfers between devices: 67.6 us -> 62.6 us
    ppermute x6 -> x3, starting transfers between devices: 31.4 us -> 16.7 us  [send(): return lax.ppermute(x, axis, [(i, i ^ step) for i in range(size)])]
    ppermute x6 -> x3, waiting for transfers between devices: 59.7 us -> 48.6 us  [send(): return lax.ppermute(x, axis, [(i, i ^ step) for i in range(size)])]
    all_to_all x3 -> x4, waiting for transfers between devices: 0.01 us -> 6.07 us  [swap(): return lax.all_to_all(x, axes, split_axis=0, concat_axis=0, tiled=True)]
    all_to_all x3 -> x4, starting transfers between devices: 40.3 us -> 43.5 us  [swap(): return lax.all_to_all(x, axes, split_axis=0, concat_axis=0, tiled=True)]
  transfers between devices with their start and end apart: 13 -> 11, of which waited for: 8 -> 6; matrix products, arithmetic and copies ran while one was open for 0% -> 0% of each run, Pallas kernels for 5% -> 7%
where the time goes in v5:
time: 170 us; the launch traced here: 169 us
  starting transfers between devices  71.8 us (42%)
  waiting for transfers between devices  62.6 us (37%)
  Pallas kernels  20.6 us (12%)
  blocking collectives  10.6 us (6%)
  local copies, waits for them, and re-layouts  2.33 us (1%)
    ppermute x3, waiting for transfers between devices, send(): return lax.ppermute(x, axis, [(i, i ^ step) for i in range(size)])  48.6 us
    all_to_all x4, starting transfers between devices, swap(): return lax.all_to_all(x, axes, split_axis=0, concat_axis=0, tiled=True)  43.5 us
    ppermute x3, starting transfers between devices, send(): return lax.ppermute(x, axis, [(i, i ^ step) for i in range(size)])  16.7 us
    all_to_all x1, blocking collectives, swap(): return lax.all_to_all(x, axes, split_axis=0, concat_axis=0, tiled=True)  10.6 us
    ppermute x3, starting transfers between devices, xor_sends(): lax.ppermute(pieces[k - 1], axis, [(i, i ^ k) for i in range(size)])  9.72 us
    ppermute x3, waiting for transfers between devices, xor_sends(): lax.ppermute(pieces[k - 1], axis, [(i, i ^ k) for i in range(size)])  7.89 us
    all_to_all x4, waiting for transfers between devices, swap(): return lax.all_to_all(x, axes, split_axis=0, concat_axis=0, tiled=True)  6.07 us
  transfers between devices with their start and end apart: 11, of which 6 were waited for; matrix products, arithmetic and copies ran while one was open for 0% of the time, Pallas kernels for 7%

profile of v5, /device:TPU:1, one launch (start us, length us, event | category | flops | bytes accessed | tf_op | source)
XLA Modules:
  0.0 169.0 jit_solution(16006587382958661714)
XLA Ops:
  0.0 0.0 copy-start.1
  0.0 0.0 copy-start.5
  0.0 3.4 %side_first.1 = (bf16[128,1024]{1,0:T(8,128)(2,1)}, s32[1,768]{1,0:T(1,128)S(1)}, s32[768,1]{1,0:T(8,128)S(1)}) custom-call(s32[1,768]{1,0:T(1,128)} %bitcast.30, bf16[768,1024]{1,0:T(8,128)(2,1)} %tok_ref.5), custom_call_target="tpu_custom_call" | custom-call | tf_op jit(solution)/shard_map/side_first/pallas_call | solution.py:368
  3.4 7.6 %all-to-all-start.5 = ((bf16[8,16,1024]{2,1,0:T(8,128)(2,1)}), bf16[8,16,1024]{2,1,0:T(8,128)(2,1)S(1)}, u32[]{:S(2)}, u32[]{:S(2)}) async-start(bf16[8,16,1024]{2,1,0:T(8,128)(2,1)} %bitcast.11), calls=%async_computation.5 | async-start | bytes 524288 | tf_op jit(solution)/shard_map/all_to_all | solution.py:25
  11.0 0.0 copy-done.1
  11.0 0.0 copy-done.5
  11.0 3.4 %place_main.1 = bf16[1024,1024]{1,0:T(8,128)(2,1)} custom-call(s32[1,768]{1,0:T(1,128)S(1)} %bitcast.31, s32[1,768]{1,0:T(1,128)S(1)} %get-tuple-element.41.seen_ref, bf16[768,1024]{1,0:T(8,128)(2,1)S(1)} %copy-done.1), custom_call_target="tpu_custom_call" | custom-call | tf_op jit(solution)/shard_map/place_main/pallas_call | solution.py:267
  14.4 6.1 %all-to-all-done.5 = bf16[8,16,1024]{2,1,0:T(8,128)(2,1)S(1)} async-done(((bf16[8,16,1024]{2,1,0:T(8,128)(2,1)}), bf16[8,16,1024]{2,1,0:T(8,128)(2,1)S(1)}, u32[]{:S(2)}, u32[]{:S(2)}) %all-to-all-start.5) | async-done | bytes 262176 | tf_op jit(solution)/shard_map/all_to_all | solution.py:25
  20.4 13.2 %all-to-all-start.4 = ((bf16[64,16,1024]{2,1,0:T(8,128)(2,1)}), bf16[64,16,1024]{2,1,0:T(8,128)(2,1)S(1)}, u32[]{:S(2)}, u32[]{:S(2)}) async-start(bf16[64,16,1024]{2,1,0:T(8,128)(2,1)} %bitcast.8), calls=%async_computation.4 | async-start | bytes 4194304 | tf_op jit(solution)/shard_map/all_to_all | solution.py:25
  33.7 0.5 side_second.1
  34.2 2.9 %collective-permute-start = (bf16[64,1024]{1,0:T(8,128)(2,1)S(1)}, bf16[64,1024]{1,0:T(8,128)(2,1)S(1)}, u32[]{:S(2)}, u32[]{:S(2)}) collective-permute-start(bf16[64,1024]{1,0:T(8,128)(2,1)S(1)} %get-tuple-element.44), channel_id=1, source_target_pairs={{0,64},{64,0},{128,192},{192,128},{256,320},{320,256},{384,448},{4... | collective-permute-start | bytes 393224 | tf_op jit(solution)/shard_map/ppermute | solution.py:321
  37.1 43.8 %collective-permute-done.refs_1_ = bf16[64,1024]{1,0:T(8,128)(2,1)S(1)} collective-permute-done((bf16[64,1024]{1,0:T(8,128)(2,1)S(1)}, bf16[64,1024]{1,0:T(8,128)(2,1)S(1)}, u32[]{:S(2)}, u32[]{:S(2)}) %collective-permute-start) | collective-permute-done | bytes 131104 | tf_op jit(solution)/shard_map/ppermute | solution.py:321
  81.0 5.6 %collective-permute-start.1 = (bf16[64,1024]{1,0:T(8,128)(2,1)S(1)}, bf16[64,1024]{1,0:T(8,128)(2,1)S(1)}, u32[]{:S(2)}, u32[]{:S(2)}) collective-permute-start(bf16[64,1024]{1,0:T(8,128)(2,1)S(1)} %pad_maximum_fusion), channel_id=1, source_target_pairs={{0,128},{64,192},{128,0},{192,64},{256,384},{320,448},{384,256},{4... | collective-permute-start | bytes 393224 | tf_op jit(solution)/shard_map/ppermute | solution.py:321
  86.6 2.4 %collective-permute-done.1.refs_2_ = bf16[64,1024]{1,0:T(8,128)(2,1)S(1)} collective-permute-done((bf16[64,1024]{1,0:T(8,128)(2,1)S(1)}, bf16[64,1024]{1,0:T(8,128)(2,1)S(1)}, u32[]{:S(2)}, u32[]{:S(2)}) %collective-permute-start.1) | collective-permute-done | bytes 131104 | tf_op jit(solution)/shard_map/ppermute | solution.py:321
  89.0 8.1 %collective-permute-start.2 = (bf16[64,1024]{1,0:T(8,128)(2,1)S(1)}, bf16[64,1024]{1,0:T(8,128)(2,1)S(1)}, u32[]{:S(2)}, u32[]{:S(2)}) collective-permute-start(bf16[64,1024]{1,0:T(8,128)(2,1)S(1)} %pad_maximum_fusion.1), channel_id=1, source_target_pairs={{0,256},{64,320},{128,384},{192,448},{256,0},{320,64},{384,128},{4... | collective-permute-start | bytes 393224 | tf_op jit(solution)/shard_map/ppermute | solution.py:321
  97.1 2.4 %collective-permute-done.2.refs_3_ = bf16[64,1024]{1,0:T(8,128)(2,1)S(1)} collective-permute-done((bf16[64,1024]{1,0:T(8,128)(2,1)S(1)}, bf16[64,1024]{1,0:T(8,128)(2,1)S(1)}, u32[]{:S(2)}, u32[]{:S(2)}) %collective-permute-start.2) | collective-permute-done | bytes 131104 | tf_op jit(solution)/shard_map/ppermute | solution.py:321
  99.5 1.9 %side_low.1 = (bf16[256,128]{1,0:T(8,128)(2,1)S(1)}, f32[8,128]{1,0:T(8,128)S(1)}) custom-call(s32[1]{0:T(128)} %bitcast.10.at_ref, bf16[64,1024]{1,0:T(8,128)(2,1)S(1)} %get-tuple-element.43.refs_0_, bf16[64,1024]{1,0:T(8,128)(2,1)S(1)} %collective-permute-done.refs_1_, bf16[64,1024]{1,0:T(8,128)(2,1)S(1)} %collective-permute-done.1.refs_2_, ...), custom_call_target="tpu_custom_call" | custom-call | tf_op jit(solution)/shard_map/side_low/pallas_call | solution.py:445
  101.5 0.0 all-to-all-done.4
  101.5 3.3 %down_main.1 = bf16[768,128]{1,0:T(8,128)(2,1)} custom-call(bf16[1024,1024]{1,0:T(8,128)(2,1)S(1)} %bitcast.21, bf16[256,128]{1,0:T(8,128)(2,1)S(1)} %get-tuple-element.45.thirds_ref, bf16[8,64,1024]{2,1,0:T(8,128)(2,1)} %down_ref.1), custom_call_target="tpu_custom_call" | custom-call | tf_op jit(solution)/shard_map/down_main/pallas_call | solution.py:477
  104.8 9.4 %all-to-all-start.6 = ((bf16[8,96,128]{2,1,0:T(8,128)(2,1)}), bf16[8,96,128]{2,1,0:T(8,128)(2,1)S(1)}, u32[]{:S(2)}, u32[]{:S(2)}) async-start(bf16[8,96,128]{2,1,0:T(8,128)(2,1)} %bitcast.13), calls=%async_computation.6 | async-start | bytes 393216 | tf_op jit(solution)/shard_map/all_to_all | solution.py:25
  114.2 0.0 copy-start
  114.2 1.6 copy-done
  115.7 0.0 copy-start.4
  115.8 3.3 %value_pieces.1 = (bf16[4,768,128]{2,1,0:T(8,128)(2,1)S(1)}, bf16[4,768,128]{2,1,0:T(8,128)(2,1)S(1)}) custom-call(s32[1]{0:T(128)} %bitcast.17.at_ref, bf16[768,1024]{1,0:T(8,128)(2,1)} %tok_ref.5, bf16[1024,1024]{1,0:T(8,128)(2,1)S(1)} %copy-done), custom_call_target="tpu_custom_call" | custom-call | tf_op jit(solution)/shard_map/value_pieces/pallas_call | solution.py:91
  119.1 1.9 %collective-permute-start.3 = (bf16[4,768,128]{2,1,0:T(8,128)(2,1)S(1)}, bf16[4,768,128]{2,1,0:T(8,128)(2,1)S(1)}, u32[]{:S(2)}, u32[]{:S(2)}) collective-permute-start(bf16[4,768,128]{2,1,0:T(8,128)(2,1)S(1)} %get-tuple-element.48), channel_id=1, source_target_pairs={{0,1},{1,0},{2,3},{3,2},{4,5},{5,4},{6,7},{7,6},{8,9},{9,8},{10,11... | collective-permute-start | bytes 2359304 | tf_op jit(solution)/shard_map/ppermute | solution.py:590
  121.0 0.0 all-to-all-done.6
  121.1 10.6 %all_to_all.45 = bf16[8,96,128]{2,1,0:T(8,128)(2,1)S(1)} all-to-all(bf16[8,96,128]{2,1,0:T(8,128)(2,1)S(1)} %broadcast_in_dim.4), channel_id=1, replica_groups=mesh['z'=8,'y'=8,'tensor_0'=4,'tensor_1'=2] {'tensor_0','tensor_1'}, dimensions={0} | all-to-all | bytes 393216 | tf_op jit(solution)/shard_map/all_to_all | solution.py:25
  131.7 0.0 copy-done.4
  131.7 1.4 up_main.1
  133.0 13.2 %all-to-all-start.8 = ((bf16[64,24,128]{2,1,0:T(8,128)(2,1)}), bf16[64,24,128]{2,1,0:T(8,128)(2,1)S(1)}, u32[]{:S(2)}, u32[]{:S(2)}) async-start(bf16[64,24,128]{2,1,0:T(8,128)(2,1)} %bitcast.15), calls=%async_computation.8 | async-start | bytes 786432 | tf_op jit(solution)/shard_map/all_to_all | solution.py:25
  146.2 0.0 collective-permute-done.3.other_ref
  146.3 0.1 pair_sum.1
  146.4 0.0 copy-start.2
  146.4 2.3 %collective-permute-start.4 = (bf16[768,128]{1,0:T(8,128)(2,1)S(1)}, bf16[768,128]{1,0:T(8,128)(2,1)S(1)}, u32[]{:S(2)}, u32[]{:S(2)}) collective-permute-start(bf16[768,128]{1,0:T(8,128)(2,1)S(1)} %get-tuple-element.49), channel_id=1, source_target_pairs={{0,2},{2,0},{4,6},{6,4},{1,3},{3,1},{5,7},{7,5},{8,10},{10,8},{12,... | collective-permute-start | bytes 589832 | tf_op jit(solution)/shard_map/ppermute | solution.py:609
  148.7 3.7 %collective-permute-start.5 = (bf16[768,128]{1,0:T(8,128)(2,1)S(1)}, bf16[768,128]{1,0:T(8,128)(2,1)S(1)}, u32[]{:S(2)}, u32[]{:S(2)}) collective-permute-start(bf16[768,128]{1,0:T(8,128)(2,1)S(1)} %get-tuple-element.50), channel_id=1, source_target_pairs={{0,4},{2,6},{4,0},{6,2},{1,5},{3,7},{5,1},{7,3},{8,12},{10,14},{12... | collective-permute-start | bytes 589832 | tf_op jit(solution)/shard_map/ppermute | solution.py:609
  152.4 3.7 %collective-permute-start.6 = (bf16[768,128]{1,0:T(8,128)(2,1)S(1)}, bf16[768,128]{1,0:T(8,128)(2,1)S(1)}, u32[]{:S(2)}, u32[]{:S(2)}) collective-permute-start(bf16[768,128]{1,0:T(8,128)(2,1)S(1)} %get-tuple-element.51), channel_id=1, source_target_pairs={{0,6},{2,4},{4,2},{6,0},{1,7},{3,5},{5,3},{7,1},{8,14},{10,12},{12... | collective-permute-start | bytes 589832 | tf_op jit(solution)/shard_map/ppermute | solution.py:609
  156.1 0.0 collective-permute-done.4.refs_0_
  156.2 2.9 %collective-permute-done.5.refs_1_ = bf16[768,128]{1,0:T(8,128)(2,1)S(1)} collective-permute-done((bf16[768,128]{1,0:T(8,128)(2,1)S(1)}, bf16[768,128]{1,0:T(8,128)(2,1)S(1)}, u32[]{:S(2)}, u32[]{:S(2)}) %collective-permute-start.5) | collective-permute-done | bytes 196640 | tf_op jit(solution)/shard_map/ppermute | solution.py:609
  159.1 5.0 %collective-permute-done.6.refs_2_ = bf16[768,128]{1,0:T(8,128)(2,1)S(1)} collective-permute-done((bf16[768,128]{1,0:T(8,128)(2,1)S(1)}, bf16[768,128]{1,0:T(8,128)(2,1)S(1)}, u32[]{:S(2)}, u32[]{:S(2)}) %collective-permute-start.6) | collective-permute-done | bytes 196640 | tf_op jit(solution)/shard_map/ppermute | solution.py:609
  164.0 0.9 base_sum.1.base_ref
  164.9 0.0 all-to-all-done.8
  164.9 2.5 %take_main.1 = (bf16[768,128]{1,0:T(8,128)(2,1)S(1)}, s32[1]{0:T(128)}) custom-call(s32[768,1]{1,0:T(8,128)S(1)} %get-tuple-element.40.at_ref, bf16[1536,128]{1,0:T(8,128)(2,1)S(1)} %bitcast.23, f32[768,128]{1,0:T(8,128)} %base_sum.1.base_ref), custom_call_target="tpu_custom_call" | custom-call | tf_op jit(solution)/shard_map/take_main/pallas_call | solution.py:538
  168.0 0.0 copy-done.2
  168.0 0.2 conditional.1
  168.3 0.0 copy-start.6
  168.3 0.7 copy-done.6
  (9 shorter events, 0.1 us)
Async XLA Ops:
  0.0 11.0 %copy-start.1 = (bf16[768,1024]{1,0:T(8,128)(2,1)S(1)}, bf16[768,1024]{1,0:T(8,128)(2,1)}, u32[]{:S(2)}) copy-start(bf16[768,1024]{1,0:T(8,128)(2,1)} %tok_ref.5) | copy-start | bytes 4718596
  0.0 11.0 %copy-start.5 = (s32[768,1]{0,1:T(1,128)S(1)}, s32[768,1]{0,1:T(1,128)}, u32[]{:S(2)}) copy-start(s32[768,1]{0,1:T(1,128)} %param.11) | copy-start | bytes 9220
  3.4 17.1 %all-to-all-start.5 = ((bf16[8,16,1024]{2,1,0:T(8,128)(2,1)}), bf16[8,16,1024]{2,1,0:T(8,128)(2,1)S(1)}, u32[]{:S(2)}, u32[]{:S(2)}) async-start(bf16[8,16,1024]{2,1,0:T(8,128)(2,1)} %bitcast.11), calls=%async_computation.5 | async-start | bytes 524288 | tf_op jit(solution)/shard_map/all_to_all | solution.py:25
  20.4 81.0 %all-to-all-start.4 = ((bf16[64,16,1024]{2,1,0:T(8,128)(2,1)}), bf16[64,16,1024]{2,1,0:T(8,128)(2,1)S(1)}, u32[]{:S(2)}, u32[]{:S(2)}) async-start(bf16[64,16,1024]{2,1,0:T(8,128)(2,1)} %bitcast.8), calls=%async_computation.4 | async-start | bytes 4194304 | tf_op jit(solution)/shard_map/all_to_all | solution.py:25
  34.2 46.7 %collective-permute-start = (bf16[64,1024]{1,0:T(8,128)(2,1)S(1)}, bf16[64,1024]{1,0:T(8,128)(2,1)S(1)}, u32[]{:S(2)}, u32[]{:S(2)}) collective-permute-start(bf16[64,1024]{1,0:T(8,128)(2,1)S(1)} %get-tuple-element.44), channel_id=1, source_target_pairs={{0,64},{64,0},{128,192},{192,128},{256,320},{320,256},{384,448},{4... | collective-permute-start | bytes 393224 | tf_op jit(solution)/shard_map/ppermute | solution.py:321
  81.0 8.0 %collective-permute-start.1 = (bf16[64,1024]{1,0:T(8,128)(2,1)S(1)}, bf16[64,1024]{1,0:T(8,128)(2,1)S(1)}, u32[]{:S(2)}, u32[]{:S(2)}) collective-permute-start(bf16[64,1024]{1,0:T(8,128)(2,1)S(1)} %pad_maximum_fusion), channel_id=1, source_target_pairs={{0,128},{64,192},{128,0},{192,64},{256,384},{320,448},{384,256},{4... | collective-permute-start | bytes 393224 | tf_op jit(solution)/shard_map/ppermute | solution.py:321
  89.0 10.6 %collective-permute-start.2 = (bf16[64,1024]{1,0:T(8,128)(2,1)S(1)}, bf16[64,1024]{1,0:T(8,128)(2,1)S(1)}, u32[]{:S(2)}, u32[]{:S(2)}) collective-permute-start(bf16[64,1024]{1,0:T(8,128)(2,1)S(1)} %pad_maximum_fusion.1), channel_id=1, source_target_pairs={{0,256},{64,320},{128,384},{192,448},{256,0},{320,64},{384,128},{4... | collective-permute-start | bytes 393224 | tf_op jit(solution)/shard_map/ppermute | solution.py:321
  104.8 16.3 %all-to-all-start.6 = ((bf16[8,96,128]{2,1,0:T(8,128)(2,1)}), bf16[8,96,128]{2,1,0:T(8,128)(2,1)S(1)}, u32[]{:S(2)}, u32[]{:S(2)}) async-start(bf16[8,96,128]{2,1,0:T(8,128)(2,1)} %bitcast.13), calls=%async_computation.6 | async-start | bytes 393216 | tf_op jit(solution)/shard_map/all_to_all | solution.py:25
  114.2 1.6 copy-start
  115.7 15.9 %copy-start.4 = (bf16[8,64,128]{2,1,0:T(8,128)(2,1)S(1)}, bf16[8,64,128]{2,1,0:T(8,128)(2,1)}, u32[]{:S(2)}) copy-start(bf16[8,64,128]{2,1,0:T(8,128)(2,1)} %up_ref.1) | copy-start | bytes 393220
  119.1 27.1 %collective-permute-start.3 = (bf16[4,768,128]{2,1,0:T(8,128)(2,1)S(1)}, bf16[4,768,128]{2,1,0:T(8,128)(2,1)S(1)}, u32[]{:S(2)}, u32[]{:S(2)}) collective-permute-start(bf16[4,768,128]{2,1,0:T(8,128)(2,1)S(1)} %get-tuple-element.48), channel_id=1, source_target_pairs={{0,1},{1,0},{2,3},{3,2},{4,5},{5,4},{6,7},{7,6},{8,9},{9,8},{10,11... | collective-permute-start | bytes 2359304 | tf_op jit(solution)/shard_map/ppermute | solution.py:590
  133.0 31.9 %all-to-all-start.8 = ((bf16[64,24,128]{2,1,0:T(8,128)(2,1)}), bf16[64,24,128]{2,1,0:T(8,128)(2,1)S(1)}, u32[]{:S(2)}, u32[]{:S(2)}) async-start(bf16[64,24,128]{2,1,0:T(8,128)(2,1)} %bitcast.15), calls=%async_computation.8 | async-start | bytes 786432 | tf_op jit(solution)/shard_map/all_to_all | solution.py:25
  146.4 21.6 %copy-start.2 = (bf16[8,64,1024]{2,1,0:T(8,128)(2,1)S(1)}, bf16[8,64,1024]{2,1,0:T(8,128)(2,1)}, u32[]{:S(2)}) copy-start(bf16[8,64,1024]{2,1,0:T(8,128)(2,1)} %down_ref.1) | copy-start | bytes 3145732
  146.4 9.7 %collective-permute-start.4 = (bf16[768,128]{1,0:T(8,128)(2,1)S(1)}, bf16[768,128]{1,0:T(8,128)(2,1)S(1)}, u32[]{:S(2)}, u32[]{:S(2)}) collective-permute-start(bf16[768,128]{1,0:T(8,128)(2,1)S(1)} %get-tuple-element.49), channel_id=1, source_target_pairs={{0,2},{2,0},{4,6},{6,4},{1,3},{3,1},{5,7},{7,5},{8,10},{10,8},{12,... | collective-permute-start | bytes 589832 | tf_op jit(solution)/shard_map/ppermute | solution.py:609
  148.7 10.3 %collective-permute-start.5 = (bf16[768,128]{1,0:T(8,128)(2,1)S(1)}, bf16[768,128]{1,0:T(8,128)(2,1)S(1)}, u32[]{:S(2)}, u32[]{:S(2)}) collective-permute-start(bf16[768,128]{1,0:T(8,128)(2,1)S(1)} %get-tuple-element.50), channel_id=1, source_target_pairs={{0,4},{2,6},{4,0},{6,2},{1,5},{3,7},{5,1},{7,3},{8,12},{10,14},{12... | collective-permute-start | bytes 589832 | tf_op jit(solution)/shard_map/ppermute | solution.py:609
  152.4 11.6 %collective-permute-start.6 = (bf16[768,128]{1,0:T(8,128)(2,1)S(1)}, bf16[768,128]{1,0:T(8,128)(2,1)S(1)}, u32[]{:S(2)}, u32[]{:S(2)}) collective-permute-start(bf16[768,128]{1,0:T(8,128)(2,1)S(1)} %get-tuple-element.51), channel_id=1, source_target_pairs={{0,6},{2,4},{4,2},{6,0},{1,7},{3,5},{5,3},{7,1},{8,14},{10,12},{12... | collective-permute-start | bytes 589832 | tf_op jit(solution)/shard_map/ppermute | solution.py:609
  168.3 0.7 copy-start.6

commit v6 on v5

--- a/solution.py
+++ b/solution.py
@@ -13,8 +13,6 @@
 MOST = 3
 MAIN = 2
 SIDE = 16
-STAY = (0, 4, 2, 6)
-LEAVE = (1, 5, 3, 7)
 LOST = 3e38
 GRANT = pltpu.CompilerParams(vmem_limit_bytes=16 * 2**20)
 
@@ -308,26 +306,6 @@
         store(k, block.astype(jnp.bfloat16))
 
 
-def arrived_blocks(refs):
-    stay, first, second, third = refs
-    spots = [(stay, 0), (first, 0), (second, 0), (second, 2)] + [(third, i) for i in range(4)]
-    return [ref[i * SIDE : (i + 1) * SIDE, :] for ref, i in spots]
-
-
-def halving_sends(stay, leave, axis):
-    size = lax.axis_size(axis)
-
-    def send(x, step):
-        return lax.ppermute(x, axis, [(i, i ^ step) for i in range(size)])
-
-    half = 2 * SIDE
-    first = send(leave, 1)
-    second = send(jnp.concatenate([stay[half:], first[half:]]), 2)
-    last = [x[i * SIDE : (i + 1) * SIDE] for x, i in ((stay, 1), (first, 1), (second, 1), (second, 3))]
-    third = send(jnp.concatenate(last), 4)
-    return stay, first, second, third
-
-
 def read_codes(blocks):
     n = 8 * SIDE
     lane = lax.broadcasted_iota(jnp.int32, (8, n), 1)
@@ -380,7 +358,8 @@
 def side_second(at, arrived):
     n, width = arrived.shape
 
-    def kernel(at_ref, in_ref, stay_ref, leave_ref, block_ref):
+    def kernel(at_ref, in_ref, *refs):
+        out_refs, block_ref = refs[:8], refs[8]
         blocks = [in_ref[k * SIDE : (k + 1) * SIDE, :] for k in range(8)]
         code, flag = read_codes(blocks)
         valid = code >= 0
@@ -391,14 +370,13 @@
             block_ref[k] = block
 
         bucket(in_ref[...], key, to_col(key), from_y * 8 + code % 8, valid, flag, store)
-        for ref, order in ((stay_ref, STAY), (leave_ref, LEAVE)):
-            for i, k in enumerate(order):
-                ref[i * SIDE : (i + 1) * SIDE, :] = block_ref[at_ref[0] ^ k]
+        for k in range(8):
+            out_refs[k][...] = block_ref[at_ref[0] ^ k]
 
     return pl.pallas_call(
         kernel,
         in_specs=[scalar_spec(), pl.BlockSpec(memory_space=pltpu.VMEM)],
-        out_shape=[jax.ShapeDtypeStruct((4 * SIDE, width), jnp.bfloat16)] * 2,
+        out_shape=[jax.ShapeDtypeStruct((SIDE, width), jnp.bfloat16)] * 8,
         scratch_shapes=[pltpu.VMEM((8, SIDE, width), jnp.bfloat16)],
         compiler_params=GRANT,
         name="side_second",
@@ -426,8 +404,8 @@
     pair = 2 * rank
 
     def kernel(at_ref, *refs):
-        down_ref, out_ref, flag_ref = refs[4:]
-        blocks = arrived_blocks(refs[:4])
+        down_ref, out_ref, flag_ref = refs[8:]
+        blocks = [ref[...] for ref in refs[:8]]
         code, flag = read_codes(blocks)
         from_z = (lax.broadcasted_iota(jnp.int32, (1, n), 1) // SIDE) ^ at_ref[0]
         slot = jnp.where(code >= 0, from_z * 64 + code, -1)
@@ -444,7 +422,7 @@
 
     return pl.pallas_call(
         kernel,
-        in_specs=[scalar_spec()] + [pl.BlockSpec(memory_space=pltpu.VMEM)] * 5,
+        in_specs=[scalar_spec()] + [pl.BlockSpec(memory_space=pltpu.VMEM)] * 9,
         out_shape=[
             jax.ShapeDtypeStruct((thirds // 2, pair), jnp.bfloat16),
             jax.ShapeDtypeStruct((8, 128), jnp.float32),
@@ -582,14 +560,15 @@
     arrived = arrived.reshape(64 * HERE * MAIN, width)
 
     blocks = side_second(at_z.reshape(1), blocks)
-    blocks = halving_sends(*blocks, "z")
+    blocks = xor_sends(blocks, "z")
     thirds, flag = side_low(at_z.reshape(1), blocks, adapter_down)
 
     at = lax.axis_index(TENSOR).astype(jnp.int32).reshape(1)
     own, other = value_pieces(tokens, value_weight, at, groups)
     other = lax.ppermute(other, TENSOR[1], [(0, 1), (1, 0)])
     pairs = pair_sum(own, other)
-    base = base_sum(own, other, xor_sends(pairs, TENSOR[0]))
+    pairs = xor_sends([own, *pairs], TENSOR[0])[1:]
+    base = base_sum(own, other, pairs)
 
     low = low_of_all(down_main(arrived, thirds, adapter_down), groups)
     delta = up_main(low, flag, adapter_up_weight)
@@ -604,9 +583,9 @@
 
 def xor_sends(pieces, axis):
     size = lax.axis_size(axis)
-    parts = []
+    parts = [pieces[0]]
     for k in range(1, size):
-        parts.append(lax.ppermute(pieces[k - 1], axis, [(i, i ^ k) for i in range(size)]))
+        parts.append(lax.ppermute(pieces[k], axis, [(i, i ^ k) for i in range(size)]))
     return parts
 
 

time: 170 us -> 160 us (0.941)
  waiting for transfers between devices: 62.6 us -> 19.1 us
  starting transfers between devices: 71.8 us -> 105 us
    ppermute x6 -> x10, waiting for transfers between devices: 56.5 us -> 13 us  [xor_sends(): lax.ppermute(pieces[k], axis, [(i, i ^ k) for i in range(size)])]
    ppermute x6 -> x10, starting transfers between devices: 26.4 us -> 60.4 us  [xor_sends(): lax.ppermute(pieces[k], axis, [(i, i ^ k) for i in range(size)])]
  transfers between devices with their start and end apart: 11 -> 15, of which waited for: 6 -> 6; matrix products, arithmetic and copies ran while one was open for 0% -> 0% of each run, Pallas kernels for 7% -> 7%
where the time goes in v6:
time: 160 us; the launch traced here: 159 us
  starting transfers between devices  105 us (66%)
  Pallas kernels  20.6 us (13%)
  waiting for transfers between devices  19.1 us (12%)
  blocking collectives  10.6 us (7%)
  local copies, waits for them, and re-layouts  2.31 us (1%)
    ppermute x10, starting transfers between devices, xor_sends(): lax.ppermute(pieces[k], axis, [(i, i ^ k) for i in range(size)])  60.4 us
    all_to_all x4, starting transfers between devices, swap(): return lax.all_to_all(x, axes, split_axis=0, concat_axis=0, tiled=True)  42.9 us
    ppermute x10, waiting for transfers between devices, xor_sends(): lax.ppermute(pieces[k], axis, [(i, i ^ k) for i in range(size)])  13 us
    all_to_all x1, blocking collectives, swap(): return lax.all_to_all(x, axes, split_axis=0, concat_axis=0, tiled=True)  10.6 us
    all_to_all x4, waiting for transfers between devices, swap(): return lax.all_to_all(x, axes, split_axis=0, concat_axis=0, tiled=True)  6.05 us
    pallas_call x1, Pallas kernels, place_main(): pl.pallas_call(kernel, grid=(slots // tile,), in_specs=[pl.BlockSpec((1,...  3.37 us
    pallas_call x1, Pallas kernels, side_first(): pl.pallas_call(kernel, out_shape=[jax.ShapeDtypeStruct((8 * SIDE, width),...  3.35 us
    pallas_call x1, Pallas kernels, value_pieces(): pl.pallas_call(kernel, in_specs=[pl.BlockSpec(memory_space=pltpu.SMEM), p...  3.33 us
  transfers between devices with their start and end apart: 15, of which 6 were waited for; matrix products, arithmetic and copies ran while one was open for 0% of the time, Pallas kernels for 7%

profile of v6, /device:TPU:1, one launch (start us, length us, event | category | flops | bytes accessed | tf_op | source)
XLA Modules:
  0.0 158.9 jit_solution(6358800406998772736)
XLA Ops:
  0.0 0.0 copy-start.1
  0.0 0.0 copy-start.5
  0.0 3.4 %side_first.1 = (bf16[128,1024]{1,0:T(8,128)(2,1)}, s32[1,768]{1,0:T(1,128)S(1)}, s32[768,1]{1,0:T(8,128)S(1)}) custom-call(s32[1,768]{1,0:T(1,128)} %bitcast.30, bf16[768,1024]{1,0:T(8,128)(2,1)} %tok_ref.5), custom_call_target="tpu_custom_call" | custom-call | tf_op jit(solution)/shard_map/side_first/pallas_call | solution.py:346
  3.4 7.6 %all-to-all-start.5 = ((bf16[8,16,1024]{2,1,0:T(8,128)(2,1)}), bf16[8,16,1024]{2,1,0:T(8,128)(2,1)S(1)}, u32[]{:S(2)}, u32[]{:S(2)}) async-start(bf16[8,16,1024]{2,1,0:T(8,128)(2,1)} %bitcast.11), calls=%async_computation.5 | async-start | bytes 524288 | tf_op jit(solution)/shard_map/all_to_all | solution.py:23
  11.0 0.0 copy-done.1
  11.0 0.0 copy-done.5
  11.0 3.4 %place_main.1 = bf16[1024,1024]{1,0:T(8,128)(2,1)} custom-call(s32[1,768]{1,0:T(1,128)S(1)} %bitcast.31, s32[1,768]{1,0:T(1,128)S(1)} %get-tuple-element.47.seen_ref, bf16[768,1024]{1,0:T(8,128)(2,1)S(1)} %copy-done.1), custom_call_target="tpu_custom_call" | custom-call | tf_op jit(solution)/shard_map/place_main/pallas_call | solution.py:265
  14.4 6.0 %all-to-all-done.5 = bf16[8,16,1024]{2,1,0:T(8,128)(2,1)S(1)} async-done(((bf16[8,16,1024]{2,1,0:T(8,128)(2,1)}), bf16[8,16,1024]{2,1,0:T(8,128)(2,1)S(1)}, u32[]{:S(2)}, u32[]{:S(2)}) %all-to-all-start.5) | async-done | bytes 262176 | tf_op jit(solution)/shard_map/all_to_all | solution.py:23
  20.4 13.2 %all-to-all-start.4 = ((bf16[64,16,1024]{2,1,0:T(8,128)(2,1)}), bf16[64,16,1024]{2,1,0:T(8,128)(2,1)S(1)}, u32[]{:S(2)}, u32[]{:S(2)}) async-start(bf16[64,16,1024]{2,1,0:T(8,128)(2,1)} %bitcast.8), calls=%async_computation.4 | async-start | bytes 4194304 | tf_op jit(solution)/shard_map/all_to_all | solution.py:23
  33.7 0.5 side_second.1
  34.2 2.9 %collective-permute-start = (bf16[16,1024]{1,0:T(8,128)(2,1)S(1)}, bf16[16,1024]{1,0:T(8,128)(2,1)S(1)}, u32[]{:S(2)}, u32[]{:S(2)}) collective-permute-start(bf16[16,1024]{1,0:T(8,128)(2,1)S(1)} %get-tuple-element.50), channel_id=1, source_target_pairs={{0,64},{64,0},{128,192},{192,128},{256,320},{320,256},{384,448},{4... | collective-permute-start | bytes 98312 | tf_op jit(solution)/shard_map/ppermute | solution.py:588
  37.1 4.0 %collective-permute-start.1 = (bf16[16,1024]{1,0:T(8,128)(2,1)S(1)}, bf16[16,1024]{1,0:T(8,128)(2,1)S(1)}, u32[]{:S(2)}, u32[]{:S(2)}) collective-permute-start(bf16[16,1024]{1,0:T(8,128)(2,1)S(1)} %get-tuple-element.51), channel_id=1, source_target_pairs={{0,128},{64,192},{128,0},{192,64},{256,384},{320,448},{384,256},{4... | collective-permute-start | bytes 98312 | tf_op jit(solution)/shard_map/ppermute | solution.py:588
  41.2 2.3 %collective-permute-start.2 = (bf16[16,1024]{1,0:T(8,128)(2,1)S(1)}, bf16[16,1024]{1,0:T(8,128)(2,1)S(1)}, u32[]{:S(2)}, u32[]{:S(2)}) collective-permute-start(bf16[16,1024]{1,0:T(8,128)(2,1)S(1)} %get-tuple-element.52), channel_id=1, source_target_pairs={{0,192},{64,128},{128,64},{192,0},{256,448},{320,384},{384,320},{4... | collective-permute-start | bytes 98312 | tf_op jit(solution)/shard_map/ppermute | solution.py:588
  43.5 6.9 %collective-permute-start.3 = (bf16[16,1024]{1,0:T(8,128)(2,1)S(1)}, bf16[16,1024]{1,0:T(8,128)(2,1)S(1)}, u32[]{:S(2)}, u32[]{:S(2)}) collective-permute-start(bf16[16,1024]{1,0:T(8,128)(2,1)S(1)} %get-tuple-element.53), channel_id=1, source_target_pairs={{0,256},{64,320},{128,384},{192,448},{256,0},{320,64},{384,128},{4... | collective-permute-start | bytes 98312 | tf_op jit(solution)/shard_map/ppermute | solution.py:588
  50.4 1.9 %collective-permute-start.4 = (bf16[16,1024]{1,0:T(8,128)(2,1)S(1)}, bf16[16,1024]{1,0:T(8,128)(2,1)S(1)}, u32[]{:S(2)}, u32[]{:S(2)}) collective-permute-start(bf16[16,1024]{1,0:T(8,128)(2,1)S(1)} %get-tuple-element.54), channel_id=1, source_target_pairs={{0,320},{64,256},{128,448},{192,384},{256,64},{320,0},{384,192},{4... | collective-permute-start | bytes 98312 | tf_op jit(solution)/shard_map/ppermute | solution.py:588
  52.3 0.0 collective-permute-done.refs_1_
  52.4 30.4 %collective-permute-start.5 = (bf16[16,1024]{1,0:T(8,128)(2,1)S(1)}, bf16[16,1024]{1,0:T(8,128)(2,1)S(1)}, u32[]{:S(2)}, u32[]{:S(2)}) collective-permute-start(bf16[16,1024]{1,0:T(8,128)(2,1)S(1)} %get-tuple-element.55), channel_id=1, source_target_pairs={{0,384},{64,448},{128,256},{192,320},{256,128},{320,192},{384,0},{... | collective-permute-start | bytes 98312 | tf_op jit(solution)/shard_map/ppermute | solution.py:588
  82.7 0.0 collective-permute-done.1.refs_2_
  82.7 2.2 %collective-permute-start.6 = (bf16[16,1024]{1,0:T(8,128)(2,1)S(1)}, bf16[16,1024]{1,0:T(8,128)(2,1)S(1)}, u32[]{:S(2)}, u32[]{:S(2)}) collective-permute-start(bf16[16,1024]{1,0:T(8,128)(2,1)S(1)} %get-tuple-element.56), channel_id=1, source_target_pairs={{0,448},{64,384},{128,320},{192,256},{256,192},{320,128},{384,64},... | collective-permute-start | bytes 98312 | tf_op jit(solution)/shard_map/ppermute | solution.py:588
  84.9 1.2 collective-permute-done.2.refs_3_
  86.1 0.0 collective-permute-done.3.refs_4_
  86.1 3.6 %collective-permute-done.4.refs_5_ = bf16[16,1024]{1,0:T(8,128)(2,1)S(1)} collective-permute-done((bf16[16,1024]{1,0:T(8,128)(2,1)S(1)}, bf16[16,1024]{1,0:T(8,128)(2,1)S(1)}, u32[]{:S(2)}, u32[]{:S(2)}) %collective-permute-start.4) | collective-permute-done | bytes 32800 | tf_op jit(solution)/shard_map/ppermute | solution.py:588
  89.7 0.0 collective-permute-done.5.refs_6_
  89.7 0.4 collective-permute-done.6.refs_7_
  90.0 1.9 %side_low.1 = (bf16[256,128]{1,0:T(8,128)(2,1)S(1)}, f32[8,128]{1,0:T(8,128)S(1)}) custom-call(s32[1]{0:T(128)} %bitcast.10.at_ref, bf16[16,1024]{1,0:T(8,128)(2,1)S(1)} %get-tuple-element.49.refs_0_, bf16[16,1024]{1,0:T(8,128)(2,1)S(1)} %collective-permute-done.refs_1_, bf16[16,1024]{1,0:T(8,128)(2,1)S(1)} %collective-permute-done.1.refs_2_, ...), custom_call_target="tpu_custom_call" | custom-call | tf_op jit(solution)/shard_map/side_low/pallas_call | solution.py:423
  92.0 0.0 all-to-all-done.4
  92.0 3.3 %down_main.1 = bf16[768,128]{1,0:T(8,128)(2,1)} custom-call(bf16[1024,1024]{1,0:T(8,128)(2,1)S(1)} %bitcast.21, bf16[256,128]{1,0:T(8,128)(2,1)S(1)} %get-tuple-element.57.thirds_ref, bf16[8,64,1024]{2,1,0:T(8,128)(2,1)} %down_ref.1), custom_call_target="tpu_custom_call" | custom-call | tf_op jit(solution)/shard_map/down_main/pallas_call | solution.py:455
  95.2 10.2 %all-to-all-start.6 = ((bf16[8,96,128]{2,1,0:T(8,128)(2,1)}), bf16[8,96,128]{2,1,0:T(8,128)(2,1)S(1)}, u32[]{:S(2)}, u32[]{:S(2)}) async-start(bf16[8,96,128]{2,1,0:T(8,128)(2,1)} %bitcast.13), calls=%async_computation.6 | async-start | bytes 393216 | tf_op jit(solution)/shard_map/all_to_all | solution.py:23
  105.4 0.0 copy-start
  105.4 1.6 copy-done
  107.0 0.0 copy-start.4
  107.0 3.3 %value_pieces.1 = (bf16[4,768,128]{2,1,0:T(8,128)(2,1)S(1)}, bf16[4,768,128]{2,1,0:T(8,128)(2,1)S(1)}) custom-call(s32[1]{0:T(128)} %bitcast.17.at_ref, bf16[768,1024]{1,0:T(8,128)(2,1)} %tok_ref.5, bf16[1024,1024]{1,0:T(8,128)(2,1)S(1)} %copy-done), custom_call_target="tpu_custom_call" | custom-call | tf_op jit(solution)/shard_map/value_pieces/pallas_call | solution.py:89
  110.3 1.9 %collective-permute-start.7 = (bf16[4,768,128]{2,1,0:T(8,128)(2,1)S(1)}, bf16[4,768,128]{2,1,0:T(8,128)(2,1)S(1)}, u32[]{:S(2)}, u32[]{:S(2)}) collective-permute-start(bf16[4,768,128]{2,1,0:T(8,128)(2,1)S(1)} %get-tuple-element.60), channel_id=1, source_target_pairs={{0,1},{1,0},{2,3},{3,2},{4,5},{5,4},{6,7},{7,6},{8,9},{9,8},{10,11... | collective-permute-start | bytes 2359304 | tf_op jit(solution)/shard_map/ppermute | solution.py:568
  112.2 0.0 all-to-all-done.6
  112.3 10.6 %all_to_all.45 = bf16[8,96,128]{2,1,0:T(8,128)(2,1)S(1)} all-to-all(bf16[8,96,128]{2,1,0:T(8,128)(2,1)S(1)} %broadcast_in_dim.4), channel_id=1, replica_groups=mesh['z'=8,'y'=8,'tensor_0'=4,'tensor_1'=2] {'tensor_0','tensor_1'}, dimensions={0} | all-to-all | bytes 393216 | tf_op jit(solution)/shard_map/all_to_all | solution.py:23
  122.9 0.0 copy-done.4
  122.9 1.4 up_main.1
  124.3 11.9 %all-to-all-start.8 = ((bf16[64,24,128]{2,1,0:T(8,128)(2,1)}), bf16[64,24,128]{2,1,0:T(8,128)(2,1)S(1)}, u32[]{:S(2)}, u32[]{:S(2)}) async-start(bf16[64,24,128]{2,1,0:T(8,128)(2,1)} %bitcast.15), calls=%async_computation.8 | async-start | bytes 786432 | tf_op jit(solution)/shard_map/all_to_all | solution.py:23
  136.2 0.0 collective-permute-done.7.other_ref
  136.2 0.1 pair_sum.1
  136.3 0.0 copy-start.2
  136.3 2.3 %collective-permute-start.8 = (bf16[768,128]{1,0:T(8,128)(2,1)S(1)}, bf16[768,128]{1,0:T(8,128)(2,1)S(1)}, u32[]{:S(2)}, u32[]{:S(2)}) collective-permute-start(bf16[768,128]{1,0:T(8,128)(2,1)S(1)} %get-tuple-element.61), channel_id=1, source_target_pairs={{0,2},{2,0},{4,6},{6,4},{1,3},{3,1},{5,7},{7,5},{8,10},{10,8},{12,... | collective-permute-start | bytes 589832 | tf_op jit(solution)/shard_map/ppermute | solution.py:588
  138.7 3.7 %collective-permute-start.9 = (bf16[768,128]{1,0:T(8,128)(2,1)S(1)}, bf16[768,128]{1,0:T(8,128)(2,1)S(1)}, u32[]{:S(2)}, u32[]{:S(2)}) collective-permute-start(bf16[768,128]{1,0:T(8,128)(2,1)S(1)} %get-tuple-element.62), channel_id=1, source_target_pairs={{0,4},{2,6},{4,0},{6,2},{1,5},{3,7},{5,1},{7,3},{8,12},{10,14},{12... | collective-permute-start | bytes 589832 | tf_op jit(solution)/shard_map/ppermute | solution.py:588
  142.4 3.7 %collective-permute-start.10 = (bf16[768,128]{1,0:T(8,128)(2,1)S(1)}, bf16[768,128]{1,0:T(8,128)(2,1)S(1)}, u32[]{:S(2)}, u32[]{:S(2)}) collective-permute-start(bf16[768,128]{1,0:T(8,128)(2,1)S(1)} %get-tuple-element.63), channel_id=1, source_target_pairs={{0,6},{2,4},{4,2},{6,0},{1,7},{3,5},{5,3},{7,1},{8,14},{10,12},{12... | collective-permute-start | bytes 589832 | tf_op jit(solution)/shard_map/ppermute | solution.py:588
  146.1 0.0 collective-permute-done.8.refs_0_
  146.1 2.9 %collective-permute-done.9.refs_1_ = bf16[768,128]{1,0:T(8,128)(2,1)S(1)} collective-permute-done((bf16[768,128]{1,0:T(8,128)(2,1)S(1)}, bf16[768,128]{1,0:T(8,128)(2,1)S(1)}, u32[]{:S(2)}, u32[]{:S(2)}) %collective-permute-start.9) | collective-permute-done | bytes 196640 | tf_op jit(solution)/shard_map/ppermute | solution.py:588
  149.0 5.0 %collective-permute-done.10.refs_2_ = bf16[768,128]{1,0:T(8,128)(2,1)S(1)} collective-permute-done((bf16[768,128]{1,0:T(8,128)(2,1)S(1)}, bf16[768,128]{1,0:T(8,128)(2,1)S(1)}, u32[]{:S(2)}, u32[]{:S(2)}) %collective-permute-start.10) | collective-permute-done | bytes 196640 | tf_op jit(solution)/shard_map/ppermute | solution.py:588
  154.0 0.9 base_sum.1.base_ref
  154.9 0.0 all-to-all-done.8
  154.9 2.5 %take_main.1 = (bf16[768,128]{1,0:T(8,128)(2,1)S(1)}, s32[1]{0:T(128)}) custom-call(s32[768,1]{1,0:T(8,128)S(1)} %get-tuple-element.46.at_ref, bf16[1536,128]{1,0:T(8,128)(2,1)S(1)} %bitcast.23, f32[768,128]{1,0:T(8,128)} %base_sum.1.base_ref), custom_call_target="tpu_custom_call" | custom-call | tf_op jit(solution)/shard_map/take_main/pallas_call | solution.py:516
  158.0 0.0 copy-done.2
  158.0 0.2 conditional.1
  158.2 0.0 copy-start.6
  158.3 0.7 copy-done.6
  (2 shorter events, 0.1 us)
Async XLA Ops:
  0.0 11.0 %copy-start.1 = (bf16[768,1024]{1,0:T(8,128)(2,1)S(1)}, bf16[768,1024]{1,0:T(8,128)(2,1)}, u32[]{:S(2)}) copy-start(bf16[768,1024]{1,0:T(8,128)(2,1)} %tok_ref.5) | copy-start | bytes 4718596
  0.0 11.0 %copy-start.5 = (s32[768,1]{0,1:T(1,128)S(1)}, s32[768,1]{0,1:T(1,128)}, u32[]{:S(2)}) copy-start(s32[768,1]{0,1:T(1,128)} %param.11) | copy-start | bytes 9220
  3.4 17.1 %all-to-all-start.5 = ((bf16[8,16,1024]{2,1,0:T(8,128)(2,1)}), bf16[8,16,1024]{2,1,0:T(8,128)(2,1)S(1)}, u32[]{:S(2)}, u32[]{:S(2)}) async-start(bf16[8,16,1024]{2,1,0:T(8,128)(2,1)} %bitcast.11), calls=%async_computation.5 | async-start | bytes 524288 | tf_op jit(solution)/shard_map/all_to_all | solution.py:23
  20.4 71.5 %all-to-all-start.4 = ((bf16[64,16,1024]{2,1,0:T(8,128)(2,1)}), bf16[64,16,1024]{2,1,0:T(8,128)(2,1)S(1)}, u32[]{:S(2)}, u32[]{:S(2)}) async-start(bf16[64,16,1024]{2,1,0:T(8,128)(2,1)} %bitcast.8), calls=%async_computation.4 | async-start | bytes 4194304 | tf_op jit(solution)/shard_map/all_to_all | solution.py:23
  34.2 18.2 %collective-permute-start = (bf16[16,1024]{1,0:T(8,128)(2,1)S(1)}, bf16[16,1024]{1,0:T(8,128)(2,1)S(1)}, u32[]{:S(2)}, u32[]{:S(2)}) collective-permute-start(bf16[16,1024]{1,0:T(8,128)(2,1)S(1)} %get-tuple-element.50), channel_id=1, source_target_pairs={{0,64},{64,0},{128,192},{192,128},{256,320},{320,256},{384,448},{4... | collective-permute-start | bytes 98312 | tf_op jit(solution)/shard_map/ppermute | solution.py:588
  37.1 45.6 %collective-permute-start.1 = (bf16[16,1024]{1,0:T(8,128)(2,1)S(1)}, bf16[16,1024]{1,0:T(8,128)(2,1)S(1)}, u32[]{:S(2)}, u32[]{:S(2)}) collective-permute-start(bf16[16,1024]{1,0:T(8,128)(2,1)S(1)} %get-tuple-element.51), channel_id=1, source_target_pairs={{0,128},{64,192},{128,0},{192,64},{256,384},{320,448},{384,256},{4... | collective-permute-start | bytes 98312 | tf_op jit(solution)/shard_map/ppermute | solution.py:588
  41.2 44.9 %collective-permute-start.2 = (bf16[16,1024]{1,0:T(8,128)(2,1)S(1)}, bf16[16,1024]{1,0:T(8,128)(2,1)S(1)}, u32[]{:S(2)}, u32[]{:S(2)}) collective-permute-start(bf16[16,1024]{1,0:T(8,128)(2,1)S(1)} %get-tuple-element.52), channel_id=1, source_target_pairs={{0,192},{64,128},{128,64},{192,0},{256,448},{320,384},{384,320},{4... | collective-permute-start | bytes 98312 | tf_op jit(solution)/shard_map/ppermute | solution.py:588
  43.5 42.6 %collective-permute-start.3 = (bf16[16,1024]{1,0:T(8,128)(2,1)S(1)}, bf16[16,1024]{1,0:T(8,128)(2,1)S(1)}, u32[]{:S(2)}, u32[]{:S(2)}) collective-permute-start(bf16[16,1024]{1,0:T(8,128)(2,1)S(1)} %get-tuple-element.53), channel_id=1, source_target_pairs={{0,256},{64,320},{128,384},{192,448},{256,0},{320,64},{384,128},{4... | collective-permute-start | bytes 98312 | tf_op jit(solution)/shard_map/ppermute | solution.py:588
  50.4 39.2 %collective-permute-start.4 = (bf16[16,1024]{1,0:T(8,128)(2,1)S(1)}, bf16[16,1024]{1,0:T(8,128)(2,1)S(1)}, u32[]{:S(2)}, u32[]{:S(2)}) collective-permute-start(bf16[16,1024]{1,0:T(8,128)(2,1)S(1)} %get-tuple-element.54), channel_id=1, source_target_pairs={{0,320},{64,256},{128,448},{192,384},{256,64},{320,0},{384,192},{4... | collective-permute-start | bytes 98312 | tf_op jit(solution)/shard_map/ppermute | solution.py:588
  52.4 37.3 %collective-permute-start.5 = (bf16[16,1024]{1,0:T(8,128)(2,1)S(1)}, bf16[16,1024]{1,0:T(8,128)(2,1)S(1)}, u32[]{:S(2)}, u32[]{:S(2)}) collective-permute-start(bf16[16,1024]{1,0:T(8,128)(2,1)S(1)} %get-tuple-element.55), channel_id=1, source_target_pairs={{0,384},{64,448},{128,256},{192,320},{256,128},{320,192},{384,0},{... | collective-permute-start | bytes 98312 | tf_op jit(solution)/shard_map/ppermute | solution.py:588
  82.7 7.3 %collective-permute-start.6 = (bf16[16,1024]{1,0:T(8,128)(2,1)S(1)}, bf16[16,1024]{1,0:T(8,128)(2,1)S(1)}, u32[]{:S(2)}, u32[]{:S(2)}) collective-permute-start(bf16[16,1024]{1,0:T(8,128)(2,1)S(1)} %get-tuple-element.56), channel_id=1, source_target_pairs={{0,448},{64,384},{128,320},{192,256},{256,192},{320,128},{384,64},... | collective-permute-start | bytes 98312 | tf_op jit(solution)/shard_map/ppermute | solution.py:588
  95.2 17.0 %all-to-all-start.6 = ((bf16[8,96,128]{2,1,0:T(8,128)(2,1)}), bf16[8,96,128]{2,1,0:T(8,128)(2,1)S(1)}, u32[]{:S(2)}, u32[]{:S(2)}) async-start(bf16[8,96,128]{2,1,0:T(8,128)(2,1)} %bitcast.13), calls=%async_computation.6 | async-start | bytes 393216 | tf_op jit(solution)/shard_map/all_to_all | solution.py:23
  105.4 1.6 %copy-start = (bf16[1024,1024]{1,0:T(8,128)(2,1)S(1)}, bf16[1024,1024]{1,0:T(8,128)(2,1)}, u32[]{:S(2)}) copy-start(bf16[1024,1024]{1,0:T(8,128)(2,1)} %w_ref.1) | copy-start | bytes 6291460
  107.0 15.9 %copy-start.4 = (bf16[8,64,128]{2,1,0:T(8,128)(2,1)S(1)}, bf16[8,64,128]{2,1,0:T(8,128)(2,1)}, u32[]{:S(2)}) copy-start(bf16[8,64,128]{2,1,0:T(8,128)(2,1)} %up_ref.1) | copy-start | bytes 393220
  110.3 25.9 %collective-permute-start.7 = (bf16[4,768,128]{2,1,0:T(8,128)(2,1)S(1)}, bf16[4,768,128]{2,1,0:T(8,128)(2,1)S(1)}, u32[]{:S(2)}, u32[]{:S(2)}) collective-permute-start(bf16[4,768,128]{2,1,0:T(8,128)(2,1)S(1)} %get-tuple-element.60), channel_id=1, source_target_pairs={{0,1},{1,0},{2,3},{3,2},{4,5},{5,4},{6,7},{7,6},{8,9},{9,8},{10,11... | collective-permute-start | bytes 2359304 | tf_op jit(solution)/shard_map/ppermute | solution.py:568
  124.3 30.6 %all-to-all-start.8 = ((bf16[64,24,128]{2,1,0:T(8,128)(2,1)}), bf16[64,24,128]{2,1,0:T(8,128)(2,1)S(1)}, u32[]{:S(2)}, u32[]{:S(2)}) async-start(bf16[64,24,128]{2,1,0:T(8,128)(2,1)} %bitcast.15), calls=%async_computation.8 | async-start | bytes 786432 | tf_op jit(solution)/shard_map/all_to_all | solution.py:23
  136.3 21.7 %copy-start.2 = (bf16[8,64,1024]{2,1,0:T(8,128)(2,1)S(1)}, bf16[8,64,1024]{2,1,0:T(8,128)(2,1)}, u32[]{:S(2)}) copy-start(bf16[8,64,1024]{2,1,0:T(8,128)(2,1)} %down_ref.1) | copy-start | bytes 3145732
  136.3 9.7 %collective-permute-start.8 = (bf16[768,128]{1,0:T(8,128)(2,1)S(1)}, bf16[768,128]{1,0:T(8,128)(2,1)S(1)}, u32[]{:S(2)}, u32[]{:S(2)}) collective-permute-start(bf16[768,128]{1,0:T(8,128)(2,1)S(1)} %get-tuple-element.61), channel_id=1, source_target_pairs={{0,2},{2,0},{4,6},{6,4},{1,3},{3,1},{5,7},{7,5},{8,10},{10,8},{12,... | collective-permute-start | bytes 589832 | tf_op jit(solution)/shard_map/ppermute | solution.py:588
  138.7 10.3 %collective-permute-start.9 = (bf16[768,128]{1,0:T(8,128)(2,1)S(1)}, bf16[768,128]{1,0:T(8,128)(2,1)S(1)}, u32[]{:S(2)}, u32[]{:S(2)}) collective-permute-start(bf16[768,128]{1,0:T(8,128)(2,1)S(1)} %get-tuple-element.62), channel_id=1, source_target_pairs={{0,4},{2,6},{4,0},{6,2},{1,5},{3,7},{5,1},{7,3},{8,12},{10,14},{12... | collective-permute-start | bytes 589832 | tf_op jit(solution)/shard_map/ppermute | solution.py:588
  142.4 11.6 %collective-permute-start.10 = (bf16[768,128]{1,0:T(8,128)(2,1)S(1)}, bf16[768,128]{1,0:T(8,128)(2,1)S(1)}, u32[]{:S(2)}, u32[]{:S(2)}) collective-permute-start(bf16[768,128]{1,0:T(8,128)(2,1)S(1)} %get-tuple-element.63), channel_id=1, source_target_pairs={{0,6},{2,4},{4,2},{6,0},{1,7},{3,5},{5,3},{7,1},{8,14},{10,12},{12... | collective-permute-start | bytes 589832 | tf_op jit(solution)/shard_map/ppermute | solution.py:588
  158.2 0.7 copy-start.6

commit v7 on v6

--- a/solution.py
+++ b/solution.py
@@ -432,32 +432,40 @@
     )(at, *blocks, down)
 
 
-def down_main(arrived, thirds, down):
+def down_main(at, arrived, thirds, down):
     slots, width = arrived.shape
     here, rank, _ = down.shape
     half = slots // 2
     tile = 256
     pair = 2 * rank
-
-    def kernel(in_ref, thirds_ref, down_ref, out_ref):
+    share = (half + thirds.shape[0]) // 2
+
+    def kernel(at_ref, in_ref, thirds_ref, down_ref, own_ref, other_ref, all_ref):
         weight = down_ref[...].reshape(here * rank, width)
         lane = lax.broadcasted_iota(jnp.int32, (tile, pair), 1)
         slot = lax.broadcasted_iota(jnp.int32, (tile, pair), 0)
         mine = slot % (HERE * MAIN) // MAIN
+        parts = []
         for first in range(0, half, tile):
             lo = fold(contract_last(in_ref[first : first + tile, :], weight), mine, rank)
             hi = fold(
                 contract_last(in_ref[half + first : half + first + tile, :], weight), mine, rank
             )
-            out_ref[first : first + tile, :] = jnp.where(lane < rank, lo, hi).astype(jnp.bfloat16)
-        out_ref[half:, :] = thirds_ref[...]
-
-    return pl.pallas_call(
-        kernel,
-        out_shape=jax.ShapeDtypeStruct((half + thirds.shape[0], pair), jnp.bfloat16),
+            parts.append(jnp.where(lane < rank, lo, hi).astype(jnp.bfloat16))
+        rows = jnp.concatenate([*parts, thirds_ref[...]], axis=0)
+        for k in range(2):
+            all_ref[k] = rows[k * share : (k + 1) * share]
+        own_ref[...] = all_ref[at_ref[0]]
+        other_ref[...] = all_ref[1 - at_ref[0]]
+
+    return pl.pallas_call(
+        kernel,
+        in_specs=[scalar_spec()] + [pl.BlockSpec(memory_space=pltpu.VMEM)] * 3,
+        out_shape=[jax.ShapeDtypeStruct((share, pair), jnp.bfloat16)] * 2,
+        scratch_shapes=[pltpu.VMEM((2, share, pair), jnp.bfloat16)],
         compiler_params=GRANT,
         name="down_main",
-    )(arrived, thirds, down)
+    )(at, arrived, thirds, down)
 
 
 def up_main(low, flag, up):
@@ -533,6 +541,15 @@
     return swap(copies, TENSOR).reshape(rows, pair)
 
 
+def low_of_pairs(own, other):
+    rounded = own.astype(jnp.float32)
+    rounded = rounded + lax.ppermute(other, TENSOR[1], [(0, 1), (1, 0)]).astype(jnp.float32)
+    chips = lax.axis_size(TENSOR[0])
+    copies = jnp.broadcast_to(rounded.astype(jnp.bfloat16)[None], (chips, *own.shape))
+    total = swap(copies, TENSOR[0]).astype(jnp.float32).sum(axis=0).astype(jnp.bfloat16)
+    return lax.all_gather(total, TENSOR[1], axis=0, tiled=True)
+
+
 def whole_exchange(tokens, adapter_down, adapter_up_weight, adapter_ids, base):
     rows, width = tokens.shape
     cols = adapter_up_weight.shape[2]
@@ -570,13 +587,17 @@
     pairs = xor_sends([own, *pairs], TENSOR[0])[1:]
     base = base_sum(own, other, pairs)
 
-    low = low_of_all(down_main(arrived, thirds, adapter_down), groups)
+    core = lax.axis_index(TENSOR[1]).astype(jnp.int32).reshape(1)
+    low = low_of_pairs(*down_main(core, arrived, thirds, adapter_down))
     delta = up_main(low, flag, adapter_up_weight)
     back = swap(delta.reshape(64, HERE * MOST, cols), ADAPTER).reshape(64 * HERE * MOST, cols)
+    back, *whole = lax.optimization_barrier(
+        (back, tokens, adapter_down, adapter_up_weight, adapter_ids, base)
+    )
     values, lost = take_main(at_col, back, base)
     return lax.cond(
         lost[0] > 0,
-        lambda: whole_exchange(tokens, adapter_down, adapter_up_weight, adapter_ids, base),
+        lambda: whole_exchange(*whole),
         lambda: values,
     )
 

time: 160 us -> 158 us (0.988)
  blocking collectives: 10.6 us -> 2.23 us
  starting transfers between devices: 105 us -> 108 us
  local copies, waits for them, and re-layouts: 2.31 us -> 4.42 us
    all_to_all x1 -> x0, blocking collectives: 10.6 us -> none  [swap(): return lax.all_to_all(x, axes, split_axis=0, concat_axis=0, tiled=True)]
    ppermute x0 -> x1, starting transfers between devices: none -> 8.1 us  [low_of_pairs(): lax.ppermute(other, TENSOR[1], [(0, 1), (1, 0)]).astype(jnp.float32)]
    all_to_all x4, starting transfers between devices: 42.9 us -> 37.2 us  [swap(): return lax.all_to_all(x, axes, split_axis=0, concat_axis=0, tiled=True)]
    all_gather x0 -> x1, blocking collectives: none -> 2.23 us  [low_of_pairs(): return lax.all_gather(total, TENSOR[1], axis=0, tiled=True)]
    all_to_all x4, waiting for transfers between devices: 6.05 us -> 4.33 us  [swap(): return lax.all_to_all(x, axes, split_axis=0, concat_axis=0, tiled=True)]
    ppermute x10, waiting for transfers between devices: 13 us -> 14.7 us  [xor_sends(): lax.ppermute(pieces[k], axis, [(i, i ^ k) for i in range(size)])]
  transfers between devices with their start and end apart: 15 -> 16, of which waited for: 6 -> 6; matrix products, arithmetic and copies ran while one was open for 0% -> 0% of each run, Pallas kernels for 7% -> 8%
where the time goes in v7:
time: 158 us; the launch traced here: 157 us
  starting transfers between devices  108 us (68%)
  Pallas kernels  21.2 us (13%)
  waiting for transfers between devices  19.9 us (13%)
  local copies, waits for them, and re-layouts  4.42 us (3%)
  blocking collectives  2.23 us (1%)
    ppermute x10, starting transfers between devices, xor_sends(): lax.ppermute(pieces[k], axis, [(i, i ^ k) for i in range(size)])  60.6 us
    all_to_all x4, starting transfers between devices, swap(): return lax.all_to_all(x, axes, split_axis=0, concat_axis=0, tiled=True)  37.2 us
    ppermute x10, waiting for transfers between devices, xor_sends(): lax.ppermute(pieces[k], axis, [(i, i ^ k) for i in range(size)])  14.7 us
    ppermute x1, starting transfers between devices, low_of_pairs(): lax.ppermute(other, TENSOR[1], [(0, 1), (1, 0)]).astype(jnp.float32)  8.1 us
    all_to_all x4, waiting for transfers between devices, swap(): return lax.all_to_all(x, axes, split_axis=0, concat_axis=0, tiled=True)  4.33 us
    pallas_call x1, Pallas kernels, value_pieces(): pl.pallas_call(kernel, in_specs=[pl.BlockSpec(memory_space=pltpu.SMEM), p...  4.24 us
    pallas_call x1, Pallas kernels, place_main(): pl.pallas_call(kernel, grid=(slots // tile,), in_specs=[pl.BlockSpec((1,...  3.75 us
    unnamed x12, local copies, waits for them, and re-layouts  3.62 us
  transfers between devices with their start and end apart: 16, of which 6 were waited for; matrix products, arithmetic and copies ran while one was open for 0% of the time, Pallas kernels for 8%

profile of v7, /device:TPU:1, one launch (start us, length us, event | category | flops | bytes accessed | tf_op | source)
XLA Modules:
  0.0 157.4 jit_solution(7623684618444661031)
XLA Ops:
  0.0 0.0 copy-start.5
  0.0 3.3 %side_first.1 = (bf16[128,1024]{1,0:T(8,128)(2,1)}, s32[1,768]{1,0:T(1,128)S(1)}, s32[768,1]{1,0:T(8,128)S(1)}) custom-call(s32[1,768]{1,0:T(1,128)} %bitcast.29, bf16[768,1024]{1,0:T(8,128)(2,1)} %tok_ref.5), custom_call_target="tpu_custom_call" | custom-call | tf_op jit(solution)/shard_map/side_first/pallas_call | solution.py:346
  3.3 7.6 %all-to-all-start.5 = ((bf16[8,16,1024]{2,1,0:T(8,128)(2,1)}), bf16[8,16,1024]{2,1,0:T(8,128)(2,1)S(1)}, u32[]{:S(2)}, u32[]{:S(2)}) async-start(bf16[8,16,1024]{2,1,0:T(8,128)(2,1)} %bitcast.12), calls=%async_computation.5 | async-start | bytes 524288 | tf_op jit(solution)/shard_map/all_to_all | solution.py:23
  10.9 0.0 copy-done.5
  10.9 3.8 %place_main.1 = bf16[1024,1024]{1,0:T(8,128)(2,1)S(1)} custom-call(s32[1,768]{1,0:T(1,128)S(1)} %bitcast.30, s32[1,768]{1,0:T(1,128)S(1)} %get-tuple-element.55.seen_ref, bf16[768,1024]{1,0:T(8,128)(2,1)} %tok_ref.5), custom_call_target="tpu_custom_call" | custom-call | tf_op jit(solution)/shard_map/place_main/pallas_call | solution.py:265
  14.7 0.0 copy-start
  14.7 1.3 copy-done
  16.0 4.3 %all-to-all-done.5 = bf16[8,16,1024]{2,1,0:T(8,128)(2,1)S(1)} async-done(((bf16[8,16,1024]{2,1,0:T(8,128)(2,1)}), bf16[8,16,1024]{2,1,0:T(8,128)(2,1)S(1)}, u32[]{:S(2)}, u32[]{:S(2)}) %all-to-all-start.5) | async-done | bytes 262176 | tf_op jit(solution)/shard_map/all_to_all | solution.py:23
  20.3 13.2 %all-to-all-start.4 = ((bf16[64,16,1024]{2,1,0:T(8,128)(2,1)}), bf16[64,16,1024]{2,1,0:T(8,128)(2,1)S(1)}, u32[]{:S(2)}, u32[]{:S(2)}) async-start(bf16[64,16,1024]{2,1,0:T(8,128)(2,1)} %bitcast.21), calls=%async_computation.4 | async-start | bytes 4194304 | tf_op jit(solution)/shard_map/all_to_all | solution.py:23
  33.6 0.5 side_second.1
  34.1 2.9 %collective-permute-start = (bf16[16,1024]{1,0:T(8,128)(2,1)S(1)}, bf16[16,1024]{1,0:T(8,128)(2,1)S(1)}, u32[]{:S(2)}, u32[]{:S(2)}) collective-permute-start(bf16[16,1024]{1,0:T(8,128)(2,1)S(1)} %get-tuple-element.58), channel_id=1, source_target_pairs={{0,64},{64,0},{128,192},{192,128},{256,320},{320,256},{384,448},{4... | collective-permute-start | bytes 98312 | tf_op jit(solution)/shard_map/ppermute | solution.py:609
  37.0 4.0 %collective-permute-start.1 = (bf16[16,1024]{1,0:T(8,128)(2,1)S(1)}, bf16[16,1024]{1,0:T(8,128)(2,1)S(1)}, u32[]{:S(2)}, u32[]{:S(2)}) collective-permute-start(bf16[16,1024]{1,0:T(8,128)(2,1)S(1)} %get-tuple-element.59), channel_id=1, source_target_pairs={{0,128},{64,192},{128,0},{192,64},{256,384},{320,448},{384,256},{4... | collective-permute-start | bytes 98312 | tf_op jit(solution)/shard_map/ppermute | solution.py:609
  41.1 2.3 %collective-permute-start.2 = (bf16[16,1024]{1,0:T(8,128)(2,1)S(1)}, bf16[16,1024]{1,0:T(8,128)(2,1)S(1)}, u32[]{:S(2)}, u32[]{:S(2)}) collective-permute-start(bf16[16,1024]{1,0:T(8,128)(2,1)S(1)} %get-tuple-element.60), channel_id=1, source_target_pairs={{0,192},{64,128},{128,64},{192,0},{256,448},{320,384},{384,320},{4... | collective-permute-start | bytes 98312 | tf_op jit(solution)/shard_map/ppermute | solution.py:609
  43.4 6.9 %collective-permute-start.3 = (bf16[16,1024]{1,0:T(8,128)(2,1)S(1)}, bf16[16,1024]{1,0:T(8,128)(2,1)S(1)}, u32[]{:S(2)}, u32[]{:S(2)}) collective-permute-start(bf16[16,1024]{1,0:T(8,128)(2,1)S(1)} %get-tuple-element.61), channel_id=1, source_target_pairs={{0,256},{64,320},{128,384},{192,448},{256,0},{320,64},{384,128},{4... | collective-permute-start | bytes 98312 | tf_op jit(solution)/shard_map/ppermute | solution.py:609
  50.3 1.9 %collective-permute-start.4 = (bf16[16,1024]{1,0:T(8,128)(2,1)S(1)}, bf16[16,1024]{1,0:T(8,128)(2,1)S(1)}, u32[]{:S(2)}, u32[]{:S(2)}) collective-permute-start(bf16[16,1024]{1,0:T(8,128)(2,1)S(1)} %get-tuple-element.62), channel_id=1, source_target_pairs={{0,320},{64,256},{128,448},{192,384},{256,64},{320,0},{384,192},{4... | collective-permute-start | bytes 98312 | tf_op jit(solution)/shard_map/ppermute | solution.py:609
  52.3 0.0 collective-permute-done.refs_1_
  52.3 30.4 %collective-permute-start.5 = (bf16[16,1024]{1,0:T(8,128)(2,1)S(1)}, bf16[16,1024]{1,0:T(8,128)(2,1)S(1)}, u32[]{:S(2)}, u32[]{:S(2)}) collective-permute-start(bf16[16,1024]{1,0:T(8,128)(2,1)S(1)} %get-tuple-element.63), channel_id=1, source_target_pairs={{0,384},{64,448},{128,256},{192,320},{256,128},{320,192},{384,0},{... | collective-permute-start | bytes 98312 | tf_op jit(solution)/shard_map/ppermute | solution.py:609
  82.6 0.0 collective-permute-done.1.refs_2_
  82.7 2.1 %collective-permute-start.6 = (bf16[16,1024]{1,0:T(8,128)(2,1)S(1)}, bf16[16,1024]{1,0:T(8,128)(2,1)S(1)}, u32[]{:S(2)}, u32[]{:S(2)}) collective-permute-start(bf16[16,1024]{1,0:T(8,128)(2,1)S(1)} %get-tuple-element.64), channel_id=1, source_target_pairs={{0,448},{64,384},{128,320},{192,256},{256,192},{320,128},{384,64},... | collective-permute-start | bytes 98312 | tf_op jit(solution)/shard_map/ppermute | solution.py:609
  84.8 1.1 collective-permute-done.2.refs_3_
  85.8 0.0 collective-permute-done.3.refs_4_
  85.8 3.7 %collective-permute-done.4.refs_5_ = bf16[16,1024]{1,0:T(8,128)(2,1)S(1)} collective-permute-done((bf16[16,1024]{1,0:T(8,128)(2,1)S(1)}, bf16[16,1024]{1,0:T(8,128)(2,1)S(1)}, u32[]{:S(2)}, u32[]{:S(2)}) %collective-permute-start.4) | collective-permute-done | bytes 32800 | tf_op jit(solution)/shard_map/ppermute | solution.py:609
  89.6 0.0 collective-permute-done.5.refs_6_
  89.6 0.0 collective-permute-done.6.refs_7_
  89.6 1.9 %side_low.1 = (bf16[256,128]{1,0:T(8,128)(2,1)S(1)}, f32[8,128]{1,0:T(8,128)S(1)}) custom-call(s32[1]{0:T(128)} %bitcast.11.at_ref, bf16[16,1024]{1,0:T(8,128)(2,1)S(1)} %get-tuple-element.57.refs_0_, bf16[16,1024]{1,0:T(8,128)(2,1)S(1)} %collective-permute-done.refs_1_, bf16[16,1024]{1,0:T(8,128)(2,1)S(1)} %collective-permute-done.1.refs_2_, ...), custom_call_target="tpu_custom_call" | custom-call | tf_op jit(solution)/shard_map/side_low/pallas_call | solution.py:423
  91.5 0.0 all-to-all-done.4
  91.5 2.6 %down_main.1 = (bf16[384,128]{1,0:T(8,128)(2,1)S(1)}, bf16[384,128]{1,0:T(8,128)(2,1)S(1)}) custom-call(s32[1]{0:T(128)} %bitcast.8.at_ref, bf16[1024,1024]{1,0:T(8,128)(2,1)S(1)} %bitcast.20, bf16[256,128]{1,0:T(8,128)(2,1)S(1)} %get-tuple-element.65.thirds_ref, bf16[8,64,1024]{2,1,0:T(8,128)(2,1)} %down_ref.1), custom_call_target="tpu_custom_call" | custom-call | tf_op jit(solution)/shard_map/down_main/pallas_call | solution.py:461
  94.2 8.1 %collective-permute-start.7 = (bf16[384,128]{1,0:T(8,128)(2,1)S(1)}, bf16[384,128]{1,0:T(8,128)(2,1)S(1)}, u32[]{:S(2)}, u32[]{:S(2)}) collective-permute-start(bf16[384,128]{1,0:T(8,128)(2,1)S(1)} %get-tuple-element.67), channel_id=1, source_target_pairs={{0,1},{1,0},{2,3},{3,2},{4,5},{5,4},{6,7},{7,6},{8,9},{9,8},{10,11... | collective-permute-start | bytes 294920 | tf_op jit(solution)/shard_map/ppermute | solution.py:546
  102.3 0.9 collective-permute-done.7
  103.2 0.8 broadcast_in_dim.4
  104.0 3.9 %all-to-all-start.6 = ((bf16[4,384,128]{2,1,0:T(8,128)(2,1)}), bf16[4,384,128]{2,1,0:T(8,128)(2,1)S(1)}, u32[]{:S(2)}, u32[]{:S(2)}) async-start(bf16[4,384,128]{2,1,0:T(8,128)(2,1)} %broadcast_in_dim.4), calls=%async_computation.6 | async-start | bytes 786432 | tf_op jit(solution)/shard_map/all_to_all | solution.py:23
  108.0 0.0 copy-start.1
  108.0 1.6 %copy-done.1 = bf16[1024,1024]{1,0:T(8,128)(2,1)S(1)} copy-done((bf16[1024,1024]{1,0:T(8,128)(2,1)S(1)}, bf16[1024,1024]{1,0:T(8,128)(2,1)}, u32[]{:S(2)}) %copy-start.1) | copy-done | bytes 2097176
  109.6 0.0 copy-start.4
  109.6 4.2 %value_pieces.1 = (bf16[4,768,128]{2,1,0:T(8,128)(2,1)S(1)}, bf16[4,768,128]{2,1,0:T(8,128)(2,1)}) custom-call(s32[1]{0:T(128)} %bitcast.16.at_ref, bf16[768,1024]{1,0:T(8,128)(2,1)} %tok_ref.5, bf16[1024,1024]{1,0:T(8,128)(2,1)S(1)} %copy-done.1), custom_call_target="tpu_custom_call" | custom-call | tf_op jit(solution)/shard_map/value_pieces/pallas_call | solution.py:89
  113.8 2.5 %collective-permute-start.8 = (bf16[4,768,128]{2,1,0:T(8,128)(2,1)}, bf16[4,768,128]{2,1,0:T(8,128)(2,1)S(1)}, u32[]{:S(2)}, u32[]{:S(2)}) collective-permute-start(bf16[4,768,128]{2,1,0:T(8,128)(2,1)} %get-tuple-element.70), channel_id=1, source_target_pairs={{0,1},{1,0},{2,3},{3,2},{4,5},{5,4},{6,7},{7,6},{8,9},{9,8},{10,11... | collective-permute-start | bytes 2359304 | tf_op jit(solution)/shard_map/ppermute | solution.py:585
  116.3 0.0 all-to-all-done.6
  116.4 0.1 reduce_sum.24
  116.4 2.2 %all_gather.3.low_ref = bf16[768,128]{1,0:T(8,128)(2,1)S(1)} all-gather(bf16[384,128]{1,0:T(8,128)(2,1)S(1)} %reduce_sum.24), channel_id=1, replica_groups=mesh['z'=8,'y'=8,'tensor_0'=4,'tensor_1'=2] {'tensor_1'}, dimensions={0}, use_global_device_ids=true | all-gather | bytes 294912 | tf_op jit(solution)/shard_map/all_gather | solution.py:550
  118.7 0.0 copy-done.4
  118.7 1.4 up_main.1
  120.0 12.4 %all-to-all-start.7 = ((bf16[64,24,128]{2,1,0:T(8,128)(2,1)}), bf16[64,24,128]{2,1,0:T(8,128)(2,1)S(1)}, u32[]{:S(2)}, u32[]{:S(2)}) async-start(bf16[64,24,128]{2,1,0:T(8,128)(2,1)} %bitcast.14), calls=%async_computation.7 | async-start | bytes 786432 | tf_op jit(solution)/shard_map/all_to_all | solution.py:23
  132.4 0.0 collective-permute-done.8.other_ref
  132.4 0.1 pair_sum.1
  132.6 0.0 copy-start.2
  132.6 3.7 %collective-permute-start.9 = (bf16[768,128]{1,0:T(8,128)(2,1)S(1)}, bf16[768,128]{1,0:T(8,128)(2,1)S(1)}, u32[]{:S(2)}, u32[]{:S(2)}) collective-permute-start(bf16[768,128]{1,0:T(8,128)(2,1)S(1)} %get-tuple-element.71), channel_id=1, source_target_pairs={{0,2},{2,0},{4,6},{6,4},{1,3},{3,1},{5,7},{7,5},{8,10},{10,8},{12,... | collective-permute-start | bytes 589832 | tf_op jit(solution)/shard_map/ppermute | solution.py:609
  136.3 4.3 %collective-permute-start.10 = (bf16[768,128]{1,0:T(8,128)(2,1)S(1)}, bf16[768,128]{1,0:T(8,128)(2,1)S(1)}, u32[]{:S(2)}, u32[]{:S(2)}) collective-permute-start(bf16[768,128]{1,0:T(8,128)(2,1)S(1)} %get-tuple-element.72), channel_id=1, source_target_pairs={{0,4},{2,6},{4,0},{6,2},{1,5},{3,7},{5,1},{7,3},{8,12},{10,14},{12... | collective-permute-start | bytes 589832 | tf_op jit(solution)/shard_map/ppermute | solution.py:609
  140.6 1.9 %collective-permute-start.11 = (bf16[768,128]{1,0:T(8,128)(2,1)S(1)}, bf16[768,128]{1,0:T(8,128)(2,1)S(1)}, u32[]{:S(2)}, u32[]{:S(2)}) collective-permute-start(bf16[768,128]{1,0:T(8,128)(2,1)S(1)} %get-tuple-element.73), channel_id=1, source_target_pairs={{0,6},{2,4},{4,2},{6,0},{1,7},{3,5},{5,3},{7,1},{8,14},{10,12},{12... | collective-permute-start | bytes 589832 | tf_op jit(solution)/shard_map/ppermute | solution.py:609
  142.5 0.0 collective-permute-done.9.refs_0_
  142.5 4.7 %collective-permute-done.10.refs_1_ = bf16[768,128]{1,0:T(8,128)(2,1)S(1)} collective-permute-done((bf16[768,128]{1,0:T(8,128)(2,1)S(1)}, bf16[768,128]{1,0:T(8,128)(2,1)S(1)}, u32[]{:S(2)}, u32[]{:S(2)}) %collective-permute-start.10) | collective-permute-done | bytes 196640 | tf_op jit(solution)/shard_map/ppermute | solution.py:609
  147.2 5.2 %collective-permute-done.11.refs_2_ = bf16[768,128]{1,0:T(8,128)(2,1)S(1)} collective-permute-done((bf16[768,128]{1,0:T(8,128)(2,1)S(1)}, bf16[768,128]{1,0:T(8,128)(2,1)S(1)}, u32[]{:S(2)}, u32[]{:S(2)}) %collective-permute-start.11) | collective-permute-done | bytes 196640 | tf_op jit(solution)/shard_map/ppermute | solution.py:609
  152.5 0.9 base_sum.1.base_ref
  153.3 0.0 all-to-all-done.7
  153.3 2.5 %take_main.1 = (bf16[768,128]{1,0:T(8,128)(2,1)S(1)}, s32[1]{0:T(128)}) custom-call(s32[768,1]{1,0:T(8,128)S(1)} %get-tuple-element.54.at_ref, bf16[1536,128]{1,0:T(8,128)(2,1)S(1)} %bitcast.23, f32[768,128]{1,0:T(8,128)} %base_sum.1.base_ref), custom_call_target="tpu_custom_call" | custom-call | tf_op jit(solution)/shard_map/take_main/pallas_call | solution.py:524
  156.5 0.0 copy-done.2
  156.5 0.2 conditional.1
  156.7 0.0 copy-start.6
  156.7 0.7 copy-done.6
  (1 shorter events, 0.0 us)
Async XLA Ops:
  0.0 10.9 %copy-start.5 = (s32[768,1]{0,1:T(1,128)S(1)}, s32[768,1]{0,1:T(1,128)}, u32[]{:S(2)}) copy-start(s32[768,1]{0,1:T(1,128)} %param.11) | copy-start | bytes 9220
  3.3 17.1 %all-to-all-start.5 = ((bf16[8,16,1024]{2,1,0:T(8,128)(2,1)}), bf16[8,16,1024]{2,1,0:T(8,128)(2,1)S(1)}, u32[]{:S(2)}, u32[]{:S(2)}) async-start(bf16[8,16,1024]{2,1,0:T(8,128)(2,1)} %bitcast.12), calls=%async_computation.5 | async-start | bytes 524288 | tf_op jit(solution)/shard_map/all_to_all | solution.py:23
  14.7 1.3 copy-start
  20.3 71.2 %all-to-all-start.4 = ((bf16[64,16,1024]{2,1,0:T(8,128)(2,1)}), bf16[64,16,1024]{2,1,0:T(8,128)(2,1)S(1)}, u32[]{:S(2)}, u32[]{:S(2)}) async-start(bf16[64,16,1024]{2,1,0:T(8,128)(2,1)} %bitcast.21), calls=%async_computation.4 | async-start | bytes 4194304 | tf_op jit(solution)/shard_map/all_to_all | solution.py:23
  34.1 18.2 %collective-permute-start = (bf16[16,1024]{1,0:T(8,128)(2,1)S(1)}, bf16[16,1024]{1,0:T(8,128)(2,1)S(1)}, u32[]{:S(2)}, u32[]{:S(2)}) collective-permute-start(bf16[16,1024]{1,0:T(8,128)(2,1)S(1)} %get-tuple-element.58), channel_id=1, source_target_pairs={{0,64},{64,0},{128,192},{192,128},{256,320},{320,256},{384,448},{4... | collective-permute-start | bytes 98312 | tf_op jit(solution)/shard_map/ppermute | solution.py:609
  37.0 45.6 %collective-permute-start.1 = (bf16[16,1024]{1,0:T(8,128)(2,1)S(1)}, bf16[16,1024]{1,0:T(8,128)(2,1)S(1)}, u32[]{:S(2)}, u32[]{:S(2)}) collective-permute-start(bf16[16,1024]{1,0:T(8,128)(2,1)S(1)} %get-tuple-element.59), channel_id=1, source_target_pairs={{0,128},{64,192},{128,0},{192,64},{256,384},{320,448},{384,256},{4... | collective-permute-start | bytes 98312 | tf_op jit(solution)/shard_map/ppermute | solution.py:609
  41.1 44.8 %collective-permute-start.2 = (bf16[16,1024]{1,0:T(8,128)(2,1)S(1)}, bf16[16,1024]{1,0:T(8,128)(2,1)S(1)}, u32[]{:S(2)}, u32[]{:S(2)}) collective-permute-start(bf16[16,1024]{1,0:T(8,128)(2,1)S(1)} %get-tuple-element.60), channel_id=1, source_target_pairs={{0,192},{64,128},{128,64},{192,0},{256,448},{320,384},{384,320},{4... | collective-permute-start | bytes 98312 | tf_op jit(solution)/shard_map/ppermute | solution.py:609
  43.4 42.5 %collective-permute-start.3 = (bf16[16,1024]{1,0:T(8,128)(2,1)S(1)}, bf16[16,1024]{1,0:T(8,128)(2,1)S(1)}, u32[]{:S(2)}, u32[]{:S(2)}) collective-permute-start(bf16[16,1024]{1,0:T(8,128)(2,1)S(1)} %get-tuple-element.61), channel_id=1, source_target_pairs={{0,256},{64,320},{128,384},{192,448},{256,0},{320,64},{384,128},{4... | collective-permute-start | bytes 98312 | tf_op jit(solution)/shard_map/ppermute | solution.py:609
  50.3 39.2 %collective-permute-start.4 = (bf16[16,1024]{1,0:T(8,128)(2,1)S(1)}, bf16[16,1024]{1,0:T(8,128)(2,1)S(1)}, u32[]{:S(2)}, u32[]{:S(2)}) collective-permute-start(bf16[16,1024]{1,0:T(8,128)(2,1)S(1)} %get-tuple-element.62), channel_id=1, source_target_pairs={{0,320},{64,256},{128,448},{192,384},{256,64},{320,0},{384,192},{4... | collective-permute-start | bytes 98312 | tf_op jit(solution)/shard_map/ppermute | solution.py:609
  52.3 37.3 %collective-permute-start.5 = (bf16[16,1024]{1,0:T(8,128)(2,1)S(1)}, bf16[16,1024]{1,0:T(8,128)(2,1)S(1)}, u32[]{:S(2)}, u32[]{:S(2)}) collective-permute-start(bf16[16,1024]{1,0:T(8,128)(2,1)S(1)} %get-tuple-element.63), channel_id=1, source_target_pairs={{0,384},{64,448},{128,256},{192,320},{256,128},{320,192},{384,0},{... | collective-permute-start | bytes 98312 | tf_op jit(solution)/shard_map/ppermute | solution.py:609
  82.7 6.9 %collective-permute-start.6 = (bf16[16,1024]{1,0:T(8,128)(2,1)S(1)}, bf16[16,1024]{1,0:T(8,128)(2,1)S(1)}, u32[]{:S(2)}, u32[]{:S(2)}) collective-permute-start(bf16[16,1024]{1,0:T(8,128)(2,1)S(1)} %get-tuple-element.64), channel_id=1, source_target_pairs={{0,448},{64,384},{128,320},{192,256},{256,192},{320,128},{384,64},... | collective-permute-start | bytes 98312 | tf_op jit(solution)/shard_map/ppermute | solution.py:609
  94.2 9.0 %collective-permute-start.7 = (bf16[384,128]{1,0:T(8,128)(2,1)S(1)}, bf16[384,128]{1,0:T(8,128)(2,1)S(1)}, u32[]{:S(2)}, u32[]{:S(2)}) collective-permute-start(bf16[384,128]{1,0:T(8,128)(2,1)S(1)} %get-tuple-element.67), channel_id=1, source_target_pairs={{0,1},{1,0},{2,3},{3,2},{4,5},{5,4},{6,7},{7,6},{8,9},{9,8},{10,11... | collective-permute-start | bytes 294920 | tf_op jit(solution)/shard_map/ppermute | solution.py:546
  104.0 12.3 %all-to-all-start.6 = ((bf16[4,384,128]{2,1,0:T(8,128)(2,1)}), bf16[4,384,128]{2,1,0:T(8,128)(2,1)S(1)}, u32[]{:S(2)}, u32[]{:S(2)}) async-start(bf16[4,384,128]{2,1,0:T(8,128)(2,1)} %broadcast_in_dim.4), calls=%async_computation.6 | async-start | bytes 786432 | tf_op jit(solution)/shard_map/all_to_all | solution.py:23
  108.0 1.6 %copy-start.1 = (bf16[1024,1024]{1,0:T(8,128)(2,1)S(1)}, bf16[1024,1024]{1,0:T(8,128)(2,1)}, u32[]{:S(2)}) copy-start(bf16[1024,1024]{1,0:T(8,128)(2,1)} %w_ref.1) | copy-start | bytes 6291460
  109.6 9.1 %copy-start.4 = (bf16[8,64,128]{2,1,0:T(8,128)(2,1)S(1)}, bf16[8,64,128]{2,1,0:T(8,128)(2,1)}, u32[]{:S(2)}) copy-start(bf16[8,64,128]{2,1,0:T(8,128)(2,1)} %up_ref.1) | copy-start | bytes 393220
  113.8 18.6 %collective-permute-start.8 = (bf16[4,768,128]{2,1,0:T(8,128)(2,1)}, bf16[4,768,128]{2,1,0:T(8,128)(2,1)S(1)}, u32[]{:S(2)}, u32[]{:S(2)}) collective-permute-start(bf16[4,768,128]{2,1,0:T(8,128)(2,1)} %get-tuple-element.70), channel_id=1, source_target_pairs={{0,1},{1,0},{2,3},{3,2},{4,5},{5,4},{6,7},{7,6},{8,9},{9,8},{10,11... | collective-permute-start | bytes 2359304 | tf_op jit(solution)/shard_map/ppermute | solution.py:585
  120.0 33.3 %all-to-all-start.7 = ((bf16[64,24,128]{2,1,0:T(8,128)(2,1)}), bf16[64,24,128]{2,1,0:T(8,128)(2,1)S(1)}, u32[]{:S(2)}, u32[]{:S(2)}) async-start(bf16[64,24,128]{2,1,0:T(8,128)(2,1)} %bitcast.14), calls=%async_computation.7 | async-start | bytes 786432 | tf_op jit(solution)/shard_map/all_to_all | solution.py:23
  132.6 23.9 %copy-start.2 = (bf16[8,64,1024]{2,1,0:T(8,128)(2,1)S(1)}, bf16[8,64,1024]{2,1,0:T(8,128)(2,1)}, u32[]{:S(2)}) copy-start(bf16[8,64,1024]{2,1,0:T(8,128)(2,1)} %down_ref.1) | copy-start | bytes 3145732
  132.6 10.0 %collective-permute-start.9 = (bf16[768,128]{1,0:T(8,128)(2,1)S(1)}, bf16[768,128]{1,0:T(8,128)(2,1)S(1)}, u32[]{:S(2)}, u32[]{:S(2)}) collective-permute-start(bf16[768,128]{1,0:T(8,128)(2,1)S(1)} %get-tuple-element.71), channel_id=1, source_target_pairs={{0,2},{2,0},{4,6},{6,4},{1,3},{3,1},{5,7},{7,5},{8,10},{10,8},{12,... | collective-permute-start | bytes 589832 | tf_op jit(solution)/shard_map/ppermute | solution.py:609
  136.3 10.9 %collective-permute-start.10 = (bf16[768,128]{1,0:T(8,128)(2,1)S(1)}, bf16[768,128]{1,0:T(8,128)(2,1)S(1)}, u32[]{:S(2)}, u32[]{:S(2)}) collective-permute-start(bf16[768,128]{1,0:T(8,128)(2,1)S(1)} %get-tuple-element.72), channel_id=1, source_target_pairs={{0,4},{2,6},{4,0},{6,2},{1,5},{3,7},{5,1},{7,3},{8,12},{10,14},{12... | collective-permute-start | bytes 589832 | tf_op jit(solution)/shard_map/ppermute | solution.py:609
  140.6 11.8 %collective-permute-start.11 = (bf16[768,128]{1,0:T(8,128)(2,1)S(1)}, bf16[768,128]{1,0:T(8,128)(2,1)S(1)}, u32[]{:S(2)}, u32[]{:S(2)}) collective-permute-start(bf16[768,128]{1,0:T(8,128)(2,1)S(1)} %get-tuple-element.73), channel_id=1, source_target_pairs={{0,6},{2,4},{4,2},{6,0},{1,7},{3,5},{5,3},{7,1},{8,14},{10,12},{12... | collective-permute-start | bytes 589832 | tf_op jit(solution)/shard_map/ppermute | solution.py:609
  156.7 0.7 copy-start.6

commit v8 on v6

--- a/solution.py
+++ b/solution.py
@@ -397,49 +397,14 @@
     return lax.dot_general(x, y, (((1,), (1,)), ((), ())), preferred_element_type=jnp.float32)
 
 
-def side_low(at, blocks, down):
-    here, rank, width = down.shape
-    n = 8 * SIDE
-    thirds = 64 * here
-    pair = 2 * rank
-
-    def kernel(at_ref, *refs):
-        down_ref, out_ref, flag_ref = refs[8:]
-        blocks = [ref[...] for ref in refs[:8]]
-        code, flag = read_codes(blocks)
-        from_z = (lax.broadcasted_iota(jnp.int32, (1, n), 1) // SIDE) ^ at_ref[0]
-        slot = jnp.where(code >= 0, from_z * 64 + code, -1)
-        rows_of = jnp.concatenate(blocks, axis=0)
-        full = contract_last(rows_of, down_ref[...].reshape(here * rank, width))
-        mine = to_col(jnp.where(code >= 0, code % 8, -1))
-        low = fold(full, mine, rank).astype(jnp.bfloat16)
-        spread = jnp.dot(pick_rows(slot, thirds), low, preferred_element_type=jnp.float32)
-        lane = lax.broadcasted_iota(jnp.int32, (thirds // 2, pair), 1)
-        out_ref[...] = jnp.where(
-            lane < rank, spread[: thirds // 2], spread[thirds // 2 :]
-        ).astype(jnp.bfloat16)
-        flag_ref[...] = jnp.broadcast_to(flag, (8, 128))
-
-    return pl.pallas_call(
-        kernel,
-        in_specs=[scalar_spec()] + [pl.BlockSpec(memory_space=pltpu.VMEM)] * 9,
-        out_shape=[
-            jax.ShapeDtypeStruct((thirds // 2, pair), jnp.bfloat16),
-            jax.ShapeDtypeStruct((8, 128), jnp.float32),
-        ],
-        compiler_params=GRANT,
-        name="side_low",
-    )(at, *blocks, down)
-
-
-def down_main(arrived, thirds, down):
+def down_main(arrived, down):
     slots, width = arrived.shape
     here, rank, _ = down.shape
     half = slots // 2
     tile = 256
     pair = 2 * rank
 
-    def kernel(in_ref, thirds_ref, down_ref, out_ref):
+    def kernel(in_ref, down_ref, out_ref):
         weight = down_ref[...].reshape(here * rank, width)
         lane = lax.broadcasted_iota(jnp.int32, (tile, pair), 1)
         slot = lax.broadcasted_iota(jnp.int32, (tile, pair), 0)
@@ -450,32 +415,85 @@
                 contract_last(in_ref[half + first : half + first + tile, :], weight), mine, rank
             )
             out_ref[first : first + tile, :] = jnp.where(lane < rank, lo, hi).astype(jnp.bfloat16)
-        out_ref[half:, :] = thirds_ref[...]
-
-    return pl.pallas_call(
-        kernel,
-        out_shape=jax.ShapeDtypeStruct((half + thirds.shape[0], pair), jnp.bfloat16),
+
+    return pl.pallas_call(
+        kernel,
+        out_shape=jax.ShapeDtypeStruct((half, pair), jnp.bfloat16),
         compiler_params=GRANT,
         name="down_main",
-    )(arrived, thirds, down)
-
-
-def up_main(low, flag, up):
+    )(arrived, down)
+
+
+def side_low(at, blocks, down, main):
+    here, rank, width = down.shape
+    n = 8 * SIDE
+    pair = 2 * rank
+    share = (main.shape[0] + n // 2) // 2
+
+    def kernel(at_ref, *refs):
+        down_ref, main_ref, own_ref, other_ref, slot_ref, flag_ref, all_ref = refs[8:]
+        blocks = [ref[...] for ref in refs[:8]]
+        code, flag = read_codes(blocks)
+        from_z = (lax.broadcasted_iota(jnp.int32, (1, n), 1) // SIDE) ^ at_ref[0]
+        slot_ref[...] = jnp.where(code >= 0, from_z * 64 + code, -1)
+        flag_ref[...] = jnp.broadcast_to(flag, (8, 128))
+        rows_of = jnp.concatenate(blocks, axis=0)
+        full = contract_last(rows_of, down_ref[...].reshape(here * rank, width))
+        low = fold(full, to_col(jnp.where(code >= 0, code % HERE, -1)), rank)
+        lane = lax.broadcasted_iota(jnp.int32, (n // 2, pair), 1)
+        packed = jnp.where(lane < rank, low[: n // 2], low[n // 2 :]).astype(jnp.bfloat16)
+        rows = jnp.concatenate([main_ref[...], packed], axis=0)
+        for k in range(2):
+            all_ref[k] = rows[k * share : (k + 1) * share]
+        own_ref[...] = all_ref[at_ref[1]]
+        other_ref[...] = all_ref[1 - at_ref[1]]
+
+    return pl.pallas_call(
+        kernel,
+        in_specs=[scalar_spec()] + [pl.BlockSpec(memory_space=pltpu.VMEM)] * 10,
+        out_shape=[
+            jax.ShapeDtypeStruct((share, pair), jnp.bfloat16),
+            jax.ShapeDtypeStruct((share, pair), jnp.bfloat16),
+            jax.ShapeDtypeStruct((1, n), jnp.int32),
+            jax.ShapeDtypeStruct((8, 128), jnp.float32),
+        ],
+        scratch_shapes=[pltpu.VMEM((2, share, pair), jnp.bfloat16)],
+        compiler_params=GRANT,
+        name="side_low",
+    )(at, *blocks, down, main)
+
+
+def chip_sum(parts):
+    def kernel(in_ref, out_ref):
+        total = in_ref[0].astype(jnp.float32)
+        for k in range(1, parts.shape[0]):
+            total = total + in_ref[k].astype(jnp.float32)
+        out_ref[...] = total.astype(jnp.bfloat16)
+
+    return pl.pallas_call(
+        kernel,
+        out_shape=jax.ShapeDtypeStruct(parts.shape[1:], jnp.bfloat16),
+        compiler_params=GRANT,
+        name="chip_sum",
+    )(parts)
+
+
+def up_main(low, slot, flag, up):
     here, rank, cols = up.shape
-    owners = 2 * low.shape[0] // (here * MOST)
-    half = owners * here * MAIN // 2
-
-    def kernel(low_ref, flag_ref, up_ref, out_ref):
+    pair = 2 * rank
+    n = slot.shape[1]
+    half = low.shape[0] - n // 2
+    owners = 2 * half // (here * MAIN)
+
+    def kernel(low_ref, slot_ref, flag_ref, up_ref, out_ref):
         weight = up_ref[...].reshape(here * rank, cols)
 
-        def mapped(part, per):
+        def mapped(part, holders):
             wide = part.astype(jnp.float32)
             turned = pltpu.roll(wide, rank, 1)
             lane = lax.broadcasted_iota(jnp.int32, wide.shape, 1)
-            slot = lax.broadcasted_iota(jnp.int32, wide.shape, 0)
-            mine = slot % (here * per) // per
             halves = []
-            for h in range(2):
+            for h, mine in enumerate(holders):
                 both = jnp.where((lane < rank) == (h == 0), wide, turned)
                 spread = []
                 for k in range(here // 2):
@@ -486,11 +504,19 @@
                         jnp.concatenate(spread, axis=1), weight, preferred_element_type=jnp.float32
                     )
                 )
-            acc = jnp.concatenate(halves, axis=0) * adapter_output_scale
-            return acc.reshape(owners, here * per, cols)
-
-        main = mapped(low_ref[:half, :], MAIN)
-        thirds = mapped(low_ref[half:, :], MOST - MAIN)
+            return jnp.concatenate(halves, axis=0) * adapter_output_scale
+
+        main_slot = lax.broadcasted_iota(jnp.int32, (half, pair), 0)
+        spot = main_slot % (here * MAIN) // MAIN
+        main = mapped(low_ref[:half, :], (spot, spot)).reshape(owners, here * MAIN, cols)
+        at = slot_ref[...]
+        spot = to_col(jnp.where(at >= 0, at % here, -1))
+        thirds = mapped(low_ref[half:, :], (spot[: n // 2], spot[n // 2 :]))
+        thirds = jnp.dot(
+            pick_rows(at, owners * here),
+            thirds.astype(jnp.bfloat16),
+            preferred_element_type=jnp.float32,
+        ).reshape(owners, here, cols)
         both = jnp.concatenate([main, thirds], axis=1).reshape(owners * here * MOST, cols)
         out_ref[...] = jnp.where(flag_ref[:1, :1] > 0.0, LOST, both).astype(jnp.bfloat16)
 
@@ -499,7 +525,7 @@
         out_shape=jax.ShapeDtypeStruct((owners * here * MOST, cols), jnp.bfloat16),
         compiler_params=GRANT,
         name="up_main",
-    )(low, flag, up)
+    )(low, slot, flag, up)
 
 
 def take_main(at_col, back, base):
@@ -531,6 +557,15 @@
     share = parts.astype(jnp.float32).sum(axis=0).astype(jnp.bfloat16)
     copies = jnp.broadcast_to(share[None], (groups, *share.shape))
     return swap(copies, TENSOR).reshape(rows, pair)
+
+
+def low_of_pairs(own, other):
+    rounded = own.astype(jnp.float32)
+    rounded = rounded + lax.ppermute(other, TENSOR[1], [(0, 1), (1, 0)]).astype(jnp.float32)
+    chips = lax.axis_size(TENSOR[0])
+    copies = jnp.broadcast_to(rounded.astype(jnp.bfloat16)[None], (chips, *own.shape))
+    total = chip_sum(swap(copies, TENSOR[0]))
+    return lax.all_gather(total, TENSOR[1], axis=0, tiled=True)
 
 
 def whole_exchange(tokens, adapter_down, adapter_up_weight, adapter_ids, base):
@@ -561,8 +596,6 @@
 
     blocks = side_second(at_z.reshape(1), blocks)
     blocks = xor_sends(blocks, "z")
-    thirds, flag = side_low(at_z.reshape(1), blocks, adapter_down)
-
     at = lax.axis_index(TENSOR).astype(jnp.int32).reshape(1)
     own, other = value_pieces(tokens, value_weight, at, groups)
     other = lax.ppermute(other, TENSOR[1], [(0, 1), (1, 0)])
@@ -570,13 +603,19 @@
     pairs = xor_sends([own, *pairs], TENSOR[0])[1:]
     base = base_sum(own, other, pairs)
 
-    low = low_of_all(down_main(arrived, thirds, adapter_down), groups)
-    delta = up_main(low, flag, adapter_up_weight)
+    main = down_main(arrived, adapter_down)
+    core = lax.axis_index(TENSOR[1]).astype(jnp.int32)
+    own, other, slot, flag = side_low(jnp.stack([at_z, core]), blocks, adapter_down, main)
+    low = low_of_pairs(own, other)
+    delta = up_main(low, slot, flag, adapter_up_weight)
     back = swap(delta.reshape(64, HERE * MOST, cols), ADAPTER).reshape(64 * HERE * MOST, cols)
+    back, *whole = lax.optimization_barrier(
+        (back, tokens, adapter_down, adapter_up_weight, adapter_ids, base)
+    )
     values, lost = take_main(at_col, back, base)
     return lax.cond(
         lost[0] > 0,
-        lambda: whole_exchange(tokens, adapter_down, adapter_up_weight, adapter_ids, base),
+        lambda: whole_exchange(*whole),
         lambda: values,
     )
 

time: 160 us -> 154 us (0.963)
  blocking collectives: 10.6 us -> 2.74 us
  starting transfers between devices: 105 us -> 107 us
    all_to_all x1 -> x0, blocking collectives: 10.6 us -> none  [swap(): return lax.all_to_all(x, axes, split_axis=0, concat_axis=0, tiled=True)]
    ppermute x0 -> x1, starting transfers between devices: none -> 7.67 us  [low_of_pairs(): lax.ppermute(other, TENSOR[1], [(0, 1), (1, 0)]).astype(jnp.float32)]
    all_to_all x4, starting transfers between devices: 42.9 us -> 36.9 us  [swap(): return lax.all_to_all(x, axes, split_axis=0, concat_axis=0, tiled=True)]
    all_gather x0 -> x1, blocking collectives: none -> 2.74 us  [low_of_pairs(): return lax.all_gather(total, TENSOR[1], axis=0, tiled=True)]
    pallas_call x1 -> x2, Pallas kernels: 3.26 us -> 2.71 us  [the longest x1 2.67 us: down_main(): pl.pallas_call(kernel, out_shape=jax.ShapeDtypeStruct((half, pair), jnp.b...]
  transfers between devices with their start and end apart: 15 -> 16, of which waited for: 6 -> 6; matrix products, arithmetic and copies ran while one was open for 0% -> 0% of each run, Pallas kernels for 7% -> 9%
where the time goes in v8:
time: 154 us; the launch traced here: 153 us
  starting transfers between devices  107 us (69%)
  Pallas kernels  20.3 us (13%)
  waiting for transfers between devices  18.9 us (12%)
  blocking collectives  2.74 us (2%)
  local copies, waits for them, and re-layouts  2.23 us (1%)
    ppermute x10, starting transfers between devices, xor_sends(): lax.ppermute(pieces[k], axis, [(i, i ^ k) for i in range(size)])  60.4 us
    all_to_all x4, starting transfers between devices, swap(): return lax.all_to_all(x, axes, split_axis=0, concat_axis=0, tiled=True)  36.9 us
    ppermute x10, waiting for transfers between devices, xor_sends(): lax.ppermute(pieces[k], axis, [(i, i ^ k) for i in range(size)])  11.9 us
    ppermute x1, starting transfers between devices, low_of_pairs(): lax.ppermute(other, TENSOR[1], [(0, 1), (1, 0)]).astype(jnp.float32)  7.67 us
    all_to_all x4, waiting for transfers between devices, swap(): return lax.all_to_all(x, axes, split_axis=0, concat_axis=0, tiled=True)  6.06 us
    pallas_call x1, Pallas kernels, value_pieces(): pl.pallas_call(kernel, in_specs=[pl.BlockSpec(memory_space=pltpu.SMEM), p...  4.23 us
    pallas_call x1, Pallas kernels, side_first(): pl.pallas_call(kernel, out_shape=[jax.ShapeDtypeStruct((8 * SIDE, width),...  3.39 us
    pallas_call x1, Pallas kernels, place_main(): pl.pallas_call(kernel, grid=(slots // tile,), in_specs=[pl.BlockSpec((1,...  3.37 us
  transfers between devices with their start and end apart: 16, of which 6 were waited for; matrix products, arithmetic and copies ran while one was open for 0% of the time, Pallas kernels for 9%

profile of v8, /device:TPU:1, one launch (start us, length us, event | category | flops | bytes accessed | tf_op | source)
XLA Modules:
  0.0 152.8 jit_solution(13965197966206006866)
XLA Ops:
  0.0 0.0 copy-start.3
  0.0 0.0 copy-start.8
  0.0 3.4 %side_first.1 = (bf16[128,1024]{1,0:T(8,128)(2,1)}, s32[1,768]{1,0:T(1,128)S(1)}, s32[768,1]{1,0:T(8,128)S(1)}) custom-call(s32[1,768]{1,0:T(1,128)} %bitcast.28, bf16[768,1024]{1,0:T(8,128)(2,1)} %tok_ref.5), custom_call_target="tpu_custom_call" | custom-call | tf_op jit(solution)/shard_map/side_first/pallas_call | solution.py:346
  3.4 0.0 copy-start.1
  3.4 0.8 copy-done.1
  4.2 7.6 %all-to-all-start.4 = ((bf16[8,16,1024]{2,1,0:T(8,128)(2,1)}), bf16[8,16,1024]{2,1,0:T(8,128)(2,1)S(1)}, u32[]{:S(2)}, u32[]{:S(2)}) async-start(bf16[8,16,1024]{2,1,0:T(8,128)(2,1)} %bitcast.10), calls=%async_computation.4 | async-start | bytes 524288 | tf_op jit(solution)/shard_map/all_to_all | solution.py:23
  11.8 0.0 copy-done.3
  11.8 0.0 copy-done.8
  11.8 3.4 %place_main.1 = bf16[1024,1024]{1,0:T(8,128)(2,1)} custom-call(s32[1,768]{1,0:T(1,128)S(1)} %bitcast.29, s32[1,768]{1,0:T(1,128)S(1)} %get-tuple-element.64.seen_ref, bf16[768,1024]{1,0:T(8,128)(2,1)S(1)} %copy-done.3), custom_call_target="tpu_custom_call" | custom-call | tf_op jit(solution)/shard_map/place_main/pallas_call | solution.py:265
  15.2 6.1 %all-to-all-done.4 = bf16[8,16,1024]{2,1,0:T(8,128)(2,1)S(1)} async-done(((bf16[8,16,1024]{2,1,0:T(8,128)(2,1)}), bf16[8,16,1024]{2,1,0:T(8,128)(2,1)S(1)}, u32[]{:S(2)}, u32[]{:S(2)}) %all-to-all-start.4) | async-done | bytes 262176 | tf_op jit(solution)/shard_map/all_to_all | solution.py:23
  21.2 13.2 %all-to-all-start.5 = ((bf16[64,16,1024]{2,1,0:T(8,128)(2,1)}), bf16[64,16,1024]{2,1,0:T(8,128)(2,1)S(1)}, u32[]{:S(2)}, u32[]{:S(2)}) async-start(bf16[64,16,1024]{2,1,0:T(8,128)(2,1)} %bitcast.12), calls=%async_computation.5 | async-start | bytes 4194304 | tf_op jit(solution)/shard_map/all_to_all | solution.py:23
  34.5 0.5 side_second.1
  35.0 2.9 %collective-permute-start = (bf16[16,1024]{1,0:T(8,128)(2,1)S(1)}, bf16[16,1024]{1,0:T(8,128)(2,1)S(1)}, u32[]{:S(2)}, u32[]{:S(2)}) collective-permute-start(bf16[16,1024]{1,0:T(8,128)(2,1)S(1)} %get-tuple-element.57), channel_id=1, source_target_pairs={{0,64},{64,0},{128,192},{192,128},{256,320},{320,256},{384,448},{4... | collective-permute-start | bytes 98312 | tf_op jit(solution)/shard_map/ppermute | solution.py:627
  37.9 4.0 %collective-permute-start.1 = (bf16[16,1024]{1,0:T(8,128)(2,1)S(1)}, bf16[16,1024]{1,0:T(8,128)(2,1)S(1)}, u32[]{:S(2)}, u32[]{:S(2)}) collective-permute-start(bf16[16,1024]{1,0:T(8,128)(2,1)S(1)} %get-tuple-element.58), channel_id=1, source_target_pairs={{0,128},{64,192},{128,0},{192,64},{256,384},{320,448},{384,256},{4... | collective-permute-start | bytes 98312 | tf_op jit(solution)/shard_map/ppermute | solution.py:627
  42.0 2.3 %collective-permute-start.2 = (bf16[16,1024]{1,0:T(8,128)(2,1)S(1)}, bf16[16,1024]{1,0:T(8,128)(2,1)S(1)}, u32[]{:S(2)}, u32[]{:S(2)}) collective-permute-start(bf16[16,1024]{1,0:T(8,128)(2,1)S(1)} %get-tuple-element.59), channel_id=1, source_target_pairs={{0,192},{64,128},{128,64},{192,0},{256,448},{320,384},{384,320},{4... | collective-permute-start | bytes 98312 | tf_op jit(solution)/shard_map/ppermute | solution.py:627
  44.3 6.9 %collective-permute-start.3 = (bf16[16,1024]{1,0:T(8,128)(2,1)S(1)}, bf16[16,1024]{1,0:T(8,128)(2,1)S(1)}, u32[]{:S(2)}, u32[]{:S(2)}) collective-permute-start(bf16[16,1024]{1,0:T(8,128)(2,1)S(1)} %get-tuple-element.60), channel_id=1, source_target_pairs={{0,256},{64,320},{128,384},{192,448},{256,0},{320,64},{384,128},{4... | collective-permute-start | bytes 98312 | tf_op jit(solution)/shard_map/ppermute | solution.py:627
  51.2 1.9 %collective-permute-start.4 = (bf16[16,1024]{1,0:T(8,128)(2,1)S(1)}, bf16[16,1024]{1,0:T(8,128)(2,1)S(1)}, u32[]{:S(2)}, u32[]{:S(2)}) collective-permute-start(bf16[16,1024]{1,0:T(8,128)(2,1)S(1)} %get-tuple-element.61), channel_id=1, source_target_pairs={{0,320},{64,256},{128,448},{192,384},{256,64},{320,0},{384,192},{4... | collective-permute-start | bytes 98312 | tf_op jit(solution)/shard_map/ppermute | solution.py:627
  53.1 0.0 collective-permute-done.refs_1_
  53.2 30.4 %collective-permute-start.5 = (bf16[16,1024]{1,0:T(8,128)(2,1)S(1)}, bf16[16,1024]{1,0:T(8,128)(2,1)S(1)}, u32[]{:S(2)}, u32[]{:S(2)}) collective-permute-start(bf16[16,1024]{1,0:T(8,128)(2,1)S(1)} %get-tuple-element.62), channel_id=1, source_target_pairs={{0,384},{64,448},{128,256},{192,320},{256,128},{320,192},{384,0},{... | collective-permute-start | bytes 98312 | tf_op jit(solution)/shard_map/ppermute | solution.py:627
  83.5 0.0 collective-permute-done.1.refs_2_
  83.5 2.2 %collective-permute-start.6 = (bf16[16,1024]{1,0:T(8,128)(2,1)S(1)}, bf16[16,1024]{1,0:T(8,128)(2,1)S(1)}, u32[]{:S(2)}, u32[]{:S(2)}) collective-permute-start(bf16[16,1024]{1,0:T(8,128)(2,1)S(1)} %get-tuple-element.63), channel_id=1, source_target_pairs={{0,448},{64,384},{128,320},{192,256},{256,192},{320,128},{384,64},... | collective-permute-start | bytes 98312 | tf_op jit(solution)/shard_map/ppermute | solution.py:627
  85.7 0.1 pad_add_fusion.at_ref
  85.8 0.0 all-to-all-done.5
  85.8 0.0 copy-start.4
  85.8 2.7 %down_main.1.refs_9_ = bf16[512,128]{1,0:T(8,128)(2,1)S(1)} custom-call(bf16[1024,1024]{1,0:T(8,128)(2,1)S(1)} %bitcast.20, bf16[8,64,1024]{2,1,0:T(8,128)(2,1)} %refs_8_.1), custom_call_target="tpu_custom_call" | custom-call | tf_op jit(solution)/shard_map/down_main/pallas_call | solution.py:419
  88.5 0.0 copy-start
  88.5 0.0 collective-permute-done.2.refs_3_
  88.5 0.0 collective-permute-done.3.refs_4_
  88.5 2.0 %collective-permute-done.4.refs_5_ = bf16[16,1024]{1,0:T(8,128)(2,1)S(1)} collective-permute-done((bf16[16,1024]{1,0:T(8,128)(2,1)S(1)}, bf16[16,1024]{1,0:T(8,128)(2,1)S(1)}, u32[]{:S(2)}, u32[]{:S(2)}) %collective-permute-start.4) | collective-permute-done | bytes 32800 | tf_op jit(solution)/shard_map/ppermute | solution.py:627
  90.5 0.0 collective-permute-done.5.refs_6_
  90.5 0.4 collective-permute-done.6.refs_7_
  90.8 0.0 copy-done.4
  90.8 1.1 side_low.1
  91.9 7.7 %collective-permute-start.7 = (bf16[288,128]{1,0:T(8,128)(2,1)S(1)}, bf16[288,128]{1,0:T(8,128)(2,1)S(1)}, u32[]{:S(2)}, u32[]{:S(2)}) collective-permute-start(bf16[288,128]{1,0:T(8,128)(2,1)S(1)} %get-tuple-element.66), channel_id=1, source_target_pairs={{0,1},{1,0},{2,3},{3,2},{4,5},{5,4},{6,7},{7,6},{8,9},{9,8},{10,11... | collective-permute-start | bytes 221192 | tf_op jit(solution)/shard_map/ppermute | solution.py:564
  99.6 0.9 collective-permute-done.7
  100.5 0.8 broadcast_in_dim.4
  101.3 4.1 %all-to-all-start.6 = ((bf16[4,288,128]{2,1,0:T(8,128)(2,1)}), bf16[4,288,128]{2,1,0:T(8,128)(2,1)S(1)}, u32[]{:S(2)}, u32[]{:S(2)}) async-start(bf16[4,288,128]{2,1,0:T(8,128)(2,1)} %broadcast_in_dim.4), calls=%async_computation.6 | async-start | bytes 589824 | tf_op jit(solution)/shard_map/all_to_all | solution.py:23
  105.4 0.0 copy-done
  105.4 0.0 copy-start.7
  105.4 4.2 %value_pieces.1 = (bf16[4,768,128]{2,1,0:T(8,128)(2,1)S(1)}, bf16[4,768,128]{2,1,0:T(8,128)(2,1)}) custom-call(s32[1]{0:T(128)} %bitcast.16.at_ref, bf16[768,1024]{1,0:T(8,128)(2,1)} %tok_ref.5, bf16[1024,1024]{1,0:T(8,128)(2,1)S(1)} %copy-done), custom_call_target="tpu_custom_call" | custom-call | tf_op jit(solution)/shard_map/value_pieces/pallas_call | solution.py:89
  109.6 2.5 %collective-permute-start.8 = (bf16[4,768,128]{2,1,0:T(8,128)(2,1)}, bf16[4,768,128]{2,1,0:T(8,128)(2,1)S(1)}, u32[]{:S(2)}, u32[]{:S(2)}) collective-permute-start(bf16[4,768,128]{2,1,0:T(8,128)(2,1)} %get-tuple-element.70), channel_id=1, source_target_pairs={{0,1},{1,0},{2,3},{3,2},{4,5},{5,4},{6,7},{7,6},{8,9},{9,8},{10,11... | collective-permute-start | bytes 2359304 | tf_op jit(solution)/shard_map/ppermute | solution.py:601
  112.2 0.0 all-to-all-done.6.in_ref
  112.2 2.7 %all_gather.3.low_ref = bf16[576,128]{1,0:T(8,128)(2,1)S(1)} all-gather(bf16[288,128]{1,0:T(8,128)(2,1)S(1)} %chip_sum.1), channel_id=1, replica_groups=mesh['z'=8,'y'=8,'tensor_0'=4,'tensor_1'=2] {'tensor_1'}, dimensions={0}, use_global_device_ids=true | all-gather | bytes 221184 | tf_op jit(solution)/shard_map/all_gather | solution.py:568
  115.0 0.0 copy-done.7
  115.0 1.5 up_main.1
  116.5 11.9 %all-to-all-start.7 = ((bf16[64,24,128]{2,1,0:T(8,128)(2,1)}), bf16[64,24,128]{2,1,0:T(8,128)(2,1)S(1)}, u32[]{:S(2)}, u32[]{:S(2)}) async-start(bf16[64,24,128]{2,1,0:T(8,128)(2,1)} %bitcast.14), calls=%async_computation.7 | async-start | bytes 786432 | tf_op jit(solution)/shard_map/all_to_all | solution.py:23
  128.4 0.0 copy-start.2
  128.4 0.0 collective-permute-done.8.other_ref
  128.4 0.1 pair_sum.1
  128.6 0.0 copy-start.5
  128.6 3.2 %collective-permute-start.9 = (bf16[768,128]{1,0:T(8,128)(2,1)S(1)}, bf16[768,128]{1,0:T(8,128)(2,1)S(1)}, u32[]{:S(2)}, u32[]{:S(2)}) collective-permute-start(bf16[768,128]{1,0:T(8,128)(2,1)S(1)} %get-tuple-element.71), channel_id=1, source_target_pairs={{0,2},{2,0},{4,6},{6,4},{1,3},{3,1},{5,7},{7,5},{8,10},{10,8},{12,... | collective-permute-start | bytes 589832 | tf_op jit(solution)/shard_map/ppermute | solution.py:627
  131.8 4.3 %collective-permute-start.10 = (bf16[768,128]{1,0:T(8,128)(2,1)S(1)}, bf16[768,128]{1,0:T(8,128)(2,1)S(1)}, u32[]{:S(2)}, u32[]{:S(2)}) collective-permute-start(bf16[768,128]{1,0:T(8,128)(2,1)S(1)} %get-tuple-element.72), channel_id=1, source_target_pairs={{0,4},{2,6},{4,0},{6,2},{1,5},{3,7},{5,1},{7,3},{8,12},{10,14},{12... | collective-permute-start | bytes 589832 | tf_op jit(solution)/shard_map/ppermute | solution.py:627
  136.1 2.2 %collective-permute-start.11 = (bf16[768,128]{1,0:T(8,128)(2,1)S(1)}, bf16[768,128]{1,0:T(8,128)(2,1)S(1)}, u32[]{:S(2)}, u32[]{:S(2)}) collective-permute-start(bf16[768,128]{1,0:T(8,128)(2,1)S(1)} %get-tuple-element.73), channel_id=1, source_target_pairs={{0,6},{2,4},{4,2},{6,0},{1,7},{3,5},{5,3},{7,1},{8,14},{10,12},{12... | collective-permute-start | bytes 589832 | tf_op jit(solution)/shard_map/ppermute | solution.py:627
  138.3 0.0 collective-permute-done.9.refs_0_
  138.3 4.4 %collective-permute-done.10.refs_1_ = bf16[768,128]{1,0:T(8,128)(2,1)S(1)} collective-permute-done((bf16[768,128]{1,0:T(8,128)(2,1)S(1)}, bf16[768,128]{1,0:T(8,128)(2,1)S(1)}, u32[]{:S(2)}, u32[]{:S(2)}) %collective-permute-start.10) | collective-permute-done | bytes 196640 | tf_op jit(solution)/shard_map/ppermute | solution.py:627
  142.7 5.2 %collective-permute-done.11.refs_2_ = bf16[768,128]{1,0:T(8,128)(2,1)S(1)} collective-permute-done((bf16[768,128]{1,0:T(8,128)(2,1)S(1)}, bf16[768,128]{1,0:T(8,128)(2,1)S(1)}, u32[]{:S(2)}, u32[]{:S(2)}) %collective-permute-start.11) | collective-permute-done | bytes 196640 | tf_op jit(solution)/shard_map/ppermute | solution.py:627
  147.9 0.9 base_sum.1.base_ref
  148.8 0.0 all-to-all-done.7
  148.8 0.0 copy-done.2
  148.8 2.5 %take_main.1 = (bf16[768,128]{1,0:T(8,128)(2,1)S(1)}, s32[1]{0:T(128)}) custom-call(s32[768,1]{1,0:T(8,128)S(1)} %copy-done.2, bf16[1536,128]{1,0:T(8,128)(2,1)S(1)} %bitcast.22, f32[768,128]{1,0:T(8,128)} %base_sum.1.base_ref), custom_call_target="tpu_custom_call" | custom-call | tf_op jit(solution)/shard_map/take_main/pallas_call | solution.py:542
  151.9 0.0 copy-done.5
  151.9 0.2 conditional.1
  152.2 0.0 copy-start.9
  152.2 0.7 copy-done.9
  (2 shorter events, 0.1 us)
Async XLA Ops:
  0.0 11.8 %copy-start.3 = (bf16[768,1024]{1,0:T(8,128)(2,1)S(1)}, bf16[768,1024]{1,0:T(8,128)(2,1)}, u32[]{:S(2)}) copy-start(bf16[768,1024]{1,0:T(8,128)(2,1)} %tok_ref.5) | copy-start | bytes 4718596
  0.0 11.8 %copy-start.8 = (s32[768,1]{0,1:T(1,128)S(1)}, s32[768,1]{0,1:T(1,128)}, u32[]{:S(2)}) copy-start(s32[768,1]{0,1:T(1,128)} %param.11) | copy-start | bytes 9220
  3.4 0.8 copy-start.1
  4.2 17.1 %all-to-all-start.4 = ((bf16[8,16,1024]{2,1,0:T(8,128)(2,1)}), bf16[8,16,1024]{2,1,0:T(8,128)(2,1)S(1)}, u32[]{:S(2)}, u32[]{:S(2)}) async-start(bf16[8,16,1024]{2,1,0:T(8,128)(2,1)} %bitcast.10), calls=%async_computation.4 | async-start | bytes 524288 | tf_op jit(solution)/shard_map/all_to_all | solution.py:23
  21.2 64.5 %all-to-all-start.5 = ((bf16[64,16,1024]{2,1,0:T(8,128)(2,1)}), bf16[64,16,1024]{2,1,0:T(8,128)(2,1)S(1)}, u32[]{:S(2)}, u32[]{:S(2)}) async-start(bf16[64,16,1024]{2,1,0:T(8,128)(2,1)} %bitcast.12), calls=%async_computation.5 | async-start | bytes 4194304 | tf_op jit(solution)/shard_map/all_to_all | solution.py:23
  35.0 18.2 %collective-permute-start = (bf16[16,1024]{1,0:T(8,128)(2,1)S(1)}, bf16[16,1024]{1,0:T(8,128)(2,1)S(1)}, u32[]{:S(2)}, u32[]{:S(2)}) collective-permute-start(bf16[16,1024]{1,0:T(8,128)(2,1)S(1)} %get-tuple-element.57), channel_id=1, source_target_pairs={{0,64},{64,0},{128,192},{192,128},{256,320},{320,256},{384,448},{4... | collective-permute-start | bytes 98312 | tf_op jit(solution)/shard_map/ppermute | solution.py:627
  37.9 45.6 %collective-permute-start.1 = (bf16[16,1024]{1,0:T(8,128)(2,1)S(1)}, bf16[16,1024]{1,0:T(8,128)(2,1)S(1)}, u32[]{:S(2)}, u32[]{:S(2)}) collective-permute-start(bf16[16,1024]{1,0:T(8,128)(2,1)S(1)} %get-tuple-element.58), channel_id=1, source_target_pairs={{0,128},{64,192},{128,0},{192,64},{256,384},{320,448},{384,256},{4... | collective-permute-start | bytes 98312 | tf_op jit(solution)/shard_map/ppermute | solution.py:627
  42.0 46.5 %collective-permute-start.2 = (bf16[16,1024]{1,0:T(8,128)(2,1)S(1)}, bf16[16,1024]{1,0:T(8,128)(2,1)S(1)}, u32[]{:S(2)}, u32[]{:S(2)}) collective-permute-start(bf16[16,1024]{1,0:T(8,128)(2,1)S(1)} %get-tuple-element.59), channel_id=1, source_target_pairs={{0,192},{64,128},{128,64},{192,0},{256,448},{320,384},{384,320},{4... | collective-permute-start | bytes 98312 | tf_op jit(solution)/shard_map/ppermute | solution.py:627
  44.3 44.2 %collective-permute-start.3 = (bf16[16,1024]{1,0:T(8,128)(2,1)S(1)}, bf16[16,1024]{1,0:T(8,128)(2,1)S(1)}, u32[]{:S(2)}, u32[]{:S(2)}) collective-permute-start(bf16[16,1024]{1,0:T(8,128)(2,1)S(1)} %get-tuple-element.60), channel_id=1, source_target_pairs={{0,256},{64,320},{128,384},{192,448},{256,0},{320,64},{384,128},{4... | collective-permute-start | bytes 98312 | tf_op jit(solution)/shard_map/ppermute | solution.py:627
  51.2 39.2 %collective-permute-start.4 = (bf16[16,1024]{1,0:T(8,128)(2,1)S(1)}, bf16[16,1024]{1,0:T(8,128)(2,1)S(1)}, u32[]{:S(2)}, u32[]{:S(2)}) collective-permute-start(bf16[16,1024]{1,0:T(8,128)(2,1)S(1)} %get-tuple-element.61), channel_id=1, source_target_pairs={{0,320},{64,256},{128,448},{192,384},{256,64},{320,0},{384,192},{4... | collective-permute-start | bytes 98312 | tf_op jit(solution)/shard_map/ppermute | solution.py:627
  53.2 37.3 %collective-permute-start.5 = (bf16[16,1024]{1,0:T(8,128)(2,1)S(1)}, bf16[16,1024]{1,0:T(8,128)(2,1)S(1)}, u32[]{:S(2)}, u32[]{:S(2)}) collective-permute-start(bf16[16,1024]{1,0:T(8,128)(2,1)S(1)} %get-tuple-element.62), channel_id=1, source_target_pairs={{0,384},{64,448},{128,256},{192,320},{256,128},{320,192},{384,0},{... | collective-permute-start | bytes 98312 | tf_op jit(solution)/shard_map/ppermute | solution.py:627
  83.5 7.3 %collective-permute-start.6 = (bf16[16,1024]{1,0:T(8,128)(2,1)S(1)}, bf16[16,1024]{1,0:T(8,128)(2,1)S(1)}, u32[]{:S(2)}, u32[]{:S(2)}) collective-permute-start(bf16[16,1024]{1,0:T(8,128)(2,1)S(1)} %get-tuple-element.63), channel_id=1, source_target_pairs={{0,448},{64,384},{128,320},{192,256},{256,192},{320,128},{384,64},... | collective-permute-start | bytes 98312 | tf_op jit(solution)/shard_map/ppermute | solution.py:627
  85.8 5.0 %copy-start.4 = (bf16[8,64,1024]{2,1,0:T(8,128)(2,1)S(1)}, bf16[8,64,1024]{2,1,0:T(8,128)(2,1)}, u32[]{:S(2)}) copy-start(bf16[8,64,1024]{2,1,0:T(8,128)(2,1)} %refs_8_.1) | copy-start | bytes 3145732
  88.5 16.9 %copy-start = (bf16[1024,1024]{1,0:T(8,128)(2,1)S(1)}, bf16[1024,1024]{1,0:T(8,128)(2,1)}, u32[]{:S(2)}) copy-start(bf16[1024,1024]{1,0:T(8,128)(2,1)} %w_ref.1) | copy-start | bytes 6291460
  91.9 8.6 %collective-permute-start.7 = (bf16[288,128]{1,0:T(8,128)(2,1)S(1)}, bf16[288,128]{1,0:T(8,128)(2,1)S(1)}, u32[]{:S(2)}, u32[]{:S(2)}) collective-permute-start(bf16[288,128]{1,0:T(8,128)(2,1)S(1)} %get-tuple-element.66), channel_id=1, source_target_pairs={{0,1},{1,0},{2,3},{3,2},{4,5},{5,4},{6,7},{7,6},{8,9},{9,8},{10,11... | collective-permute-start | bytes 221192 | tf_op jit(solution)/shard_map/ppermute | solution.py:564
  101.3 10.9 %all-to-all-start.6 = ((bf16[4,288,128]{2,1,0:T(8,128)(2,1)}), bf16[4,288,128]{2,1,0:T(8,128)(2,1)S(1)}, u32[]{:S(2)}, u32[]{:S(2)}) async-start(bf16[4,288,128]{2,1,0:T(8,128)(2,1)} %broadcast_in_dim.4), calls=%async_computation.6 | async-start | bytes 589824 | tf_op jit(solution)/shard_map/all_to_all | solution.py:23
  105.4 9.6 %copy-start.7 = (bf16[8,64,128]{2,1,0:T(8,128)(2,1)S(1)}, bf16[8,64,128]{2,1,0:T(8,128)(2,1)}, u32[]{:S(2)}) copy-start(bf16[8,64,128]{2,1,0:T(8,128)(2,1)} %up_ref.1) | copy-start | bytes 393220
  109.6 18.8 %collective-permute-start.8 = (bf16[4,768,128]{2,1,0:T(8,128)(2,1)}, bf16[4,768,128]{2,1,0:T(8,128)(2,1)S(1)}, u32[]{:S(2)}, u32[]{:S(2)}) collective-permute-start(bf16[4,768,128]{2,1,0:T(8,128)(2,1)} %get-tuple-element.70), channel_id=1, source_target_pairs={{0,1},{1,0},{2,3},{3,2},{4,5},{5,4},{6,7},{7,6},{8,9},{9,8},{10,11... | collective-permute-start | bytes 2359304 | tf_op jit(solution)/shard_map/ppermute | solution.py:601
  116.5 32.3 %all-to-all-start.7 = ((bf16[64,24,128]{2,1,0:T(8,128)(2,1)}), bf16[64,24,128]{2,1,0:T(8,128)(2,1)S(1)}, u32[]{:S(2)}, u32[]{:S(2)}) async-start(bf16[64,24,128]{2,1,0:T(8,128)(2,1)} %bitcast.14), calls=%async_computation.7 | async-start | bytes 786432 | tf_op jit(solution)/shard_map/all_to_all | solution.py:23
  128.4 20.4 %copy-start.2 = (s32[768,1]{1,0:T(8,128)S(1)}, s32[768,1]{1,0:T(8,128)}, u32[]{:S(2)}) copy-start(s32[768,1]{1,0:T(8,128)} %copy-done.1) | copy-start | bytes 9220
  128.6 23.4 %copy-start.5 = (bf16[8,64,1024]{2,1,0:T(8,128)(2,1)S(1)}, bf16[8,64,1024]{2,1,0:T(8,128)(2,1)}, u32[]{:S(2)}) copy-start(bf16[8,64,1024]{2,1,0:T(8,128)(2,1)} %refs_8_.1) | copy-start | bytes 3145732
  128.6 9.7 %collective-permute-start.9 = (bf16[768,128]{1,0:T(8,128)(2,1)S(1)}, bf16[768,128]{1,0:T(8,128)(2,1)S(1)}, u32[]{:S(2)}, u32[]{:S(2)}) collective-permute-start(bf16[768,128]{1,0:T(8,128)(2,1)S(1)} %get-tuple-element.71), channel_id=1, source_target_pairs={{0,2},{2,0},{4,6},{6,4},{1,3},{3,1},{5,7},{7,5},{8,10},{10,8},{12,... | collective-permute-start | bytes 589832 | tf_op jit(solution)/shard_map/ppermute | solution.py:627
  131.8 10.9 %collective-permute-start.10 = (bf16[768,128]{1,0:T(8,128)(2,1)S(1)}, bf16[768,128]{1,0:T(8,128)(2,1)S(1)}, u32[]{:S(2)}, u32[]{:S(2)}) collective-permute-start(bf16[768,128]{1,0:T(8,128)(2,1)S(1)} %get-tuple-element.72), channel_id=1, source_target_pairs={{0,4},{2,6},{4,0},{6,2},{1,5},{3,7},{5,1},{7,3},{8,12},{10,14},{12... | collective-permute-start | bytes 589832 | tf_op jit(solution)/shard_map/ppermute | solution.py:627
  136.1 11.8 %collective-permute-start.11 = (bf16[768,128]{1,0:T(8,128)(2,1)S(1)}, bf16[768,128]{1,0:T(8,128)(2,1)S(1)}, u32[]{:S(2)}, u32[]{:S(2)}) collective-permute-start(bf16[768,128]{1,0:T(8,128)(2,1)S(1)} %get-tuple-element.73), channel_id=1, source_target_pairs={{0,6},{2,4},{4,2},{6,0},{1,7},{3,5},{5,3},{7,1},{8,14},{10,12},{12... | collective-permute-start | bytes 589832 | tf_op jit(solution)/shard_map/ppermute | solution.py:627
  152.2 0.7 copy-start.9

commit v9 on v8

--- a/solution.py
+++ b/solution.py
@@ -322,16 +322,12 @@
 def side_first(ids_row, tokens):
     rows, width = tokens.shape
 
-    def kernel(row_ref, tok_ref, out_ref, seen_ref, at_col_ref):
+    def kernel(row_ref, tok_ref, out_ref, seen_ref):
         row = row_ref[...]
         seen = count_before(row, to_col(row))
         seen_ref[...] = seen
         home = row // HERE
         spot = row % HERE
-        back = home * (HERE * MOST) + jnp.where(
-            seen < MAIN, spot * MAIN + seen, HERE * MAIN + spot
-        )
-        at_col_ref[...] = to_col(back)
         third = seen >= MAIN
         key = home % 8
 
@@ -348,7 +344,6 @@
         out_shape=[
             jax.ShapeDtypeStruct((8 * SIDE, width), jnp.bfloat16),
             jax.ShapeDtypeStruct((1, rows), jnp.int32),
-            jax.ShapeDtypeStruct((rows, 1), jnp.int32),
         ],
         compiler_params=GRANT,
         name="side_first",
@@ -528,14 +523,32 @@
     )(low, slot, flag, up)
 
 
-def take_main(at_col, back, base):
+def pick_all(ids_row, seen, slots):
+    rows = ids_row.shape[1]
+
+    def kernel(row_ref, seen_ref, out_ref):
+        row = row_ref[...]
+        seen = seen_ref[...]
+        spot = row % HERE
+        back = row // HERE * (HERE * MOST) + jnp.where(
+            seen < MAIN, spot * MAIN + seen, HERE * MAIN + spot
+        )
+        slot = lax.broadcasted_iota(jnp.int32, (rows, slots), 1)
+        out_ref[...] = jnp.where(slot == to_col(back), 1.0, 0.0).astype(jnp.bfloat16)
+
+    return pl.pallas_call(
+        kernel,
+        out_shape=jax.ShapeDtypeStruct((rows, slots), jnp.bfloat16),
+        compiler_params=GRANT,
+        name="pick_all",
+    )(ids_row, seen)
+
+
+def take_main(pick, back, base):
     rows, cols = base.shape
-    slots = back.shape[0]
-
-    def kernel(at_ref, back_ref, base_ref, out_ref, lost_ref):
-        slot = lax.broadcasted_iota(jnp.int32, (rows, slots), 1)
-        pick = jnp.where(slot == at_ref[...], 1.0, 0.0).astype(jnp.bfloat16)
-        mine = jnp.dot(pick, back_ref[...], preferred_element_type=jnp.float32)
+
+    def kernel(pick_ref, back_ref, base_ref, out_ref, lost_ref):
+        mine = jnp.dot(pick_ref[...], back_ref[...], preferred_element_type=jnp.float32)
         out_ref[...] = (base_ref[...] + mine).astype(jnp.bfloat16)
         lost_ref[0] = (jnp.max(back_ref[...].astype(jnp.float32)) > LOST / 2).astype(jnp.int32)
 
@@ -548,7 +561,7 @@
         ],
         compiler_params=GRANT,
         name="take_main",
-    )(at_col, back, base)
+    )(pick, back, base)
 
 
 def low_of_all(low_part, groups):
@@ -588,7 +601,7 @@
     ids_row = adapter_ids.reshape(1, rows)
     at_z = lax.axis_index("z").astype(jnp.int32)
 
-    blocks, seen, at_col = side_first(ids_row, tokens)
+    blocks, seen = side_first(ids_row, tokens)
     blocks = swap(blocks.reshape(8, SIDE, width), "y").reshape(8 * SIDE, width)
     placed = place_main(ids_row, seen, tokens, 64 * HERE * MAIN)
     arrived = swap(placed.reshape(64, HERE * MAIN, width), ADAPTER)
@@ -608,11 +621,13 @@
     own, other, slot, flag = side_low(jnp.stack([at_z, core]), blocks, adapter_down, main)
     low = low_of_pairs(own, other)
     delta = up_main(low, slot, flag, adapter_up_weight)
-    back = swap(delta.reshape(64, HERE * MOST, cols), ADAPTER).reshape(64 * HERE * MOST, cols)
+    back = swap(delta.reshape(64, HERE * MOST, cols), ADAPTER)
+    back = back.reshape(64 * HERE * MOST, cols)
+    pick = pick_all(ids_row, seen, 64 * HERE * MOST)
     back, *whole = lax.optimization_barrier(
         (back, tokens, adapter_down, adapter_up_weight, adapter_ids, base)
     )
-    values, lost = take_main(at_col, back, base)
+    values, lost = take_main(pick, back, base)
     return lax.cond(
         lost[0] > 0,
         lambda: whole_exchange(*whole),

time: 154 us -> 153 us (level)
  transfers between devices with their start and end apart: 16 -> 16, of which waited for: 6 -> 5; matrix products, arithmetic and copies ran while one was open for 0% -> 0% of each run, Pallas kernels for 9% -> 9%
where the time goes in v9:
time: 153 us; the launch traced here: 152 us
  starting transfers between devices  108 us (71%)
  Pallas kernels  20.8 us (14%)
  waiting for transfers between devices  17.9 us (12%)
  blocking collectives  2.75 us (2%)
    ppermute x10, starting transfers between devices, xor_sends(): lax.ppermute(pieces[k], axis, [(i, i ^ k) for i in range(size)])  60.2 us
    all_to_all x4, starting transfers between devices, swap(): return lax.all_to_all(x, axes, split_axis=0, concat_axis=0, tiled=True)  36.7 us
    ppermute x10, waiting for transfers between devices, xor_sends(): lax.ppermute(pieces[k], axis, [(i, i ^ k) for i in range(size)])  11 us
    ppermute x1, starting transfers between devices, low_of_pairs(): lax.ppermute(other, TENSOR[1], [(0, 1), (1, 0)]).astype(jnp.float32)  8.09 us
    all_to_all x4, waiting for transfers between devices, swap(): return lax.all_to_all(x, axes, split_axis=0, concat_axis=0, tiled=True)  6.06 us
    pallas_call x1, Pallas kernels, value_pieces(): pl.pallas_call(kernel, in_specs=[pl.BlockSpec(memory_space=pltpu.SMEM), p...  4.22 us
    pallas_call x1, Pallas kernels, place_main(): pl.pallas_call(kernel, grid=(slots // tile,), in_specs=[pl.BlockSpec((1,...  3.37 us
    pallas_call x1, Pallas kernels, side_first(): pl.pallas_call(kernel, out_shape=[jax.ShapeDtypeStruct((8 * SIDE, width),...  3.35 us
  transfers between devices with their start and end apart: 16, of which 5 were waited for; matrix products, arithmetic and copies ran while one was open for 0% of the time, Pallas kernels for 9%

profile of v9, /device:TPU:1, one launch (start us, length us, event | category | flops | bytes accessed | tf_op | source)
XLA Modules:
  0.0 151.8 jit_solution(15090871095584014920)
XLA Ops:
  0.0 3.4 %side_first.1 = (bf16[128,1024]{1,0:T(8,128)(2,1)}, s32[1,768]{1,0:T(1,128)S(1)}) custom-call(s32[1,768]{1,0:T(1,128)} %bitcast.28, bf16[768,1024]{1,0:T(8,128)(2,1)} %tok_ref.5), custom_call_target="tpu_custom_call" | custom-call | tf_op jit(solution)/shard_map/side_first/pallas_call | solution.py:342
  3.4 7.6 %all-to-all-start.4 = ((bf16[8,16,1024]{2,1,0:T(8,128)(2,1)}), bf16[8,16,1024]{2,1,0:T(8,128)(2,1)S(1)}, u32[]{:S(2)}, u32[]{:S(2)}) async-start(bf16[8,16,1024]{2,1,0:T(8,128)(2,1)} %bitcast.10), calls=%async_computation.4 | async-start | bytes 524288 | tf_op jit(solution)/shard_map/all_to_all | solution.py:23
  11.0 0.0 copy-done.3
  11.0 0.0 copy-done.10
  11.0 3.4 %place_main.1 = bf16[1024,1024]{1,0:T(8,128)(2,1)} custom-call(s32[1,768]{1,0:T(1,128)S(1)} %bitcast.29, s32[1,768]{1,0:T(1,128)S(1)} %get-tuple-element.53.seen_ref, bf16[768,1024]{1,0:T(8,128)(2,1)S(1)} %copy-done.3), custom_call_target="tpu_custom_call" | custom-call | tf_op jit(solution)/shard_map/place_main/pallas_call | solution.py:265
  14.4 6.0 %all-to-all-done.4 = bf16[8,16,1024]{2,1,0:T(8,128)(2,1)S(1)} async-done(((bf16[8,16,1024]{2,1,0:T(8,128)(2,1)}), bf16[8,16,1024]{2,1,0:T(8,128)(2,1)S(1)}, u32[]{:S(2)}, u32[]{:S(2)}) %all-to-all-start.4) | async-done | bytes 262176 | tf_op jit(solution)/shard_map/all_to_all | solution.py:23
  20.4 13.2 %all-to-all-start.5 = ((bf16[64,16,1024]{2,1,0:T(8,128)(2,1)}), bf16[64,16,1024]{2,1,0:T(8,128)(2,1)S(1)}, u32[]{:S(2)}, u32[]{:S(2)}) async-start(bf16[64,16,1024]{2,1,0:T(8,128)(2,1)} %bitcast.12), calls=%async_computation.5 | async-start | bytes 4194304 | tf_op jit(solution)/shard_map/all_to_all | solution.py:23
  33.7 0.5 side_second.1
  34.2 2.9 %collective-permute-start = (bf16[16,1024]{1,0:T(8,128)(2,1)S(1)}, bf16[16,1024]{1,0:T(8,128)(2,1)S(1)}, u32[]{:S(2)}, u32[]{:S(2)}) collective-permute-start(bf16[16,1024]{1,0:T(8,128)(2,1)S(1)} %get-tuple-element.56), channel_id=1, source_target_pairs={{0,64},{64,0},{128,192},{192,128},{256,320},{320,256},{384,448},{4... | collective-permute-start | bytes 98312 | tf_op jit(solution)/shard_map/ppermute | solution.py:642
  37.1 4.0 %collective-permute-start.1 = (bf16[16,1024]{1,0:T(8,128)(2,1)S(1)}, bf16[16,1024]{1,0:T(8,128)(2,1)S(1)}, u32[]{:S(2)}, u32[]{:S(2)}) collective-permute-start(bf16[16,1024]{1,0:T(8,128)(2,1)S(1)} %get-tuple-element.57), channel_id=1, source_target_pairs={{0,128},{64,192},{128,0},{192,64},{256,384},{320,448},{384,256},{4... | collective-permute-start | bytes 98312 | tf_op jit(solution)/shard_map/ppermute | solution.py:642
  41.2 2.3 %collective-permute-start.2 = (bf16[16,1024]{1,0:T(8,128)(2,1)S(1)}, bf16[16,1024]{1,0:T(8,128)(2,1)S(1)}, u32[]{:S(2)}, u32[]{:S(2)}) collective-permute-start(bf16[16,1024]{1,0:T(8,128)(2,1)S(1)} %get-tuple-element.58), channel_id=1, source_target_pairs={{0,192},{64,128},{128,64},{192,0},{256,448},{320,384},{384,320},{4... | collective-permute-start | bytes 98312 | tf_op jit(solution)/shard_map/ppermute | solution.py:642
  43.5 6.9 %collective-permute-start.3 = (bf16[16,1024]{1,0:T(8,128)(2,1)S(1)}, bf16[16,1024]{1,0:T(8,128)(2,1)S(1)}, u32[]{:S(2)}, u32[]{:S(2)}) collective-permute-start(bf16[16,1024]{1,0:T(8,128)(2,1)S(1)} %get-tuple-element.59), channel_id=1, source_target_pairs={{0,256},{64,320},{128,384},{192,448},{256,0},{320,64},{384,128},{4... | collective-permute-start | bytes 98312 | tf_op jit(solution)/shard_map/ppermute | solution.py:642
  50.4 1.9 %collective-permute-start.4 = (bf16[16,1024]{1,0:T(8,128)(2,1)S(1)}, bf16[16,1024]{1,0:T(8,128)(2,1)S(1)}, u32[]{:S(2)}, u32[]{:S(2)}) collective-permute-start(bf16[16,1024]{1,0:T(8,128)(2,1)S(1)} %get-tuple-element.60), channel_id=1, source_target_pairs={{0,320},{64,256},{128,448},{192,384},{256,64},{320,0},{384,192},{4... | collective-permute-start | bytes 98312 | tf_op jit(solution)/shard_map/ppermute | solution.py:642
  52.4 0.0 collective-permute-done.refs_1_
  52.4 30.4 %collective-permute-start.5 = (bf16[16,1024]{1,0:T(8,128)(2,1)S(1)}, bf16[16,1024]{1,0:T(8,128)(2,1)S(1)}, u32[]{:S(2)}, u32[]{:S(2)}) collective-permute-start(bf16[16,1024]{1,0:T(8,128)(2,1)S(1)} %get-tuple-element.61), channel_id=1, source_target_pairs={{0,384},{64,448},{128,256},{192,320},{256,128},{320,192},{384,0},{... | collective-permute-start | bytes 98312 | tf_op jit(solution)/shard_map/ppermute | solution.py:642
  82.7 0.0 collective-permute-done.1.refs_2_
  82.8 2.1 %collective-permute-start.6 = (bf16[16,1024]{1,0:T(8,128)(2,1)S(1)}, bf16[16,1024]{1,0:T(8,128)(2,1)S(1)}, u32[]{:S(2)}, u32[]{:S(2)}) collective-permute-start(bf16[16,1024]{1,0:T(8,128)(2,1)S(1)} %get-tuple-element.62), channel_id=1, source_target_pairs={{0,448},{64,384},{128,320},{192,256},{256,192},{320,128},{384,64},... | collective-permute-start | bytes 98312 | tf_op jit(solution)/shard_map/ppermute | solution.py:642
  84.9 0.1 pad_add_fusion.at_ref
  85.0 0.0 all-to-all-done.5
  85.0 2.7 %down_main.1.refs_9_ = bf16[512,128]{1,0:T(8,128)(2,1)S(1)} custom-call(bf16[1024,1024]{1,0:T(8,128)(2,1)S(1)} %bitcast.20, bf16[8,64,1024]{2,1,0:T(8,128)(2,1)} %refs_8_.1), custom_call_target="tpu_custom_call" | custom-call | tf_op jit(solution)/shard_map/down_main/pallas_call | solution.py:414
  87.6 0.0 copy-start.2
  87.7 0.0 collective-permute-done.2.refs_3_
  87.7 0.0 collective-permute-done.3.refs_4_
  87.7 2.0 %collective-permute-done.4.refs_5_ = bf16[16,1024]{1,0:T(8,128)(2,1)S(1)} collective-permute-done((bf16[16,1024]{1,0:T(8,128)(2,1)S(1)}, bf16[16,1024]{1,0:T(8,128)(2,1)S(1)}, u32[]{:S(2)}, u32[]{:S(2)}) %collective-permute-start.4) | collective-permute-done | bytes 32800 | tf_op jit(solution)/shard_map/ppermute | solution.py:642
  89.7 0.0 collective-permute-done.5.refs_6_
  89.7 0.0 collective-permute-done.6.refs_7_
  89.7 0.0 copy-done.5
  89.7 1.1 side_low.1
  90.8 8.1 %collective-permute-start.7 = (bf16[288,128]{1,0:T(8,128)(2,1)S(1)}, bf16[288,128]{1,0:T(8,128)(2,1)S(1)}, u32[]{:S(2)}, u32[]{:S(2)}) collective-permute-start(bf16[288,128]{1,0:T(8,128)(2,1)S(1)} %get-tuple-element.64), channel_id=1, source_target_pairs={{0,1},{1,0},{2,3},{3,2},{4,5},{5,4},{6,7},{7,6},{8,9},{9,8},{10,11... | collective-permute-start | bytes 221192 | tf_op jit(solution)/shard_map/ppermute | solution.py:577
  98.9 0.9 collective-permute-done.7
  99.8 0.8 broadcast_in_dim.4
  100.6 4.0 %all-to-all-start.6 = ((bf16[4,288,128]{2,1,0:T(8,128)(2,1)}), bf16[4,288,128]{2,1,0:T(8,128)(2,1)S(1)}, u32[]{:S(2)}, u32[]{:S(2)}) async-start(bf16[4,288,128]{2,1,0:T(8,128)(2,1)} %broadcast_in_dim.4), calls=%async_computation.6 | async-start | bytes 589824 | tf_op jit(solution)/shard_map/all_to_all | solution.py:23
  104.6 0.0 copy-done.2
  104.6 4.2 %value_pieces.1 = (bf16[4,768,128]{2,1,0:T(8,128)(2,1)S(1)}, bf16[4,768,128]{2,1,0:T(8,128)(2,1)}) custom-call(s32[1]{0:T(128)} %bitcast.16.at_ref, bf16[768,1024]{1,0:T(8,128)(2,1)} %tok_ref.5, bf16[1024,1024]{1,0:T(8,128)(2,1)S(1)} %copy-done.2), custom_call_target="tpu_custom_call" | custom-call | tf_op jit(solution)/shard_map/value_pieces/pallas_call | solution.py:89
  108.8 2.5 %collective-permute-start.8 = (bf16[4,768,128]{2,1,0:T(8,128)(2,1)}, bf16[4,768,128]{2,1,0:T(8,128)(2,1)S(1)}, u32[]{:S(2)}, u32[]{:S(2)}) collective-permute-start(bf16[4,768,128]{2,1,0:T(8,128)(2,1)} %get-tuple-element.68), channel_id=1, source_target_pairs={{0,1},{1,0},{2,3},{3,2},{4,5},{5,4},{6,7},{7,6},{8,9},{9,8},{10,11... | collective-permute-start | bytes 2359304 | tf_op jit(solution)/shard_map/ppermute | solution.py:614
  111.4 0.0 all-to-all-done.6.in_ref
  111.4 2.8 %all_gather.3.low_ref = bf16[576,128]{1,0:T(8,128)(2,1)S(1)} all-gather(bf16[288,128]{1,0:T(8,128)(2,1)S(1)} %chip_sum.1), channel_id=1, replica_groups=mesh['z'=8,'y'=8,'tensor_0'=4,'tensor_1'=2] {'tensor_1'}, dimensions={0}, use_global_device_ids=true | all-gather | bytes 221184 | tf_op jit(solution)/shard_map/all_gather | solution.py:581
  114.2 0.0 copy-done.8
  114.2 1.5 up_main.1
  115.7 11.8 %all-to-all-start.7 = ((bf16[64,24,128]{2,1,0:T(8,128)(2,1)}), bf16[64,24,128]{2,1,0:T(8,128)(2,1)S(1)}, u32[]{:S(2)}, u32[]{:S(2)}) async-start(bf16[64,24,128]{2,1,0:T(8,128)(2,1)} %bitcast.14), calls=%async_computation.7 | async-start | bytes 786432 | tf_op jit(solution)/shard_map/all_to_all | solution.py:23
  127.5 0.0 collective-permute-done.8.other_ref
  127.5 0.0 copy-start
  127.5 0.1 pair_sum.1
  127.7 3.0 %collective-permute-start.9 = (bf16[768,128]{1,0:T(8,128)(2,1)S(1)}, bf16[768,128]{1,0:T(8,128)(2,1)S(1)}, u32[]{:S(2)}, u32[]{:S(2)}) collective-permute-start(bf16[768,128]{1,0:T(8,128)(2,1)S(1)} %get-tuple-element.69), channel_id=1, source_target_pairs={{0,2},{2,0},{4,6},{6,4},{1,3},{3,1},{5,7},{7,5},{8,10},{10,8},{12,... | collective-permute-start | bytes 589832 | tf_op jit(solution)/shard_map/ppermute | solution.py:642
  130.7 4.3 %collective-permute-start.10 = (bf16[768,128]{1,0:T(8,128)(2,1)S(1)}, bf16[768,128]{1,0:T(8,128)(2,1)S(1)}, u32[]{:S(2)}, u32[]{:S(2)}) collective-permute-start(bf16[768,128]{1,0:T(8,128)(2,1)S(1)} %get-tuple-element.70), channel_id=1, source_target_pairs={{0,4},{2,6},{4,0},{6,2},{1,5},{3,7},{5,1},{7,3},{8,12},{10,14},{12... | collective-permute-start | bytes 589832 | tf_op jit(solution)/shard_map/ppermute | solution.py:642
  135.0 0.0 copy-done
  135.0 2.2 %collective-permute-start.11 = (bf16[768,128]{1,0:T(8,128)(2,1)S(1)}, bf16[768,128]{1,0:T(8,128)(2,1)S(1)}, u32[]{:S(2)}, u32[]{:S(2)}) collective-permute-start(bf16[768,128]{1,0:T(8,128)(2,1)S(1)} %get-tuple-element.71), channel_id=1, source_target_pairs={{0,6},{2,4},{4,2},{6,0},{1,7},{3,5},{5,3},{7,1},{8,14},{10,12},{12... | collective-permute-start | bytes 589832 | tf_op jit(solution)/shard_map/ppermute | solution.py:642
  137.3 0.0 copy-start.1
  137.3 0.6 pick_all.1.pick_ref
  137.9 0.0 collective-permute-done.9.refs_0_
  137.9 3.8 %collective-permute-done.10.refs_1_ = bf16[768,128]{1,0:T(8,128)(2,1)S(1)} collective-permute-done((bf16[768,128]{1,0:T(8,128)(2,1)S(1)}, bf16[768,128]{1,0:T(8,128)(2,1)S(1)}, u32[]{:S(2)}, u32[]{:S(2)}) %collective-permute-start.10) | collective-permute-done | bytes 196640 | tf_op jit(solution)/shard_map/ppermute | solution.py:642
  141.6 5.2 %collective-permute-done.11.refs_2_ = bf16[768,128]{1,0:T(8,128)(2,1)S(1)} collective-permute-done((bf16[768,128]{1,0:T(8,128)(2,1)S(1)}, bf16[768,128]{1,0:T(8,128)(2,1)S(1)}, u32[]{:S(2)}, u32[]{:S(2)}) %collective-permute-start.11) | collective-permute-done | bytes 196640 | tf_op jit(solution)/shard_map/ppermute | solution.py:642
  146.9 0.0 copy-done.1
  146.9 0.9 base_sum.1.base_ref
  147.8 0.0 all-to-all-done.7
  147.8 0.0 copy-start.6
  147.8 2.4 %take_main.1 = (bf16[768,128]{1,0:T(8,128)(2,1)S(1)}, s32[1]{0:T(128)}) custom-call(bf16[768,1536]{1,0:T(8,128)(2,1)S(1)} %pick_all.1.pick_ref, bf16[1536,128]{1,0:T(8,128)(2,1)S(1)} %bitcast.22, f32[768,128]{1,0:T(8,128)} %base_sum.1.base_ref), custom_call_target="tpu_custom_call" | custom-call | tf_op jit(solution)/shard_map/take_main/pallas_call | solution.py:555
  150.8 0.0 copy-done.7
  150.8 0.0 copy-done.9
  150.8 0.0 copy-done.4
  150.9 0.0 copy-done.6
  150.9 0.2 conditional.1
  151.1 0.0 copy-start.11
  151.1 0.7 copy-done.11
  (9 shorter events, 0.1 us)
Async XLA Ops:
  0.0 11.0 %copy-start.3 = (bf16[768,1024]{1,0:T(8,128)(2,1)S(1)}, bf16[768,1024]{1,0:T(8,128)(2,1)}, u32[]{:S(2)}) copy-start(bf16[768,1024]{1,0:T(8,128)(2,1)} %tok_ref.5) | copy-start | bytes 4718596
  0.0 11.0 %copy-start.10 = (s32[768,1]{0,1:T(1,128)S(1)}, s32[768,1]{0,1:T(1,128)}, u32[]{:S(2)}) copy-start(s32[768,1]{0,1:T(1,128)} %param.11) | copy-start | bytes 9220
  3.4 17.1 %all-to-all-start.4 = ((bf16[8,16,1024]{2,1,0:T(8,128)(2,1)}), bf16[8,16,1024]{2,1,0:T(8,128)(2,1)S(1)}, u32[]{:S(2)}, u32[]{:S(2)}) async-start(bf16[8,16,1024]{2,1,0:T(8,128)(2,1)} %bitcast.10), calls=%async_computation.4 | async-start | bytes 524288 | tf_op jit(solution)/shard_map/all_to_all | solution.py:23
  20.4 64.5 %all-to-all-start.5 = ((bf16[64,16,1024]{2,1,0:T(8,128)(2,1)}), bf16[64,16,1024]{2,1,0:T(8,128)(2,1)S(1)}, u32[]{:S(2)}, u32[]{:S(2)}) async-start(bf16[64,16,1024]{2,1,0:T(8,128)(2,1)} %bitcast.12), calls=%async_computation.5 | async-start | bytes 4194304 | tf_op jit(solution)/shard_map/all_to_all | solution.py:23
  34.2 18.2 %collective-permute-start = (bf16[16,1024]{1,0:T(8,128)(2,1)S(1)}, bf16[16,1024]{1,0:T(8,128)(2,1)S(1)}, u32[]{:S(2)}, u32[]{:S(2)}) collective-permute-start(bf16[16,1024]{1,0:T(8,128)(2,1)S(1)} %get-tuple-element.56), channel_id=1, source_target_pairs={{0,64},{64,0},{128,192},{192,128},{256,320},{320,256},{384,448},{4... | collective-permute-start | bytes 98312 | tf_op jit(solution)/shard_map/ppermute | solution.py:642
  37.1 45.6 %collective-permute-start.1 = (bf16[16,1024]{1,0:T(8,128)(2,1)S(1)}, bf16[16,1024]{1,0:T(8,128)(2,1)S(1)}, u32[]{:S(2)}, u32[]{:S(2)}) collective-permute-start(bf16[16,1024]{1,0:T(8,128)(2,1)S(1)} %get-tuple-element.57), channel_id=1, source_target_pairs={{0,128},{64,192},{128,0},{192,64},{256,384},{320,448},{384,256},{4... | collective-permute-start | bytes 98312 | tf_op jit(solution)/shard_map/ppermute | solution.py:642
  41.2 46.5 %collective-permute-start.2 = (bf16[16,1024]{1,0:T(8,128)(2,1)S(1)}, bf16[16,1024]{1,0:T(8,128)(2,1)S(1)}, u32[]{:S(2)}, u32[]{:S(2)}) collective-permute-start(bf16[16,1024]{1,0:T(8,128)(2,1)S(1)} %get-tuple-element.58), channel_id=1, source_target_pairs={{0,192},{64,128},{128,64},{192,0},{256,448},{320,384},{384,320},{4... | collective-permute-start | bytes 98312 | tf_op jit(solution)/shard_map/ppermute | solution.py:642
  43.5 44.2 %collective-permute-start.3 = (bf16[16,1024]{1,0:T(8,128)(2,1)S(1)}, bf16[16,1024]{1,0:T(8,128)(2,1)S(1)}, u32[]{:S(2)}, u32[]{:S(2)}) collective-permute-start(bf16[16,1024]{1,0:T(8,128)(2,1)S(1)} %get-tuple-element.59), channel_id=1, source_target_pairs={{0,256},{64,320},{128,384},{192,448},{256,0},{320,64},{384,128},{4... | collective-permute-start | bytes 98312 | tf_op jit(solution)/shard_map/ppermute | solution.py:642
  50.4 39.2 %collective-permute-start.4 = (bf16[16,1024]{1,0:T(8,128)(2,1)S(1)}, bf16[16,1024]{1,0:T(8,128)(2,1)S(1)}, u32[]{:S(2)}, u32[]{:S(2)}) collective-permute-start(bf16[16,1024]{1,0:T(8,128)(2,1)S(1)} %get-tuple-element.60), channel_id=1, source_target_pairs={{0,320},{64,256},{128,448},{192,384},{256,64},{320,0},{384,192},{4... | collective-permute-start | bytes 98312 | tf_op jit(solution)/shard_map/ppermute | solution.py:642
  52.4 37.3 %collective-permute-start.5 = (bf16[16,1024]{1,0:T(8,128)(2,1)S(1)}, bf16[16,1024]{1,0:T(8,128)(2,1)S(1)}, u32[]{:S(2)}, u32[]{:S(2)}) collective-permute-start(bf16[16,1024]{1,0:T(8,128)(2,1)S(1)} %get-tuple-element.61), channel_id=1, source_target_pairs={{0,384},{64,448},{128,256},{192,320},{256,128},{320,192},{384,0},{... | collective-permute-start | bytes 98312 | tf_op jit(solution)/shard_map/ppermute | solution.py:642
  82.8 6.9 %collective-permute-start.6 = (bf16[16,1024]{1,0:T(8,128)(2,1)S(1)}, bf16[16,1024]{1,0:T(8,128)(2,1)S(1)}, u32[]{:S(2)}, u32[]{:S(2)}) collective-permute-start(bf16[16,1024]{1,0:T(8,128)(2,1)S(1)} %get-tuple-element.62), channel_id=1, source_target_pairs={{0,448},{64,384},{128,320},{192,256},{256,192},{320,128},{384,64},... | collective-permute-start | bytes 98312 | tf_op jit(solution)/shard_map/ppermute | solution.py:642
  85.0 4.7 %copy-start.5 = (bf16[8,64,1024]{2,1,0:T(8,128)(2,1)S(1)}, bf16[8,64,1024]{2,1,0:T(8,128)(2,1)}, u32[]{:S(2)}) copy-start(bf16[8,64,1024]{2,1,0:T(8,128)(2,1)} %refs_8_.1) | copy-start | bytes 3145732
  87.6 16.9 %copy-start.2 = (bf16[1024,1024]{1,0:T(8,128)(2,1)S(1)}, bf16[1024,1024]{1,0:T(8,128)(2,1)}, u32[]{:S(2)}) copy-start(bf16[1024,1024]{1,0:T(8,128)(2,1)} %w_ref.1) | copy-start | bytes 6291460
  90.8 9.0 %collective-permute-start.7 = (bf16[288,128]{1,0:T(8,128)(2,1)S(1)}, bf16[288,128]{1,0:T(8,128)(2,1)S(1)}, u32[]{:S(2)}, u32[]{:S(2)}) collective-permute-start(bf16[288,128]{1,0:T(8,128)(2,1)S(1)} %get-tuple-element.64), channel_id=1, source_target_pairs={{0,1},{1,0},{2,3},{3,2},{4,5},{5,4},{6,7},{7,6},{8,9},{9,8},{10,11... | collective-permute-start | bytes 221192 | tf_op jit(solution)/shard_map/ppermute | solution.py:577
  100.6 10.8 %all-to-all-start.6 = ((bf16[4,288,128]{2,1,0:T(8,128)(2,1)}), bf16[4,288,128]{2,1,0:T(8,128)(2,1)S(1)}, u32[]{:S(2)}, u32[]{:S(2)}) async-start(bf16[4,288,128]{2,1,0:T(8,128)(2,1)} %broadcast_in_dim.4), calls=%async_computation.6 | async-start | bytes 589824 | tf_op jit(solution)/shard_map/all_to_all | solution.py:23
  104.6 9.6 %copy-start.8 = (bf16[8,64,128]{2,1,0:T(8,128)(2,1)S(1)}, bf16[8,64,128]{2,1,0:T(8,128)(2,1)}, u32[]{:S(2)}) copy-start(bf16[8,64,128]{2,1,0:T(8,128)(2,1)} %up_ref.1) | copy-start | bytes 393220
  108.8 18.7 %collective-permute-start.8 = (bf16[4,768,128]{2,1,0:T(8,128)(2,1)}, bf16[4,768,128]{2,1,0:T(8,128)(2,1)S(1)}, u32[]{:S(2)}, u32[]{:S(2)}) collective-permute-start(bf16[4,768,128]{2,1,0:T(8,128)(2,1)} %get-tuple-element.68), channel_id=1, source_target_pairs={{0,1},{1,0},{2,3},{3,2},{4,5},{5,4},{6,7},{7,6},{8,9},{9,8},{10,11... | collective-permute-start | bytes 2359304 | tf_op jit(solution)/shard_map/ppermute | solution.py:614
  115.7 32.1 %all-to-all-start.7 = ((bf16[64,24,128]{2,1,0:T(8,128)(2,1)}), bf16[64,24,128]{2,1,0:T(8,128)(2,1)S(1)}, u32[]{:S(2)}, u32[]{:S(2)}) async-start(bf16[64,24,128]{2,1,0:T(8,128)(2,1)} %bitcast.14), calls=%async_computation.7 | async-start | bytes 786432 | tf_op jit(solution)/shard_map/all_to_all | solution.py:23
  127.5 7.5 %copy-start = (bf16[4,768,128]{2,1,0:T(8,128)(2,1)}, bf16[4,768,128]{2,1,0:T(8,128)(2,1)S(1)}, u32[]{:S(2)}) copy-start(bf16[4,768,128]{2,1,0:T(8,128)(2,1)S(1)} %collective-permute-done.8.other_ref) | copy-start | bytes 2359300
  127.7 10.2 %collective-permute-start.9 = (bf16[768,128]{1,0:T(8,128)(2,1)S(1)}, bf16[768,128]{1,0:T(8,128)(2,1)S(1)}, u32[]{:S(2)}, u32[]{:S(2)}) collective-permute-start(bf16[768,128]{1,0:T(8,128)(2,1)S(1)} %get-tuple-element.69), channel_id=1, source_target_pairs={{0,2},{2,0},{4,6},{6,4},{1,3},{3,1},{5,7},{7,5},{8,10},{10,8},{12,... | collective-permute-start | bytes 589832 | tf_op jit(solution)/shard_map/ppermute | solution.py:642
  130.7 10.9 %collective-permute-start.10 = (bf16[768,128]{1,0:T(8,128)(2,1)S(1)}, bf16[768,128]{1,0:T(8,128)(2,1)S(1)}, u32[]{:S(2)}, u32[]{:S(2)}) collective-permute-start(bf16[768,128]{1,0:T(8,128)(2,1)S(1)} %get-tuple-element.70), channel_id=1, source_target_pairs={{0,4},{2,6},{4,0},{6,2},{1,5},{3,7},{5,1},{7,3},{8,12},{10,14},{12... | collective-permute-start | bytes 589832 | tf_op jit(solution)/shard_map/ppermute | solution.py:642
  135.0 11.8 %collective-permute-start.11 = (bf16[768,128]{1,0:T(8,128)(2,1)S(1)}, bf16[768,128]{1,0:T(8,128)(2,1)S(1)}, u32[]{:S(2)}, u32[]{:S(2)}) collective-permute-start(bf16[768,128]{1,0:T(8,128)(2,1)S(1)} %get-tuple-element.71), channel_id=1, source_target_pairs={{0,6},{2,4},{4,2},{6,0},{1,7},{3,5},{5,3},{7,1},{8,14},{10,12},{12... | collective-permute-start | bytes 589832 | tf_op jit(solution)/shard_map/ppermute | solution.py:642
  137.3 9.6 %copy-start.1 = (bf16[4,768,128]{2,1,0:T(8,128)(2,1)S(1)}, bf16[4,768,128]{2,1,0:T(8,128)(2,1)}, u32[]{:S(2)}) copy-start(bf16[4,768,128]{2,1,0:T(8,128)(2,1)} %copy-done) | copy-start | bytes 2359300
  147.8 3.1 %copy-start.7 = (f32[768,128]{1,0:T(8,128)S(1)}, f32[768,128]{1,0:T(8,128)}, u32[]{:S(2)}) copy-start(f32[768,128]{1,0:T(8,128)} %base_sum.1.base_ref) | copy-start | bytes 1179652
  147.8 3.1 %copy-start.9 = (bf16[8,64,128]{2,1,0:T(8,128)(2,1)S(1)}, bf16[8,64,128]{2,1,0:T(8,128)(2,1)}, u32[]{:S(2)}) copy-start(bf16[8,64,128]{2,1,0:T(8,128)(2,1)} %up_ref.1) | copy-start | bytes 393220
  147.8 3.1 %copy-start.4 = (bf16[768,1024]{1,0:T(8,128)(2,1)S(1)}, bf16[768,1024]{1,0:T(8,128)(2,1)}, u32[]{:S(2)}) copy-start(bf16[768,1024]{1,0:T(8,128)(2,1)} %tok_ref.5) | copy-start | bytes 4718596
  147.8 3.1 %copy-start.6 = (bf16[8,64,1024]{2,1,0:T(8,128)(2,1)S(1)}, bf16[8,64,1024]{2,1,0:T(8,128)(2,1)}, u32[]{:S(2)}) copy-start(bf16[8,64,1024]{2,1,0:T(8,128)(2,1)} %refs_8_.1) | copy-start | bytes 3145732
  151.1 0.7 copy-start.11

commit v10 on v9

--- a/solution.py
+++ b/solution.py
@@ -523,7 +523,7 @@
     )(low, slot, flag, up)
 
 
-def pick_all(ids_row, seen, slots):
+def answer_slots(ids_row, seen):
     rows = ids_row.shape[1]
 
     def kernel(row_ref, seen_ref, out_ref):
@@ -533,22 +533,24 @@
         back = row // HERE * (HERE * MOST) + jnp.where(
             seen < MAIN, spot * MAIN + seen, HERE * MAIN + spot
         )
+        out_ref[...] = to_col(back)
+
+    return pl.pallas_call(
+        kernel,
+        out_shape=jax.ShapeDtypeStruct((rows, 1), jnp.int32),
+        compiler_params=GRANT,
+        name="answer_slots",
+    )(ids_row, seen)
+
+
+def take_main(at_col, back, base):
+    rows, cols = base.shape
+    slots = back.shape[0]
+
+    def kernel(at_ref, back_ref, base_ref, out_ref, lost_ref):
         slot = lax.broadcasted_iota(jnp.int32, (rows, slots), 1)
-        out_ref[...] = jnp.where(slot == to_col(back), 1.0, 0.0).astype(jnp.bfloat16)
-
-    return pl.pallas_call(
-        kernel,
-        out_shape=jax.ShapeDtypeStruct((rows, slots), jnp.bfloat16),
-        compiler_params=GRANT,
-        name="pick_all",
-    )(ids_row, seen)
-
-
-def take_main(pick, back, base):
-    rows, cols = base.shape
-
-    def kernel(pick_ref, back_ref, base_ref, out_ref, lost_ref):
-        mine = jnp.dot(pick_ref[...], back_ref[...], preferred_element_type=jnp.float32)
+        pick = jnp.where(slot == at_ref[...], 1.0, 0.0).astype(jnp.bfloat16)
+        mine = jnp.dot(pick, back_ref[...], preferred_element_type=jnp.float32)
         out_ref[...] = (base_ref[...] + mine).astype(jnp.bfloat16)
         lost_ref[0] = (jnp.max(back_ref[...].astype(jnp.float32)) > LOST / 2).astype(jnp.int32)
 
@@ -561,7 +563,7 @@
         ],
         compiler_params=GRANT,
         name="take_main",
-    )(pick, back, base)
+    )(at_col, back, base)
 
 
 def low_of_all(low_part, groups):
@@ -604,6 +606,7 @@
     blocks, seen = side_first(ids_row, tokens)
     blocks = swap(blocks.reshape(8, SIDE, width), "y").reshape(8 * SIDE, width)
     placed = place_main(ids_row, seen, tokens, 64 * HERE * MAIN)
+    at_col = answer_slots(ids_row, seen)
     arrived = swap(placed.reshape(64, HERE * MAIN, width), ADAPTER)
     arrived = arrived.reshape(64 * HERE * MAIN, width)
 
@@ -623,11 +626,10 @@
     delta = up_main(low, slot, flag, adapter_up_weight)
     back = swap(delta.reshape(64, HERE * MOST, cols), ADAPTER)
     back = back.reshape(64 * HERE * MOST, cols)
-    pick = pick_all(ids_row, seen, 64 * HERE * MOST)
     back, *whole = lax.optimization_barrier(
         (back, tokens, adapter_down, adapter_up_weight, adapter_ids, base)
     )
-    values, lost = take_main(pick, back, base)
+    values, lost = take_main(at_col, back, base)
     return lax.cond(
         lost[0] > 0,
         lambda: whole_exchange(*whole),

time: 153 us -> 151 us (0.987)
  Pallas kernels: 20.8 us -> 18.7 us
where the time goes in v10:
time: 151 us; the launch traced here: 150 us
  starting transfers between devices  108 us (72%)
  Pallas kernels  18.7 us (12%)
  waiting for transfers between devices  18.4 us (12%)
  blocking collectives  2.73 us (2%)
    ppermute x10, starting transfers between devices, xor_sends(): lax.ppermute(pieces[k], axis, [(i, i ^ k) for i in range(size)])  60.2 us
    all_to_all x4, starting transfers between devices, swap(): return lax.all_to_all(x, axes, split_axis=0, concat_axis=0, tiled=True)  36.7 us
    ppermute x10, waiting for transfers between devices, xor_sends(): lax.ppermute(pieces[k], axis, [(i, i ^ k) for i in range(size)])  11.4 us
    ppermute x1, starting transfers between devices, low_of_pairs(): lax.ppermute(other, TENSOR[1], [(0, 1), (1, 0)]).astype(jnp.float32)  8.09 us
    all_to_all x4, waiting for transfers between devices, swap(): return lax.all_to_all(x, axes, split_axis=0, concat_axis=0, tiled=True)  6.07 us
    pallas_call x1, Pallas kernels, value_pieces(): pl.pallas_call(kernel, in_specs=[pl.BlockSpec(memory_space=pltpu.SMEM), p...  4.25 us
    pallas_call x1, Pallas kernels, side_first(): pl.pallas_call(kernel, out_shape=[jax.ShapeDtypeStruct((8 * SIDE, width),...  3.37 us
    pallas_call x1, Pallas kernels, place_main(): pl.pallas_call(kernel, grid=(slots // tile,), in_specs=[pl.BlockSpec((1,...  3.36 us
  transfers between devices with their start and end apart: 16, of which 5 were waited for; matrix products, arithmetic and copies ran while one was open for 0% of the time, Pallas kernels for 9%

profile of v10, /device:TPU:1, one launch (start us, length us, event | category | flops | bytes accessed | tf_op | source)
XLA Modules:
  0.0 150.1 jit_solution(8967564030375366401)
XLA Ops:
  0.0 0.0 copy-start.1
  0.0 0.0 copy-start.5
  0.0 3.4 %side_first.1 = (bf16[128,1024]{1,0:T(8,128)(2,1)}, s32[1,768]{1,0:T(1,128)S(1)}) custom-call(s32[1,768]{1,0:T(1,128)} %bitcast.28, bf16[768,1024]{1,0:T(8,128)(2,1)} %tok_ref.5), custom_call_target="tpu_custom_call" | custom-call | tf_op jit(solution)/shard_map/side_first/pallas_call | solution.py:342
  3.4 7.6 %all-to-all-start.4 = ((bf16[8,16,1024]{2,1,0:T(8,128)(2,1)}), bf16[8,16,1024]{2,1,0:T(8,128)(2,1)S(1)}, u32[]{:S(2)}, u32[]{:S(2)}) async-start(bf16[8,16,1024]{2,1,0:T(8,128)(2,1)} %bitcast.10), calls=%async_computation.4 | async-start | bytes 524288 | tf_op jit(solution)/shard_map/all_to_all | solution.py:23
  11.0 0.0 copy-done.1
  11.0 0.0 copy-done.5
  11.0 3.4 %place_main.1 = bf16[1024,1024]{1,0:T(8,128)(2,1)} custom-call(s32[1,768]{1,0:T(1,128)S(1)} %bitcast.29, s32[1,768]{1,0:T(1,128)S(1)} %get-tuple-element.53.seen_ref, bf16[768,1024]{1,0:T(8,128)(2,1)S(1)} %copy-done.1), custom_call_target="tpu_custom_call" | custom-call | tf_op jit(solution)/shard_map/place_main/pallas_call | solution.py:265
  14.4 6.1 %all-to-all-done.4 = bf16[8,16,1024]{2,1,0:T(8,128)(2,1)S(1)} async-done(((bf16[8,16,1024]{2,1,0:T(8,128)(2,1)}), bf16[8,16,1024]{2,1,0:T(8,128)(2,1)S(1)}, u32[]{:S(2)}, u32[]{:S(2)}) %all-to-all-start.4) | async-done | bytes 262176 | tf_op jit(solution)/shard_map/all_to_all | solution.py:23
  20.4 13.2 %all-to-all-start.5 = ((bf16[64,16,1024]{2,1,0:T(8,128)(2,1)}), bf16[64,16,1024]{2,1,0:T(8,128)(2,1)S(1)}, u32[]{:S(2)}, u32[]{:S(2)}) async-start(bf16[64,16,1024]{2,1,0:T(8,128)(2,1)} %bitcast.12), calls=%async_computation.5 | async-start | bytes 4194304 | tf_op jit(solution)/shard_map/all_to_all | solution.py:23
  33.7 0.5 side_second.1
  34.2 2.9 %collective-permute-start = (bf16[16,1024]{1,0:T(8,128)(2,1)S(1)}, bf16[16,1024]{1,0:T(8,128)(2,1)S(1)}, u32[]{:S(2)}, u32[]{:S(2)}) collective-permute-start(bf16[16,1024]{1,0:T(8,128)(2,1)S(1)} %get-tuple-element.56), channel_id=1, source_target_pairs={{0,64},{64,0},{128,192},{192,128},{256,320},{320,256},{384,448},{4... | collective-permute-start | bytes 98312 | tf_op jit(solution)/shard_map/ppermute | solution.py:644
  37.1 4.0 %collective-permute-start.1 = (bf16[16,1024]{1,0:T(8,128)(2,1)S(1)}, bf16[16,1024]{1,0:T(8,128)(2,1)S(1)}, u32[]{:S(2)}, u32[]{:S(2)}) collective-permute-start(bf16[16,1024]{1,0:T(8,128)(2,1)S(1)} %get-tuple-element.57), channel_id=1, source_target_pairs={{0,128},{64,192},{128,0},{192,64},{256,384},{320,448},{384,256},{4... | collective-permute-start | bytes 98312 | tf_op jit(solution)/shard_map/ppermute | solution.py:644
  41.2 2.3 %collective-permute-start.2 = (bf16[16,1024]{1,0:T(8,128)(2,1)S(1)}, bf16[16,1024]{1,0:T(8,128)(2,1)S(1)}, u32[]{:S(2)}, u32[]{:S(2)}) collective-permute-start(bf16[16,1024]{1,0:T(8,128)(2,1)S(1)} %get-tuple-element.58), channel_id=1, source_target_pairs={{0,192},{64,128},{128,64},{192,0},{256,448},{320,384},{384,320},{4... | collective-permute-start | bytes 98312 | tf_op jit(solution)/shard_map/ppermute | solution.py:644
  43.5 6.9 %collective-permute-start.3 = (bf16[16,1024]{1,0:T(8,128)(2,1)S(1)}, bf16[16,1024]{1,0:T(8,128)(2,1)S(1)}, u32[]{:S(2)}, u32[]{:S(2)}) collective-permute-start(bf16[16,1024]{1,0:T(8,128)(2,1)S(1)} %get-tuple-element.59), channel_id=1, source_target_pairs={{0,256},{64,320},{128,384},{192,448},{256,0},{320,64},{384,128},{4... | collective-permute-start | bytes 98312 | tf_op jit(solution)/shard_map/ppermute | solution.py:644
  50.4 1.9 %collective-permute-start.4 = (bf16[16,1024]{1,0:T(8,128)(2,1)S(1)}, bf16[16,1024]{1,0:T(8,128)(2,1)S(1)}, u32[]{:S(2)}, u32[]{:S(2)}) collective-permute-start(bf16[16,1024]{1,0:T(8,128)(2,1)S(1)} %get-tuple-element.60), channel_id=1, source_target_pairs={{0,320},{64,256},{128,448},{192,384},{256,64},{320,0},{384,192},{4... | collective-permute-start | bytes 98312 | tf_op jit(solution)/shard_map/ppermute | solution.py:644
  52.4 0.0 collective-permute-done.refs_1_
  52.4 30.4 %collective-permute-start.5 = (bf16[16,1024]{1,0:T(8,128)(2,1)S(1)}, bf16[16,1024]{1,0:T(8,128)(2,1)S(1)}, u32[]{:S(2)}, u32[]{:S(2)}) collective-permute-start(bf16[16,1024]{1,0:T(8,128)(2,1)S(1)} %get-tuple-element.61), channel_id=1, source_target_pairs={{0,384},{64,448},{128,256},{192,320},{256,128},{320,192},{384,0},{... | collective-permute-start | bytes 98312 | tf_op jit(solution)/shard_map/ppermute | solution.py:644
  82.8 0.0 collective-permute-done.1.refs_2_
  82.8 2.1 %collective-permute-start.6 = (bf16[16,1024]{1,0:T(8,128)(2,1)S(1)}, bf16[16,1024]{1,0:T(8,128)(2,1)S(1)}, u32[]{:S(2)}, u32[]{:S(2)}) collective-permute-start(bf16[16,1024]{1,0:T(8,128)(2,1)S(1)} %get-tuple-element.62), channel_id=1, source_target_pairs={{0,448},{64,384},{128,320},{192,256},{256,192},{320,128},{384,64},... | collective-permute-start | bytes 98312 | tf_op jit(solution)/shard_map/ppermute | solution.py:644
  84.9 0.1 pad_add_fusion.at_ref
  85.0 0.0 all-to-all-done.5
  85.0 0.0 copy-start.2
  85.0 2.7 %down_main.1.refs_9_ = bf16[512,128]{1,0:T(8,128)(2,1)S(1)} custom-call(bf16[1024,1024]{1,0:T(8,128)(2,1)S(1)} %bitcast.20, bf16[8,64,1024]{2,1,0:T(8,128)(2,1)} %refs_8_.1), custom_call_target="tpu_custom_call" | custom-call | tf_op jit(solution)/shard_map/down_main/pallas_call | solution.py:414
  87.7 0.0 copy-start
  87.7 0.0 collective-permute-done.2.refs_3_
  87.7 0.0 collective-permute-done.3.refs_4_
  87.7 2.0 %collective-permute-done.4.refs_5_ = bf16[16,1024]{1,0:T(8,128)(2,1)S(1)} collective-permute-done((bf16[16,1024]{1,0:T(8,128)(2,1)S(1)}, bf16[16,1024]{1,0:T(8,128)(2,1)S(1)}, u32[]{:S(2)}, u32[]{:S(2)}) %collective-permute-start.4) | collective-permute-done | bytes 32800 | tf_op jit(solution)/shard_map/ppermute | solution.py:644
  89.7 0.0 collective-permute-done.5.refs_6_
  89.7 0.0 collective-permute-done.6.refs_7_
  89.7 0.0 copy-done.2
  89.7 1.1 side_low.1
  90.8 8.1 %collective-permute-start.7 = (bf16[288,128]{1,0:T(8,128)(2,1)S(1)}, bf16[288,128]{1,0:T(8,128)(2,1)S(1)}, u32[]{:S(2)}, u32[]{:S(2)}) collective-permute-start(bf16[288,128]{1,0:T(8,128)(2,1)S(1)} %get-tuple-element.64), channel_id=1, source_target_pairs={{0,1},{1,0},{2,3},{3,2},{4,5},{5,4},{6,7},{7,6},{8,9},{9,8},{10,11... | collective-permute-start | bytes 221192 | tf_op jit(solution)/shard_map/ppermute | solution.py:579
  98.9 0.9 collective-permute-done.7
  99.8 0.8 broadcast_in_dim.4
  100.6 4.0 %all-to-all-start.6 = ((bf16[4,288,128]{2,1,0:T(8,128)(2,1)}), bf16[4,288,128]{2,1,0:T(8,128)(2,1)S(1)}, u32[]{:S(2)}, u32[]{:S(2)}) async-start(bf16[4,288,128]{2,1,0:T(8,128)(2,1)} %broadcast_in_dim.4), calls=%async_computation.6 | async-start | bytes 589824 | tf_op jit(solution)/shard_map/all_to_all | solution.py:23
  104.6 0.0 copy-done
  104.6 0.0 copy-start.4
  104.6 4.3 %value_pieces.1 = (bf16[4,768,128]{2,1,0:T(8,128)(2,1)S(1)}, bf16[4,768,128]{2,1,0:T(8,128)(2,1)}) custom-call(s32[1]{0:T(128)} %bitcast.16.at_ref, bf16[768,1024]{1,0:T(8,128)(2,1)} %tok_ref.5, bf16[1024,1024]{1,0:T(8,128)(2,1)S(1)} %copy-done), custom_call_target="tpu_custom_call" | custom-call | tf_op jit(solution)/shard_map/value_pieces/pallas_call | solution.py:89
  108.9 2.5 %collective-permute-start.8 = (bf16[4,768,128]{2,1,0:T(8,128)(2,1)}, bf16[4,768,128]{2,1,0:T(8,128)(2,1)S(1)}, u32[]{:S(2)}, u32[]{:S(2)}) collective-permute-start(bf16[4,768,128]{2,1,0:T(8,128)(2,1)} %get-tuple-element.68), channel_id=1, source_target_pairs={{0,1},{1,0},{2,3},{3,2},{4,5},{5,4},{6,7},{7,6},{8,9},{9,8},{10,11... | collective-permute-start | bytes 2359304 | tf_op jit(solution)/shard_map/ppermute | solution.py:617
  111.4 0.0 all-to-all-done.6.in_ref
  111.5 2.7 %all_gather.3.low_ref = bf16[576,128]{1,0:T(8,128)(2,1)S(1)} all-gather(bf16[288,128]{1,0:T(8,128)(2,1)S(1)} %chip_sum.1), channel_id=1, replica_groups=mesh['z'=8,'y'=8,'tensor_0'=4,'tensor_1'=2] {'tensor_1'}, dimensions={0}, use_global_device_ids=true | all-gather | bytes 221184 | tf_op jit(solution)/shard_map/all_gather | solution.py:583
  114.2 0.0 copy-done.4
  114.2 1.5 %up_main.1 = bf16[1536,128]{1,0:T(8,128)(2,1)} custom-call(bf16[576,128]{1,0:T(8,128)(2,1)S(1)} %all_gather.3.low_ref, s32[1,128]{1,0:T(1,128)S(1)} %get-tuple-element.65.slot_ref, f32[8,128]{1,0:T(8,128)S(1)} %get-tuple-element.66.flag_ref, bf16[8,64,128]{2,1,0:T(8,128)(2,1)S(1)} %copy-done.4), custom_call_target="tpu_custom_call" | custom-call | tf_op jit(solution)/shard_map/up_main/pallas_call | solution.py:518
  115.7 11.8 %all-to-all-start.7 = ((bf16[64,24,128]{2,1,0:T(8,128)(2,1)}), bf16[64,24,128]{2,1,0:T(8,128)(2,1)S(1)}, u32[]{:S(2)}, u32[]{:S(2)}) async-start(bf16[64,24,128]{2,1,0:T(8,128)(2,1)} %bitcast.14), calls=%async_computation.7 | async-start | bytes 786432 | tf_op jit(solution)/shard_map/all_to_all | solution.py:23
  127.5 0.0 collective-permute-done.8.other_ref
  127.5 0.1 pair_sum.1
  127.7 3.1 %collective-permute-start.9 = (bf16[768,128]{1,0:T(8,128)(2,1)S(1)}, bf16[768,128]{1,0:T(8,128)(2,1)S(1)}, u32[]{:S(2)}, u32[]{:S(2)}) collective-permute-start(bf16[768,128]{1,0:T(8,128)(2,1)S(1)} %get-tuple-element.69), channel_id=1, source_target_pairs={{0,2},{2,0},{4,6},{6,4},{1,3},{3,1},{5,7},{7,5},{8,10},{10,8},{12,... | collective-permute-start | bytes 589832 | tf_op jit(solution)/shard_map/ppermute | solution.py:644
  130.8 4.3 %collective-permute-start.10 = (bf16[768,128]{1,0:T(8,128)(2,1)S(1)}, bf16[768,128]{1,0:T(8,128)(2,1)S(1)}, u32[]{:S(2)}, u32[]{:S(2)}) collective-permute-start(bf16[768,128]{1,0:T(8,128)(2,1)S(1)} %get-tuple-element.70), channel_id=1, source_target_pairs={{0,4},{2,6},{4,0},{6,2},{1,5},{3,7},{5,1},{7,3},{8,12},{10,14},{12... | collective-permute-start | bytes 589832 | tf_op jit(solution)/shard_map/ppermute | solution.py:644
  135.1 2.2 %collective-permute-start.11 = (bf16[768,128]{1,0:T(8,128)(2,1)S(1)}, bf16[768,128]{1,0:T(8,128)(2,1)S(1)}, u32[]{:S(2)}, u32[]{:S(2)}) collective-permute-start(bf16[768,128]{1,0:T(8,128)(2,1)S(1)} %get-tuple-element.71), channel_id=1, source_target_pairs={{0,6},{2,4},{4,2},{6,0},{1,7},{3,5},{5,3},{7,1},{8,14},{10,12},{12... | collective-permute-start | bytes 589832 | tf_op jit(solution)/shard_map/ppermute | solution.py:644
  137.3 0.2 answer_slots.1.at_ref
  137.5 0.0 collective-permute-done.9.refs_0_
  137.5 4.2 %collective-permute-done.10.refs_1_ = bf16[768,128]{1,0:T(8,128)(2,1)S(1)} collective-permute-done((bf16[768,128]{1,0:T(8,128)(2,1)S(1)}, bf16[768,128]{1,0:T(8,128)(2,1)S(1)}, u32[]{:S(2)}, u32[]{:S(2)}) %collective-permute-start.10) | collective-permute-done | bytes 196640 | tf_op jit(solution)/shard_map/ppermute | solution.py:644
  141.7 5.2 %collective-permute-done.11.refs_2_ = bf16[768,128]{1,0:T(8,128)(2,1)S(1)} collective-permute-done((bf16[768,128]{1,0:T(8,128)(2,1)S(1)}, bf16[768,128]{1,0:T(8,128)(2,1)S(1)}, u32[]{:S(2)}, u32[]{:S(2)}) %collective-permute-start.11) | collective-permute-done | bytes 196640 | tf_op jit(solution)/shard_map/ppermute | solution.py:644
  146.9 0.1 base_sum.1.base_ref
  147.0 0.0 all-to-all-done.7
  147.1 1.5 take_main.1
  149.2 0.2 conditional.1
  149.4 0.0 copy-start.6
  149.4 0.7 copy-done.6
  (2 shorter events, 0.1 us)
Async XLA Ops:
  0.0 11.0 %copy-start.1 = (bf16[768,1024]{1,0:T(8,128)(2,1)S(1)}, bf16[768,1024]{1,0:T(8,128)(2,1)}, u32[]{:S(2)}) copy-start(bf16[768,1024]{1,0:T(8,128)(2,1)} %tok_ref.5) | copy-start | bytes 4718596
  0.0 11.0 %copy-start.5 = (s32[768,1]{0,1:T(1,128)S(1)}, s32[768,1]{0,1:T(1,128)}, u32[]{:S(2)}) copy-start(s32[768,1]{0,1:T(1,128)} %param.11) | copy-start | bytes 9220
  3.4 17.1 %all-to-all-start.4 = ((bf16[8,16,1024]{2,1,0:T(8,128)(2,1)}), bf16[8,16,1024]{2,1,0:T(8,128)(2,1)S(1)}, u32[]{:S(2)}, u32[]{:S(2)}) async-start(bf16[8,16,1024]{2,1,0:T(8,128)(2,1)} %bitcast.10), calls=%async_computation.4 | async-start | bytes 524288 | tf_op jit(solution)/shard_map/all_to_all | solution.py:23
  20.4 64.5 %all-to-all-start.5 = ((bf16[64,16,1024]{2,1,0:T(8,128)(2,1)}), bf16[64,16,1024]{2,1,0:T(8,128)(2,1)S(1)}, u32[]{:S(2)}, u32[]{:S(2)}) async-start(bf16[64,16,1024]{2,1,0:T(8,128)(2,1)} %bitcast.12), calls=%async_computation.5 | async-start | bytes 4194304 | tf_op jit(solution)/shard_map/all_to_all | solution.py:23
  34.2 18.2 %collective-permute-start = (bf16[16,1024]{1,0:T(8,128)(2,1)S(1)}, bf16[16,1024]{1,0:T(8,128)(2,1)S(1)}, u32[]{:S(2)}, u32[]{:S(2)}) collective-permute-start(bf16[16,1024]{1,0:T(8,128)(2,1)S(1)} %get-tuple-element.56), channel_id=1, source_target_pairs={{0,64},{64,0},{128,192},{192,128},{256,320},{320,256},{384,448},{4... | collective-permute-start | bytes 98312 | tf_op jit(solution)/shard_map/ppermute | solution.py:644
  37.1 45.6 %collective-permute-start.1 = (bf16[16,1024]{1,0:T(8,128)(2,1)S(1)}, bf16[16,1024]{1,0:T(8,128)(2,1)S(1)}, u32[]{:S(2)}, u32[]{:S(2)}) collective-permute-start(bf16[16,1024]{1,0:T(8,128)(2,1)S(1)} %get-tuple-element.57), channel_id=1, source_target_pairs={{0,128},{64,192},{128,0},{192,64},{256,384},{320,448},{384,256},{4... | collective-permute-start | bytes 98312 | tf_op jit(solution)/shard_map/ppermute | solution.py:644
  41.2 46.5 %collective-permute-start.2 = (bf16[16,1024]{1,0:T(8,128)(2,1)S(1)}, bf16[16,1024]{1,0:T(8,128)(2,1)S(1)}, u32[]{:S(2)}, u32[]{:S(2)}) collective-permute-start(bf16[16,1024]{1,0:T(8,128)(2,1)S(1)} %get-tuple-element.58), channel_id=1, source_target_pairs={{0,192},{64,128},{128,64},{192,0},{256,448},{320,384},{384,320},{4... | collective-permute-start | bytes 98312 | tf_op jit(solution)/shard_map/ppermute | solution.py:644
  43.5 44.2 %collective-permute-start.3 = (bf16[16,1024]{1,0:T(8,128)(2,1)S(1)}, bf16[16,1024]{1,0:T(8,128)(2,1)S(1)}, u32[]{:S(2)}, u32[]{:S(2)}) collective-permute-start(bf16[16,1024]{1,0:T(8,128)(2,1)S(1)} %get-tuple-element.59), channel_id=1, source_target_pairs={{0,256},{64,320},{128,384},{192,448},{256,0},{320,64},{384,128},{4... | collective-permute-start | bytes 98312 | tf_op jit(solution)/shard_map/ppermute | solution.py:644
  50.4 39.2 %collective-permute-start.4 = (bf16[16,1024]{1,0:T(8,128)(2,1)S(1)}, bf16[16,1024]{1,0:T(8,128)(2,1)S(1)}, u32[]{:S(2)}, u32[]{:S(2)}) collective-permute-start(bf16[16,1024]{1,0:T(8,128)(2,1)S(1)} %get-tuple-element.60), channel_id=1, source_target_pairs={{0,320},{64,256},{128,448},{192,384},{256,64},{320,0},{384,192},{4... | collective-permute-start | bytes 98312 | tf_op jit(solution)/shard_map/ppermute | solution.py:644
  52.4 37.3 %collective-permute-start.5 = (bf16[16,1024]{1,0:T(8,128)(2,1)S(1)}, bf16[16,1024]{1,0:T(8,128)(2,1)S(1)}, u32[]{:S(2)}, u32[]{:S(2)}) collective-permute-start(bf16[16,1024]{1,0:T(8,128)(2,1)S(1)} %get-tuple-element.61), channel_id=1, source_target_pairs={{0,384},{64,448},{128,256},{192,320},{256,128},{320,192},{384,0},{... | collective-permute-start | bytes 98312 | tf_op jit(solution)/shard_map/ppermute | solution.py:644
  82.8 6.9 %collective-permute-start.6 = (bf16[16,1024]{1,0:T(8,128)(2,1)S(1)}, bf16[16,1024]{1,0:T(8,128)(2,1)S(1)}, u32[]{:S(2)}, u32[]{:S(2)}) collective-permute-start(bf16[16,1024]{1,0:T(8,128)(2,1)S(1)} %get-tuple-element.62), channel_id=1, source_target_pairs={{0,448},{64,384},{128,320},{192,256},{256,192},{320,128},{384,64},... | collective-permute-start | bytes 98312 | tf_op jit(solution)/shard_map/ppermute | solution.py:644
  85.0 4.7 %copy-start.2 = (bf16[8,64,1024]{2,1,0:T(8,128)(2,1)S(1)}, bf16[8,64,1024]{2,1,0:T(8,128)(2,1)}, u32[]{:S(2)}) copy-start(bf16[8,64,1024]{2,1,0:T(8,128)(2,1)} %refs_8_.1) | copy-start | bytes 3145732
  87.7 17.0 %copy-start = (bf16[1024,1024]{1,0:T(8,128)(2,1)S(1)}, bf16[1024,1024]{1,0:T(8,128)(2,1)}, u32[]{:S(2)}) copy-start(bf16[1024,1024]{1,0:T(8,128)(2,1)} %w_ref.1) | copy-start | bytes 6291460
  90.8 9.0 %collective-permute-start.7 = (bf16[288,128]{1,0:T(8,128)(2,1)S(1)}, bf16[288,128]{1,0:T(8,128)(2,1)S(1)}, u32[]{:S(2)}, u32[]{:S(2)}) collective-permute-start(bf16[288,128]{1,0:T(8,128)(2,1)S(1)} %get-tuple-element.64), channel_id=1, source_target_pairs={{0,1},{1,0},{2,3},{3,2},{4,5},{5,4},{6,7},{7,6},{8,9},{9,8},{10,11... | collective-permute-start | bytes 221192 | tf_op jit(solution)/shard_map/ppermute | solution.py:579
  100.6 10.8 %all-to-all-start.6 = ((bf16[4,288,128]{2,1,0:T(8,128)(2,1)}), bf16[4,288,128]{2,1,0:T(8,128)(2,1)S(1)}, u32[]{:S(2)}, u32[]{:S(2)}) async-start(bf16[4,288,128]{2,1,0:T(8,128)(2,1)} %broadcast_in_dim.4), calls=%async_computation.6 | async-start | bytes 589824 | tf_op jit(solution)/shard_map/all_to_all | solution.py:23
  104.6 9.6 %copy-start.4 = (bf16[8,64,128]{2,1,0:T(8,128)(2,1)S(1)}, bf16[8,64,128]{2,1,0:T(8,128)(2,1)}, u32[]{:S(2)}) copy-start(bf16[8,64,128]{2,1,0:T(8,128)(2,1)} %up_ref.1) | copy-start | bytes 393220
  108.9 18.7 %collective-permute-start.8 = (bf16[4,768,128]{2,1,0:T(8,128)(2,1)}, bf16[4,768,128]{2,1,0:T(8,128)(2,1)S(1)}, u32[]{:S(2)}, u32[]{:S(2)}) collective-permute-start(bf16[4,768,128]{2,1,0:T(8,128)(2,1)} %get-tuple-element.68), channel_id=1, source_target_pairs={{0,1},{1,0},{2,3},{3,2},{4,5},{5,4},{6,7},{7,6},{8,9},{9,8},{10,11... | collective-permute-start | bytes 2359304 | tf_op jit(solution)/shard_map/ppermute | solution.py:617
  115.7 31.3 %all-to-all-start.7 = ((bf16[64,24,128]{2,1,0:T(8,128)(2,1)}), bf16[64,24,128]{2,1,0:T(8,128)(2,1)S(1)}, u32[]{:S(2)}, u32[]{:S(2)}) async-start(bf16[64,24,128]{2,1,0:T(8,128)(2,1)} %bitcast.14), calls=%async_computation.7 | async-start | bytes 786432 | tf_op jit(solution)/shard_map/all_to_all | solution.py:23
  127.7 9.8 %collective-permute-start.9 = (bf16[768,128]{1,0:T(8,128)(2,1)S(1)}, bf16[768,128]{1,0:T(8,128)(2,1)S(1)}, u32[]{:S(2)}, u32[]{:S(2)}) collective-permute-start(bf16[768,128]{1,0:T(8,128)(2,1)S(1)} %get-tuple-element.69), channel_id=1, source_target_pairs={{0,2},{2,0},{4,6},{6,4},{1,3},{3,1},{5,7},{7,5},{8,10},{10,8},{12,... | collective-permute-start | bytes 589832 | tf_op jit(solution)/shard_map/ppermute | solution.py:644
  130.8 10.9 %collective-permute-start.10 = (bf16[768,128]{1,0:T(8,128)(2,1)S(1)}, bf16[768,128]{1,0:T(8,128)(2,1)S(1)}, u32[]{:S(2)}, u32[]{:S(2)}) collective-permute-start(bf16[768,128]{1,0:T(8,128)(2,1)S(1)} %get-tuple-element.70), channel_id=1, source_target_pairs={{0,4},{2,6},{4,0},{6,2},{1,5},{3,7},{5,1},{7,3},{8,12},{10,14},{12... | collective-permute-start | bytes 589832 | tf_op jit(solution)/shard_map/ppermute | solution.py:644
  135.1 11.8 %collective-permute-start.11 = (bf16[768,128]{1,0:T(8,128)(2,1)S(1)}, bf16[768,128]{1,0:T(8,128)(2,1)S(1)}, u32[]{:S(2)}, u32[]{:S(2)}) collective-permute-start(bf16[768,128]{1,0:T(8,128)(2,1)S(1)} %get-tuple-element.71), channel_id=1, source_target_pairs={{0,6},{2,4},{4,2},{6,0},{1,7},{3,5},{5,3},{7,1},{8,14},{10,12},{12... | collective-permute-start | bytes 589832 | tf_op jit(solution)/shard_map/ppermute | solution.py:644
  149.4 0.7 copy-start.6

commit v11 on v10

--- a/solution.py
+++ b/solution.py
@@ -253,7 +253,7 @@
 
 def place_main(ids_row, seen, tokens, slots):
     rows, width = tokens.shape
-    tile = 256
+    tile = 512
 
     def kernel(row_ref, seen_ref, tok_ref, out_ref):
         at_row = jnp.where(seen_ref[...] < MAIN, row_ref[...] * MAIN + seen_ref[...], -1)
@@ -279,13 +279,13 @@
 
 def bucket(rows_of, key, key_col, code, valid, flag, store):
     n = key.shape[1]
-    width = rows_of.shape[1]
     q = count_before(key, key_col)
     fits = valid & (q < SIDE - 1)
     lost = jnp.max(jnp.where(valid & (q >= SIDE - 1), 1.0, 0.0), axis=1, keepdims=True)
     flag = jnp.maximum(flag, lost)
     pick = pick_rows(jnp.where(fits, key * SIDE + q, -1), 8 * SIDE)
-    data = jnp.dot(pick, rows_of, preferred_element_type=jnp.float32)
+    data = jnp.dot(pick, rows_of(), preferred_element_type=jnp.float32)
+    width = data.shape[1]
     which = lax.broadcasted_iota(jnp.int32, (8, n), 0)
     owned = jnp.where(fits & (which == key), (code + 1).astype(jnp.float32), 0.0)
     place = lax.broadcasted_iota(jnp.int32, (128, n), 0)
@@ -322,7 +322,9 @@
 def side_first(ids_row, tokens):
     rows, width = tokens.shape
 
-    def kernel(row_ref, tok_ref, out_ref, seen_ref):
+    def kernel(row_ref, tok_ref, out_ref, seen_ref, buffer_ref, sem):
+        load = pltpu.make_async_copy(tok_ref, buffer_ref, sem)
+        load.start()
         row = row_ref[...]
         seen = count_before(row, to_col(row))
         seen_ref[...] = seen
@@ -331,16 +333,22 @@
         third = seen >= MAIN
         key = home % 8
 
+        def rows_of():
+            load.wait()
+            return buffer_ref[...]
+
         def store(k, block):
             out_ref[k * SIDE : (k + 1) * SIDE, :] = block
 
         bucket(
-            tok_ref[...], key, to_col(jnp.where(third, key, -1)), home // 8 * 8 + spot, third,
+            rows_of, key, to_col(jnp.where(third, key, -1)), home // 8 * 8 + spot, third,
             jnp.zeros((1, 1), jnp.float32), store,
         )
 
     return pl.pallas_call(
         kernel,
+        in_specs=[pl.BlockSpec(memory_space=pltpu.VMEM), pl.BlockSpec(memory_space=pl.ANY)],
+        scratch_shapes=[pltpu.VMEM((rows, width), tokens.dtype), pltpu.SemaphoreType.DMA],
         out_shape=[
             jax.ShapeDtypeStruct((8 * SIDE, width), jnp.bfloat16),
             jax.ShapeDtypeStruct((1, rows), jnp.int32),
@@ -364,7 +372,7 @@
         def store(k, block):
             block_ref[k] = block
 
-        bucket(in_ref[...], key, to_col(key), from_y * 8 + code % 8, valid, flag, store)
+        bucket(lambda: in_ref[...], key, to_col(key), from_y * 8 + code % 8, valid, flag, store)
         for k in range(8):
             out_refs[k][...] = block_ref[at_ref[0] ^ k]
 
@@ -396,7 +404,7 @@
     slots, width = arrived.shape
     here, rank, _ = down.shape
     half = slots // 2
-    tile = 256
+    tile = half
     pair = 2 * rank
 
     def kernel(in_ref, down_ref, out_ref):

time: 151 us -> 152 us (level)
  transfers between devices with their start and end apart: 16 -> 16, of which waited for: 5 -> 5; matrix products, arithmetic and copies ran while one was open for 0% -> 0% of each run, Pallas kernels for 9% -> 8%
where the time goes in v11:
time: 152 us; the launch traced here: 151 us
  starting transfers between devices  108 us (71%)
  Pallas kernels  18.8 us (12%)
  waiting for transfers between devices  18.8 us (12%)
  blocking collectives  2.73 us (2%)
    ppermute x10, starting transfers between devices, xor_sends(): lax.ppermute(pieces[k], axis, [(i, i ^ k) for i in range(size)])  60.2 us
    all_to_all x4, starting transfers between devices, swap(): return lax.all_to_all(x, axes, split_axis=0, concat_axis=0, tiled=True)  36.7 us
    ppermute x10, waiting for transfers between devices, xor_sends(): lax.ppermute(pieces[k], axis, [(i, i ^ k) for i in range(size)])  11.4 us
    ppermute x1, starting transfers between devices, low_of_pairs(): lax.ppermute(other, TENSOR[1], [(0, 1), (1, 0)]).astype(jnp.float32)  8.1 us
    all_to_all x4, waiting for transfers between devices, swap(): return lax.all_to_all(x, axes, split_axis=0, concat_axis=0, tiled=True)  6.47 us
    pallas_call x1, Pallas kernels, value_pieces(): pl.pallas_call(kernel, in_specs=[pl.BlockSpec(memory_space=pltpu.SMEM), p...  4.24 us
    pallas_call x1, Pallas kernels, side_first(): pl.pallas_call(kernel, in_specs=[pl.BlockSpec(memory_space=pltpu.VMEM), p...  3.84 us
  transfers between devices with their start and end apart: 16, of which 5 were waited for; matrix products, arithmetic and copies ran while one was open for 0% of the time, Pallas kernels for 8%

profile of v11, /device:TPU:1, one launch (start us, length us, event | category | flops | bytes accessed | tf_op | source)
XLA Modules:
  0.0 150.6 jit_solution(1709214677588184667)
XLA Ops:
  0.0 0.0 copy-start.1
  0.0 0.0 copy-start.5
  0.0 3.8 %side_first.1 = (bf16[128,1024]{1,0:T(8,128)(2,1)}, s32[1,768]{1,0:T(1,128)S(1)}) custom-call(s32[1,768]{1,0:T(1,128)} %bitcast.28, bf16[768,1024]{1,0:T(8,128)(2,1)} %tok_ref.5), custom_call_target="tpu_custom_call" | custom-call | tf_op jit(solution)/shard_map/side_first/pallas_call | solution.py:348
  3.9 7.7 %all-to-all-start.4 = ((bf16[8,16,1024]{2,1,0:T(8,128)(2,1)}), bf16[8,16,1024]{2,1,0:T(8,128)(2,1)S(1)}, u32[]{:S(2)}, u32[]{:S(2)}) async-start(bf16[8,16,1024]{2,1,0:T(8,128)(2,1)} %bitcast.10), calls=%async_computation.4 | async-start | bytes 524288 | tf_op jit(solution)/shard_map/all_to_all | solution.py:23
  11.5 0.0 copy-done.1
  11.5 0.0 copy-done.5
  11.5 3.0 %place_main.1 = bf16[1024,1024]{1,0:T(8,128)(2,1)} custom-call(s32[1,768]{1,0:T(1,128)S(1)} %bitcast.29, s32[1,768]{1,0:T(1,128)S(1)} %get-tuple-element.53.seen_ref, bf16[768,1024]{1,0:T(8,128)(2,1)S(1)} %copy-done.1), custom_call_target="tpu_custom_call" | custom-call | tf_op jit(solution)/shard_map/place_main/pallas_call | solution.py:265
  14.5 6.5 %all-to-all-done.4 = bf16[8,16,1024]{2,1,0:T(8,128)(2,1)S(1)} async-done(((bf16[8,16,1024]{2,1,0:T(8,128)(2,1)}), bf16[8,16,1024]{2,1,0:T(8,128)(2,1)S(1)}, u32[]{:S(2)}, u32[]{:S(2)}) %all-to-all-start.4) | async-done | bytes 262176 | tf_op jit(solution)/shard_map/all_to_all | solution.py:23
  20.9 13.2 %all-to-all-start.5 = ((bf16[64,16,1024]{2,1,0:T(8,128)(2,1)}), bf16[64,16,1024]{2,1,0:T(8,128)(2,1)S(1)}, u32[]{:S(2)}, u32[]{:S(2)}) async-start(bf16[64,16,1024]{2,1,0:T(8,128)(2,1)} %bitcast.12), calls=%async_computation.5 | async-start | bytes 4194304 | tf_op jit(solution)/shard_map/all_to_all | solution.py:23
  34.2 0.5 side_second.1
  34.7 2.9 %collective-permute-start = (bf16[16,1024]{1,0:T(8,128)(2,1)S(1)}, bf16[16,1024]{1,0:T(8,128)(2,1)S(1)}, u32[]{:S(2)}, u32[]{:S(2)}) collective-permute-start(bf16[16,1024]{1,0:T(8,128)(2,1)S(1)} %get-tuple-element.56), channel_id=1, source_target_pairs={{0,64},{64,0},{128,192},{192,128},{256,320},{320,256},{384,448},{4... | collective-permute-start | bytes 98312 | tf_op jit(solution)/shard_map/ppermute | solution.py:652
  37.6 4.0 %collective-permute-start.1 = (bf16[16,1024]{1,0:T(8,128)(2,1)S(1)}, bf16[16,1024]{1,0:T(8,128)(2,1)S(1)}, u32[]{:S(2)}, u32[]{:S(2)}) collective-permute-start(bf16[16,1024]{1,0:T(8,128)(2,1)S(1)} %get-tuple-element.57), channel_id=1, source_target_pairs={{0,128},{64,192},{128,0},{192,64},{256,384},{320,448},{384,256},{4... | collective-permute-start | bytes 98312 | tf_op jit(solution)/shard_map/ppermute | solution.py:652
  41.7 2.3 %collective-permute-start.2 = (bf16[16,1024]{1,0:T(8,128)(2,1)S(1)}, bf16[16,1024]{1,0:T(8,128)(2,1)S(1)}, u32[]{:S(2)}, u32[]{:S(2)}) collective-permute-start(bf16[16,1024]{1,0:T(8,128)(2,1)S(1)} %get-tuple-element.58), channel_id=1, source_target_pairs={{0,192},{64,128},{128,64},{192,0},{256,448},{320,384},{384,320},{4... | collective-permute-start | bytes 98312 | tf_op jit(solution)/shard_map/ppermute | solution.py:652
  44.0 6.9 %collective-permute-start.3 = (bf16[16,1024]{1,0:T(8,128)(2,1)S(1)}, bf16[16,1024]{1,0:T(8,128)(2,1)S(1)}, u32[]{:S(2)}, u32[]{:S(2)}) collective-permute-start(bf16[16,1024]{1,0:T(8,128)(2,1)S(1)} %get-tuple-element.59), channel_id=1, source_target_pairs={{0,256},{64,320},{128,384},{192,448},{256,0},{320,64},{384,128},{4... | collective-permute-start | bytes 98312 | tf_op jit(solution)/shard_map/ppermute | solution.py:652
  50.9 1.9 %collective-permute-start.4 = (bf16[16,1024]{1,0:T(8,128)(2,1)S(1)}, bf16[16,1024]{1,0:T(8,128)(2,1)S(1)}, u32[]{:S(2)}, u32[]{:S(2)}) collective-permute-start(bf16[16,1024]{1,0:T(8,128)(2,1)S(1)} %get-tuple-element.60), channel_id=1, source_target_pairs={{0,320},{64,256},{128,448},{192,384},{256,64},{320,0},{384,192},{4... | collective-permute-start | bytes 98312 | tf_op jit(solution)/shard_map/ppermute | solution.py:652
  52.9 0.0 collective-permute-done.refs_1_
  52.9 30.4 %collective-permute-start.5 = (bf16[16,1024]{1,0:T(8,128)(2,1)S(1)}, bf16[16,1024]{1,0:T(8,128)(2,1)S(1)}, u32[]{:S(2)}, u32[]{:S(2)}) collective-permute-start(bf16[16,1024]{1,0:T(8,128)(2,1)S(1)} %get-tuple-element.61), channel_id=1, source_target_pairs={{0,384},{64,448},{128,256},{192,320},{256,128},{320,192},{384,0},{... | collective-permute-start | bytes 98312 | tf_op jit(solution)/shard_map/ppermute | solution.py:652
  83.3 0.0 collective-permute-done.1.refs_2_
  83.3 2.1 %collective-permute-start.6 = (bf16[16,1024]{1,0:T(8,128)(2,1)S(1)}, bf16[16,1024]{1,0:T(8,128)(2,1)S(1)}, u32[]{:S(2)}, u32[]{:S(2)}) collective-permute-start(bf16[16,1024]{1,0:T(8,128)(2,1)S(1)} %get-tuple-element.62), channel_id=1, source_target_pairs={{0,448},{64,384},{128,320},{192,256},{256,192},{320,128},{384,64},... | collective-permute-start | bytes 98312 | tf_op jit(solution)/shard_map/ppermute | solution.py:652
  85.4 0.1 pad_add_fusion.at_ref
  85.5 0.0 all-to-all-done.5
  85.5 0.0 copy-start.2
  85.5 2.7 %down_main.1.refs_9_ = bf16[512,128]{1,0:T(8,128)(2,1)S(1)} custom-call(bf16[1024,1024]{1,0:T(8,128)(2,1)S(1)} %bitcast.20, bf16[8,64,1024]{2,1,0:T(8,128)(2,1)} %refs_8_.1), custom_call_target="tpu_custom_call" | custom-call | tf_op jit(solution)/shard_map/down_main/pallas_call | solution.py:422
  88.2 0.0 copy-start
  88.2 0.0 collective-permute-done.2.refs_3_
  88.2 0.0 collective-permute-done.3.refs_4_
  88.2 2.0 %collective-permute-done.4.refs_5_ = bf16[16,1024]{1,0:T(8,128)(2,1)S(1)} collective-permute-done((bf16[16,1024]{1,0:T(8,128)(2,1)S(1)}, bf16[16,1024]{1,0:T(8,128)(2,1)S(1)}, u32[]{:S(2)}, u32[]{:S(2)}) %collective-permute-start.4) | collective-permute-done | bytes 32800 | tf_op jit(solution)/shard_map/ppermute | solution.py:652
  90.2 0.0 collective-permute-done.5.refs_6_
  90.2 0.0 collective-permute-done.6.refs_7_
  90.2 0.0 copy-done.2
  90.2 1.1 side_low.1
  91.3 8.1 %collective-permute-start.7 = (bf16[288,128]{1,0:T(8,128)(2,1)S(1)}, bf16[288,128]{1,0:T(8,128)(2,1)S(1)}, u32[]{:S(2)}, u32[]{:S(2)}) collective-permute-start(bf16[288,128]{1,0:T(8,128)(2,1)S(1)} %get-tuple-element.64), channel_id=1, source_target_pairs={{0,1},{1,0},{2,3},{3,2},{4,5},{5,4},{6,7},{7,6},{8,9},{9,8},{10,11... | collective-permute-start | bytes 221192 | tf_op jit(solution)/shard_map/ppermute | solution.py:587
  99.4 0.9 collective-permute-done.7
  100.3 0.8 broadcast_in_dim.4
  101.1 4.0 %all-to-all-start.6 = ((bf16[4,288,128]{2,1,0:T(8,128)(2,1)}), bf16[4,288,128]{2,1,0:T(8,128)(2,1)S(1)}, u32[]{:S(2)}, u32[]{:S(2)}) async-start(bf16[4,288,128]{2,1,0:T(8,128)(2,1)} %broadcast_in_dim.4), calls=%async_computation.6 | async-start | bytes 589824 | tf_op jit(solution)/shard_map/all_to_all | solution.py:23
  105.1 0.0 copy-done
  105.1 0.0 copy-start.4
  105.1 4.2 %value_pieces.1 = (bf16[4,768,128]{2,1,0:T(8,128)(2,1)S(1)}, bf16[4,768,128]{2,1,0:T(8,128)(2,1)}) custom-call(s32[1]{0:T(128)} %bitcast.16.at_ref, bf16[768,1024]{1,0:T(8,128)(2,1)} %tok_ref.5, bf16[1024,1024]{1,0:T(8,128)(2,1)S(1)} %copy-done), custom_call_target="tpu_custom_call" | custom-call | tf_op jit(solution)/shard_map/value_pieces/pallas_call | solution.py:89
  109.4 2.5 %collective-permute-start.8 = (bf16[4,768,128]{2,1,0:T(8,128)(2,1)}, bf16[4,768,128]{2,1,0:T(8,128)(2,1)S(1)}, u32[]{:S(2)}, u32[]{:S(2)}) collective-permute-start(bf16[4,768,128]{2,1,0:T(8,128)(2,1)} %get-tuple-element.68), channel_id=1, source_target_pairs={{0,1},{1,0},{2,3},{3,2},{4,5},{5,4},{6,7},{7,6},{8,9},{9,8},{10,11... | collective-permute-start | bytes 2359304 | tf_op jit(solution)/shard_map/ppermute | solution.py:625
  111.9 0.0 all-to-all-done.6.in_ref
  112.0 2.7 %all_gather.3.low_ref = bf16[576,128]{1,0:T(8,128)(2,1)S(1)} all-gather(bf16[288,128]{1,0:T(8,128)(2,1)S(1)} %chip_sum.1), channel_id=1, replica_groups=mesh['z'=8,'y'=8,'tensor_0'=4,'tensor_1'=2] {'tensor_1'}, dimensions={0}, use_global_device_ids=true | all-gather | bytes 221184 | tf_op jit(solution)/shard_map/all_gather | solution.py:591
  114.7 0.0 copy-done.4
  114.7 1.5 %up_main.1 = bf16[1536,128]{1,0:T(8,128)(2,1)} custom-call(bf16[576,128]{1,0:T(8,128)(2,1)S(1)} %all_gather.3.low_ref, s32[1,128]{1,0:T(1,128)S(1)} %get-tuple-element.65.slot_ref, f32[8,128]{1,0:T(8,128)S(1)} %get-tuple-element.66.flag_ref, bf16[8,64,128]{2,1,0:T(8,128)(2,1)S(1)} %copy-done.4), custom_call_target="tpu_custom_call" | custom-call | tf_op jit(solution)/shard_map/up_main/pallas_call | solution.py:526
  116.2 11.8 %all-to-all-start.7 = ((bf16[64,24,128]{2,1,0:T(8,128)(2,1)}), bf16[64,24,128]{2,1,0:T(8,128)(2,1)S(1)}, u32[]{:S(2)}, u32[]{:S(2)}) async-start(bf16[64,24,128]{2,1,0:T(8,128)(2,1)} %bitcast.14), calls=%async_computation.7 | async-start | bytes 786432 | tf_op jit(solution)/shard_map/all_to_all | solution.py:23
  128.0 0.0 collective-permute-done.8.other_ref
  128.1 0.1 pair_sum.1
  128.2 3.1 %collective-permute-start.9 = (bf16[768,128]{1,0:T(8,128)(2,1)S(1)}, bf16[768,128]{1,0:T(8,128)(2,1)S(1)}, u32[]{:S(2)}, u32[]{:S(2)}) collective-permute-start(bf16[768,128]{1,0:T(8,128)(2,1)S(1)} %get-tuple-element.69), channel_id=1, source_target_pairs={{0,2},{2,0},{4,6},{6,4},{1,3},{3,1},{5,7},{7,5},{8,10},{10,8},{12,... | collective-permute-start | bytes 589832 | tf_op jit(solution)/shard_map/ppermute | solution.py:652
  131.3 4.3 %collective-permute-start.10 = (bf16[768,128]{1,0:T(8,128)(2,1)S(1)}, bf16[768,128]{1,0:T(8,128)(2,1)S(1)}, u32[]{:S(2)}, u32[]{:S(2)}) collective-permute-start(bf16[768,128]{1,0:T(8,128)(2,1)S(1)} %get-tuple-element.70), channel_id=1, source_target_pairs={{0,4},{2,6},{4,0},{6,2},{1,5},{3,7},{5,1},{7,3},{8,12},{10,14},{12... | collective-permute-start | bytes 589832 | tf_op jit(solution)/shard_map/ppermute | solution.py:652
  135.6 2.2 %collective-permute-start.11 = (bf16[768,128]{1,0:T(8,128)(2,1)S(1)}, bf16[768,128]{1,0:T(8,128)(2,1)S(1)}, u32[]{:S(2)}, u32[]{:S(2)}) collective-permute-start(bf16[768,128]{1,0:T(8,128)(2,1)S(1)} %get-tuple-element.71), channel_id=1, source_target_pairs={{0,6},{2,4},{4,2},{6,0},{1,7},{3,5},{5,3},{7,1},{8,14},{10,12},{12... | collective-permute-start | bytes 589832 | tf_op jit(solution)/shard_map/ppermute | solution.py:652
  137.8 0.2 answer_slots.1.at_ref
  138.0 0.0 collective-permute-done.9.refs_0_
  138.0 4.2 %collective-permute-done.10.refs_1_ = bf16[768,128]{1,0:T(8,128)(2,1)S(1)} collective-permute-done((bf16[768,128]{1,0:T(8,128)(2,1)S(1)}, bf16[768,128]{1,0:T(8,128)(2,1)S(1)}, u32[]{:S(2)}, u32[]{:S(2)}) %collective-permute-start.10) | collective-permute-done | bytes 196640 | tf_op jit(solution)/shard_map/ppermute | solution.py:652
  142.2 5.2 %collective-permute-done.11.refs_2_ = bf16[768,128]{1,0:T(8,128)(2,1)S(1)} collective-permute-done((bf16[768,128]{1,0:T(8,128)(2,1)S(1)}, bf16[768,128]{1,0:T(8,128)(2,1)S(1)}, u32[]{:S(2)}, u32[]{:S(2)}) %collective-permute-start.11) | collective-permute-done | bytes 196640 | tf_op jit(solution)/shard_map/ppermute | solution.py:652
  147.4 0.1 base_sum.1.base_ref
  147.6 0.0 all-to-all-done.7
  147.6 1.5 take_main.1
  149.7 0.2 conditional.1
  150.0 0.0 copy-start.6
  150.0 0.7 copy-done.6
  (2 shorter events, 0.1 us)
Async XLA Ops:
  0.0 11.5 %copy-start.1 = (bf16[768,1024]{1,0:T(8,128)(2,1)S(1)}, bf16[768,1024]{1,0:T(8,128)(2,1)}, u32[]{:S(2)}) copy-start(bf16[768,1024]{1,0:T(8,128)(2,1)} %tok_ref.5) | copy-start | bytes 4718596
  0.0 11.5 %copy-start.5 = (s32[768,1]{0,1:T(1,128)S(1)}, s32[768,1]{0,1:T(1,128)}, u32[]{:S(2)}) copy-start(s32[768,1]{0,1:T(1,128)} %param.11) | copy-start | bytes 9220
  3.9 17.1 %all-to-all-start.4 = ((bf16[8,16,1024]{2,1,0:T(8,128)(2,1)}), bf16[8,16,1024]{2,1,0:T(8,128)(2,1)S(1)}, u32[]{:S(2)}, u32[]{:S(2)}) async-start(bf16[8,16,1024]{2,1,0:T(8,128)(2,1)} %bitcast.10), calls=%async_computation.4 | async-start | bytes 524288 | tf_op jit(solution)/shard_map/all_to_all | solution.py:23
  20.9 64.5 %all-to-all-start.5 = ((bf16[64,16,1024]{2,1,0:T(8,128)(2,1)}), bf16[64,16,1024]{2,1,0:T(8,128)(2,1)S(1)}, u32[]{:S(2)}, u32[]{:S(2)}) async-start(bf16[64,16,1024]{2,1,0:T(8,128)(2,1)} %bitcast.12), calls=%async_computation.5 | async-start | bytes 4194304 | tf_op jit(solution)/shard_map/all_to_all | solution.py:23
  34.7 18.2 %collective-permute-start = (bf16[16,1024]{1,0:T(8,128)(2,1)S(1)}, bf16[16,1024]{1,0:T(8,128)(2,1)S(1)}, u32[]{:S(2)}, u32[]{:S(2)}) collective-permute-start(bf16[16,1024]{1,0:T(8,128)(2,1)S(1)} %get-tuple-element.56), channel_id=1, source_target_pairs={{0,64},{64,0},{128,192},{192,128},{256,320},{320,256},{384,448},{4... | collective-permute-start | bytes 98312 | tf_op jit(solution)/shard_map/ppermute | solution.py:652
  37.6 45.6 %collective-permute-start.1 = (bf16[16,1024]{1,0:T(8,128)(2,1)S(1)}, bf16[16,1024]{1,0:T(8,128)(2,1)S(1)}, u32[]{:S(2)}, u32[]{:S(2)}) collective-permute-start(bf16[16,1024]{1,0:T(8,128)(2,1)S(1)} %get-tuple-element.57), channel_id=1, source_target_pairs={{0,128},{64,192},{128,0},{192,64},{256,384},{320,448},{384,256},{4... | collective-permute-start | bytes 98312 | tf_op jit(solution)/shard_map/ppermute | solution.py:652
  41.7 46.5 %collective-permute-start.2 = (bf16[16,1024]{1,0:T(8,128)(2,1)S(1)}, bf16[16,1024]{1,0:T(8,128)(2,1)S(1)}, u32[]{:S(2)}, u32[]{:S(2)}) collective-permute-start(bf16[16,1024]{1,0:T(8,128)(2,1)S(1)} %get-tuple-element.58), channel_id=1, source_target_pairs={{0,192},{64,128},{128,64},{192,0},{256,448},{320,384},{384,320},{4... | collective-permute-start | bytes 98312 | tf_op jit(solution)/shard_map/ppermute | solution.py:652
  44.0 44.2 %collective-permute-start.3 = (bf16[16,1024]{1,0:T(8,128)(2,1)S(1)}, bf16[16,1024]{1,0:T(8,128)(2,1)S(1)}, u32[]{:S(2)}, u32[]{:S(2)}) collective-permute-start(bf16[16,1024]{1,0:T(8,128)(2,1)S(1)} %get-tuple-element.59), channel_id=1, source_target_pairs={{0,256},{64,320},{128,384},{192,448},{256,0},{320,64},{384,128},{4... | collective-permute-start | bytes 98312 | tf_op jit(solution)/shard_map/ppermute | solution.py:652
  50.9 39.2 %collective-permute-start.4 = (bf16[16,1024]{1,0:T(8,128)(2,1)S(1)}, bf16[16,1024]{1,0:T(8,128)(2,1)S(1)}, u32[]{:S(2)}, u32[]{:S(2)}) collective-permute-start(bf16[16,1024]{1,0:T(8,128)(2,1)S(1)} %get-tuple-element.60), channel_id=1, source_target_pairs={{0,320},{64,256},{128,448},{192,384},{256,64},{320,0},{384,192},{4... | collective-permute-start | bytes 98312 | tf_op jit(solution)/shard_map/ppermute | solution.py:652
  52.9 37.3 %collective-permute-start.5 = (bf16[16,1024]{1,0:T(8,128)(2,1)S(1)}, bf16[16,1024]{1,0:T(8,128)(2,1)S(1)}, u32[]{:S(2)}, u32[]{:S(2)}) collective-permute-start(bf16[16,1024]{1,0:T(8,128)(2,1)S(1)} %get-tuple-element.61), channel_id=1, source_target_pairs={{0,384},{64,448},{128,256},{192,320},{256,128},{320,192},{384,0},{... | collective-permute-start | bytes 98312 | tf_op jit(solution)/shard_map/ppermute | solution.py:652
  83.3 6.9 %collective-permute-start.6 = (bf16[16,1024]{1,0:T(8,128)(2,1)S(1)}, bf16[16,1024]{1,0:T(8,128)(2,1)S(1)}, u32[]{:S(2)}, u32[]{:S(2)}) collective-permute-start(bf16[16,1024]{1,0:T(8,128)(2,1)S(1)} %get-tuple-element.62), channel_id=1, source_target_pairs={{0,448},{64,384},{128,320},{192,256},{256,192},{320,128},{384,64},... | collective-permute-start | bytes 98312 | tf_op jit(solution)/shard_map/ppermute | solution.py:652
  85.5 4.7 %copy-start.2 = (bf16[8,64,1024]{2,1,0:T(8,128)(2,1)S(1)}, bf16[8,64,1024]{2,1,0:T(8,128)(2,1)}, u32[]{:S(2)}) copy-start(bf16[8,64,1024]{2,1,0:T(8,128)(2,1)} %refs_8_.1) | copy-start | bytes 3145732
  88.2 17.0 %copy-start = (bf16[1024,1024]{1,0:T(8,128)(2,1)S(1)}, bf16[1024,1024]{1,0:T(8,128)(2,1)}, u32[]{:S(2)}) copy-start(bf16[1024,1024]{1,0:T(8,128)(2,1)} %w_ref.1) | copy-start | bytes 6291460
  91.3 9.0 %collective-permute-start.7 = (bf16[288,128]{1,0:T(8,128)(2,1)S(1)}, bf16[288,128]{1,0:T(8,128)(2,1)S(1)}, u32[]{:S(2)}, u32[]{:S(2)}) collective-permute-start(bf16[288,128]{1,0:T(8,128)(2,1)S(1)} %get-tuple-element.64), channel_id=1, source_target_pairs={{0,1},{1,0},{2,3},{3,2},{4,5},{5,4},{6,7},{7,6},{8,9},{9,8},{10,11... | collective-permute-start | bytes 221192 | tf_op jit(solution)/shard_map/ppermute | solution.py:587
  101.1 10.8 %all-to-all-start.6 = ((bf16[4,288,128]{2,1,0:T(8,128)(2,1)}), bf16[4,288,128]{2,1,0:T(8,128)(2,1)S(1)}, u32[]{:S(2)}, u32[]{:S(2)}) async-start(bf16[4,288,128]{2,1,0:T(8,128)(2,1)} %broadcast_in_dim.4), calls=%async_computation.6 | async-start | bytes 589824 | tf_op jit(solution)/shard_map/all_to_all | solution.py:23
  105.1 9.6 %copy-start.4 = (bf16[8,64,128]{2,1,0:T(8,128)(2,1)S(1)}, bf16[8,64,128]{2,1,0:T(8,128)(2,1)}, u32[]{:S(2)}) copy-start(bf16[8,64,128]{2,1,0:T(8,128)(2,1)} %up_ref.1) | copy-start | bytes 393220
  109.4 18.7 %collective-permute-start.8 = (bf16[4,768,128]{2,1,0:T(8,128)(2,1)}, bf16[4,768,128]{2,1,0:T(8,128)(2,1)S(1)}, u32[]{:S(2)}, u32[]{:S(2)}) collective-permute-start(bf16[4,768,128]{2,1,0:T(8,128)(2,1)} %get-tuple-element.68), channel_id=1, source_target_pairs={{0,1},{1,0},{2,3},{3,2},{4,5},{5,4},{6,7},{7,6},{8,9},{9,8},{10,11... | collective-permute-start | bytes 2359304 | tf_op jit(solution)/shard_map/ppermute | solution.py:625
  116.2 31.3 %all-to-all-start.7 = ((bf16[64,24,128]{2,1,0:T(8,128)(2,1)}), bf16[64,24,128]{2,1,0:T(8,128)(2,1)S(1)}, u32[]{:S(2)}, u32[]{:S(2)}) async-start(bf16[64,24,128]{2,1,0:T(8,128)(2,1)} %bitcast.14), calls=%async_computation.7 | async-start | bytes 786432 | tf_op jit(solution)/shard_map/all_to_all | solution.py:23
  128.2 9.8 %collective-permute-start.9 = (bf16[768,128]{1,0:T(8,128)(2,1)S(1)}, bf16[768,128]{1,0:T(8,128)(2,1)S(1)}, u32[]{:S(2)}, u32[]{:S(2)}) collective-permute-start(bf16[768,128]{1,0:T(8,128)(2,1)S(1)} %get-tuple-element.69), channel_id=1, source_target_pairs={{0,2},{2,0},{4,6},{6,4},{1,3},{3,1},{5,7},{7,5},{8,10},{10,8},{12,... | collective-permute-start | bytes 589832 | tf_op jit(solution)/shard_map/ppermute | solution.py:652
  131.3 10.9 %collective-permute-start.10 = (bf16[768,128]{1,0:T(8,128)(2,1)S(1)}, bf16[768,128]{1,0:T(8,128)(2,1)S(1)}, u32[]{:S(2)}, u32[]{:S(2)}) collective-permute-start(bf16[768,128]{1,0:T(8,128)(2,1)S(1)} %get-tuple-element.70), channel_id=1, source_target_pairs={{0,4},{2,6},{4,0},{6,2},{1,5},{3,7},{5,1},{7,3},{8,12},{10,14},{12... | collective-permute-start | bytes 589832 | tf_op jit(solution)/shard_map/ppermute | solution.py:652
  135.6 11.8 %collective-permute-start.11 = (bf16[768,128]{1,0:T(8,128)(2,1)S(1)}, bf16[768,128]{1,0:T(8,128)(2,1)S(1)}, u32[]{:S(2)}, u32[]{:S(2)}) collective-permute-start(bf16[768,128]{1,0:T(8,128)(2,1)S(1)} %get-tuple-element.71), channel_id=1, source_target_pairs={{0,6},{2,4},{4,2},{6,0},{1,7},{3,5},{5,3},{7,1},{8,14},{10,12},{12... | collective-permute-start | bytes 589832 | tf_op jit(solution)/shard_map/ppermute | solution.py:652
  150.0 0.7 copy-start.6
